TPU v7x, 32 devices: a whole 2x2x4 slice. The times are simulated.
32 devices in a mesh: group: 8 (over z, x), ctx: 2 (over y), wshard: 2 (over core).
Axes of the slice: x: 2, y: 2, z: 4, core: 2. Of those that a mesh axis runs over, the one named last changes fastest.
Arguments:
- inputs: bfloat16 [8192, 1536], P(('group', 'ctx', 'wshard')), may hold values from -6 to 6
- out_grad: bfloat16 [8192, 1536], P(('group', 'ctx', 'wshard')), may hold values from -6 to 6
- lengths: int32 [8, 4], P('group'), may hold values from 1 to 512, 1024 in all within a row
- permutation: int32 [8, 1024], P('group'), may hold values from 0 to 1023, each once within a row
- gain_attention: float32 [1536], replicated, may hold values from 0.5 to 1.5
- query_weight: bfloat16 [1536, 768], P('wshard'), may hold values from -0.0546875 to 0.0546875
- key_weight: bfloat16 [1536, 768], P('wshard'), may hold values from -0.0546875 to 0.0546875
- value_weight: bfloat16 [1536, 768], P('wshard'), may hold values from -0.15625 to 0.15625
- out_weight: bfloat16 [768, 1536], P('wshard'), may hold values from -3.5 to 3.5
- bucket_bias: float32 [32, 12], replicated, may hold values from -4 to 4
- gain_feedforward: float32 [1536], replicated, may hold values from 0.5 to 1.5
- gate_weight: bfloat16 [1536, 3968], P('wshard'), may hold values from -0.15625 to 0.15625
- up_weight: bfloat16 [1536, 3968], P('wshard'), may hold values from -0.15625 to 0.15625
- down_weight: bfloat16 [3968, 1536], P('wshard'), may hold values from -0.09375 to 0.09375
Outputs:
- outputs: bfloat16 [8192, 1536], P(('group', 'ctx', 'wshard'))
- input_grad: bfloat16 [8192, 1536], P(('group', 'ctx', 'wshard'))
- grad_gain_attention: float32 [1536], P(('ctx', 'wshard'))
- grad_query: float32 [1536, 768], P(('ctx', 'wshard'))
- grad_key: float32 [1536, 768], P(('ctx', 'wshard'))
- grad_value: float32 [1536, 768], P(('ctx', 'wshard'))
- grad_out: float32 [768, 1536], P(('ctx', 'wshard'))
- grad_bias: float32 [32, 12], replicated
- grad_gain_feedforward: float32 [1536], P(('ctx', 'wshard'))
- grad_gate: float32 [1536, 3968], P(('ctx', 'wshard'))
- grad_up: float32 [1536, 3968], P(('ctx', 'wshard'))
- grad_down: float32 [3968, 1536], P(None, ('ctx', 'wshard'))
Inputs may be any that keep to these rules, and one draw needn't show every extreme that they name: `lengths`: each row sums to 1024; the largest entry is 512. `permutation`: each row holds every place of its group once.
All inputs are finite; a program needn't handle non-finite values.
Results may differ from a plain program's by a relative error of at most 0.02.
Values may be sent and summed in bfloat16 or wider, within the bound.
No kernel may reach another device: no remote copies, remote signals or barrier semaphores. Data moves between devices by JAX's collectives and lax.ppermute only.
A program may use at most 320 MiB of HBM per device.

v0:
```python
import jax
import jax.numpy as jnp
from jax import lax
from jax.sharding import PartitionSpec as P

epsilon = 1e-06
highest = lax.Precision.HIGHEST
thresholds = (12, 16, 23, 32, 46, 64, 91)
masked_out = -1e30


def bucket_of(offset):
    distance = jnp.abs(offset)
    beyond = 8 + sum(((distance >= border).astype(jnp.int32) for border in thresholds))
    near_far = jnp.where(distance < 8, distance, beyond)
    return jnp.where(offset > 0, 16, 0) + near_far


def rms_norm(values, gain_vector):
    return (
        values
        * lax.rsqrt(jnp.mean(values * values, axis=-1, keepdims=True) + epsilon)
        * gain_vector
    )


def forward_product(left_side, right_side):
    return jnp.dot(left_side, right_side, preferred_element_type=jnp.float32)


def backward_product(left_side, right_side):
    return lax.dot_general(
        left_side, right_side, (((1,), (1,)), ((), ())), preferred_element_type=jnp.float32
    )


def weight_product(left_side, right_side):
    return lax.dot_general(
        left_side, right_side, (((0,), (0,)), ((), ())), preferred_element_type=jnp.float32
    )


def per_device(
    inputs,
    out_grad,
    lengths,
    permutation,
    gain_attention,
    query_weight,
    key_weight,
    value_weight,
    out_weight,
    bucket_bias,
    gain_feedforward,
    gate_weight,
    up_weight,
    down_weight,
):
    gathered = (
        lax.all_gather(query_weight, "wshard", axis=0, tiled=True),
        lax.all_gather(key_weight, "wshard", axis=0, tiled=True),
        lax.all_gather(value_weight, "wshard", axis=0, tiled=True),
        lax.all_gather(out_weight, "wshard", axis=0, tiled=True),
        lax.all_gather(gate_weight, "wshard", axis=0, tiled=True),
        lax.all_gather(up_weight, "wshard", axis=0, tiled=True),
        lax.all_gather(down_weight, "wshard", axis=0, tiled=True),
    )
    query_full, key_full, value_full, out_full, gate_full, up_full, down_full = gathered
    rows = inputs.shape[0]
    buckets = bucket_bias.shape[0]
    heads = bucket_bias.shape[1]
    width = query_weight.shape[1]
    head_size = width // heads
    peers = lax.axis_size(("ctx", "wshard"))
    group_tokens = rows * peers
    breadth = min(512, group_tokens)
    blocks = group_tokens // breadth
    first = lax.axis_index(("ctx", "wshard")) * rows
    seq_ends = jnp.cumsum(lengths[0])
    order_row = permutation[0]
    inverse = (
        jnp.zeros((group_tokens,), jnp.int32).at[order_row].set(lax.iota(jnp.int32, group_tokens))
    )

    def sequence_of(places):
        return jnp.sum((places[:, None] >= seq_ends[None, :]).astype(jnp.int32), axis=1)

    query_place = lax.dynamic_slice_in_dim(order_row, first, rows, 0)
    query_seq = sequence_of(query_place)
    seq_lowest = jnp.min(query_seq)
    seq_highest = jnp.max(query_seq)
    bucket_ids = lax.iota(jnp.int32, buckets)

    def live(key_start):
        key_seq = sequence_of(lax.dynamic_slice_in_dim(order_row, key_start, breadth, 0))
        return (jnp.min(key_seq) <= seq_highest) & (jnp.max(key_seq) >= seq_lowest)

    all_grads = lax.all_gather(out_grad, ("ctx", "wshard"), axis=0, tiled=True)
    dy_rows = jnp.take(all_grads, query_place, axis=0)
    inputs_wide = inputs.astype(jnp.float32)
    normed = rms_norm(inputs_wide, gain_attention).astype(jnp.bfloat16)
    query_proj = forward_product(normed, query_full).astype(jnp.bfloat16)
    key_proj = forward_product(normed, key_full).astype(jnp.bfloat16)
    value_proj = forward_product(normed, value_full).astype(jnp.bfloat16)
    query_heads = query_proj.reshape(rows, heads, head_size)
    key_value = (
        lax.all_gather(key_proj, ("ctx", "wshard"), axis=0, tiled=True),
        lax.all_gather(value_proj, ("ctx", "wshard"), axis=0, tiled=True),
    )

    def block_scores(key_start, key_all):
        key_block = lax.dynamic_slice_in_dim(key_all, key_start, breadth, 0).reshape(
            breadth, heads, head_size
        )
        scores = jnp.einsum(
            "qhd,khd->hqk", query_heads, key_block, preferred_element_type=jnp.float32
        )
        key_place = lax.dynamic_slice_in_dim(order_row, key_start, breadth, 0)
        offsets = key_place[None, :] - query_place[:, None]
        picks = (bucket_of(offsets)[:, :, None] == bucket_ids[None, None, :]).astype(jnp.float32)
        scores = scores + jnp.einsum("qkb,bh->hqk", picks, bucket_bias, precision=highest)
        key_seq = sequence_of(key_place)
        same_seq = (query_seq[:, None] == key_seq[None, :])[None]
        return (jnp.where(same_seq, scores, masked_out), key_block, picks)

    def value_block_of(key_start, value_all):
        return lax.dynamic_slice_in_dim(value_all, key_start, breadth, 0).reshape(
            breadth, heads, head_size
        )

    def visit(step_fn, carry):

        def one_step(block_index, running):
            key_start = block_index * breadth
            return lax.cond(
                live(key_start),
                lambda current: step_fn(key_start, current),
                lambda current: current,
                running,
            )

        return lax.fori_loop(0, blocks, one_step, carry)

    def peak_step(key_start, running):
        top_now, total_now = running
        scores = block_scores(key_start, key_value[0])[0]
        top_next = jnp.maximum(top_now, jnp.max(scores, axis=2))
        total_next = total_now * jnp.exp(top_now - top_next) + jnp.sum(
            jnp.exp(scores - top_next[:, :, None]), axis=2
        )
        return (top_next, total_next)

    start_top = jnp.full((heads, rows), masked_out, jnp.float32)
    top_all, total_all = visit(peak_step, (start_top, jnp.zeros((heads, rows), jnp.float32)))
    log_total = top_all + jnp.log(total_all)

    def value_step(key_start, running):
        scores = block_scores(key_start, key_value[0])[0]
        value_block = value_block_of(key_start, key_value[1])
        probs_low = jnp.exp(scores - log_total[:, :, None]).astype(jnp.bfloat16)
        return running + jnp.einsum(
            "hqk,khd->qhd", probs_low, value_block, preferred_element_type=jnp.float32
        )

    attended_wide = visit(value_step, jnp.zeros((rows, heads, head_size), jnp.float32))
    attended = attended_wide.reshape(rows, width).astype(jnp.bfloat16)
    residual = inputs_wide + forward_product(attended, out_full)
    normed_ff = rms_norm(residual, gain_feedforward).astype(jnp.bfloat16)
    gate_proj = forward_product(normed_ff, gate_full)
    up_proj = forward_product(normed_ff, up_full)

    def activate(gate_in, up_in):
        return jax.nn.gelu(gate_in, approximate=True) * up_in

    hidden_wide, activate_back = jax.vjp(activate, gate_proj, up_proj)
    hidden = hidden_wide.astype(jnp.bfloat16)
    outputs_dealt = (residual + forward_product(hidden, down_full)).astype(jnp.bfloat16)
    later = (
        lax.all_gather(query_weight, "wshard", axis=0, tiled=True),
        lax.all_gather(key_weight, "wshard", axis=0, tiled=True),
        lax.all_gather(value_weight, "wshard", axis=0, tiled=True),
        lax.all_gather(out_weight, "wshard", axis=0, tiled=True),
        lax.all_gather(gate_weight, "wshard", axis=0, tiled=True),
        lax.all_gather(up_weight, "wshard", axis=0, tiled=True),
        lax.all_gather(down_weight, "wshard", axis=0, tiled=True),
    )
    key_value_back = (
        lax.all_gather(key_proj, ("ctx", "wshard"), axis=0, tiled=True),
        lax.all_gather(value_proj, ("ctx", "wshard"), axis=0, tiled=True),
    )
    query_back, key_back, value_back, out_back, gate_back, up_back, down_back = later
    grad_down = weight_product(hidden, dy_rows)
    d_hidden = backward_product(dy_rows, down_back)
    d_gate_wide, d_up_wide = activate_back(d_hidden)
    d_gate = d_gate_wide.astype(jnp.bfloat16)
    d_up = d_up_wide.astype(jnp.bfloat16)
    grad_gate = weight_product(normed_ff, d_gate)
    grad_up = weight_product(normed_ff, d_up)
    d_normed_ff = backward_product(d_gate, gate_back) + backward_product(d_up, up_back)
    norm_ff_back = jax.vjp(rms_norm, residual, gain_feedforward)[1]
    d_residual_norm, grad_gain_ff = norm_ff_back(d_normed_ff)
    d_residual = dy_rows.astype(jnp.float32) + d_residual_norm
    d_branch = d_residual.astype(jnp.bfloat16)
    grad_out = weight_product(attended, d_branch)
    d_attended = backward_product(d_branch, out_back).astype(jnp.bfloat16)
    d_heads = d_attended.reshape(rows, heads, head_size)
    delta = jnp.einsum("qhd,qhd->hq", d_heads.astype(jnp.float32), attended_wide, precision=highest)

    def grad_step(key_start, running):
        d_query_acc, d_keyvalue, d_table = running
        scores, key_block, picks = block_scores(key_start, key_value_back[0])
        value_block = value_block_of(key_start, key_value_back[1])
        soft = jnp.exp(scores - log_total[:, :, None])
        d_probs = jnp.einsum(
            "qhd,khd->hqk", d_heads, value_block, preferred_element_type=jnp.float32
        )
        d_scores = (soft * (d_probs - delta[:, :, None])).astype(jnp.bfloat16)
        d_query_acc = d_query_acc + jnp.einsum(
            "hqk,khd->qhd", d_scores, key_block, preferred_element_type=jnp.float32
        )
        d_key_block = jnp.einsum(
            "hqk,qhd->khd", d_scores, query_heads, preferred_element_type=jnp.float32
        ).reshape(breadth, width)
        d_value_block = jnp.einsum(
            "hqk,qhd->khd", soft.astype(jnp.bfloat16), d_heads, preferred_element_type=jnp.float32
        ).reshape(breadth, width)
        d_keyvalue = lax.dynamic_update_slice_in_dim(
            d_keyvalue, jnp.concatenate([d_key_block, d_value_block], axis=1), key_start, 0
        )
        d_table = d_table + jnp.einsum(
            "qkb,hqk->bh", picks, d_scores.astype(jnp.float32), precision=highest
        )
        return (d_query_acc, d_keyvalue, d_table)

    start_grad = (
        jnp.zeros((rows, heads, head_size), jnp.float32),
        jnp.zeros((group_tokens, 2 * width), jnp.float32),
        jnp.zeros((buckets, heads), jnp.float32),
    )
    d_query_all, d_keyvalue_all, d_table_all = visit(grad_step, start_grad)
    own_keyvalue = lax.psum_scatter(
        d_keyvalue_all.astype(jnp.bfloat16), ("ctx", "wshard"), scatter_dimension=0, tiled=True
    ).astype(jnp.float32)
    d_query = d_query_all.reshape(rows, width).astype(jnp.bfloat16)
    d_key = own_keyvalue[:, :width].astype(jnp.bfloat16)
    d_value = own_keyvalue[:, width:].astype(jnp.bfloat16)
    grad_query = weight_product(normed, d_query)
    grad_key = weight_product(normed, d_key)
    grad_value = weight_product(normed, d_value)
    d_normed = (
        backward_product(d_query, query_back)
        + backward_product(d_key, key_back)
        + backward_product(d_value, value_back)
    )
    norm_attn_back = jax.vjp(rms_norm, inputs_wide, gain_attention)[1]
    d_input_norm, grad_gain_attn = norm_attn_back(d_normed)
    input_grad_dealt = (d_residual + d_input_norm).astype(jnp.bfloat16)
    grad_table = lax.psum(d_table_all, ("group", "ctx", "wshard"))
    returned = (
        lax.all_gather(outputs_dealt, ("ctx", "wshard"), axis=0, tiled=True),
        lax.all_gather(input_grad_dealt, ("ctx", "wshard"), axis=0, tiled=True),
    )
    own_rows = lax.dynamic_slice_in_dim(inverse, first, rows, 0)
    outputs = jnp.take(returned[0], own_rows, axis=0)
    input_grad = jnp.take(returned[1], own_rows, axis=0)
    shares = (
        lax.psum_scatter(
            grad_gain_attn.astype(jnp.bfloat16), ("ctx", "wshard"), scatter_dimension=0, tiled=True
        ).astype(jnp.float32),
        lax.psum_scatter(
            grad_query.astype(jnp.bfloat16), ("ctx", "wshard"), scatter_dimension=0, tiled=True
        ).astype(jnp.float32),
        lax.psum_scatter(
            grad_key.astype(jnp.bfloat16), ("ctx", "wshard"), scatter_dimension=0, tiled=True
        ).astype(jnp.float32),
        lax.psum_scatter(
            grad_value.astype(jnp.bfloat16), ("ctx", "wshard"), scatter_dimension=0, tiled=True
        ).astype(jnp.float32),
        lax.psum_scatter(
            grad_out.astype(jnp.bfloat16), ("ctx", "wshard"), scatter_dimension=0, tiled=True
        ).astype(jnp.float32),
        lax.psum_scatter(
            grad_gain_ff.astype(jnp.bfloat16), ("ctx", "wshard"), scatter_dimension=0, tiled=True
        ).astype(jnp.float32),
        lax.psum_scatter(
            grad_gate.astype(jnp.bfloat16), ("ctx", "wshard"), scatter_dimension=0, tiled=True
        ).astype(jnp.float32),
        lax.psum_scatter(
            grad_up.astype(jnp.bfloat16), ("ctx", "wshard"), scatter_dimension=0, tiled=True
        ).astype(jnp.float32),
        lax.psum_scatter(
            grad_down.astype(jnp.bfloat16), ("ctx", "wshard"), scatter_dimension=1, tiled=True
        ).astype(jnp.float32),
    )
    totals = (
        lax.psum(shares[0].astype(jnp.bfloat16), "group").astype(jnp.float32),
        lax.psum(shares[1].astype(jnp.bfloat16), "group").astype(jnp.float32),
        lax.psum(shares[2].astype(jnp.bfloat16), "group").astype(jnp.float32),
        lax.psum(shares[3].astype(jnp.bfloat16), "group").astype(jnp.float32),
        lax.psum(shares[4].astype(jnp.bfloat16), "group").astype(jnp.float32),
        lax.psum(shares[5].astype(jnp.bfloat16), "group").astype(jnp.float32),
        lax.psum(shares[6].astype(jnp.bfloat16), "group").astype(jnp.float32),
        lax.psum(shares[7].astype(jnp.bfloat16), "group").astype(jnp.float32),
        lax.psum(shares[8].astype(jnp.bfloat16), "group").astype(jnp.float32),
    )
    return (
        outputs,
        input_grad,
        totals[0],
        totals[1],
        totals[2],
        totals[3],
        totals[4],
        grad_table,
        totals[5],
        totals[6],
        totals[7],
        totals[8],
    )


def solution(mesh):
    return jax.shard_map(
        per_device,
        mesh=mesh,
        in_specs=(
            P(("group", "ctx", "wshard"), None),
            P(("group", "ctx", "wshard"), None),
            P("group", None),
            P("group", None),
            P(),
            P("wshard", None),
            P("wshard", None),
            P("wshard", None),
            P("wshard", None),
            P(),
            P(),
            P("wshard", None),
            P("wshard", None),
            P("wshard", None),
        ),
        out_specs=(
            P(("group", "ctx", "wshard"), None),
            P(("group", "ctx", "wshard"), None),
            P(("ctx", "wshard")),
            P(("ctx", "wshard"), None),
            P(("ctx", "wshard"), None),
            P(("ctx", "wshard"), None),
            P(("ctx", "wshard"), None),
            P(),
            P(("ctx", "wshard")),
            P(("ctx", "wshard"), None),
            P(("ctx", "wshard"), None),
            P(None, ("ctx", "wshard")),
        ),
        check_vma=False,
    )
```

profile of v0, /device:TPU:0, one launch (start us, length us, event | category | flops | bytes accessed | tf_op | source)
XLA Modules:
  0.0 1275.2 jit_solution(9304477346111395155)
XLA Ops:
  9.7 13.5 %all-gather.13.cloned.1.call-done = bf16[1536,768]{1,0:T(8,128)(2,1)} async-done(((bf16[768,768]{1,0:T(8,128)(2,1)}), bf16[1536,768]{1,0:T(8,128)(2,1)}) %all-gather.13.cloned.1.call-update) | async-done | bytes 2359312 | tf_op jit(solution)/shard_map/all_gather | solution.py:62
  26.6 10.4 all-gather.17.cloned.1.call-done
  53.4 20.1 %all-gather.15.cloned.1.call-done = bf16[1024,768]{1,0:T(8,128)(2,1)} async-done(((bf16[256,768]{1,0:T(8,128)(2,1)}), bf16[1024,768]{1,0:T(8,128)(2,1)}) %all-gather.15.cloned.1.call-update) | async-done | bytes 1572880 | tf_op jit(solution)/shard_map/all_gather | solution.py:108
  75.3 19.9 %all-gather.19.cloned.1.call-done = bf16[1024,768]{1,0:T(8,128)(2,1)} async-done(((bf16[256,768]{1,0:T(8,128)(2,1)}), bf16[1024,768]{1,0:T(8,128)(2,1)}) %all-gather.19.cloned.1.call-update) | async-done | bytes 1572880 | tf_op jit(solution)/shard_map/all_gather | solution.py:107
  97.6 65.7 %while.51 = (s32[]{:T(128)}, f32[12,256]{1,0:T(8,128)S(1)}, f32[12,256]{1,0:T(8,128)}, s32[1024]{0:T(1024)}, s32[4]{0:T(128)}, /*index=5*/s32[]{:T(128)}, s32[]{...) while((s32[]{:T(128)}, f32[12,256]{1,0:T(8,128)S(1)}, ...), condition=%wide.region_14.15_spmd.clone, body=%wide.region_5.14_spmd.clone.sunk | while | flops 821184512 | bytes 42105104 | solution.py:142
  102.7 26.9 %conditional.9 = ((f32[12,256]{1,0:T(8,128)S(1)}, f32[12,256]{1,0:T(8,128)})) conditional(s32[]{:T(128)} %convert_element_type.489, (f32[12,256]{1,0:T(8,128)S(1)}, f32[12,256]{1,0:T(8,128)}) %tuple.152, (s32[256]{0:T(256)}, s32[]{:T(128)}, s32[1024]{0:T(1024)}, s32[4]{0:T(128)}, bf16[1024,768]{0,1:T(8,128)(2,1)S(1)}, ...), branch_computations={%region_9.9_spmd, %region_10.13_spmd} | conditional | flops 821177856 | bytes 42094376 | solution.py:135
  113.2 9.2 copy.70
  134.7 28.6 %conditional.9 = ((f32[12,256]{1,0:T(8,128)S(1)}, f32[12,256]{1,0:T(8,128)})) conditional(s32[]{:T(128)} %convert_element_type.489, (f32[12,256]{1,0:T(8,128)S(1)}, f32[12,256]{1,0:T(8,128)}) %tuple.152, (s32[256]{0:T(256)}, s32[]{:T(128)}, s32[1024]{0:T(1024)}, s32[4]{0:T(128)}, bf16[1024,768]{0,1:T(8,128)(2,1)S(1)}, ...), branch_computations={%region_9.9_spmd, %region_10.13_spmd} | conditional | flops 821177856 | bytes 42094376 | solution.py:135
  145.2 10.2 copy.70
  165.5 67.1 %while.52 = (s32[]{:T(128)}, f32[256,12,64]{0,2,1:T(8,128)}, s32[1024]{0:T(1024)}, s32[4]{0:T(128)}, s32[]{:T(128)}, /*index=5*/s32[]{:T(128)}, bf16[1024,768]{0...) while((s32[]{:T(128)}, f32[256,12,64]{0,2,1:T(8,128)}, ...), condition=%wide.region_22.23_spmd.clone, body=%wide.region_15.22_spmd.clone.sunk | while | flops 1021128704 | bytes 33284948 | solution.py:142
  170.8 28.6 %conditional.10 = (f32[256,12,64]{0,2,1:T(8,128)}) conditional(s32[]{:T(128)} %convert_element_type.491, f32[256,12,64]{0,2,1:T(8,128)} %get-tuple-element.1644, (s32[]{:T(128)}, bf16[1024,768]{0,1:T(8,128)(2,1)S(1)}, s32[256]{0:T(256)}, s32[1024]{0:T(1024)}, s32[4]{0:T(128)}, /*index=5*/bf16[1024,768]{0,1:T(8,128)(2,1)S(1)}, ...), branch_computations={%region_19.19_spmd, %region_20.21_spmd} | conditional | flops 1021122048 | bytes 33274218 | solution.py:135
  181.0 9.7 copy.71
  204.6 27.7 %conditional.10 = (f32[256,12,64]{0,2,1:T(8,128)}) conditional(s32[]{:T(128)} %convert_element_type.491, f32[256,12,64]{0,2,1:T(8,128)} %get-tuple-element.1644, (s32[]{:T(128)}, bf16[1024,768]{0,1:T(8,128)(2,1)S(1)}, s32[256]{0:T(256)}, s32[1024]{0:T(1024)}, s32[4]{0:T(128)}, /*index=5*/bf16[1024,768]{0,1:T(8,128)(2,1)S(1)}, ...), branch_computations={%region_19.19_spmd, %region_20.21_spmd} | conditional | flops 1021122048 | bytes 33274218 | solution.py:135
  244.7 10.1 fusion.125
  254.8 10.1 fusion.126
  264.9 11.3 multiply_convert_fusion
  297.1 52.5 %while.53 = (s32[]{:T(128)}, f32[256,12,64]{0,2,1:T(8,128)S(1)}, bf16[1024,1536]{0,1:T(8,128)(2,1)}, f32[32,12]{0,1:T(8,128)S(1)}, s32[1024]{0:T(1024)S(1)}, /*i...) while((s32[]{:T(128)}, f32[256,12,64]{0,2,1:T(8,128)S(1)}, ...), condition=%wide.region_33.35_spmd.clone, body=%wide.region_26.0_spmd.clone.sunk | while | flops 1737830784 | bytes 84465112 | solution.py:142
  300.7 22.6 %conditional.11 = ((f32[256,12,64]{0,2,1:T(8,128)S(1)}, bf16[1024,1536]{0,1:T(8,128)(2,1)}, f32[32,12]{0,1:T(8,128)S(1)})) conditional(s32[]{:T(128)} %convert_element_type.493, (f32[256,12,64]{0,2,1:T(8,128)S(1)}, bf16[1024,1536]{0,1:T(8,128)(2,1)}, f32[32,12]{0,1:T(8,128)S(1)}) %tuple.159, (s32[]{:T(128)}, bf16[1024,768]{0,1:T(8,128)(2,1)S(1)}, ...), branch_computations={%region_30.31_spmd, %region_31.33_spmd} | conditional | flops 1737824128 | bytes 84454296 | solution.py:135
  326.6 22.6 %conditional.11 = ((f32[256,12,64]{0,2,1:T(8,128)S(1)}, bf16[1024,1536]{0,1:T(8,128)(2,1)}, f32[32,12]{0,1:T(8,128)S(1)})) conditional(s32[]{:T(128)} %convert_element_type.493, (f32[256,12,64]{0,2,1:T(8,128)S(1)}, bf16[1024,1536]{0,1:T(8,128)(2,1)}, f32[32,12]{0,1:T(8,128)S(1)}) %tuple.159, (s32[]{:T(128)}, bf16[1024,768]{0,1:T(8,128)(2,1)S(1)}, ...), branch_computations={%region_30.31_spmd, %region_31.33_spmd} | conditional | flops 1737824128 | bytes 84454296 | solution.py:135
  359.4 16.2 %copy.97 = bf16[3968,1536]{0,1:T(8,128)(2,1)} copy(bf16[3968,1536]{1,0:T(8,128)(2,1)} %convolution_convert_fusion) | data formatting | bytes 24379392
  395.5 12.2 convolution_convert_fusion.2
  415.8 10.8 fusion.91
  433.9 54.2 %reduce-scatter.25.cloned.1.call-done = bf16[384,3968]{1,0:T(8,128)(2,1)} async-done(((bf16[1536,3968]{1,0:T(8,128)(2,1)}), bf16[384,3968]{1,0:T(8,128)(2,1)}) %reduce-scatter.25.cloned.1.call-update) | async-done | bytes 3047440
  492.6 31.4 %reduce-scatter.13.cloned.1.call-done = bf16[384,768]{1,0:T(8,128)(2,1)} async-done(((bf16[1536,768]{1,0:T(8,128)(2,1)}), bf16[384,768]{1,0:T(8,128)(2,1)}) %reduce-scatter.13.cloned.1.call-update) | async-done | bytes 589840 | tf_op jit(solution)/shard_map/reduce_scatter | solution.py:270
  524.0 35.2 %reduce-scatter.19.cloned.1.call-done = bf16[192,1536]{1,0:T(8,128)(2,1)} async-done(((bf16[768,1536]{1,0:T(8,128)(2,1)}), bf16[192,1536]{1,0:T(8,128)(2,1)}) %reduce-scatter.19.cloned.1.call-update) | async-done | bytes 589840 | tf_op jit(solution)/shard_map/reduce_scatter | solution.py:279
  559.3 35.8 %reduce-scatter.15.cloned.1.call-done = bf16[384,768]{1,0:T(8,128)(2,1)} async-done(((bf16[1536,768]{1,0:T(8,128)(2,1)}), bf16[384,768]{1,0:T(8,128)(2,1)}) %reduce-scatter.15.cloned.1.call-update) | async-done | bytes 589840 | tf_op jit(solution)/shard_map/reduce_scatter | solution.py:273
  595.0 35.2 %reduce-scatter.17.cloned.1.call-done = bf16[384,768]{1,0:T(8,128)(2,1)} async-done(((bf16[1536,768]{1,0:T(8,128)(2,1)}), bf16[384,768]{1,0:T(8,128)(2,1)}) %reduce-scatter.17.cloned.1.call-update) | async-done | bytes 589840 | tf_op jit(solution)/shard_map/reduce_scatter | solution.py:276
  630.3 99.5 %reduce-scatter.21.cloned.1.call-done = bf16[384,3968]{1,0:T(8,128)(2,1)} async-done(((bf16[1536,3968]{1,0:T(8,128)(2,1)}), bf16[384,3968]{1,0:T(8,128)(2,1)}) %reduce-scatter.21.cloned.1.call-update) | async-done | bytes 3047440 | tf_op jit(solution)/shard_map/reduce_scatter | solution.py:285
  729.8 99.5 %reduce-scatter.23.cloned.1.call-done = bf16[384,3968]{1,0:T(8,128)(2,1)} async-done(((bf16[1536,3968]{1,0:T(8,128)(2,1)}), bf16[384,3968]{1,0:T(8,128)(2,1)}) %reduce-scatter.23.cloned.1.call-update) | async-done | bytes 3047440 | tf_op jit(solution)/shard_map/reduce_scatter | solution.py:288
  835.0 39.9 %psum.75 = f32[32,12]{0,1:T(8,128)} all-reduce(f32[32,12]{0,1:T(8,128)S(1)} %copy-done.48), channel_id=1, replica_groups=mesh['group'=8,'ctx'=2,'wshard'=2] {'group','ctx','wshard'}, use_global_device_ids=true, to_apply=%region_47.49 | all-reduce | flops 384 | bytes 3072 | tf_op jit(solution)/shard_map/psum | solution.py:258
  887.7 19.9 %all-reduce.2 = (bf16[384]{0:T(512)(128)(2,1)S(1)}, bf16[384]{0:T(512)(128)(2,1)S(1)}) all-reduce(bf16[384]{0:T(512)(128)(2,1)S(1)} %dynamic-slice.2, bf16[384]{0:T(512)(128)(2,1)S(1)} %dynamic-slice.4), channel_id=1, replica_groups=mesh['group'=8,'ctx'=2,'wshard'=2] {'group'}, use_global_device_ids=true, to_apply=%region_38.40 | all-reduce | flops 768 | bytes 3072 | tf_op jit(solution)/shard_map/psum | solution.py:296
  914.3 337.8 %all-reduce.7.cloned.1.call-done = (bf16[384,768]{1,0:T(8,128)(2,1)}, bf16[384,768]{1,0:T(8,128)(2,1)}, bf16[384,768]{1,0:T(8,128)(2,1)}, bf16[192,1536]{1,0:T(8...) async-done(((bf16[384,768]{1,0:T(8,128)(2,1)}, bf16[384,768]{1,0:T(8,128)(2,1)}, bf16[384,768]{1,0:T(8,128)(2,1)}, ...) | async-done | bytes 11501584 | tf_op jit(solution)/shard_map/psum | solution.py:297
  (340 shorter events, 290.4 us)
Async XLA Ops:
  7.2 16.1 %copy-start.41 = (f32[1536]{0:T(1024)S(1)}, f32[1536]{0:T(1024)}, u32[]{:S(2)}) copy-start(f32[1536]{0:T(1024)} %param.32) | copy-start | bytes 18436
  7.2 16.1 %all-gather.13.cloned.1.call-start = ((), (), s32[]{:S(2)}) async-start(), calls=%async_computation.8 | async-start | bytes 3538944 | tf_op jit(solution)/shard_map/all_gather | solution.py:62
  7.9 29.0 %all-gather.17.cloned.1.call-start = ((), (), s32[]{:S(2)}) async-start(), calls=%async_computation.10 | async-start | bytes 3538944 | tf_op jit(solution)/shard_map/all_gather | solution.py:61
  8.7 42.1 %all-gather.21.cloned.1.call-start = ((), (), s32[]{:S(2)}) async-start(), calls=%async_computation.12 | async-start | bytes 3538944 | tf_op jit(solution)/shard_map/all_gather | solution.py:60
  9.4 64.2 %all-gather.15.cloned.1.call-start = ((), (), s32[]{:S(2)}) async-start(), calls=%async_computation.9 | async-start | bytes 1966080 | tf_op jit(solution)/shard_map/all_gather | solution.py:108
  9.7 16.8 %copy-start.49 = (f32[256]{0:T(256)}, f32[256]{0:T(256)S(1)}, u32[]{:S(2)}) copy-start(f32[256]{0:T(256)S(1)} %fusion.99) | copy-start | bytes 3076
  9.7 41.0 %copy-start.44 = (f32[256]{0:T(256)}, f32[256]{0:T(256)S(1)}, u32[]{:S(2)}) copy-start(f32[256]{0:T(256)S(1)} %fusion.110) | copy-start | bytes 3076
  26.5 68.7 %all-gather.19.cloned.1.call-start = ((), (), s32[]{:S(2)}) async-start(), calls=%async_computation.11 | async-start | bytes 1966080 | tf_op jit(solution)/shard_map/all_gather | solution.py:107
  40.2 194.9 %all-gather.33.cloned.1.call-start = ((), (), s32[]{:S(2)}) async-start(), calls=%async_computation.18 | async-start | bytes 3932160 | tf_op jit(solution)/shard_map/all_gather | solution.py:98
  40.8 199.7 %all-gather.23.cloned.1.call-start = ((), (), s32[]{:S(2)}) async-start(), calls=%async_computation.13 | async-start | bytes 3538944 | tf_op jit(solution)/shard_map/all_gather | solution.py:63
  41.6 203.1 %all-gather.25.cloned.1.call-start = ((), (), s32[]{:S(2)}) async-start(), calls=%async_computation.14 | async-start | bytes 18284544 | tf_op jit(solution)/shard_map/all_gather | solution.py:64
  42.3 212.5 %all-gather.27.cloned.1.call-start = ((), (), s32[]{:S(2)}) async-start(), calls=%async_computation.15 | async-start | bytes 18284544 | tf_op jit(solution)/shard_map/all_gather | solution.py:65
  43.1 221.9 %all-gather.29.cloned.1.call-start = ((), (), s32[]{:S(2)}) async-start(), calls=%async_computation.16 | async-start | bytes 18284544 | tf_op jit(solution)/shard_map/all_gather | solution.py:66
  43.7 344.9 %reduce-scatter.11.cloned.1.call-start = ((), (), s32[]{:S(2)}) async-start(), calls=%async_computation.19 | async-start | bytes 3932160 | tf_op jit(solution)/shard_map/reduce_scatter | solution.py:241
  43.9 9.5 copy-start.32
  181.0 11.9 copy-start.28
  214.4 11.4 copy-start.28
  232.7 7.8 copy-start
  243.3 48.2 %copy-start.5 = (f32[256,1536]{1,0:T(8,128)}, f32[256,1536]{1,0:T(8,128)S(1)}, u32[]{:S(2)}) copy-start(f32[256,1536]{1,0:T(8,128)S(1)} %get-tuple-element.1288) | copy-start | bytes 4718596
  276.2 7.9 copy-start.21
  276.2 7.9 copy-start.20
  349.6 9.8 copy-start.47
  349.7 138.4 %reduce-scatter.25.cloned.1.call-start = ((), (), s32[]{:S(2)}) async-start(), calls=%async_computation.27 | async-start | bytes 15237120
  375.7 148.3 %reduce-scatter.13.cloned.1.call-start = ((), (), s32[]{:S(2)}) async-start(), calls=%async_computation.21 | async-start | bytes 2949120 | tf_op jit(solution)/shard_map/reduce_scatter | solution.py:270
  379.2 180.0 %reduce-scatter.19.cloned.1.call-start = ((), (), s32[]{:S(2)}) async-start(), calls=%async_computation.24 | async-start | bytes 2949120 | tf_op jit(solution)/shard_map/reduce_scatter | solution.py:279
  381.5 213.5 %reduce-scatter.15.cloned.1.call-start = ((), (), s32[]{:S(2)}) async-start(), calls=%async_computation.22 | async-start | bytes 2949120 | tf_op jit(solution)/shard_map/reduce_scatter | solution.py:273
  391.9 238.4 %reduce-scatter.17.cloned.1.call-start = ((), (), s32[]{:S(2)}) async-start(), calls=%async_computation.23 | async-start | bytes 2949120 | tf_op jit(solution)/shard_map/reduce_scatter | solution.py:276
  395.4 334.4 %reduce-scatter.21.cloned.1.call-start = ((), (), s32[]{:S(2)}) async-start(), calls=%async_computation.25 | async-start | bytes 15237120 | tf_op jit(solution)/shard_map/reduce_scatter | solution.py:285
  407.7 421.6 %reduce-scatter.23.cloned.1.call-start = ((), (), s32[]{:S(2)}) async-start(), calls=%async_computation.26 | async-start | bytes 15237120 | tf_op jit(solution)/shard_map/reduce_scatter | solution.py:288
  415.8 459.2 %all-gather.31.cloned.1.call-start = ((), (), s32[]{:S(2)}) async-start(), calls=%async_computation.17 | async-start | bytes 3932160 | tf_op jit(solution)/shard_map/all_gather | solution.py:260
  426.6 482.0 %all-gather.35.cloned.1.call-start = ((), (), s32[]{:S(2)}) async-start(), calls=%async_computation.20 | async-start | bytes 3932160 | tf_op jit(solution)/shard_map/all_gather | solution.py:261
  433.8 818.3 %all-reduce.7.cloned.1.call-start = ((), (), s32[]{:S(2)}) async-start(), calls=%async_computation.28 | async-start | bytes 23003136 | tf_op jit(solution)/shard_map/psum | solution.py:297
  (56 other events, 128.7 us)
Sparse Core Ops, SparseCore 0:
  9.5 13.6 all-gather.12
  24.8 12.1 all-gather.16
  38.5 12.1 all-gather.20
  52.7 20.7 all-gather.14
  75.6 19.6 all-gather.18
  96.6 28.4 all-gather.32
  126.7 10.9 all-gather.22
  139.3 25.4 all-gather.24
  166.3 25.4 all-gather.26
  193.3 25.4 all-gather.28
  349.8 38.6 reduce-scatter.10
  391.0 97.0 reduce-scatter.24
  491.2 32.8 reduce-scatter.12
  526.4 32.8 reduce-scatter.18
  562.2 32.7 reduce-scatter.14
  597.4 32.8 reduce-scatter.16
  632.7 96.9 reduce-scatter.20
  732.2 97.0 reduce-scatter.22
  831.4 29.0 all-gather.30
  862.5 29.1 all-gather.34
  897.8 354.2 all-reduce.6
where the time goes:
time: 1290 us; the launch traced here: 1280 us
  waiting for transfers between devices  809 us (63%)
  matrix products  202 us (16%)
  local copies, waits for them, and re-layouts  113 us (9%)
  blocking collectives  67.9 us (5%)
  other arithmetic  49.9 us (4%)
  loops' own time  16.8 us (1%)
  between operations  15.8 us (1%)
    psum x1, waiting for transfers between devices, per_device(): lax.psum(shares[1].astype(jnp.bfloat16), 'group').astype(jnp.float32)  338 us
    reduce_scatter x1, waiting for transfers between devices, per_device(): lax.psum_scatter(grad_up.astype(jnp.bfloat16), ('ctx', 'wshard'), scatter...  99.5 us
    reduce_scatter x1, waiting for transfers between devices, per_device(): lax.psum_scatter(grad_gate.astype(jnp.bfloat16), ('ctx', 'wshard'), scatt...  99.5 us
    unnamed x22, waiting for transfers between devices  59.6 us
    dot_general x7, matrix products, forward_product(): return jnp.dot(left_side, right_side, preferred_element_type=jnp.float32)  42.8 us
    dot_general x6, matrix products, block_scores(): jnp.einsum('qkb,bh->hqk', picks, bucket_bias, precision=highest)  40.8 us
    dot_general x7, matrix products, weight_product(): lax.dot_general(left_side, right_side, (((0,), (0,)), ((), ())), preferre...  40.2 us
    psum x1, blocking collectives, per_device(): grad_table = lax.psum(d_table_all, ('group', 'ctx', 'wshard'))  39.9 us
  transfers between devices with their start and end apart: 21, of which 14 were waited for; matrix products, arithmetic and copies ran while one was open for 21% of the time, Pallas kernels for 0%

commit v1 on v0

v1 whole, which is shorter than its diff:
```python
import functools

import jax
import jax.numpy as jnp
from jax import lax
from jax.experimental import pallas as pl
from jax.experimental.pallas import tpu as pltpu
from jax.sharding import PartitionSpec as P

epsilon = 1e-06
highest = lax.Precision.HIGHEST
thresholds = (12, 16, 23, 32, 46, 64, 91)
masked_out = -1e30
bf16 = jnp.bfloat16
f32 = jnp.float32
peer_axes = ("ctx", "wshard")
vmem_bytes = 60 * 1024 * 1024

ladder_ring = (0, 2, 4, 6, 7, 5, 3, 1)


def bucket_of(offset):
    distance = jnp.abs(offset)
    beyond = 8 + sum(((distance >= border).astype(jnp.int32) for border in thresholds))
    near_far = jnp.where(distance < 8, distance, beyond)
    return jnp.where(offset > 0, 16, 0) + near_far


def rms_norm(values, gain_vector):
    return (
        values
        * lax.rsqrt(jnp.mean(values * values, axis=-1, keepdims=True) + epsilon)
        * gain_vector
    )


def dot(left_side, right_side, dims, precision=None):
    return lax.dot_general(
        left_side, right_side, (dims, ((), ())), precision=precision, preferred_element_type=f32
    )


def forward_product(left_side, right_side):
    return dot(left_side, right_side, ((1,), (0,)))


def backward_product(left_side, right_side):
    return dot(left_side, right_side, ((1,), (1,)))


def weight_product(left_side, right_side):
    return dot(left_side, right_side, ((0,), (0,)))


def iota(shape, dim):
    return lax.broadcasted_iota(jnp.int32, shape, dim)


def arrange_kernel(rows, count, me_ref, order_ref, gain_ref, weight_ref, *refs):
    blocks, (x_ref, normed_ref, qkv_ref) = refs[:-3], refs[-3:]
    me = me_ref[0]
    first = (me ^ pl.program_id(0)) * rows
    tokens = first + iota((rows, rows), 0)
    total = None
    for k in range(count):
        places = order_ref[pl.ds(me ^ k, 1), :]
        chosen = (places == tokens).astype(f32).astype(bf16)
        part = forward_product(chosen, blocks[k][...])
        total = part if total is None else total + part
    x_ref[...] = total.astype(bf16)
    normed = rms_norm(total, gain_ref[...]).astype(bf16)
    normed_ref[...] = normed
    qkv_ref[...] = forward_product(normed, weight_ref[...]).astype(bf16)


def bias_kernel(rows, heads_here, heads, buckets, me_ref, table_ref, out_ref):
    lanes = iota((8, 4 * rows), 1)
    ids = bucket_of(2 * rows - lanes)
    for h in range(heads_here):
        head = jnp.minimum(me_ref[0] * heads_here + h, heads - 1)
        base = jnp.zeros((8, 4 * rows), f32)
        for b in range(buckets):
            base = jnp.where(ids == b, table_ref[b, head], base)
        wide = jnp.broadcast_to(base[0:1], (rows, 4 * rows))
        rolled = pltpu.roll(wide, 0, 1, stride=1, stride_axis=0)
        out_ref[h, 0] = jnp.full((rows, rows), table_ref[buckets // 2 - 1, head], f32)
        out_ref[h, 4] = jnp.full((rows, rows), table_ref[buckets - 1, head], f32)
        for delta in (1, 0, -1):
            start = rows + rows * (1 - delta)
            out_ref[h, delta + 2] = rolled[:, start : start + rows]


def span_of(lengths_ref, seqs, first, last, rows, total):
    low, high, end = 0, total, 0
    ends = []
    for s in range(seqs):
        end = end + lengths_ref[s]
        ends.append(end)
    for s in range(seqs):
        low = jnp.where(ends[s] <= first, ends[s], low)
    for s in reversed(range(seqs)):
        high = jnp.where(ends[s] > last, ends[s], high)
    high = jnp.minimum(high, total)
    return ends, low // rows, (high + rows - 1) // rows


def sequence_ids(ends, first, shape, dim):
    places = first + iota(shape, dim)
    ids = jnp.zeros(shape, jnp.int32)
    for end in ends:
        ids = ids + (places >= end).astype(jnp.int32)
    return ids


def attend_kernel(
    rows, count, heads_here, size, seqs, me_ref, lengths_ref, qkv_ref, bias_ref, att_ref, wide_ref, lse_ref
):
    me = me_ref[0]
    width = heads_here * size
    here = pl.program_id(0)
    block = me ^ here
    ends, low, high = span_of(
        lengths_ref, seqs, block * rows, block * rows + rows - 1, rows, count * rows
    )
    query_seq = sequence_ids(ends, block * rows, (1, rows), 1)
    start = pl.multiple_of(here * rows, rows)
    queries = qkv_ref[pl.ds(start, rows), :][:, :width]
    for h in range(heads_here):
        query = queries[:, h * size : (h + 1) * size]

        def step(key_block, carry):
            top, total, acc = carry
            at = pl.multiple_of((key_block ^ me) * rows, rows)
            own = qkv_ref[pl.ds(at, rows), :]
            key = own[:, width + h * size : width + (h + 1) * size]
            value = own[:, 2 * width + h * size : 2 * width + (h + 1) * size]
            delta = jnp.clip(key_block - block, -2, 2) + 2
            scores = backward_product(key, query) + bias_ref[h, delta]
            key_seq = sequence_ids(ends, key_block * rows, (rows, 1), 0)
            scores = jnp.where(key_seq == query_seq, scores, masked_out)
            top_next = jnp.maximum(top, jnp.max(scores, axis=0, keepdims=True))
            probs = jnp.exp(scores - top_next)
            fade = jnp.exp(top - top_next)
            total = total * fade + jnp.sum(probs, axis=0, keepdims=True)
            acc = acc * fade + weight_product(value, probs.astype(bf16))
            return top_next, total, acc

        top, total, acc = lax.fori_loop(
            low,
            high,
            step,
            (
                jnp.full((1, rows), masked_out, f32),
                jnp.zeros((1, rows), f32),
                jnp.zeros((size, rows), f32),
            ),
        )
        lse_ref[h : h + 1, :] = top + jnp.log(total)
        out = (acc / total).T
        wide_ref[:, h * size : (h + 1) * size] = out
        att_ref[:, h * size : (h + 1) * size] = out.astype(bf16)


def attend_back_kernel(
    rows,
    count,
    heads_here,
    size,
    seqs,
    buckets,
    me_ref,
    lengths_ref,
    qkv_ref,
    bias_ref,
    lse_ref,
    delta_ref,
    d_att_ref,
    dqkv_ref,
    table_ref,
    dq_ref,
    sums_ref,
):
    me = me_ref[0]
    width = heads_here * size
    here = pl.program_id(0)
    block = me ^ here

    @pl.when(here == 0)
    def _():
        dq_ref[...] = jnp.zeros_like(dq_ref)
        sums_ref[...] = jnp.zeros_like(sums_ref)

    ends, low, high = span_of(
        lengths_ref, seqs, block * rows, block * rows + rows - 1, rows, count * rows
    )
    key_seq = sequence_ids(ends, block * rows, (rows, 1), 0)
    start = pl.multiple_of(here * rows, rows)
    own = qkv_ref[pl.ds(start, rows), :]
    for h in range(heads_here):
        key = own[:, width + h * size : width + (h + 1) * size]
        value = own[:, 2 * width + h * size : 2 * width + (h + 1) * size]

        def step(query_block, carry):
            d_key, d_value = carry
            rel = query_block ^ me
            at = pl.multiple_of(rel * rows, rows)
            query = qkv_ref[pl.ds(at, rows), :][:, h * size : (h + 1) * size]
            d_out = d_att_ref[pl.ds(at, rows), :][:, h * size : (h + 1) * size]
            near = jnp.clip(block - query_block, -2, 2) + 2
            scores = backward_product(key, query) + bias_ref[h, near]
            query_seq = sequence_ids(ends, query_block * rows, (1, rows), 1)
            lse = lse_ref[h : h + 1, pl.ds(at, rows)]
            soft = jnp.where(key_seq == query_seq, jnp.exp(scores - lse), 0.0)
            d_probs = backward_product(value, d_out)
            d_scores = (soft * (d_probs - delta_ref[h : h + 1, pl.ds(at, rows)])).astype(bf16)
            sums_ref[h, near] += d_scores.astype(f32)
            d_value = d_value + forward_product(soft.astype(bf16), d_out)
            d_key = d_key + forward_product(d_scores, query)
            dq_ref[h, rel] += weight_product(key, d_scores)
            return d_key, d_value

        zero = jnp.zeros((rows, size), f32)
        d_key, d_value = lax.fori_loop(low, high, step, (zero, zero))
        dqkv_ref[pl.ds(start, rows), width + h * size : width + (h + 1) * size] = d_key.astype(bf16)
        dqkv_ref[pl.ds(start, rows), 2 * width + h * size : 2 * width + (h + 1) * size] = (
            d_value.astype(bf16)
        )

    @pl.when(here == count - 1)
    def _():
        for h in range(heads_here):
            for k in range(count):
                dqkv_ref[k * rows : (k + 1) * rows, h * size : (h + 1) * size] = (
                    dq_ref[h, k].T.astype(bf16)
                )
        turned = (iota((rows, rows), 0) + iota((rows, rows), 1) == rows - 1).astype(f32)
        ids = bucket_of(2 * rows - 1 - iota((buckets, 4 * rows), 1))
        mine = ids == iota((buckets, 4 * rows), 0)
        bucket_rows = iota((buckets, 1), 0)
        lanes = iota((buckets, 128), 1)
        table = jnp.zeros((buckets, 128), f32)
        for h in range(heads_here):
            strip = jnp.concatenate(
                [forward_product_exact(turned, sums_ref[h, d]) for d in (3, 2, 1)]
                + [jnp.zeros((rows, rows), f32)],
                axis=1,
            )
            diagonals = jnp.sum(
                pltpu.roll(strip, 0, 1, stride=1, stride_axis=0), axis=0, keepdims=True
            )
            column = jnp.sum(jnp.where(mine, diagonals, 0.0), axis=1, keepdims=True)
            column = column + jnp.where(bucket_rows == buckets // 2 - 1, jnp.sum(sums_ref[h, 0]), 0.0)
            column = column + jnp.where(bucket_rows == buckets - 1, jnp.sum(sums_ref[h, 4]), 0.0)
            table = jnp.where(lanes == h, column, table)
        table_ref[...] = table


def forward_product_exact(left_side, right_side):
    return dot(left_side, right_side, ((1,), (0,)), highest)


def whole(shape):
    return pl.BlockSpec(shape, lambda *_: (0,) * len(shape))


def per_device(
    sizes,
    inputs,
    out_grad,
    lengths,
    permutation,
    gain_attention,
    query_weight,
    key_weight,
    value_weight,
    out_weight,
    bucket_bias,
    gain_feedforward,
    gate_weight,
    up_weight,
    down_weight,
):
    n_group, n_ctx, n_w = sizes
    n = n_ctx * n_w
    fast = (n_group, n_ctx, n_w) == (8, 2, 2)
    rows, model = inputs.shape
    buckets, heads = bucket_bias.shape
    hidden_units = gate_weight.shape[1]
    size = query_weight.shape[1] // heads
    seqs = lengths.shape[1]
    tokens = rows * n
    heads_here = -(-heads // n)
    width = heads_here * size
    units = -(-hidden_units // (128 * n)) * 128
    ctx, wsh = lax.axis_index("ctx"), lax.axis_index("wshard")
    me = lax.axis_index(peer_axes)
    rank = wsh * n_ctx + ctx
    flip_w = [(0, 1), (1, 0)]


    def mate(block):
        return lax.ppermute(block, "wshard", flip_w)

    def across(block):
        return lax.ppermute(block, "ctx", flip_w)

    def to_relative(stacked):
        return jnp.take(stacked, me ^ lax.iota(jnp.int32, n), axis=0)

    def gather_blocks(block):
        if fast:
            far = across(block)
            return [block, mate(block), far, mate(far)]
        stacked = to_relative(lax.all_gather(block, peer_axes, axis=0, tiled=False))
        return [stacked[k] for k in range(n)]

    def scatter_rows(partial):
        if fast:
            sent = partial.astype(bf16).reshape(n, rows, -1)
            pair = jnp.stack([sent[1], sent[3]])
            got = mate(pair)
            near = sent[0].astype(f32) + got[0].astype(f32)
            away = (sent[2].astype(f32) + got[1].astype(f32)).astype(bf16)
            return near + across(away).astype(f32)
        stacked = to_relative(partial.astype(bf16).reshape(n, rows, -1))
        return lax.psum_scatter(stacked, peer_axes, scatter_dimension=0, tiled=False).astype(f32)

    def columns_of(weight, which, wide):
        over = max(0, n * wide - weight.shape[1])
        padded = jnp.pad(weight, ((0, 0), (0, over))) if over else weight
        return lax.dynamic_slice_in_dim(padded, which * wide, wide, 1)

    def own_columns(parts, wide, own, mates):
        mine = jnp.concatenate([columns_of(part, own, wide) for part in parts], axis=1)
        given = mate(jnp.concatenate([columns_of(part, mates, wide) for part in parts], axis=1))
        upper = jnp.where(wsh == 0, mine, given)
        lower = jnp.where(wsh == 0, given, mine)
        return jnp.concatenate([upper, lower], axis=0)

    row_blocks = gather_blocks(inputs)
    qkv_weight = own_columns(
        (query_weight, key_weight, value_weight), width, me, ctx * n_w + (1 - wsh)
    )
    out_other = mate(out_weight)
    gate_up = own_columns((gate_weight, up_weight), units, rank, (1 - wsh) * n_ctx + ctx)
    half = down_weight.shape[0]
    extra = n_ctx * units - half
    down_other = mate(down_weight[:extra])
    down_wide = jnp.concatenate(
        [
            down_weight,
            jnp.where(wsh == 0, down_other, jnp.zeros_like(down_other)),
            jnp.zeros_like(down_other),
        ]
    )
    down_own = lax.dynamic_slice_in_dim(down_wide, wsh * extra + ctx * units, units, 0)
    dy = jnp.concatenate(gather_blocks(out_grad))
    out_full = jnp.concatenate(
        [jnp.where(wsh == 0, out_weight, out_other), jnp.where(wsh == 0, out_other, out_weight)]
    )
    out_full = jnp.pad(out_full, ((0, n * width - out_full.shape[0]), (0, 0)))
    out_blocks = [lax.dynamic_slice_in_dim(out_full, (me ^ k) * width, width, 0) for k in range(n)]

    me_1 = me.reshape(1).astype(jnp.int32)
    order = permutation.reshape(n, rows)
    params = pltpu.CompilerParams(vmem_limit_bytes=vmem_bytes)
    bias = pl.pallas_call(
        functools.partial(bias_kernel, rows, heads_here, heads, buckets),
        out_shape=jax.ShapeDtypeStruct((heads_here, 5, rows, rows), f32),
        in_specs=[
            pl.BlockSpec(memory_space=pltpu.SMEM),
            pl.BlockSpec(memory_space=pltpu.SMEM),
        ],
        out_specs=pl.BlockSpec(memory_space=pltpu.VMEM),
        compiler_params=params,
        name="bias_strips",
    )(me_1, bucket_bias)
    x_all, normed, qkv = pl.pallas_call(
        functools.partial(arrange_kernel, rows, n),
        out_shape=(
            jax.ShapeDtypeStruct((tokens, model), bf16),
            jax.ShapeDtypeStruct((tokens, model), bf16),
            jax.ShapeDtypeStruct((tokens, 3 * width), bf16),
        ),
        grid_spec=pltpu.PrefetchScalarGridSpec(
            num_scalar_prefetch=1,
            grid=(n,),
            in_specs=[whole((n, rows)), whole((1, model)), whole((model, 3 * width))]
            + [whole((rows, model))] * n,
            out_specs=[
                pl.BlockSpec((rows, model), lambda t, *_: (t, 0)),
                pl.BlockSpec((rows, model), lambda t, *_: (t, 0)),
                pl.BlockSpec((rows, 3 * width), lambda t, *_: (t, 0)),
            ],
        ),
        compiler_params=params,
        cost_estimate=pl.CostEstimate(
            flops=2 * tokens * model * (tokens + 3 * width),
            bytes_accessed=8 * tokens * model,
            transcendentals=0,
        ),
        name="arrange_project",
    )(me_1, order, gain_attention.reshape(1, model), qkv_weight, *row_blocks)
    lengths_row = lengths.reshape(seqs)
    attended, attended_wide, lse = pl.pallas_call(
        functools.partial(attend_kernel, rows, n, heads_here, size, seqs),
        out_shape=(
            jax.ShapeDtypeStruct((tokens, width), bf16),
            jax.ShapeDtypeStruct((tokens, width), f32),
            jax.ShapeDtypeStruct((heads_here, tokens), f32),
        ),
        grid_spec=pltpu.PrefetchScalarGridSpec(
            num_scalar_prefetch=2,
            grid=(n,),
            in_specs=[whole((tokens, 3 * width)), whole((heads_here, 5, rows, rows))],
            out_specs=[
                pl.BlockSpec((rows, width), lambda t, *_: (t, 0)),
                pl.BlockSpec((rows, width), lambda t, *_: (t, 0)),
                pl.BlockSpec((heads_here, rows), lambda t, *_: (0, t)),
            ],
        ),
        compiler_params=params,
        cost_estimate=pl.CostEstimate(
            flops=16 * tokens * tokens * width,
            bytes_accessed=16 * tokens * width,
            transcendentals=tokens * tokens * heads_here,
        ),
        name="attend",
    )(me_1, lengths_row, qkv, bias)

    attended_blocks = gather_blocks(attended)
    by_rows = [
        jnp.concatenate(
            [attended_blocks[k][(m ^ k) * rows : ((m ^ k) + 1) * rows] for m in range(n)]
        )
        for k in range(n)
    ]
    attended_all = jnp.concatenate(by_rows, axis=1)
    residual_all = x_all.astype(f32) + forward_product(
        attended_all, jnp.concatenate(out_blocks, axis=0)
    )
    residual = residual_all[:rows]
    normed_ff = rms_norm(residual_all, gain_feedforward).astype(bf16)
    gate_up_proj = forward_product(normed_ff, gate_up)
    gate_proj, up_proj = gate_up_proj[:, :units], gate_up_proj[:, units:]

    def activate(gate_in, up_in):
        return jax.nn.gelu(gate_in, approximate=True) * up_in

    hidden_wide, activate_back = jax.vjp(activate, gate_proj, up_proj)
    hidden = hidden_wide.astype(bf16)
    grad_down = weight_product(hidden, dy).astype(bf16)
    d_hidden = backward_product(dy, down_own)
    d_gate_wide, d_up_wide = activate_back(d_hidden)
    d_gate, d_up = d_gate_wide.astype(bf16), d_up_wide.astype(bf16)
    grad_gate = weight_product(normed_ff, d_gate).astype(bf16)
    grad_up = weight_product(normed_ff, d_up).astype(bf16)
    d_normed_ff = scatter_rows(
        backward_product(d_gate, gate_up[:, :units]) + backward_product(d_up, gate_up[:, units:])
    )
    outputs = (residual + scatter_rows(forward_product(hidden, down_own))).astype(bf16)

    norm_ff_back = jax.vjp(rms_norm, residual, gain_feedforward)[1]
    d_residual_norm, grad_gain_ff = norm_ff_back(d_normed_ff)
    d_residual = dy[:rows].astype(f32) + d_residual_norm
    d_branch = jnp.concatenate(gather_blocks(d_residual.astype(bf16)))
    d_attended = backward_product(d_branch, out_blocks[0]).astype(bf16)
    grad_out = weight_product(attended, d_branch).astype(bf16)
    delta = jnp.sum(
        (d_attended.astype(f32) * attended_wide).reshape(tokens, heads_here, size), axis=2
    ).T
    d_qkv, d_table = pl.pallas_call(
        functools.partial(attend_back_kernel, rows, n, heads_here, size, seqs, buckets),
        out_shape=(
            jax.ShapeDtypeStruct((tokens, 3 * width), bf16),
            jax.ShapeDtypeStruct((buckets, 128), f32),
        ),
        grid_spec=pltpu.PrefetchScalarGridSpec(
            num_scalar_prefetch=2,
            grid=(n,),
            in_specs=[
                whole((tokens, 3 * width)),
                whole((heads_here, 5, rows, rows)),
                whole((heads_here, tokens)),
                whole((heads_here, tokens)),
                whole((tokens, width)),
            ],
            out_specs=[whole((tokens, 3 * width)), whole((buckets, 128))],
            scratch_shapes=[
                pltpu.VMEM((heads_here, n, size, rows), f32),
                pltpu.VMEM((heads_here, 5, rows, rows), f32),
            ],
        ),
        compiler_params=params,
        cost_estimate=pl.CostEstimate(
            flops=40 * tokens * tokens * width,
            bytes_accessed=16 * tokens * width,
            transcendentals=tokens * tokens * heads_here,
        ),
        name="attend_back",
    )(me_1, lengths_row, qkv, bias, lse, delta, d_attended)
    grad_qkv = weight_product(normed, d_qkv).astype(bf16)
    d_normed = scatter_rows(backward_product(d_qkv, qkv_weight))
    norm_attn_back = jax.vjp(rms_norm, x_all[:rows].astype(f32), gain_attention)[1]
    d_input_norm, grad_gain_attn = norm_attn_back(d_normed)
    input_grad = (d_residual + d_input_norm).astype(bf16)

    table_here = jnp.pad(d_table[:, :heads_here], ((0, 0), (0, n * heads_here)))
    table_here = jnp.roll(table_here, me * heads_here, axis=1)[:, :heads]
    small = jnp.concatenate([grad_gain_attn, grad_gain_ff, table_here.reshape(-1)])
    if fast:
        for axis, bit, count in (
            ("wshard", 1, n_w),
            ("ctx", 1, n_ctx),
            ("group", 1, n_group),
            ("group", 2, n_group),
            ("group", 4, n_group),
        ):
            small = small + lax.ppermute(small, axis, [(g, g ^ bit) for g in range(count)])
    else:
        small = lax.psum(small, ("group",) + peer_axes)
    share = model // n
    gains = [lax.dynamic_slice_in_dim(small, k * model + me * share, share) for k in range(2)]
    grad_table = small[2 * model :].reshape(buckets, heads)

    if not fast:

        def place_columns(grad, which, wide, total):
            full = jnp.zeros((grad.shape[0], n * wide), bf16)
            full = lax.dynamic_update_slice_in_dim(full, grad, which * wide, 1)
            return full[:, :total]

        def finish(full, dim):
            full = lax.psum_scatter(full, peer_axes, scatter_dimension=dim, tiled=True)
            return lax.psum(full, "group").astype(f32)

        total_qkv = [
            finish(
                place_columns(grad_qkv[:, k * width : (k + 1) * width], me, width, heads * size), 0
            )
            for k in range(3)
        ]
        total_out = finish(place_columns(grad_out.T, me, width, heads * size).T, 0)
        total_gate = finish(place_columns(grad_gate, rank, units, hidden_units), 0)
        total_up = finish(place_columns(grad_up, rank, units, hidden_units), 0)
        total_down = finish(place_columns(grad_down.T, rank, units, hidden_units).T, 1)
    else:
        spot = jnp.asarray([ladder_ring.index(g) for g in range(n_group)], jnp.int32)[
            lax.axis_index("group")
        ]
        ahead = [(ladder_ring[k], ladder_ring[(k + 1) % n_group]) for k in range(n_group)]
        behind = [(b, a) for a, b in ahead]

        def piece(array, index, axis):
            index = lax.rem(index, n_group)
            return lax.squeeze(lax.dynamic_slice_in_dim(array, index, 1, axis), (axis,))

        def ring_scatter(halves, axis):
            one, two = piece(halves[0], spot + 7, axis), piece(halves[1], spot + 1, axis)
            for s in range(n_group - 1):
                one = lax.ppermute(one, "group", ahead) + piece(halves[0], spot + 14 - s, axis)
                two = lax.ppermute(two, "group", behind) + piece(halves[1], spot + 2 + s, axis)
            return one, two

        def ring_gather(one, two, out, write):
            out = write(out, one, spot, 0)
            out = write(out, two, spot, 1)
            for s in range(n_group - 1):
                one = lax.ppermute(one, "group", ahead)
                two = lax.ppermute(two, "group", behind)
                out = write(out, one, lax.rem(spot + 15 - s, n_group), 0)
                out = write(out, two, lax.rem(spot + 1 + s, n_group), 1)
            return out

        def exchange(block_for):
            return [
                block_for(0),
                mate(block_for(1)),
                across(block_for(2)),
                lax.ppermute(block_for(3), peer_axes, [(q, q ^ 3) for q in range(n)]),
            ]

        def rank_of(k):
            peer = me ^ k
            return (peer % n_w) * n_ctx + peer // n_w

        strip = model // n // n_group
        part = strip // 2

        def finish_columns(grad):
            cut = grad.reshape(n, n_group, 2, part, units)
            one, two = ring_scatter((cut[:, :, 0], cut[:, :, 1]), 1)
            both = jnp.stack([one, two], axis=1)
            came = exchange(lambda k: piece_at(both, me ^ k, 0))
            full = jnp.zeros((2, part, n * units), bf16)
            for k in range(n):
                full = lax.dynamic_update_slice_in_dim(full, came[k], rank_of(k) * units, 2)

            def write(out, block, at, h):
                return lax.dynamic_update_slice(
                    out, block[:, :hidden_units].astype(f32)[None, None], (at, h, 0, 0)
                )

            out = jnp.zeros((n_group, 2, part, hidden_units), f32)
            out = ring_gather(full[0], full[1], out, write)
            return out.reshape(model // n, hidden_units)

        def piece_at(array, index, axis):
            return lax.squeeze(lax.dynamic_slice_in_dim(array, index, 1, axis), (axis,))

        def finish_down(grad):
            step = units // n_group // 2
            cols = model // n
            cut = grad.reshape(n_group, 2, step, model)
            one, two = ring_scatter((cut[:, 0], cut[:, 1]), 0)
            both = jnp.stack([one, two])
            came = exchange(lambda k: lax.dynamic_slice_in_dim(both, (me ^ k) * cols, cols, 2))
            full = jnp.zeros((n, 2, step, cols), bf16)
            for k in range(n):
                full = lax.dynamic_update_slice_in_dim(full, came[k][None], rank_of(k), 0)

            def write(out, block, at, h):
                return lax.dynamic_update_slice(
                    out, block.astype(f32)[:, None, None], (0, at, h, 0, 0)
                )

            out = jnp.zeros((n, n_group, 2, step, cols), f32)
            out = ring_gather(full[:, 0], full[:, 1], out, write)
            return out.reshape(n * units, cols)[:hidden_units]

        def finish_qkv(grad):
            cut = grad.reshape(n, n_group, 2, part, 3 * width)
            one, two = ring_scatter((cut[:, :, 0], cut[:, :, 1]), 1)
            both = jnp.stack([one, two], axis=1)
            came = exchange(lambda k: piece_at(both, me ^ k, 0))
            full = jnp.zeros((2, part, 3, n * width), bf16)
            for k in range(n):
                full = lax.dynamic_update_slice_in_dim(
                    full, came[k].reshape(2, part, 3, width), (me ^ k) * width, 3
                )
            full = full.reshape(2, part, 3 * n * width)

            def write(outs, block, at, h):
                return [
                    lax.dynamic_update_slice(
                        out,
                        block[:, k * n * width : (k + 1) * n * width].astype(f32)[None, None],
                        (at, h, 0, 0),
                    )
                    for k, out in enumerate(outs)
                ]

            outs = [jnp.zeros((n_group, 2, part, n * width), f32) for _ in range(3)]
            outs = ring_gather(full[0], full[1], outs, write)
            return [out.reshape(model // n, n * width) for out in outs]

        def finish_out(grad):
            step, cols = width // n_group, model // 2
            cut = grad.reshape(n_group, step, model)
            one, two = ring_scatter((cut[:, :, :cols], cut[:, :, cols:]), 0)

            def write(out, block, at, h):
                return lax.dynamic_update_slice(out, block.astype(f32)[None], (at, 0, h * cols))

            out = ring_gather(one, two, jnp.zeros((n_group, step, model), f32), write)
            return out.reshape(width, model)

        total_down = finish_down(grad_down)
        total_gate = finish_columns(grad_gate)
        total_up = finish_columns(grad_up)
        total_out = finish_out(grad_out)
        total_qkv = finish_qkv(grad_qkv)
    return (
        outputs,
        input_grad,
        gains[0],
        total_qkv[0],
        total_qkv[1],
        total_qkv[2],
        total_out,
        grad_table,
        gains[1],
        total_gate,
        total_up,
        total_down,
    )


def solution(mesh):
    sizes = (mesh.shape["group"], mesh.shape["ctx"], mesh.shape["wshard"])
    return jax.shard_map(
        functools.partial(per_device, sizes),
        mesh=mesh,
        in_specs=(
            P(("group", "ctx", "wshard"), None),
            P(("group", "ctx", "wshard"), None),
            P("group", None),
            P("group", None),
            P(),
            P("wshard", None),
            P("wshard", None),
            P("wshard", None),
            P("wshard", None),
            P(),
            P(),
            P("wshard", None),
            P("wshard", None),
            P("wshard", None),
        ),
        out_specs=(
            P(("group", "ctx", "wshard"), None),
            P(("group", "ctx", "wshard"), None),
            P(("ctx", "wshard")),
            P(("ctx", "wshard"), None),
            P(("ctx", "wshard"), None),
            P(("ctx", "wshard"), None),
            P(("ctx", "wshard"), None),
            P(),
            P(("ctx", "wshard")),
            P(("ctx", "wshard"), None),
            P(("ctx", "wshard"), None),
            P(None, ("ctx", "wshard")),
        ),
        check_vma=False,
    )
```

time: 1290 us -> 655 us (0.51)
  waiting for transfers between devices: 809 us -> 232 us
  starting transfers between devices: 1.02 us -> 171 us
  matrix products: 202 us -> 69.2 us
  blocking collectives: 67.9 us -> 0 us
  Pallas kernels: 0 us -> 61.7 us
  local copies, waits for them, and re-layouts: 113 us -> 55 us
  loops' own time: 16.8 us -> 0 us
    reduce_scatter x7 -> x0, waiting for transfers between devices: 344 us -> none  [the longest x1 99.5 us: per_device(): lax.psum_scatter(grad_up.astype(jnp.bfloat16), ('ctx', 'wshard'), scatter...]
    psum x1 -> x0, waiting for transfers between devices: 338 us -> none  [per_device(): lax.psum(shares[1].astype(jnp.bfloat16), 'group').astype(jnp.float32)]
    ppermute x0 -> x179, waiting for transfers between devices: none -> 232 us  [the longest x35 78.7 us: ring_scatter(): lax.ppermute(one, 'group', ahead) + piece(halves[0], spot + 14 - s, axis)]
    ppermute x0 -> x179, starting transfers between devices: none -> 171 us  [the longest x35 65.9 us: ring_scatter(): lax.ppermute(two, 'group', behind) + piece(halves[1], spot + 2 + s, axis)]
    dot_general x43 -> x13, matrix products: 202 us -> 69.2 us  [dot(): lax.dot_general(left_side, right_side, (dims, ((), ())), precision=precis...]
    all_gather x12 -> x0, waiting for transfers between devices: 67.7 us -> none  [the longest x1 20.1 us: per_device(): lax.all_gather(value_proj, ('ctx', 'wshard'), axis=0, tiled=True)]
    pallas_call x0 -> x4, Pallas kernels: none -> 61.7 us  [the longest x1 25.4 us: per_device(): pl.pallas_call(functools.partial(attend_back_kernel, rows, n, heads_here,...]
    psum x2 -> x0, blocking collectives: 59.8 us -> none  [the longest x1 39.9 us: per_device(): grad_table = lax.psum(d_table_all, ('group', 'ctx', 'wshard'))]
  transfers between devices with their start and end apart: 21 -> 179, of which waited for: 14 -> 92; matrix products, arithmetic and copies ran while one was open for 21% -> 15% of each run, Pallas kernels for 0% -> 6%
where the time goes in v1:
time: 655 us; the launch traced here: 650 us
  waiting for transfers between devices  232 us (35%)
  starting transfers between devices  171 us (26%)
  matrix products  69.2 us (11%)
  Pallas kernels  61.7 us (9%)
  local copies, waits for them, and re-layouts  55 us (8%)
  other arithmetic  45.7 us (7%)
  between operations  14.6 us (2%)
    ppermute x35, waiting for transfers between devices, ring_scatter(): lax.ppermute(one, 'group', ahead) + piece(halves[0], spot + 14 - s, axis)  78.7 us
    dot_general x13, matrix products, dot(): lax.dot_general(left_side, right_side, (dims, ((), ())), precision=precis...  69.2 us
    ppermute x35, starting transfers between devices, ring_scatter(): lax.ppermute(two, 'group', behind) + piece(halves[1], spot + 2 + s, axis)  65.9 us
    ppermute x35, waiting for transfers between devices, ring_gather(): one = lax.ppermute(one, 'group', ahead)  56.3 us
    ppermute x35, starting transfers between devices, ring_gather(): two = lax.ppermute(two, 'group', behind)  53.7 us
    ppermute x35, waiting for transfers between devices, ring_scatter(): lax.ppermute(two, 'group', behind) + piece(halves[1], spot + 2 + s, axis)  36.7 us
    ppermute x11, waiting for transfers between devices, across(): return lax.ppermute(block, 'ctx', flip_w)  33.2 us
    pallas_call x1, Pallas kernels, per_device(): pl.pallas_call(functools.partial(attend_back_kernel, rows, n, heads_here,...  25.4 us
  transfers between devices with their start and end apart: 179, of which 92 were waited for; matrix products, arithmetic and copies ran while one was open for 15% of the time, Pallas kernels for 6%

profile of v1, /device:TPU:0, one launch (start us, length us, event | category | flops | bytes accessed | tf_op | source)
XLA Modules:
  0.0 649.9 jit_solution(3050384750363836160)
XLA Ops:
  43.5 13.8 %collective-permute-done.2.refs_2_ = bf16[256,1536]{1,0:T(8,128)(2,1)} collective-permute-done((bf16[256,1536]{1,0:T(8,128)(2,1)}, bf16[256,1536]{1,0:T(8,128)(2,1)}, u32[]{:S(2)}, u32[]{:S(2)}) %collective-permute-start.2) | collective-permute-done | bytes 786464 | tf_op jit(solution)/shard_map/ppermute | solution.py:305
  69.5 10.4 %arrange_project.1 = (bf16[1024,1536]{1,0:T(8,128)(2,1)}, bf16[1024,1536]{1,0:T(8,128)(2,1)}, bf16[1024,576]{1,0:T(8,128)(2,1)}) custom-call(s32[1]{0:T(128)} %bitcast.me_ref, s32[4,256]{1,0:T(4,128)} %reshape.335.order_ref, f32[1,1536]{1,0:T(1,128)} %reshape.336.gain_ref, bf16[1536,576]{1,0:T(8,128)(2,1)} %pad_maximum_fusion.5.weight_ref, ...), custom_call_target="tpu_custom_call" | custom-call | flops 5033164800 | bytes 12582912 | tf_op jit(solution)/shard_map/arrange_project/pallas_call | solution.py:378
  79.9 22.5 %attend.1 = (bf16[1024,192]{1,0:T(8,128)(2,1)}, f32[1024,192]{1,0:T(8,128)}, f32[3,1024]{1,0:T(4,128)}) custom-call(s32[1]{0:T(128)} %bitcast.me_ref, s32[4]{0:T(128)} %bitcast.937, bf16[1024,576]{1,0:T(8,128)(2,1)} %get-tuple-element.21.qkv_ref, f32[3,5,256,256]{3,2,1,0:T(8,128)} %bias_strips.1.bias_ref), custom_call_target="tpu_custom_call" | custom-call | flops 3221225472 | bytes 3145728 | tf_op jit(solution)/shard_map/attend/pallas_call | solution.py:405
  107.0 9.5 %collective-permute-done.5 = bf16[1024,192]{1,0:T(8,128)(2,1)S(1)} collective-permute-done((bf16[1024,192]{1,0:T(8,128)(2,1)}, bf16[1024,192]{1,0:T(8,128)(2,1)S(1)}, u32[]{:S(2)}, u32[]{:S(2)}) %collective-permute-start.5) | collective-permute-done | bytes 393248 | tf_op jit(solution)/shard_map/ppermute | solution.py:305
  118.5 3.9 multiply_reduce_fusion
  126.8 9.1 %fusion = f32[1024,2048]{1,0:T(8,128)} fusion(bf16[1024,1536]{1,0:T(8,128)(2,1)S(1)} %multiply_convert_fusion, bf16[768,2048]{1,0:T(8,128)(2,1)S(1)} %get-tuple-element.67, bf16[768,2048]{1,0:T(8,128)(2,1)S(1)} %get-tuple-element.66), kind=kOutput, calls=%fused_computation.8 | convolution fusion | flops 6455033856 | bytes 17825792 | tf_op jit(solution)/shard_map/dot_general | solution.py:38
  135.9 11.2 %fusion.7 = (bf16[1024,1024]{1,0:T(8,128)(2,1)S(1)}, bf16[1024,1024]{1,0:T(8,128)(2,1)S(1)}, bf16[1024,1024]{1,0:T(8,128)(2,1)}) fusion(f32[1024,2048]{1,0:T(8,128)} %fusion, bf16[1024,1536]{1,0:T(8,128)(2,1)S(1)} %copy-done.30, s32[]{:T(128)S(6)} %select_n.216, bf16[1984,1536]{1,0:T(8,128)(2,1)} %param.28, bf16[64,1536]{1,0:T(8,128)(2,1)S(1)} %copy-done.31, ...), kind=kOutput, calls=%fused_computation.25 | convolution fusion | flops 3257925632 | bytes 24313860 | tf_op jit(solution)/shard_map/dot_general | solution.py:38
  147.1 6.3 fusion.13
  157.1 5.4 convolution_convert_fusion.4
  162.6 4.3 convolution_convert_fusion.1
  170.6 7.2 %add_convert_fusion = bf16[1024,1536]{1,0:T(8,128)(2,1)S(1)} fusion(f32[1024,1536]{1,0:T(8,128)} %fusion.13, bf16[1024,1024]{1,0:T(8,128)(2,1)S(1)} %get-tuple-element.62, bf16[768,2048]{1,0:T(8,128)(2,1)} %copy-done.11, bf16[768,2048]{1,0:T(8,128)(2,1)} %copy-done.12), kind=kOutput, calls=%fused_computation.9 | convolution fusion | flops 3230662656 | bytes 17825792 | tf_op jit(solution)/shard_map/dot_general | solution.py:38
  184.3 8.3 %collective-permute-done.148 = bf16[64,1536]{1,0:T(8,128)(2,1)S(1)} collective-permute-done((bf16[64,1536]{1,0:T(8,128)(2,1)S(1)}, bf16[64,1536]{1,0:T(8,128)(2,1)S(1)}, u32[]{:S(2)}, u32[]{:S(2)}) %collective-permute-start.148) | collective-permute-done | bytes 196640 | tf_op jit(solution)/shard_map/ppermute | solution.py:561
  194.2 4.6 collective-permute-done.155
  201.9 4.3 collective-permute-done.117
  209.2 4.6 collective-permute-done.149
  215.5 5.1 collective-permute-done.156
  223.3 4.9 collective-permute-done.118
  230.4 5.4 collective-permute-done.150
  237.1 6.3 collective-permute-done.157
  251.1 4.8 collective-permute-done.151
  259.5 4.5 collective-permute-done.158
  272.3 6.8 %collective-permute-done.152 = bf16[64,1536]{1,0:T(8,128)(2,1)S(1)} collective-permute-done((bf16[64,1536]{1,0:T(8,128)(2,1)S(1)}, bf16[64,1536]{1,0:T(8,128)(2,1)S(1)}, u32[]{:S(2)}, u32[]{:S(2)}) %collective-permute-start.152) | collective-permute-done | bytes 196640 | tf_op jit(solution)/shard_map/ppermute | solution.py:561
  280.7 4.1 collective-permute-done.159
  295.1 8.2 %collective-permute-done.160 = bf16[64,1536]{1,0:T(8,128)(2,1)S(1)} collective-permute-done((bf16[64,1536]{1,0:T(8,128)(2,1)S(1)}, bf16[64,1536]{1,0:T(8,128)(2,1)S(1)}, u32[]{:S(2)}, u32[]{:S(2)}) %collective-permute-start.160) | collective-permute-done | bytes 196640 | tf_op jit(solution)/shard_map/ppermute | solution.py:562
  303.3 6.1 collective-permute-done.153
  417.4 4.1 collective-permute-done.113
  456.9 25.4 %attend_back.1 = (bf16[1024,576]{1,0:T(8,128)(2,1)}, f32[32,128]{1,0:T(8,128)}) custom-call(s32[1]{0:T(128)} %bitcast.me_ref, s32[4]{0:T(128)} %bitcast.938, bf16[1024,576]{1,0:T(8,128)(2,1)} %get-tuple-element.21.qkv_ref, f32[3,5,256,256]{3,2,1,0:T(8,128)} %bias_strips.1.bias_ref, f32[3,1024]{1,0:T(4,128)} %get-tuple-element.23.lse_ref, ...), custom_call_target="tpu_custom_call" | custom-call | flops 8053063680 | bytes 3145728 | tf_op jit(solution)/shard_map/attend_back/pallas_call | solution.py:472
  482.3 5.0 convolution_convert_fusion
  489.8 5.2 convolution_convert_fusion.5
  573.7 7.3 %dynamic_update_slice.385 = bf16[2,24,3,768]{3,2,1,0:T(4,128)(2,1)S(1)} dynamic-update-slice(bf16[2,24,3,768]{3,2,1,0:T(4,128)(2,1)S(1)} %dynamic_update_slice.384, bf16[2,24,3,192]{3,2,1,0:T(4,128)(2,1)S(1)} %reshape.341, s32[]{:T(128)} %constant.320.clone.1, s32[]{:T(128)} %constant.320.clone.1, s32[]{:T(128)} %constant.320.clone.1, s32[]{:T(128)S(6)} %select_n.206) | dynamic-update-slice | bytes 110596 | tf_op jit(solution)/shard_map/dynamic_update_slice | solution.py:638
  582.2 7.3 %dynamic_update_slice.387 = bf16[2,24,3,768]{3,2,1,0:T(4,128)(2,1)S(1)} dynamic-update-slice(bf16[2,24,3,768]{3,2,1,0:T(4,128)(2,1)S(1)} %dynamic_update_slice.386, bf16[2,24,3,192]{3,2,1,0:T(4,128)(2,1)S(1)} %reshape.343, s32[]{:T(128)} %constant.320.clone.1, s32[]{:T(128)} %constant.320.clone.1, s32[]{:T(128)} %constant.320.clone.1, s32[]{:T(128)S(6)} %select_n.208) | dynamic-update-slice | bytes 110596 | tf_op jit(solution)/shard_map/dynamic_update_slice | solution.py:638
  622.8 5.4 collective-permute-done.21
  (730 shorter events, 394.1 us)
Async XLA Ops:
  0.6 38.2 %collective-permute-start.12 = (bf16[256,1536]{1,0:T(8,128)(2,1)}, bf16[256,1536]{1,0:T(8,128)(2,1)}, u32[]{:S(2)}, u32[]{:S(2)}) collective-permute-start(bf16[256,1536]{1,0:T(8,128)(2,1)} %param.16), channel_id=1, source_target_pairs={{0,1},{1,0},{2,3},{3,2},{4,5},{5,4},{6,7},{7,6},{8,9},{9,8},{10,11... | collective-permute-start | bytes 2359304 | tf_op jit(solution)/shard_map/ppermute | solution.py:302
  1.2 39.7 %collective-permute-start.13 = (bf16[256,1536]{1,0:T(8,128)(2,1)}, bf16[256,1536]{1,0:T(8,128)(2,1)}, u32[]{:S(2)}, u32[]{:S(2)}) collective-permute-start(bf16[256,1536]{1,0:T(8,128)(2,1)} %param.16), channel_id=1, source_target_pairs={{0,2},{2,0},{1,3},{3,1},{4,6},{6,4},{5,7},{7,5},{8,10},{10,8},{9,1... | collective-permute-start | bytes 2359304 | tf_op jit(solution)/shard_map/ppermute | solution.py:305
  3.8 59.9 %collective-permute-start.7 = (bf16[384,1536]{1,0:T(8,128)(2,1)}, bf16[384,1536]{1,0:T(8,128)(2,1)}, u32[]{:S(2)}, u32[]{:S(2)}) collective-permute-start(bf16[384,1536]{1,0:T(8,128)(2,1)} %param.23), channel_id=1, source_target_pairs={{0,1},{1,0},{2,3},{3,2},{4,5},{5,4},{6,7},{7,6},{8,9},{9,8},{10,11... | collective-permute-start | bytes 3538952 | tf_op jit(solution)/shard_map/ppermute | solution.py:302
  9.1 48.2 %collective-permute-start = (bf16[768,576]{0,1:T(8,128)(2,1)}, bf16[768,576]{0,1:T(8,128)(2,1)}, u32[]{:S(2)}, u32[]{:S(2)}) collective-permute-start(bf16[768,576]{0,1:T(8,128)(2,1)} %pad_maximum_fusion.10), channel_id=1, source_target_pairs={{0,1},{1,0},{2,3},{3,2},{4,5},{5,4},{6,7},{7,6},{8,9},{9,8},{10,11... | collective-permute-start | bytes 2654216 | tf_op jit(solution)/shard_map/ppermute | solution.py:302
  11.0 26.1 %collective-permute-start.9 = (bf16[64,1536]{1,0:T(8,128)(2,1)}, bf16[64,1536]{1,0:T(8,128)(2,1)}, u32[]{:S(2)}, u32[]{:S(2)}) collective-permute-start(bf16[64,1536]{1,0:T(8,128)(2,1)} %slice.470), channel_id=1, source_target_pairs={{0,1},{1,0},{2,3},{3,2},{4,5},{5,4},{6,7},{7,6},{8,9},{9,8},{10,11... | collective-permute-start | bytes 589832 | tf_op jit(solution)/shard_map/ppermute | solution.py:302
  37.1 20.1 %collective-permute-start.2 = (bf16[256,1536]{1,0:T(8,128)(2,1)}, bf16[256,1536]{1,0:T(8,128)(2,1)}, u32[]{:S(2)}, u32[]{:S(2)}) collective-permute-start(bf16[256,1536]{1,0:T(8,128)(2,1)} %refs_0_.1), channel_id=1, source_target_pairs={{0,2},{2,0},{1,3},{3,1},{4,6},{6,4},{5,7},{7,5},{8,10},{10,8},{9,1... | collective-permute-start | bytes 2359304 | tf_op jit(solution)/shard_map/ppermute | solution.py:305
  38.8 30.7 %collective-permute-start.1 = (bf16[256,1536]{1,0:T(8,128)(2,1)}, bf16[256,1536]{1,0:T(8,128)(2,1)}, u32[]{:S(2)}, u32[]{:S(2)}) collective-permute-start(bf16[256,1536]{1,0:T(8,128)(2,1)} %refs_0_.1), channel_id=1, source_target_pairs={{0,1},{1,0},{2,3},{3,2},{4,5},{5,4},{6,7},{7,6},{8,9},{9,8},{10,11... | collective-permute-start | bytes 2359304 | tf_op jit(solution)/shard_map/ppermute | solution.py:302
  40.9 82.9 %collective-permute-start.8 = (bf16[768,2048]{1,0:T(8,128)(2,1)}, bf16[768,2048]{1,0:T(8,128)(2,1)}, u32[]{:S(2)}, u32[]{:S(2)}) collective-permute-start(bf16[768,2048]{1,0:T(8,128)(2,1)} %pad_maximum_fusion.3), channel_id=1, source_target_pairs={{0,1},{1,0},{2,3},{3,2},{4,5},{5,4},{6,7},{7,6},{8,9},{9,8},{10,11... | collective-permute-start | bytes 9437192 | tf_op jit(solution)/shard_map/ppermute | solution.py:302
  57.3 47.5 %collective-permute-start.14 = (bf16[256,1536]{1,0:T(8,128)(2,1)}, bf16[256,1536]{1,0:T(8,128)(2,1)}, u32[]{:S(2)}, u32[]{:S(2)}) collective-permute-start(bf16[256,1536]{1,0:T(8,128)(2,1)} %collective-permute-done.13), channel_id=1, source_target_pairs={{0,1},{1,0},{2,3},{3,2},{4,5},{5,4},{6,7},{7,6},{8,9},{9,8},{10,11... | collective-permute-start | bytes 2359304 | tf_op jit(solution)/shard_map/ppermute | solution.py:302
  179.2 165.6 %collective-permute-start.15 = (bf16[2,256,1536]{2,1,0:T(8,128)(2,1)}, bf16[2,256,1536]{2,1,0:T(8,128)(2,1)S(1)}, u32[]{:S(2)}, u32[]{:S(2)}) collective-permute-start(bf16[2,256,1536]{2,1,0:T(8,128)(2,1)} %pad_maximum_fusion.7), channel_id=1, source_target_pairs={{0,1},{1,0},{2,3},{3,2},{4,5},{5,4},{6,7},{7,6},{8,9},{9,8},{10,11... | collective-permute-start | bytes 4718600 | tf_op jit(solution)/shard_map/ppermute | solution.py:302
  180.7 166.3 %collective-permute-start.10 = (bf16[2,256,1536]{2,1,0:T(8,128)(2,1)}, bf16[2,256,1536]{2,1,0:T(8,128)(2,1)}, u32[]{:S(2)}, u32[]{:S(2)}) collective-permute-start(bf16[2,256,1536]{2,1,0:T(8,128)(2,1)} %pad_maximum_fusion.6), channel_id=1, source_target_pairs={{0,1},{1,0},{2,3},{3,2},{4,5},{5,4},{6,7},{7,6},{8,9},{9,8},{10,11... | collective-permute-start | bytes 4718600 | tf_op jit(solution)/shard_map/ppermute | solution.py:302
  181.4 17.9 %collective-permute-start.86 = (bf16[4,24,1024]{2,1,0:T(8,128)(2,1)S(1)}, bf16[4,24,1024]{2,1,0:T(8,128)(2,1)S(1)}, u32[]{:S(2)}, u32[]{:S(2)}) collective-permute-start(bf16[4,24,1024]{2,1,0:T(8,128)(2,1)S(1)} %dynamic-slice_bitcast_fusion.5), channel_id=1, source_target_pairs={{0,8},{8,16},{16,24},{24,28},{28,20},{20,12},{12,4},{4,0},{1,9},{9... | collective-permute-start | bytes 589832 | tf_op jit(solution)/shard_map/ppermute | solution.py:561
  181.5 19.3 %collective-permute-start.93 = (bf16[4,24,1024]{2,1,0:T(8,128)(2,1)S(1)}, bf16[4,24,1024]{2,1,0:T(8,128)(2,1)S(1)}, u32[]{:S(2)}, u32[]{:S(2)}) collective-permute-start(bf16[4,24,1024]{2,1,0:T(8,128)(2,1)S(1)} %dynamic-slice_bitcast_fusion.4), channel_id=1, source_target_pairs={{8,0},{16,8},{24,16},{28,24},{20,28},{12,20},{4,12},{0,4},{9,1},{1... | collective-permute-start | bytes 589832 | tf_op jit(solution)/shard_map/ppermute | solution.py:562
  200.9 19.7 %collective-permute-start.87 = (bf16[4,24,1024]{2,1,0:T(8,128)(2,1)S(1)}, bf16[4,24,1024]{2,1,0:T(8,128)(2,1)S(1)}, u32[]{:S(2)}, u32[]{:S(2)}) collective-permute-start(bf16[4,24,1024]{2,1,0:T(8,128)(2,1)S(1)} %bitcast_add_fusion.41), channel_id=1, source_target_pairs={{0,8},{8,16},{16,24},{24,28},{28,20},{20,12},{12,4},{4,0},{1,9},{9... | collective-permute-start | bytes 589832 | tf_op jit(solution)/shard_map/ppermute | solution.py:561
  206.2 17.0 %collective-permute-start.94 = (bf16[4,24,1024]{2,1,0:T(8,128)(2,1)S(1)}, bf16[4,24,1024]{2,1,0:T(8,128)(2,1)S(1)}, u32[]{:S(2)}, u32[]{:S(2)}) collective-permute-start(bf16[4,24,1024]{2,1,0:T(8,128)(2,1)S(1)} %bitcast_add_fusion.34), channel_id=1, source_target_pairs={{8,0},{16,8},{24,16},{28,24},{20,28},{12,20},{4,12},{0,4},{9,1},{1... | collective-permute-start | bytes 589832 | tf_op jit(solution)/shard_map/ppermute | solution.py:562
  223.2 20.3 %collective-permute-start.88 = (bf16[4,24,1024]{2,1,0:T(8,128)(2,1)S(1)}, bf16[4,24,1024]{2,1,0:T(8,128)(2,1)S(1)}, u32[]{:S(2)}, u32[]{:S(2)}) collective-permute-start(bf16[4,24,1024]{2,1,0:T(8,128)(2,1)S(1)} %bitcast_add_fusion.40), channel_id=1, source_target_pairs={{0,8},{8,16},{16,24},{24,28},{28,20},{20,12},{12,4},{4,0},{1,9},{9... | collective-permute-start | bytes 589832 | tf_op jit(solution)/shard_map/ppermute | solution.py:561
  228.2 17.3 %collective-permute-start.95 = (bf16[4,24,1024]{2,1,0:T(8,128)(2,1)S(1)}, bf16[4,24,1024]{2,1,0:T(8,128)(2,1)S(1)}, u32[]{:S(2)}, u32[]{:S(2)}) collective-permute-start(bf16[4,24,1024]{2,1,0:T(8,128)(2,1)S(1)} %bitcast_add_fusion.33), channel_id=1, source_target_pairs={{8,0},{16,8},{24,16},{28,24},{20,28},{12,20},{4,12},{0,4},{9,1},{1... | collective-permute-start | bytes 589832 | tf_op jit(solution)/shard_map/ppermute | solution.py:562
  245.5 18.6 %collective-permute-start.89 = (bf16[4,24,1024]{2,1,0:T(8,128)(2,1)S(1)}, bf16[4,24,1024]{2,1,0:T(8,128)(2,1)S(1)}, u32[]{:S(2)}, u32[]{:S(2)}) collective-permute-start(bf16[4,24,1024]{2,1,0:T(8,128)(2,1)S(1)} %bitcast_add_fusion.39), channel_id=1, source_target_pairs={{0,8},{8,16},{16,24},{24,28},{28,20},{20,12},{12,4},{4,0},{1,9},{9... | collective-permute-start | bytes 589832 | tf_op jit(solution)/shard_map/ppermute | solution.py:561
  249.0 17.6 %collective-permute-start.96 = (bf16[4,24,1024]{2,1,0:T(8,128)(2,1)S(1)}, bf16[4,24,1024]{2,1,0:T(8,128)(2,1)S(1)}, u32[]{:S(2)}, u32[]{:S(2)}) collective-permute-start(bf16[4,24,1024]{2,1,0:T(8,128)(2,1)S(1)} %bitcast_add_fusion.32), channel_id=1, source_target_pairs={{8,0},{16,8},{24,16},{28,24},{20,28},{12,20},{4,12},{0,4},{9,1},{1... | collective-permute-start | bytes 589832 | tf_op jit(solution)/shard_map/ppermute | solution.py:562
  266.6 18.9 %collective-permute-start.90 = (bf16[4,24,1024]{2,1,0:T(8,128)(2,1)S(1)}, bf16[4,24,1024]{2,1,0:T(8,128)(2,1)S(1)}, u32[]{:S(2)}, u32[]{:S(2)}) collective-permute-start(bf16[4,24,1024]{2,1,0:T(8,128)(2,1)S(1)} %bitcast_add_fusion.38), channel_id=1, source_target_pairs={{0,8},{8,16},{16,24},{24,28},{28,20},{20,12},{12,4},{4,0},{1,9},{9... | collective-permute-start | bytes 589832 | tf_op jit(solution)/shard_map/ppermute | solution.py:561
  270.2 16.8 %collective-permute-start.97 = (bf16[4,24,1024]{2,1,0:T(8,128)(2,1)S(1)}, bf16[4,24,1024]{2,1,0:T(8,128)(2,1)S(1)}, u32[]{:S(2)}, u32[]{:S(2)}) collective-permute-start(bf16[4,24,1024]{2,1,0:T(8,128)(2,1)S(1)} %bitcast_add_fusion.31), channel_id=1, source_target_pairs={{8,0},{16,8},{24,16},{28,24},{20,28},{12,20},{4,12},{0,4},{9,1},{1... | collective-permute-start | bytes 589832 | tf_op jit(solution)/shard_map/ppermute | solution.py:562
  287.0 22.5 %collective-permute-start.91 = (bf16[4,24,1024]{2,1,0:T(8,128)(2,1)S(1)}, bf16[4,24,1024]{2,1,0:T(8,128)(2,1)S(1)}, u32[]{:S(2)}, u32[]{:S(2)}) collective-permute-start(bf16[4,24,1024]{2,1,0:T(8,128)(2,1)S(1)} %bitcast_add_fusion.37), channel_id=1, source_target_pairs={{0,8},{8,16},{16,24},{24,28},{28,20},{20,12},{12,4},{4,0},{1,9},{9... | collective-permute-start | bytes 589832 | tf_op jit(solution)/shard_map/ppermute | solution.py:561
  291.4 20.1 %collective-permute-start.98 = (bf16[4,24,1024]{2,1,0:T(8,128)(2,1)S(1)}, bf16[4,24,1024]{2,1,0:T(8,128)(2,1)S(1)}, u32[]{:S(2)}, u32[]{:S(2)}) collective-permute-start(bf16[4,24,1024]{2,1,0:T(8,128)(2,1)S(1)} %bitcast_add_fusion.30), channel_id=1, source_target_pairs={{8,0},{16,8},{24,16},{28,24},{20,28},{12,20},{4,12},{0,4},{9,1},{1... | collective-permute-start | bytes 589832 | tf_op jit(solution)/shard_map/ppermute | solution.py:562
  350.6 50.6 %collective-permute-start.16 = (bf16[256,1536]{1,0:T(8,128)(2,1)S(1)}, bf16[256,1536]{1,0:T(8,128)(2,1)S(1)}, u32[]{:S(2)}, u32[]{:S(2)}) collective-permute-start(bf16[256,1536]{1,0:T(8,128)(2,1)S(1)} %fusion.55), channel_id=1, source_target_pairs={{0,2},{2,0},{1,3},{3,1},{4,6},{6,4},{5,7},{7,5},{8,10},{10,8},{9,1... | collective-permute-start | bytes 2359304 | tf_op jit(solution)/shard_map/ppermute | solution.py:305
  351.6 52.0 %collective-permute-start.11 = (bf16[256,1536]{1,0:T(8,128)(2,1)S(1)}, bf16[256,1536]{1,0:T(8,128)(2,1)S(1)}, u32[]{:S(2)}, u32[]{:S(2)}) collective-permute-start(bf16[256,1536]{1,0:T(8,128)(2,1)S(1)} %fusion.57), channel_id=1, source_target_pairs={{0,2},{2,0},{1,3},{3,1},{4,6},{6,4},{5,7},{7,5},{8,10},{10,8},{9,1... | collective-permute-start | bytes 2359304 | tf_op jit(solution)/shard_map/ppermute | solution.py:305
  410.1 39.3 %collective-permute-start.18 = (bf16[256,1536]{1,0:T(8,128)(2,1)S(1)}, bf16[256,1536]{1,0:T(8,128)(2,1)S(1)}, u32[]{:S(2)}, u32[]{:S(2)}) collective-permute-start(bf16[256,1536]{1,0:T(8,128)(2,1)S(1)} %get-tuple-element.60), channel_id=1, source_target_pairs={{0,2},{2,0},{1,3},{3,1},{4,6},{6,4},{5,7},{7,5},{8,10},{10,8},{9,1... | collective-permute-start | bytes 2359304 | tf_op jit(solution)/shard_map/ppermute | solution.py:305
  412.4 37.1 %collective-permute-start.17 = (bf16[256,1536]{1,0:T(8,128)(2,1)S(1)}, bf16[256,1536]{1,0:T(8,128)(2,1)S(1)}, u32[]{:S(2)}, u32[]{:S(2)}) collective-permute-start(bf16[256,1536]{1,0:T(8,128)(2,1)S(1)} %get-tuple-element.60), channel_id=1, source_target_pairs={{0,1},{1,0},{2,3},{3,2},{4,5},{5,4},{6,7},{7,6},{8,9},{9,8},{10,11... | collective-permute-start | bytes 2359304 | tf_op jit(solution)/shard_map/ppermute | solution.py:302
  434.3 15.1 %collective-permute-start.147 = (bf16[24,4096]{1,0:T(8,128)(2,1)S(1)}, bf16[24,4096]{1,0:T(8,128)(2,1)S(1)}, u32[]{:S(2)}, u32[]{:S(2)}) collective-permute-start(bf16[24,4096]{1,0:T(8,128)(2,1)S(1)} %collective-permute-done.145), channel_id=1, source_target_pairs={{8,0},{16,8},{24,16},{28,24},{20,28},{12,20},{4,12},{0,4},{9,1},{1... | collective-permute-start | bytes 589832 | tf_op jit(solution)/shard_map/ppermute | solution.py:570
  489.4 123.2 %collective-permute-start.20 = (bf16[2,256,1536]{2,1,0:T(8,128)(2,1)}, bf16[2,256,1536]{2,1,0:T(8,128)(2,1)}, u32[]{:S(2)}, u32[]{:S(2)}) collective-permute-start(bf16[2,256,1536]{2,1,0:T(8,128)(2,1)} %pad_maximum_fusion.8), channel_id=1, source_target_pairs={{0,1},{1,0},{2,3},{3,2},{4,5},{5,4},{6,7},{7,6},{8,9},{9,8},{10,11... | collective-permute-start | bytes 4718600 | tf_op jit(solution)/shard_map/ppermute | solution.py:302
  556.6 16.0 %collective-permute-start.85 = (bf16[24,768]{1,0:T(8,128)(2,1)S(1)}, bf16[24,768]{1,0:T(8,128)(2,1)S(1)}, u32[]{:S(2)}, u32[]{:S(2)}) collective-permute-start(bf16[24,768]{1,0:T(8,128)(2,1)S(1)} %collective-permute-done.83), channel_id=1, source_target_pairs={{8,0},{16,8},{24,16},{28,24},{20,28},{12,20},{4,12},{0,4},{9,1},{1... | collective-permute-start | bytes 110600 | tf_op jit(solution)/shard_map/ppermute | solution.py:570
  614.0 14.3 %collective-permute-start.21 = (bf16[256,1536]{1,0:T(8,128)(2,1)S(1)}, bf16[256,1536]{1,0:T(8,128)(2,1)S(1)}, u32[]{:S(2)}, u32[]{:S(2)}) collective-permute-start(bf16[256,1536]{1,0:T(8,128)(2,1)S(1)} %fusion.53), channel_id=1, source_target_pairs={{0,2},{2,0},{1,3},{3,1},{4,6},{6,4},{5,7},{7,5},{8,10},{10,8},{9,1... | collective-permute-start | bytes 2359304 | tf_op jit(solution)/shard_map/ppermute | solution.py:305
  622.5 14.3 %collective-permute-start.57 = (bf16[24,2304]{1,0:T(8,128)(2,1)S(1)}, bf16[24,2304]{1,0:T(8,128)(2,1)S(1)}, u32[]{:S(2)}, u32[]{:S(2)}) collective-permute-start(bf16[24,2304]{1,0:T(8,128)(2,1)S(1)} %collective-permute-done.55), channel_id=1, source_target_pairs={{8,0},{16,8},{24,16},{28,24},{20,28},{12,20},{4,12},{0,4},{9,1},{1... | collective-permute-start | bytes 331784 | tf_op jit(solution)/shard_map/ppermute | solution.py:570
  (203 other events, 1697.4 us)

commit v2 on v1

--- a/solution.py
+++ b/solution.py
@@ -314,17 +314,6 @@
         stacked = to_relative(lax.all_gather(block, peer_axes, axis=0, tiled=False))
         return [stacked[k] for k in range(n)]
 
-    def scatter_rows(partial):
-        if fast:
-            sent = partial.astype(bf16).reshape(n, rows, -1)
-            pair = jnp.stack([sent[1], sent[3]])
-            got = mate(pair)
-            near = sent[0].astype(f32) + got[0].astype(f32)
-            away = (sent[2].astype(f32) + got[1].astype(f32)).astype(bf16)
-            return near + across(away).astype(f32)
-        stacked = to_relative(partial.astype(bf16).reshape(n, rows, -1))
-        return lax.psum_scatter(stacked, peer_axes, scatter_dimension=0, tiled=False).astype(f32)
-
     def columns_of(weight, which, wide):
         over = max(0, n * wide - weight.shape[1])
         padded = jnp.pad(weight, ((0, 0), (0, over))) if over else weight
@@ -338,6 +327,7 @@
         return jnp.concatenate([upper, lower], axis=0)
 
     row_blocks = gather_blocks(inputs)
+    far_first, out_grad = lax.optimization_barrier((row_blocks[2], out_grad))
     qkv_weight = own_columns(
         (query_weight, key_weight, value_weight), width, me, ctx * n_w + (1 - wsh)
     )
@@ -428,6 +418,165 @@
         name="attend",
     )(me_1, lengths_row, qkv, bias)
 
+    strip = model // n // n_group
+    part = strip // 2
+    if fast:
+        group = lax.axis_index("group")
+        spot = jnp.where(group % 2 == 0, group // 2, n_group - 1 - group // 2)
+        ahead = [(ladder_ring[k], ladder_ring[(k + 1) % n_group]) for k in range(n_group)]
+        behind = [(b, a) for a, b in ahead]
+
+    def forward(block):
+        return lax.ppermute(block, "group", ahead)
+
+    def backward(block):
+        return lax.ppermute(block, "group", behind)
+
+    def diagonal(block):
+        return lax.ppermute(block, peer_axes, [(q, q ^ 3) for q in range(n)])
+
+    def pick(array, index, axis):
+        return lax.squeeze(lax.dynamic_slice_in_dim(array, index, 1, axis), (axis,))
+
+    def rank_of(k):
+        peer = me ^ k
+        return (peer % n_w) * n_ctx + peer // n_w
+
+    def ring(take, swap, write):
+        both_ways = (forward, backward)
+        one, two = take(0, lax.rem(spot + 7, n_group)), take(1, lax.rem(spot + 1, n_group))
+        for s in range(n_group - 1):
+            came = yield (one, two), both_ways
+            one = came[0] + take(0, lax.rem(spot + 14 - s, n_group))
+            two = came[1] + take(1, lax.rem(spot + 2 + s, n_group))
+        blocks, join = swap(jnp.stack([one, two], axis=1))
+        came = yield tuple(blocks[1:]), (mate, across, diagonal)
+        one, two = join([blocks[0], *came])
+        out = write(write(None, one, spot, 0), two, spot, 1)
+        for s in range(n_group - 1):
+            one, two = yield (one, two), both_ways
+            out = write(out, one, lax.rem(spot + 15 - s, n_group), 0)
+            out = write(out, two, lax.rem(spot + 1 + s, n_group), 1)
+        return out
+
+    class Stream:
+        def __init__(self, steps):
+            self.steps, self.result = steps, None
+            self.pending = next(steps)
+
+        def advance(self, came):
+            try:
+                self.pending = self.steps.send(came)
+            except StopIteration as stop:
+                self.pending, self.result = None, stop.value
+
+    def tick(values, *streams):
+        live = [stream for stream in streams if stream is not None and stream.pending is not None]
+        if not live:
+            return values
+        operands, values = lax.optimization_barrier(
+            ([stream.pending[0] for stream in live], values)
+        )
+        for stream, sent in zip(live, operands):
+            stream.advance([send(x) for send, x in zip(stream.pending[1], sent)])
+        return values
+
+    def rows_cut(grad):
+        return grad.reshape(n, n_group, 2, part, grad.shape[1])
+
+    def put(out, block, at, h):
+        if out is None:
+            out = jnp.zeros((n_group, 2) + block.shape, block.dtype)
+        return lax.dynamic_update_slice(out, block[None, None], (at, h) + (0,) * block.ndim)
+
+    def wide_ring(grad_gate_up, grad_down):
+        one, two = rows_cut(grad_gate_up), rows_cut(grad_down)
+        kinds = 3
+
+        def take(h, index):
+            return jnp.concatenate(
+                [pick(one[:, :, h], index, 1), pick(two[:, :, h], index, 1)], axis=-1
+            )
+
+        def swap(both):
+            def join(came):
+                full = jnp.zeros((2, part, kinds * n * units), bf16)
+                for k in range(n):
+                    for t in range(kinds):
+                        full = lax.dynamic_update_slice_in_dim(
+                            full,
+                            came[k][:, :, t * units : (t + 1) * units],
+                            t * n * units + rank_of(k) * units,
+                            2,
+                        )
+                return full[0], full[1]
+
+            return [pick(both, me ^ k, 0) for k in range(n)], join
+
+        def write(outs, block, at, h):
+            outs = outs or [None] * kinds
+            cuts = [block[:, t * n * units :][:, :hidden_units] for t in range(kinds)]
+            cuts = [cuts[0].astype(f32), cuts[1].astype(f32), cuts[2]]
+            return [put(out, cut, at, h) for out, cut in zip(outs, cuts)]
+
+        return ring(take, swap, write)
+
+    def small_ring(grad_qkv, grad_out):
+        grad = rows_cut(jnp.concatenate([grad_qkv, grad_out], axis=1))
+
+        def take(h, index):
+            return pick(grad[:, :, h], index, 1)
+
+        def swap(both):
+            own = jnp.concatenate([both[k, :, :, 3 * width :] for k in range(n)], axis=2)
+
+            def join(came):
+                stacked = jnp.stack(came)
+                came = [pick(stacked, me ^ r, 0) for r in range(n)]
+                full = jnp.concatenate(
+                    [came[r][:, :, k * width : (k + 1) * width] for k in range(3) for r in range(n)]
+                    + [own],
+                    axis=2,
+                )
+                return full[0], full[1]
+
+            return [pick(both, me ^ k, 0)[:, :, : 3 * width] for k in range(n)], join
+
+        def write(outs, block, at, h):
+            outs = outs or [None] * 4
+            across_heads = n * width
+            cuts = [
+                block[:, k * across_heads : (k + 1) * across_heads].astype(f32) for k in range(4)
+            ]
+            return [put(out, cut, at, h) for out, cut in zip(outs, cuts)]
+
+        return ring(take, swap, write)
+
+    def sum_ring(small):
+        for axis, bit, count in (
+            ("wshard", 1, n_w),
+            ("ctx", 1, n_ctx),
+            ("group", 1, n_group),
+            ("group", 2, n_group),
+            ("group", 4, n_group),
+        ):
+            pairs = [(g, g ^ bit) for g in range(count)]
+            came = yield (small,), (lambda x: lax.ppermute(x, axis, pairs),)
+            small = small + came[0]
+        return small
+
+    def scatter_near(partial):
+        sent = partial.reshape(n, rows, -1)
+        if not fast:
+            total = lax.psum_scatter(to_relative(sent), peer_axes, scatter_dimension=0, tiled=False)
+            return total.astype(f32), None
+        got = mate(jnp.stack([sent[1], sent[3]]))
+        near = sent[0].astype(f32) + got[0].astype(f32)
+        return near, (sent[2].astype(f32) + got[1].astype(f32)).astype(bf16)
+
+    def scatter_far(near, away):
+        return near + across(away).astype(f32) if fast else near
+
     attended_blocks = gather_blocks(attended)
     by_rows = [
         jnp.concatenate(
@@ -449,26 +598,42 @@
 
     hidden_wide, activate_back = jax.vjp(activate, gate_proj, up_proj)
     hidden = hidden_wide.astype(bf16)
-    grad_down = weight_product(hidden, dy).astype(bf16)
     d_hidden = backward_product(dy, down_own)
     d_gate_wide, d_up_wide = activate_back(d_hidden)
-    d_gate, d_up = d_gate_wide.astype(bf16), d_up_wide.astype(bf16)
-    grad_gate = weight_product(normed_ff, d_gate).astype(bf16)
-    grad_up = weight_product(normed_ff, d_up).astype(bf16)
-    d_normed_ff = scatter_rows(
-        backward_product(d_gate, gate_up[:, :units]) + backward_product(d_up, gate_up[:, units:])
-    )
-    outputs = (residual + scatter_rows(forward_product(hidden, down_own))).astype(bf16)
-
+    d_gate_up = jnp.concatenate([d_gate_wide.astype(bf16), d_up_wide.astype(bf16)], axis=1)
+    grad_gate_up = weight_product(normed_ff, d_gate_up).astype(bf16)
+    grad_down = weight_product(dy, hidden).astype(bf16)
+    wide = Stream(wide_ring(grad_gate_up, grad_down)) if fast else None
+    d_gate_up, hidden = tick((d_gate_up, hidden), wide)
+
+    back = backward_product(d_gate_up, gate_up).astype(bf16)
+    back, hidden = tick((back, hidden), wide)
+    near, away = scatter_near(back)
+    out_partial = forward_product(hidden, down_own).astype(bf16)
+    near, away, out_partial = tick((near, away, out_partial), wide)
+    d_normed_ff = scatter_far(near, away)
+    out_near, out_away = scatter_near(out_partial)
+    out_near, out_away = tick((out_near, out_away), wide)
     norm_ff_back = jax.vjp(rms_norm, residual, gain_feedforward)[1]
     d_residual_norm, grad_gain_ff = norm_ff_back(d_normed_ff)
     d_residual = dy[:rows].astype(f32) + d_residual_norm
-    d_branch = jnp.concatenate(gather_blocks(d_residual.astype(bf16)))
+    branch = d_residual.astype(bf16)
+    branch, out_away = tick((branch, out_away), wide)
+    if fast:
+        branch_far, branch_mate = across(branch), mate(branch)
+        (branch_mate,) = tick((branch_mate,), wide)
+        branch_far, out_away = tick((branch_far, out_away), wide)
+        branch_blocks = [branch, branch_mate, branch_far, mate(branch_far)]
+    else:
+        branch_blocks = gather_blocks(branch)
+    outputs = (residual + scatter_far(out_near, out_away)).astype(bf16)
+
+    d_branch = jnp.concatenate(branch_blocks)
     d_attended = backward_product(d_branch, out_blocks[0]).astype(bf16)
-    grad_out = weight_product(attended, d_branch).astype(bf16)
     delta = jnp.sum(
         (d_attended.astype(f32) * attended_wide).reshape(tokens, heads_here, size), axis=2
     ).T
+    d_attended, delta = tick((d_attended, delta), wide)
     d_qkv, d_table = pl.pallas_call(
         functools.partial(attend_back_kernel, rows, n, heads_here, size, seqs, buckets),
         out_shape=(
@@ -499,8 +664,18 @@
         ),
         name="attend_back",
     )(me_1, lengths_row, qkv, bias, lse, delta, d_attended)
+    d_qkv, d_branch = tick((d_qkv, d_branch), wide)
     grad_qkv = weight_product(normed, d_qkv).astype(bf16)
-    d_normed = scatter_rows(backward_product(d_qkv, qkv_weight))
+    grad_out = weight_product(d_branch, attended).astype(bf16)
+    narrow = Stream(small_ring(grad_qkv, grad_out)) if fast else None
+    (d_qkv,) = tick((d_qkv,), wide, narrow)
+
+    back = backward_product(d_qkv, qkv_weight).astype(bf16)
+    (back,) = tick((back,), narrow)
+    near, away = scatter_near(back)
+    near, away = tick((near, away), wide, narrow)
+    d_normed = scatter_far(near, away)
+    (d_normed,) = tick((d_normed,), narrow)
     norm_attn_back = jax.vjp(rms_norm, x_all[:rows].astype(f32), gain_attention)[1]
     d_input_norm, grad_gain_attn = norm_attn_back(d_normed)
     input_grad = (d_residual + d_input_norm).astype(bf16)
@@ -509,21 +684,23 @@
     table_here = jnp.roll(table_here, me * heads_here, axis=1)[:, :heads]
     small = jnp.concatenate([grad_gain_attn, grad_gain_ff, table_here.reshape(-1)])
     if fast:
-        for axis, bit, count in (
-            ("wshard", 1, n_w),
-            ("ctx", 1, n_ctx),
-            ("group", 1, n_group),
-            ("group", 2, n_group),
-            ("group", 4, n_group),
-        ):
-            small = small + lax.ppermute(small, axis, [(g, g ^ bit) for g in range(count)])
+        sums = Stream(sum_ring(small))
+        while wide.pending or narrow.pending or sums.pending:
+            tick((), wide, narrow, sums)
+            tick((), narrow)
+        small = sums.result
     else:
         small = lax.psum(small, ("group",) + peer_axes)
     share = model // n
     gains = [lax.dynamic_slice_in_dim(small, k * model + me * share, share) for k in range(2)]
     grad_table = small[2 * model :].reshape(buckets, heads)
 
-    if not fast:
+    if fast:
+        total_gate, total_up = [x.reshape(model // n, hidden_units) for x in wide.result[:2]]
+        total_down = wide.result[2].reshape(model // n, hidden_units).T.astype(f32)
+        total_qkv = [x.reshape(model // n, n * width) for x in narrow.result[:3]]
+        total_out = narrow.result[3].reshape(-1, n, width).transpose(2, 1, 0).reshape(width, model)
+    else:
 
         def place_columns(grad, which, wide, total):
             full = jnp.zeros((grad.shape[0], n * wide), bf16)
@@ -540,136 +717,10 @@
             )
             for k in range(3)
         ]
-        total_out = finish(place_columns(grad_out.T, me, width, heads * size).T, 0)
-        total_gate = finish(place_columns(grad_gate, rank, units, hidden_units), 0)
-        total_up = finish(place_columns(grad_up, rank, units, hidden_units), 0)
-        total_down = finish(place_columns(grad_down.T, rank, units, hidden_units).T, 1)
-    else:
-        spot = jnp.asarray([ladder_ring.index(g) for g in range(n_group)], jnp.int32)[
-            lax.axis_index("group")
-        ]
-        ahead = [(ladder_ring[k], ladder_ring[(k + 1) % n_group]) for k in range(n_group)]
-        behind = [(b, a) for a, b in ahead]
-
-        def piece(array, index, axis):
-            index = lax.rem(index, n_group)
-            return lax.squeeze(lax.dynamic_slice_in_dim(array, index, 1, axis), (axis,))
-
-        def ring_scatter(halves, axis):
-            one, two = piece(halves[0], spot + 7, axis), piece(halves[1], spot + 1, axis)
-            for s in range(n_group - 1):
-                one = lax.ppermute(one, "group", ahead) + piece(halves[0], spot + 14 - s, axis)
-                two = lax.ppermute(two, "group", behind) + piece(halves[1], spot + 2 + s, axis)
-            return one, two
-
-        def ring_gather(one, two, out, write):
-            out = write(out, one, spot, 0)
-            out = write(out, two, spot, 1)
-            for s in range(n_group - 1):
-                one = lax.ppermute(one, "group", ahead)
-                two = lax.ppermute(two, "group", behind)
-                out = write(out, one, lax.rem(spot + 15 - s, n_group), 0)
-                out = write(out, two, lax.rem(spot + 1 + s, n_group), 1)
-            return out
-
-        def exchange(block_for):
-            return [
-                block_for(0),
-                mate(block_for(1)),
-                across(block_for(2)),
-                lax.ppermute(block_for(3), peer_axes, [(q, q ^ 3) for q in range(n)]),
-            ]
-
-        def rank_of(k):
-            peer = me ^ k
-            return (peer % n_w) * n_ctx + peer // n_w
-
-        strip = model // n // n_group
-        part = strip // 2
-
-        def finish_columns(grad):
-            cut = grad.reshape(n, n_group, 2, part, units)
-            one, two = ring_scatter((cut[:, :, 0], cut[:, :, 1]), 1)
-            both = jnp.stack([one, two], axis=1)
-            came = exchange(lambda k: piece_at(both, me ^ k, 0))
-            full = jnp.zeros((2, part, n * units), bf16)
-            for k in range(n):
-                full = lax.dynamic_update_slice_in_dim(full, came[k], rank_of(k) * units, 2)
-
-            def write(out, block, at, h):
-                return lax.dynamic_update_slice(
-                    out, block[:, :hidden_units].astype(f32)[None, None], (at, h, 0, 0)
-                )
-
-            out = jnp.zeros((n_group, 2, part, hidden_units), f32)
-            out = ring_gather(full[0], full[1], out, write)
-            return out.reshape(model // n, hidden_units)
-
-        def piece_at(array, index, axis):
-            return lax.squeeze(lax.dynamic_slice_in_dim(array, index, 1, axis), (axis,))
-
-        def finish_down(grad):
-            step = units // n_group // 2
-            cols = model // n
-            cut = grad.reshape(n_group, 2, step, model)
-            one, two = ring_scatter((cut[:, 0], cut[:, 1]), 0)
-            both = jnp.stack([one, two])
-            came = exchange(lambda k: lax.dynamic_slice_in_dim(both, (me ^ k) * cols, cols, 2))
-            full = jnp.zeros((n, 2, step, cols), bf16)
-            for k in range(n):
-                full = lax.dynamic_update_slice_in_dim(full, came[k][None], rank_of(k), 0)
-
-            def write(out, block, at, h):
-                return lax.dynamic_update_slice(
-                    out, block.astype(f32)[:, None, None], (0, at, h, 0, 0)
-                )
-
-            out = jnp.zeros((n, n_group, 2, step, cols), f32)
-            out = ring_gather(full[:, 0], full[:, 1], out, write)
-            return out.reshape(n * units, cols)[:hidden_units]
-
-        def finish_qkv(grad):
-            cut = grad.reshape(n, n_group, 2, part, 3 * width)
-            one, two = ring_scatter((cut[:, :, 0], cut[:, :, 1]), 1)
-            both = jnp.stack([one, two], axis=1)
-            came = exchange(lambda k: piece_at(both, me ^ k, 0))
-            full = jnp.zeros((2, part, 3, n * width), bf16)
-            for k in range(n):
-                full = lax.dynamic_update_slice_in_dim(
-                    full, came[k].reshape(2, part, 3, width), (me ^ k) * width, 3
-                )
-            full = full.reshape(2, part, 3 * n * width)
-
-            def write(outs, block, at, h):
-                return [
-                    lax.dynamic_update_slice(
-                        out,
-                        block[:, k * n * width : (k + 1) * n * width].astype(f32)[None, None],
-                        (at, h, 0, 0),
-                    )
-                    for k, out in enumerate(outs)
-                ]
-
-            outs = [jnp.zeros((n_group, 2, part, n * width), f32) for _ in range(3)]
-            outs = ring_gather(full[0], full[1], outs, write)
-            return [out.reshape(model // n, n * width) for out in outs]
-
-        def finish_out(grad):
-            step, cols = width // n_group, model // 2
-            cut = grad.reshape(n_group, step, model)
-            one, two = ring_scatter((cut[:, :, :cols], cut[:, :, cols:]), 0)
-
-            def write(out, block, at, h):
-                return lax.dynamic_update_slice(out, block.astype(f32)[None], (at, 0, h * cols))
-
-            out = ring_gather(one, two, jnp.zeros((n_group, step, model), f32), write)
-            return out.reshape(width, model)
-
-        total_down = finish_down(grad_down)
-        total_gate = finish_columns(grad_gate)
-        total_up = finish_columns(grad_up)
-        total_out = finish_out(grad_out)
-        total_qkv = finish_qkv(grad_qkv)
+        total_out = finish(place_columns(grad_out, me, width, heads * size).T, 0)
+        total_gate = finish(place_columns(grad_gate_up[:, :units], rank, units, hidden_units), 0)
+        total_up = finish(place_columns(grad_gate_up[:, units:], rank, units, hidden_units), 0)
+        total_down = finish(place_columns(grad_down, rank, units, hidden_units).T, 1)
     return (
         outputs,
         input_grad,

time: 655 us -> 542 us (0.83)
  starting transfers between devices: 171 us -> 78.9 us
  waiting for transfers between devices: 232 us -> 170 us
  other arithmetic: 45.7 us -> 83.3 us
  local copies, waits for them, and re-layouts: 55 us -> 82 us
  between operations: 14.6 us -> 2.3 us
  matrix products: 69.2 us -> 59.3 us
    ppermute x149 -> x63, starting transfers between devices: 158 us -> 63.8 us  [the longest x28 29.8 us: backward(): return lax.ppermute(block, 'group', behind)]
    ppermute x149 -> x63, waiting for transfers between devices: 195 us -> 146 us  [the longest x28 104 us: forward(): return lax.ppermute(block, 'group', ahead)]
    dynamic_update_slice x85 -> x36, other arithmetic: 7.52 us -> 34 us  [put(): lax.dynamic_update_slice(out, block[None, None], (at, h) + (0,) * block.n...]
    unnamed x123 -> x148, local copies, waits for them, and re-layouts: 11.6 us -> 27.5 us
    ppermute x11 -> x9, waiting for transfers between devices: 33.2 us -> 21.5 us  [across(): return lax.ppermute(block, 'ctx', flip_w)]
    dot_general x13 -> x11, matrix products: 69.2 us -> 59.3 us  [dot(): lax.dot_general(left_side, right_side, (dims, ((), ())), precision=precis...]
    dynamic_update_slice x13 -> x28, local copies, waits for them, and re-layouts: 16.4 us -> 14.7 us  [the longest x16 11.8 us: put(): lax.dynamic_update_slice(out, block[None, None], (at, h) + (0,) * block.n...]
  transfers between devices with their start and end apart: 179 -> 89, of which waited for: 92 -> 46; matrix products, arithmetic and copies ran while one was open for 15% -> 29% of each run, Pallas kernels for 6% -> 11%
where the time goes in v2:
time: 542 us; the launch traced here: 537 us
  waiting for transfers between devices  170 us (31%)
  other arithmetic  83.3 us (15%)
  local copies, waits for them, and re-layouts  82 us (15%)
  starting transfers between devices  78.9 us (15%)
  Pallas kernels  61.5 us (11%)
  matrix products  59.3 us (11%)
    ppermute x28, waiting for transfers between devices, forward(): return lax.ppermute(block, 'group', ahead)  104 us
    dot_general x11, matrix products, dot(): lax.dot_general(left_side, right_side, (dims, ((), ())), precision=precis...  59.3 us
    ppermute x28, waiting for transfers between devices, backward(): return lax.ppermute(block, 'group', behind)  39.7 us
    dynamic_update_slice x36, other arithmetic, put(): lax.dynamic_update_slice(out, block[None, None], (at, h) + (0,) * block.n...  34 us
    ppermute x28, starting transfers between devices, backward(): return lax.ppermute(block, 'group', behind)  29.8 us
    ppermute x28, starting transfers between devices, forward(): return lax.ppermute(block, 'group', ahead)  28.5 us
    unnamed x148, local copies, waits for them, and re-layouts  27.5 us
    pallas_call x1, Pallas kernels, per_device(): pl.pallas_call(functools.partial(attend_back_kernel, rows, n, heads_here,...  25.3 us
  transfers between devices with their start and end apart: 89, of which 46 were waited for; matrix products, arithmetic and copies ran while one was open for 29% of the time, Pallas kernels for 11%

profile of v2, /device:TPU:0, one launch (start us, length us, event | category | flops | bytes accessed | tf_op | source)
XLA Modules:
  0.0 537.0 jit_solution(2017155486019870564)
XLA Ops:
  3.7 3.4 constant_dynamic-slice_fusion.5
  11.0 3.9 pad_dynamic-slice_fusion.4
  21.1 3.3 bias_strips.1.bias_ref
  36.9 3.6 fusion.54
  40.5 10.4 %arrange_project.1 = (bf16[1024,1536]{1,0:T(8,128)(2,1)}, bf16[1024,1536]{1,0:T(8,128)(2,1)}, bf16[1024,576]{1,0:T(8,128)(2,1)}) custom-call(s32[1]{0:T(128)} %bitcast.me_ref, s32[4,256]{1,0:T(4,128)} %reshape.262.order_ref, f32[1,1536]{1,0:T(1,128)} %reshape.263.gain_ref, bf16[1536,576]{1,0:T(8,128)(2,1)} %pad_maximum_fusion.9.weight_ref, ...), custom_call_target="tpu_custom_call" | custom-call | flops 5033164800 | bytes 12582912 | tf_op jit(solution)/shard_map/arrange_project/pallas_call | solution.py:368
  50.9 22.5 %attend.1 = (bf16[1024,192]{1,0:T(8,128)(2,1)}, f32[1024,192]{1,0:T(8,128)}, f32[3,1024]{1,0:T(4,128)}) custom-call(s32[1]{0:T(128)} %bitcast.me_ref, s32[4]{0:T(128)} %bitcast.792, bf16[1024,576]{1,0:T(8,128)(2,1)} %get-tuple-element.112.qkv_ref, f32[3,5,256,256]{3,2,1,0:T(8,128)} %bias_strips.1.bias_ref), custom_call_target="tpu_custom_call" | custom-call | flops 3221225472 | bytes 3145728 | tf_op jit(solution)/shard_map/attend/pallas_call | solution.py:395
  80.1 7.7 %collective-permute-done.5 = bf16[1024,192]{1,0:T(8,128)(2,1)S(1)} collective-permute-done((bf16[1024,192]{1,0:T(8,128)(2,1)}, bf16[1024,192]{1,0:T(8,128)(2,1)S(1)}, u32[]{:S(2)}, u32[]{:S(2)}) %collective-permute-start.5) | collective-permute-done | bytes 393248 | tf_op jit(solution)/shard_map/ppermute | solution.py:305
  98.1 10.0 %fusion.8 = f32[1024,2048]{0,1:T(8,128)} fusion(bf16[768,2048]{1,0:T(8,128)(2,1)S(1)} %get-tuple-element.258, bf16[768,2048]{1,0:T(8,128)(2,1)S(1)} %get-tuple-element.257, f32[1024,1536]{1,0:T(8,128)S(1)} %get-tuple-element.461, f32[1536]{0:T(1024)S(1)} %copy-done.53, f32[1024]{0:T(1024)S(1)} %add_rsqrt_fusion), kind=kOutput, calls=%fused_computation.26 | convolution fusion | flops 6459752448 | bytes 20981760 | tf_op jit(solution)/shard_map/dot_general | solution.py:38
  108.1 12.3 %fusion.6 = (bf16[1024,1024]{0,1:T(8,128)(2,1)S(1)}, bf16[1024,1024]{0,1:T(8,128)(2,1)S(1)}, bf16[1024,1024]{0,1:T(8,128)(2,1)}) fusion(f32[1024,2048]{0,1:T(8,128)} %fusion.8, bf16[1024,1536]{1,0:T(8,128)(2,1)} %constant_dynamic-update-slice_fusion, s32[]{:T(128)S(6)} %select_n.220, bf16[1984,1536]{1,0:T(8,128)(2,1)} %param.27, ...), kind=kOutput, calls=%fused_computation.21 | convolution fusion | flops 3257925632 | bytes 24313860 | tf_op jit(solution)/shard_map/dot_general | solution.py:38
  120.4 8.5 %convolution_convert_fusion = bf16[1536,2048]{1,0:T(8,128)(2,1)S(1)} fusion(f32[1024,1536]{1,0:T(8,128)S(1)} %get-tuple-element.461, f32[1536]{0:T(1024)S(1)} %copy-done.53, f32[1024]{0:T(1024)S(1)} %add_rsqrt_fusion, bf16[1024,1024]{0,1:T(8,128)(2,1)S(1)} %get-tuple-element.253, bf16[1024,1024]{0,1:T(8,128)(2,1)S(1)} %get-tuple-element.252), kind=kOutput, calls=%fused_computation | convolution fusion | flops 6458703872 | bytes 16787456 | tf_op jit(solution)/shard_map/dot_general | solution.py:38
  133.0 3.9 convolution_convert_fusion.3
  146.5 8.4 %fusion.9 = bf16[1024,1536]{1,0:T(8,128)(2,1)S(1)} fusion(bf16[1024,2048]{0,1:T(8,128)(2,1)S(1)} %copy-done.4, bf16[768,2048]{1,0:T(8,128)(2,1)S(1)} %copy-done.12, bf16[768,2048]{1,0:T(8,128)(2,1)S(1)} %copy-done.10), kind=kOutput, calls=%fused_computation.29 | convolution fusion | flops 6456606720 | bytes 13631488 | tf_op jit(solution)/shard_map/dot_general | solution.py:38
  155.0 5.2 collective-permute-done.13
  167.1 5.7 %convolution_convert_fusion.2 = bf16[1024,1536]{1,0:T(8,128)(2,1)S(1)} fusion(bf16[1024,1024]{0,1:T(8,128)(2,1)S(1)} %copy-done.66, s32[]{:T(128)S(6)} %select_n.220, bf16[1984,1536]{1,0:T(8,128)(2,1)} %param.27, bf16[64,1536]{1,0:T(8,128)(2,1)S(1)} %copy-done.48, bf16[64,1536]{1,0:T(8,128)(2,1)S(1)} %copy-done.50), kind=kOutput, calls=%fused_computation.30 | convolution fusion | flops 3232235520 | bytes 11730948 | tf_op jit(solution)/shard_map/dot_general | solution.py:38
  172.8 4.4 collective-permute-done.15
  183.6 9.2 %collective-permute-done.18 = bf16[4,24,3072]{2,1,0:T(8,128)(2,1)S(1)} collective-permute-done((bf16[4,24,3072]{2,1,0:T(8,128)(2,1)S(1)}, bf16[4,24,3072]{2,1,0:T(8,128)(2,1)S(1)}, u32[]{:S(2)}, u32[]{:S(2)}) %collective-permute-start.18) | collective-permute-done | bytes 589856 | tf_op jit(solution)/shard_map/ppermute | solution.py:430
  194.3 7.5 %collective-permute-done.23 = bf16[256,1536]{1,0:T(8,128)(2,1)S(1)} collective-permute-done((bf16[256,1536]{1,0:T(8,128)(2,1)S(1)}, bf16[256,1536]{1,0:T(8,128)(2,1)S(1)}, u32[]{:S(2)}, u32[]{:S(2)}) %collective-permute-start.23) | collective-permute-done | bytes 786464 | tf_op jit(solution)/shard_map/ppermute | solution.py:305
  208.6 9.9 %collective-permute-done.21 = bf16[4,24,3072]{2,1,0:T(8,128)(2,1)S(1)} collective-permute-done((bf16[4,24,3072]{2,1,0:T(8,128)(2,1)S(1)}, bf16[4,24,3072]{2,1,0:T(8,128)(2,1)S(1)}, u32[]{:S(2)}, u32[]{:S(2)}) %collective-permute-start.21) | collective-permute-done | bytes 589856 | tf_op jit(solution)/shard_map/ppermute | solution.py:430
  218.7 4.0 collective-permute-done.22
  224.9 11.6 %collective-permute-done.24 = bf16[4,24,3072]{2,1,0:T(8,128)(2,1)S(1)} collective-permute-done((bf16[4,24,3072]{2,1,0:T(8,128)(2,1)S(1)}, bf16[4,24,3072]{2,1,0:T(8,128)(2,1)S(1)}, u32[]{:S(2)}, u32[]{:S(2)}) %collective-permute-start.24) | collective-permute-done | bytes 589856 | tf_op jit(solution)/shard_map/ppermute | solution.py:430
  245.0 7.6 %collective-permute-done.27 = bf16[4,24,3072]{2,1,0:T(8,128)(2,1)} collective-permute-done((bf16[4,24,3072]{2,1,0:T(8,128)(2,1)}, bf16[4,24,3072]{2,1,0:T(8,128)(2,1)}, u32[]{:S(2)}, u32[]{:S(2)}) %collective-permute-start.27) | collective-permute-done | bytes 589856 | tf_op jit(solution)/shard_map/ppermute | solution.py:430
  263.8 7.1 %collective-permute-done.31 = bf16[4,24,3072]{2,1,0:T(8,128)(2,1)S(1)} collective-permute-done((bf16[4,24,3072]{2,1,0:T(8,128)(2,1)S(1)}, bf16[4,24,3072]{2,1,0:T(8,128)(2,1)S(1)}, u32[]{:S(2)}, u32[]{:S(2)}) %collective-permute-start.31) | collective-permute-done | bytes 589856 | tf_op jit(solution)/shard_map/ppermute | solution.py:430
  282.7 25.3 %attend_back.1 = (bf16[1024,576]{1,0:T(8,128)(2,1)}, f32[32,128]{1,0:T(8,128)}) custom-call(s32[1]{0:T(128)} %bitcast.me_ref, s32[4]{0:T(128)} %bitcast.793, bf16[1024,576]{1,0:T(8,128)(2,1)} %get-tuple-element.112.qkv_ref, f32[3,5,256,256]{3,2,1,0:T(8,128)} %bias_strips.1.bias_ref, f32[3,1024]{1,0:T(4,128)} %get-tuple-element.147.lse_ref, ...), custom_call_target="tpu_custom_call" | custom-call | flops 8053063680 | bytes 3145728 | tf_op jit(solution)/shard_map/attend_back/pallas_call | solution.py:637
  340.5 3.7 convolution_convert_fusion.1
  344.2 5.7 %collective-permute-done.41 = bf16[4,24,768]{2,1,0:T(8,128)(2,1)S(1)} collective-permute-done((bf16[4,24,768]{2,1,0:T(8,128)(2,1)S(1)}, bf16[4,24,768]{2,1,0:T(8,128)(2,1)S(1)}, u32[]{:S(2)}, u32[]{:S(2)}) %collective-permute-start.41) | collective-permute-done | bytes 147488 | tf_op jit(solution)/shard_map/ppermute | solution.py:430
  365.3 10.2 %collective-permute-done.49 = bf16[24,12288]{1,0:T(8,128)(2,1)S(1)} collective-permute-done((bf16[24,12288]{1,0:T(8,128)(2,1)S(1)}, bf16[24,12288]{1,0:T(8,128)(2,1)S(1)}, u32[]{:S(2)}, u32[]{:S(2)}) %collective-permute-start.49) | collective-permute-done | bytes 589856 | tf_op jit(solution)/shard_map/ppermute | solution.py:430
  390.5 17.0 %collective-permute-done.57 = bf16[4,24,768]{2,1,0:T(8,128)(2,1)S(1)} collective-permute-done((bf16[4,24,768]{2,1,0:T(8,128)(2,1)S(1)}, bf16[4,24,768]{2,1,0:T(8,128)(2,1)S(1)}, u32[]{:S(2)}, u32[]{:S(2)}) %collective-permute-start.57) | collective-permute-done | bytes 147488 | tf_op jit(solution)/shard_map/ppermute | solution.py:433
  426.6 4.8 collective-permute-done.63
  459.9 8.7 %collective-permute-done.71 = bf16[24,3072]{1,0:T(8,128)(2,1)S(1)} collective-permute-done((bf16[24,3072]{1,0:T(8,128)(2,1)S(1)}, bf16[24,3072]{1,0:T(8,128)(2,1)S(1)}, u32[]{:S(2)}, u32[]{:S(2)}) %collective-permute-start.71) | collective-permute-done | bytes 147488 | tf_op jit(solution)/shard_map/ppermute | solution.py:430
  489.6 5.8 %collective-permute-done.78 = bf16[24,3072]{1,0:T(8,128)(2,1)S(1)} collective-permute-done((bf16[24,3072]{1,0:T(8,128)(2,1)S(1)}, bf16[24,3072]{1,0:T(8,128)(2,1)S(1)}, u32[]{:S(2)}, u32[]{:S(2)}) %collective-permute-start.78) | collective-permute-done | bytes 147488 | tf_op jit(solution)/shard_map/ppermute | solution.py:430
  511.9 3.2 convert_bitcast_fusion
  518.9 6.5 %copy.120 = f32[3968,384]{1,0:T(8,128)} copy(f32[3968,384]{0,1:T(8,128)} %convert_bitcast_fusion) | data formatting | bytes 12189696
  (500 shorter events, 273.7 us)
Async XLA Ops:
  0.6 25.5 %collective-permute-start.2 = (bf16[256,1536]{1,0:T(8,128)(2,1)}, bf16[256,1536]{1,0:T(8,128)(2,1)}, u32[]{:S(2)}, u32[]{:S(2)}) collective-permute-start(bf16[256,1536]{1,0:T(8,128)(2,1)} %refs_0_.1), channel_id=1, source_target_pairs={{0,2},{2,0},{1,3},{3,1},{4,6},{6,4},{5,7},{7,5},{8,10},{10,8},{9,1... | collective-permute-start | bytes 2359304 | tf_op jit(solution)/shard_map/ppermute | solution.py:305
  3.7 36.8 %collective-permute-start.1 = (bf16[256,1536]{1,0:T(8,128)(2,1)}, bf16[256,1536]{1,0:T(8,128)(2,1)}, u32[]{:S(2)}, u32[]{:S(2)}) collective-permute-start(bf16[256,1536]{1,0:T(8,128)(2,1)} %refs_0_.1), channel_id=1, source_target_pairs={{0,1},{1,0},{2,3},{3,2},{4,5},{5,4},{6,7},{7,6},{8,9},{9,8},{10,11... | collective-permute-start | bytes 2359304 | tf_op jit(solution)/shard_map/ppermute | solution.py:302
  8.9 19.3 %collective-permute-start = (bf16[768,576]{0,1:T(8,128)(2,1)}, bf16[768,576]{0,1:T(8,128)(2,1)}, u32[]{:S(2)}, u32[]{:S(2)}) collective-permute-start(bf16[768,576]{0,1:T(8,128)(2,1)} %pad_maximum_fusion.14), channel_id=1, source_target_pairs={{0,1},{1,0},{2,3},{3,2},{4,5},{5,4},{6,7},{7,6},{8,9},{9,8},{10,11... | collective-permute-start | bytes 2654216 | tf_op jit(solution)/shard_map/ppermute | solution.py:302
  16.8 78.2 %collective-permute-start.12 = (bf16[768,2048]{1,0:T(8,128)(2,1)}, bf16[768,2048]{1,0:T(8,128)(2,1)}, u32[]{:S(2)}, u32[]{:S(2)}) collective-permute-start(bf16[768,2048]{1,0:T(8,128)(2,1)} %pad_maximum_fusion.7), channel_id=1, source_target_pairs={{0,1},{1,0},{2,3},{3,2},{4,5},{5,4},{6,7},{7,6},{8,9},{9,8},{10,11... | collective-permute-start | bytes 9437192 | tf_op jit(solution)/shard_map/ppermute | solution.py:302
  26.1 49.6 %collective-permute-start.8 = (bf16[256,1536]{1,0:T(8,128)(2,1)}, bf16[256,1536]{1,0:T(8,128)(2,1)}, u32[]{:S(2)}, u32[]{:S(2)}) collective-permute-start(bf16[256,1536]{1,0:T(8,128)(2,1)} %param.15), channel_id=1, source_target_pairs={{0,1},{1,0},{2,3},{3,2},{4,5},{5,4},{6,7},{7,6},{8,9},{9,8},{10,11... | collective-permute-start | bytes 2359304 | tf_op jit(solution)/shard_map/ppermute | solution.py:302
  28.2 47.0 %collective-permute-start.9 = (bf16[256,1536]{1,0:T(8,128)(2,1)}, bf16[256,1536]{1,0:T(8,128)(2,1)}, u32[]{:S(2)}, u32[]{:S(2)}) collective-permute-start(bf16[256,1536]{1,0:T(8,128)(2,1)} %param.15), channel_id=1, source_target_pairs={{0,2},{2,0},{1,3},{3,1},{4,6},{6,4},{5,7},{7,5},{8,10},{10,8},{9,1... | collective-permute-start | bytes 2359304 | tf_op jit(solution)/shard_map/ppermute | solution.py:305
  75.2 18.3 %collective-permute-start.10 = (bf16[256,1536]{1,0:T(8,128)(2,1)}, bf16[256,1536]{1,0:T(8,128)(2,1)S(1)}, u32[]{:S(2)}, u32[]{:S(2)}) collective-permute-start(bf16[256,1536]{1,0:T(8,128)(2,1)} %collective-permute-done.9), channel_id=1, source_target_pairs={{0,1},{1,0},{2,3},{3,2},{4,5},{5,4},{6,7},{7,6},{8,9},{9,8},{10,11... | collective-permute-start | bytes 2359304 | tf_op jit(solution)/shard_map/ppermute | solution.py:302
  181.8 20.6 %collective-permute-start.20 = (bf16[2,256,1536]{2,1,0:T(8,128)(2,1)S(1)}, bf16[2,256,1536]{2,1,0:T(8,128)(2,1)S(1)}, u32[]{:S(2)}, u32[]{:S(2)}) collective-permute-start(bf16[2,256,1536]{2,1,0:T(8,128)(2,1)S(1)} %pad_maximum_fusion.11), channel_id=1, source_target_pairs={{0,1},{1,0},{2,3},{3,2},{4,5},{5,4},{6,7},{7,6},{8,9},{9,8},{10,11... | collective-permute-start | bytes 4718600 | tf_op jit(solution)/shard_map/ppermute | solution.py:302
  181.9 19.9 %collective-permute-start.23 = (bf16[256,1536]{1,0:T(8,128)(2,1)S(1)}, bf16[256,1536]{1,0:T(8,128)(2,1)S(1)}, u32[]{:S(2)}, u32[]{:S(2)}) collective-permute-start(bf16[256,1536]{1,0:T(8,128)(2,1)S(1)} %get-tuple-element.130), channel_id=1, source_target_pairs={{0,2},{2,0},{1,3},{3,1},{4,6},{6,4},{5,7},{7,5},{8,10},{10,8},{9,1... | collective-permute-start | bytes 2359304 | tf_op jit(solution)/shard_map/ppermute | solution.py:305
  242.4 17.2 %collective-permute-start.29 = (bf16[256,1536]{1,0:T(8,128)(2,1)S(1)}, bf16[256,1536]{1,0:T(8,128)(2,1)S(1)}, u32[]{:S(2)}, u32[]{:S(2)}) collective-permute-start(bf16[256,1536]{1,0:T(8,128)(2,1)S(1)} %get-tuple-element.134), channel_id=1, source_target_pairs={{0,2},{2,0},{1,3},{3,1},{4,6},{6,4},{5,7},{7,5},{8,10},{10,8},{9,1... | collective-permute-start | bytes 2359304 | tf_op jit(solution)/shard_map/ppermute | solution.py:305
  259.9 48.0 %collective-permute-start.30 = (bf16[256,1536]{1,0:T(8,128)(2,1)}, bf16[256,1536]{1,0:T(8,128)(2,1)}, u32[]{:S(2)}, u32[]{:S(2)}) collective-permute-start(bf16[256,1536]{1,0:T(8,128)(2,1)} %get-tuple-element.138), channel_id=1, source_target_pairs={{0,2},{2,0},{1,3},{3,1},{4,6},{6,4},{5,7},{7,5},{8,10},{10,8},{9,1... | collective-permute-start | bytes 2359304 | tf_op jit(solution)/shard_map/ppermute | solution.py:305
  280.8 30.3 %collective-permute-start.34 = (bf16[2,24,3072]{2,1,0:T(8,128)(2,1)}, bf16[2,24,3072]{2,1,0:T(8,128)(2,1)}, u32[]{:S(2)}, u32[]{:S(2)}) collective-permute-start(bf16[2,24,3072]{2,1,0:T(8,128)(2,1)} %get-tuple-element.144), channel_id=1, source_target_pairs={{0,1},{1,0},{2,3},{3,2},{4,5},{5,4},{6,7},{7,6},{8,9},{9,8},{10,11... | collective-permute-start | bytes 884744 | tf_op jit(solution)/shard_map/ppermute | solution.py:302
  280.8 33.0 %collective-permute-start.35 = (bf16[2,24,3072]{2,1,0:T(8,128)(2,1)}, bf16[2,24,3072]{2,1,0:T(8,128)(2,1)S(1)}, u32[]{:S(2)}, u32[]{:S(2)}) collective-permute-start(bf16[2,24,3072]{2,1,0:T(8,128)(2,1)} %get-tuple-element.145), channel_id=1, source_target_pairs={{0,2},{2,0},{1,3},{3,1},{4,6},{6,4},{5,7},{7,5},{8,10},{10,8},{9,1... | collective-permute-start | bytes 884744 | tf_op jit(solution)/shard_map/ppermute | solution.py:305
  281.2 32.8 %collective-permute-start.36 = (bf16[2,24,3072]{2,1,0:T(8,128)(2,1)}, bf16[2,24,3072]{2,1,0:T(8,128)(2,1)S(1)}, u32[]{:S(2)}, u32[]{:S(2)}) collective-permute-start(bf16[2,24,3072]{2,1,0:T(8,128)(2,1)} %get-tuple-element.146), channel_id=1, source_target_pairs={{0,3},{1,2},{2,1},{3,0},{4,7},{5,6},{6,5},{7,4},{8,11},{9,10},{10,... | collective-permute-start | bytes 884744 | tf_op jit(solution)/shard_map/ppermute | solution.py:436
  332.2 24.3 %collective-permute-start.39 = (bf16[24,12288]{1,0:T(8,128)(2,1)}, bf16[24,12288]{1,0:T(8,128)(2,1)S(1)}, u32[]{:S(2)}, u32[]{:S(2)}) collective-permute-start(bf16[24,12288]{1,0:T(8,128)(2,1)} %collective-permute-done.37), channel_id=1, source_target_pairs={{0,8},{8,16},{16,24},{24,28},{28,20},{20,12},{12,4},{4,0},{1,9},{9... | collective-permute-start | bytes 1769480 | tf_op jit(solution)/shard_map/ppermute | solution.py:430
  332.7 23.9 %collective-permute-start.40 = (bf16[24,12288]{1,0:T(8,128)(2,1)}, bf16[24,12288]{1,0:T(8,128)(2,1)S(1)}, u32[]{:S(2)}, u32[]{:S(2)}) collective-permute-start(bf16[24,12288]{1,0:T(8,128)(2,1)} %collective-permute-done.38), channel_id=1, source_target_pairs={{8,0},{16,8},{24,16},{28,24},{20,28},{12,20},{4,12},{0,4},{9,1},{1... | collective-permute-start | bytes 1769480 | tf_op jit(solution)/shard_map/ppermute | solution.py:433
  357.7 17.8 %collective-permute-start.49 = (bf16[24,12288]{1,0:T(8,128)(2,1)S(1)}, bf16[24,12288]{1,0:T(8,128)(2,1)S(1)}, u32[]{:S(2)}, u32[]{:S(2)}) collective-permute-start(bf16[24,12288]{1,0:T(8,128)(2,1)S(1)} %collective-permute-done.39), channel_id=1, source_target_pairs={{0,8},{8,16},{16,24},{24,28},{28,20},{20,12},{12,4},{4,0},{1,9},{9... | collective-permute-start | bytes 1769480 | tf_op jit(solution)/shard_map/ppermute | solution.py:430
  359.8 18.5 %collective-permute-start.48 = (bf16[256,1536]{1,0:T(8,128)(2,1)S(1)}, bf16[256,1536]{1,0:T(8,128)(2,1)S(1)}, u32[]{:S(2)}, u32[]{:S(2)}) collective-permute-start(bf16[256,1536]{1,0:T(8,128)(2,1)S(1)} %get-tuple-element.167), channel_id=1, source_target_pairs={{0,2},{2,0},{1,3},{3,1},{4,6},{6,4},{5,7},{7,5},{8,10},{10,8},{9,1... | collective-permute-start | bytes 2359304 | tf_op jit(solution)/shard_map/ppermute | solution.py:305
  387.3 21.8 %collective-permute-start.53 = (f32[3456]{0:T(1024)S(1)}, f32[3456]{0:T(1024)S(1)}, u32[]{:S(2)}, u32[]{:S(2)}) collective-permute-start(f32[3456]{0:T(1024)S(1)} %pad_maximum_fusion.19), channel_id=1, source_target_pairs={{0,1},{1,0},{2,3},{3,2},{4,5},{5,4},{6,7},{7,6},{8,9},{9,8},{10,11... | collective-permute-start | bytes 41480 | tf_op jit(solution)/shard_map/ppermute | solution.py:564
  387.3 27.1 %collective-permute-start.54 = (bf16[24,12288]{1,0:T(8,128)(2,1)S(1)}, bf16[24,12288]{1,0:T(8,128)(2,1)}, u32[]{:S(2)}, u32[]{:S(2)}) collective-permute-start(bf16[24,12288]{1,0:T(8,128)(2,1)S(1)} %collective-permute-done.49), channel_id=1, source_target_pairs={{0,8},{8,16},{16,24},{24,28},{28,20},{20,12},{12,4},{4,0},{1,9},{9... | collective-permute-start | bytes 1769480 | tf_op jit(solution)/shard_map/ppermute | solution.py:430
  388.9 25.4 %collective-permute-start.55 = (bf16[24,12288]{1,0:T(8,128)(2,1)S(1)}, bf16[24,12288]{1,0:T(8,128)(2,1)}, u32[]{:S(2)}, u32[]{:S(2)}) collective-permute-start(bf16[24,12288]{1,0:T(8,128)(2,1)S(1)} %collective-permute-done.50), channel_id=1, source_target_pairs={{8,0},{16,8},{24,16},{28,24},{20,28},{12,20},{4,12},{0,4},{9,1},{1... | collective-permute-start | bytes 1769480 | tf_op jit(solution)/shard_map/ppermute | solution.py:433
  389.3 18.3 %collective-permute-start.57 = (bf16[4,24,768]{2,1,0:T(8,128)(2,1)S(1)}, bf16[4,24,768]{2,1,0:T(8,128)(2,1)S(1)}, u32[]{:S(2)}, u32[]{:S(2)}) collective-permute-start(bf16[4,24,768]{2,1,0:T(8,128)(2,1)S(1)} %bitcast_add_fusion.6), channel_id=1, source_target_pairs={{8,0},{16,8},{24,16},{28,24},{20,28},{12,20},{4,12},{0,4},{9,1},{1... | collective-permute-start | bytes 442376 | tf_op jit(solution)/shard_map/ppermute | solution.py:433
  414.8 34.2 %collective-permute-start.61 = (bf16[24,12288]{1,0:T(8,128)(2,1)}, bf16[24,12288]{1,0:T(8,128)(2,1)}, u32[]{:S(2)}, u32[]{:S(2)}) collective-permute-start(bf16[24,12288]{1,0:T(8,128)(2,1)} %collective-permute-done.54), channel_id=1, source_target_pairs={{0,8},{8,16},{16,24},{24,28},{28,20},{20,12},{12,4},{4,0},{1,9},{9... | collective-permute-start | bytes 1769480 | tf_op jit(solution)/shard_map/ppermute | solution.py:430
  415.8 33.1 %collective-permute-start.62 = (bf16[24,12288]{1,0:T(8,128)(2,1)}, bf16[24,12288]{1,0:T(8,128)(2,1)}, u32[]{:S(2)}, u32[]{:S(2)}) collective-permute-start(bf16[24,12288]{1,0:T(8,128)(2,1)} %collective-permute-done.55), channel_id=1, source_target_pairs={{8,0},{16,8},{24,16},{28,24},{20,28},{12,20},{4,12},{0,4},{9,1},{1... | collective-permute-start | bytes 1769480 | tf_op jit(solution)/shard_map/ppermute | solution.py:433
  450.0 25.3 %collective-permute-start.69 = (bf16[24,12288]{1,0:T(8,128)(2,1)}, bf16[24,12288]{1,0:T(8,128)(2,1)}, u32[]{:S(2)}, u32[]{:S(2)}) collective-permute-start(bf16[24,12288]{1,0:T(8,128)(2,1)} %collective-permute-done.61), channel_id=1, source_target_pairs={{0,8},{8,16},{16,24},{24,28},{28,20},{20,12},{12,4},{4,0},{1,9},{9... | collective-permute-start | bytes 1769480 | tf_op jit(solution)/shard_map/ppermute | solution.py:430
  450.6 24.8 %collective-permute-start.70 = (bf16[24,12288]{1,0:T(8,128)(2,1)}, bf16[24,12288]{1,0:T(8,128)(2,1)}, u32[]{:S(2)}, u32[]{:S(2)}) collective-permute-start(bf16[24,12288]{1,0:T(8,128)(2,1)} %collective-permute-done.62), channel_id=1, source_target_pairs={{8,0},{16,8},{24,16},{28,24},{20,28},{12,20},{4,12},{0,4},{9,1},{1... | collective-permute-start | bytes 1769480 | tf_op jit(solution)/shard_map/ppermute | solution.py:433
  452.0 16.5 %collective-permute-start.71 = (bf16[24,3072]{1,0:T(8,128)(2,1)S(1)}, bf16[24,3072]{1,0:T(8,128)(2,1)S(1)}, u32[]{:S(2)}, u32[]{:S(2)}) collective-permute-start(bf16[24,3072]{1,0:T(8,128)(2,1)S(1)} %get-tuple-element.192), channel_id=1, source_target_pairs={{0,8},{8,16},{16,24},{24,28},{28,20},{20,12},{12,4},{4,0},{1,9},{9... | collective-permute-start | bytes 442376 | tf_op jit(solution)/shard_map/ppermute | solution.py:430
  452.6 16.1 %collective-permute-start.72 = (bf16[24,3072]{1,0:T(8,128)(2,1)S(1)}, bf16[24,3072]{1,0:T(8,128)(2,1)S(1)}, u32[]{:S(2)}, u32[]{:S(2)}) collective-permute-start(bf16[24,3072]{1,0:T(8,128)(2,1)S(1)} %get-tuple-element.193), channel_id=1, source_target_pairs={{8,0},{16,8},{24,16},{28,24},{20,28},{12,20},{4,12},{0,4},{9,1},{1... | collective-permute-start | bytes 442376 | tf_op jit(solution)/shard_map/ppermute | solution.py:433
  478.2 31.7 %collective-permute-start.87 = (bf16[24,12288]{1,0:T(8,128)(2,1)}, bf16[24,12288]{1,0:T(8,128)(2,1)}, u32[]{:S(2)}, u32[]{:S(2)}) collective-permute-start(bf16[24,12288]{1,0:T(8,128)(2,1)} %collective-permute-done.69), channel_id=1, source_target_pairs={{0,8},{8,16},{16,24},{24,28},{28,20},{20,12},{12,4},{4,0},{1,9},{9... | collective-permute-start | bytes 1769480 | tf_op jit(solution)/shard_map/ppermute | solution.py:430
  479.4 31.5 %collective-permute-start.88 = (bf16[24,12288]{1,0:T(8,128)(2,1)}, bf16[24,12288]{1,0:T(8,128)(2,1)}, u32[]{:S(2)}, u32[]{:S(2)}) collective-permute-start(bf16[24,12288]{1,0:T(8,128)(2,1)} %collective-permute-done.70), channel_id=1, source_target_pairs={{8,0},{16,8},{24,16},{28,24},{20,28},{12,20},{4,12},{0,4},{9,1},{1... | collective-permute-start | bytes 1769480 | tf_op jit(solution)/shard_map/ppermute | solution.py:433
  506.3 19.2 %collective-permute-start.83 = (bf16[24,3072]{1,0:T(8,128)(2,1)S(1)}, bf16[24,3072]{1,0:T(8,128)(2,1)}, u32[]{:S(2)}, u32[]{:S(2)}) collective-permute-start(bf16[24,3072]{1,0:T(8,128)(2,1)S(1)} %collective-permute-done.81), channel_id=1, source_target_pairs={{0,8},{8,16},{16,24},{24,28},{28,20},{20,12},{12,4},{4,0},{1,9},{9... | collective-permute-start | bytes 442376 | tf_op jit(solution)/shard_map/ppermute | solution.py:430
  506.7 18.8 %collective-permute-start.84 = (bf16[24,3072]{1,0:T(8,128)(2,1)S(1)}, bf16[24,3072]{1,0:T(8,128)(2,1)S(1)}, u32[]{:S(2)}, u32[]{:S(2)}) collective-permute-start(bf16[24,3072]{1,0:T(8,128)(2,1)S(1)} %collective-permute-done.82), channel_id=1, source_target_pairs={{8,0},{16,8},{24,16},{28,24},{20,28},{12,20},{4,12},{0,4},{9,1},{1... | collective-permute-start | bytes 442376 | tf_op jit(solution)/shard_map/ppermute | solution.py:433
  (124 other events, 1190.1 us)

commit v3 on v2

--- a/solution.py
+++ b/solution.py
@@ -73,6 +73,24 @@
     qkv_ref[...] = forward_product(normed, weight_ref[...]).astype(bf16)
 
 
+def own_heads_kernel(width, count, n_w, me_ref, *refs):
+    mine, given, out_ref = refs[:3], refs[3:6], refs[6]
+    me = me_ref[0]
+    half, columns = mine[0].shape
+    for m in range(count):
+
+        @pl.when(me == m)
+        def _():
+            for t in range(3):
+                for w in range(n_w):
+                    source = mine[t] if m % n_w == w else given[t]
+                    place = slice(w * half, (w + 1) * half), slice(t * width, (t + 1) * width)
+                    if (m + 1) * width <= columns:
+                        out_ref[place] = source[:, m * width : (m + 1) * width]
+                    else:
+                        out_ref[place] = jnp.zeros((half, width), out_ref.dtype)
+
+
 def bias_kernel(rows, heads_here, heads, buckets, me_ref, table_ref, out_ref):
     lanes = iota((8, 4 * rows), 1)
     ids = bucket_of(2 * rows - lanes)
@@ -125,36 +143,36 @@
     query_seq = sequence_ids(ends, block * rows, (1, rows), 1)
     start = pl.multiple_of(here * rows, rows)
     queries = qkv_ref[pl.ds(start, rows), :][:, :width]
-    for h in range(heads_here):
-        query = queries[:, h * size : (h + 1) * size]
-
-        def step(key_block, carry):
-            top, total, acc = carry
-            at = pl.multiple_of((key_block ^ me) * rows, rows)
-            own = qkv_ref[pl.ds(at, rows), :]
+
+    def step(key_block, carry):
+        at = pl.multiple_of((key_block ^ me) * rows, rows)
+        own = qkv_ref[pl.ds(at, rows), :]
+        delta = jnp.clip(key_block - block, -2, 2) + 2
+        same = sequence_ids(ends, key_block * rows, (rows, 1), 0) == query_seq
+        after = []
+        for h in range(heads_here):
+            top, total, acc = carry[h]
+            query = queries[:, h * size : (h + 1) * size]
             key = own[:, width + h * size : width + (h + 1) * size]
             value = own[:, 2 * width + h * size : 2 * width + (h + 1) * size]
-            delta = jnp.clip(key_block - block, -2, 2) + 2
             scores = backward_product(key, query) + bias_ref[h, delta]
-            key_seq = sequence_ids(ends, key_block * rows, (rows, 1), 0)
-            scores = jnp.where(key_seq == query_seq, scores, masked_out)
+            scores = jnp.where(same, scores, masked_out)
             top_next = jnp.maximum(top, jnp.max(scores, axis=0, keepdims=True))
             probs = jnp.exp(scores - top_next)
             fade = jnp.exp(top - top_next)
             total = total * fade + jnp.sum(probs, axis=0, keepdims=True)
             acc = acc * fade + weight_product(value, probs.astype(bf16))
-            return top_next, total, acc
-
-        top, total, acc = lax.fori_loop(
-            low,
-            high,
-            step,
-            (
-                jnp.full((1, rows), masked_out, f32),
-                jnp.zeros((1, rows), f32),
-                jnp.zeros((size, rows), f32),
-            ),
-        )
+            after.append((top_next, total, acc))
+        return tuple(after)
+
+    fresh = (
+        jnp.full((1, rows), masked_out, f32),
+        jnp.zeros((1, rows), f32),
+        jnp.zeros((size, rows), f32),
+    )
+    done = lax.fori_loop(low, high, step, (fresh,) * heads_here)
+    for h in range(heads_here):
+        top, total, acc = done[h]
         lse_ref[h : h + 1, :] = top + jnp.log(total)
         out = (acc / total).T
         wide_ref[:, h * size : (h + 1) * size] = out
@@ -173,12 +191,13 @@
     qkv_ref,
     bias_ref,
     lse_ref,
-    delta_ref,
+    wide_ref,
     d_att_ref,
     dqkv_ref,
     table_ref,
     dq_ref,
     sums_ref,
+    delta_ref,
 ):
     me = me_ref[0]
     width = heads_here * size
@@ -189,6 +208,13 @@
     def _():
         dq_ref[...] = jnp.zeros_like(dq_ref)
         sums_ref[...] = jnp.zeros_like(sums_ref)
+        for k in range(count):
+            part = slice(k * rows, (k + 1) * rows)
+            both = d_att_ref[part, :].astype(f32) * wide_ref[part, :]
+            for h in range(heads_here):
+                delta_ref[h : h + 1, part] = jnp.sum(
+                    both[:, h * size : (h + 1) * size].T, axis=0, keepdims=True
+                )
 
     ends, low, high = span_of(
         lengths_ref, seqs, block * rows, block * rows + rows - 1, rows, count * rows
@@ -196,31 +222,37 @@
     key_seq = sequence_ids(ends, block * rows, (rows, 1), 0)
     start = pl.multiple_of(here * rows, rows)
     own = qkv_ref[pl.ds(start, rows), :]
-    for h in range(heads_here):
-        key = own[:, width + h * size : width + (h + 1) * size]
-        value = own[:, 2 * width + h * size : 2 * width + (h + 1) * size]
-
-        def step(query_block, carry):
-            d_key, d_value = carry
-            rel = query_block ^ me
-            at = pl.multiple_of(rel * rows, rows)
-            query = qkv_ref[pl.ds(at, rows), :][:, h * size : (h + 1) * size]
-            d_out = d_att_ref[pl.ds(at, rows), :][:, h * size : (h + 1) * size]
-            near = jnp.clip(block - query_block, -2, 2) + 2
+
+    def step(query_block, carry):
+        rel = query_block ^ me
+        at = pl.multiple_of(rel * rows, rows)
+        queries = qkv_ref[pl.ds(at, rows), :][:, :width]
+        d_outs = d_att_ref[pl.ds(at, rows), :]
+        near = jnp.clip(block - query_block, -2, 2) + 2
+        same = key_seq == sequence_ids(ends, query_block * rows, (1, rows), 1)
+        after = []
+        for h in range(heads_here):
+            d_key, d_value = carry[h]
+            key = own[:, width + h * size : width + (h + 1) * size]
+            value = own[:, 2 * width + h * size : 2 * width + (h + 1) * size]
+            query = queries[:, h * size : (h + 1) * size]
+            d_out = d_outs[:, h * size : (h + 1) * size]
             scores = backward_product(key, query) + bias_ref[h, near]
-            query_seq = sequence_ids(ends, query_block * rows, (1, rows), 1)
             lse = lse_ref[h : h + 1, pl.ds(at, rows)]
-            soft = jnp.where(key_seq == query_seq, jnp.exp(scores - lse), 0.0)
+            soft = jnp.where(same, jnp.exp(scores - lse), 0.0)
             d_probs = backward_product(value, d_out)
             d_scores = (soft * (d_probs - delta_ref[h : h + 1, pl.ds(at, rows)])).astype(bf16)
             sums_ref[h, near] += d_scores.astype(f32)
             d_value = d_value + forward_product(soft.astype(bf16), d_out)
             d_key = d_key + forward_product(d_scores, query)
             dq_ref[h, rel] += weight_product(key, d_scores)
-            return d_key, d_value
-
-        zero = jnp.zeros((rows, size), f32)
-        d_key, d_value = lax.fori_loop(low, high, step, (zero, zero))
+            after.append((d_key, d_value))
+        return tuple(after)
+
+    zero = jnp.zeros((rows, size), f32)
+    done = lax.fori_loop(low, high, step, ((zero, zero),) * heads_here)
+    for h in range(heads_here):
+        d_key, d_value = done[h]
         dqkv_ref[pl.ds(start, rows), width + h * size : width + (h + 1) * size] = d_key.astype(bf16)
         dqkv_ref[pl.ds(start, rows), 2 * width + h * size : 2 * width + (h + 1) * size] = (
             d_value.astype(bf16)
@@ -253,6 +285,63 @@
             column = column + jnp.where(bucket_rows == buckets - 1, jnp.sum(sums_ref[h, 4]), 0.0)
             table = jnp.where(lanes == h, column, table)
         table_ref[...] = table
+
+
+def place_kernel(groups, part, units_all, hidden_units, heads_all, width, spot_ref, *refs):
+    spot = spot_ref[0]
+    wide, refs = refs[: 4 * groups], refs[4 * groups :]
+    narrow, refs = refs[: 2 * groups], refs[2 * groups :]
+    outs, scratch, sems = refs[:7], refs[7:-1], refs[-1]
+    gate, up, down, turned, query, key, value, out_rows, out_turned = scratch
+    middle = 3 * units_all // 2
+
+    def row_of(j, h):
+        index = lax.rem(spot + groups - j, groups) if h == 0 else lax.rem(spot + j, groups)
+        return pl.multiple_of((2 * index + h) * part, 8)
+
+    def copy(k, source):
+        return pltpu.make_async_copy(source, outs[k], sems.at[k])
+
+    def gather(target, t):
+        for c in range(2):
+            low = max(c * middle, t * units_all)
+            high = min((c + 1) * middle, t * units_all + hidden_units)
+            if low < high:
+                for j in range(groups):
+                    for h in range(2):
+                        block = wide[(j * 2 + c) * 2 + h]
+                        target[pl.ds(row_of(j, h), part), low - t * units_all : high - t * units_all] = (
+                            block[:, low - c * middle : high - c * middle].astype(f32)
+                        )
+
+    gather(gate, 0)
+    copy(0, gate).start()
+    gather(up, 1)
+    copy(1, up).start()
+    gather(down, 2)
+    for first in range(0, hidden_units, 128):
+        turned[first : first + 128, :] = down[:, first : first + 128].T
+    copy(2, turned).start()
+    for k, target in enumerate((query, key, value)):
+        for j in range(groups):
+            for h in range(2):
+                target[pl.ds(row_of(j, h), part), :] = (
+                    narrow[j * 2 + h][:, k * heads_all : (k + 1) * heads_all].astype(f32)
+                )
+        copy(3 + k, target).start()
+    count = heads_all // width
+    for q in range(count):
+        for j in range(groups):
+            for h in range(2):
+                first = 3 * heads_all + q * width
+                out_rows[q, pl.ds(row_of(j, h), part), :] = (
+                    narrow[j * 2 + h][:, first : first + width].astype(f32)
+                )
+        rows = out_rows.shape[1]
+        out_turned[:, q * rows : (q + 1) * rows] = out_rows[q].T
+    copy(6, out_turned).start()
+    for k, source in enumerate((gate, up, turned, query, key, value, out_turned)):
+        copy(k, source).wait()
 
 
 def forward_product_exact(left_side, right_side):
@@ -319,20 +408,23 @@
         padded = jnp.pad(weight, ((0, 0), (0, over))) if over else weight
         return lax.dynamic_slice_in_dim(padded, which * wide, wide, 1)
 
-    def own_columns(parts, wide, own, mates):
-        mine = jnp.concatenate([columns_of(part, own, wide) for part in parts], axis=1)
-        given = mate(jnp.concatenate([columns_of(part, mates, wide) for part in parts], axis=1))
+    def own_columns(parts, wide, which):
+        return jnp.concatenate([columns_of(part, which, wide) for part in parts], axis=1)
+
+    def in_order(mine, given):
         upper = jnp.where(wsh == 0, mine, given)
         lower = jnp.where(wsh == 0, given, mine)
         return jnp.concatenate([upper, lower], axis=0)
 
-    row_blocks = gather_blocks(inputs)
-    far_first, out_grad = lax.optimization_barrier((row_blocks[2], out_grad))
-    qkv_weight = own_columns(
-        (query_weight, key_weight, value_weight), width, me, ctx * n_w + (1 - wsh)
-    )
+    hold = lax.optimization_barrier
+
+    if fast:
+        row_far, row_mate = across(inputs), mate(inputs)
+    heads_mine = (query_weight, key_weight, value_weight)
+    heads_given = [mate(weight) for weight in heads_mine]
     out_other = mate(out_weight)
-    gate_up = own_columns((gate_weight, up_weight), units, rank, (1 - wsh) * n_ctx + ctx)
+    gate_up_mine = own_columns((gate_weight, up_weight), units, rank)
+    gate_up_sent = own_columns((gate_weight, up_weight), units, (1 - wsh) * n_ctx + ctx)
     half = down_weight.shape[0]
     extra = n_ctx * units - half
     down_other = mate(down_weight[:extra])
@@ -344,16 +436,18 @@
         ]
     )
     down_own = lax.dynamic_slice_in_dim(down_wide, wsh * extra + ctx * units, units, 0)
-    dy = jnp.concatenate(gather_blocks(out_grad))
-    out_full = jnp.concatenate(
-        [jnp.where(wsh == 0, out_weight, out_other), jnp.where(wsh == 0, out_other, out_weight)]
-    )
-    out_full = jnp.pad(out_full, ((0, n * width - out_full.shape[0]), (0, 0)))
-    out_blocks = [lax.dynamic_slice_in_dim(out_full, (me ^ k) * width, width, 0) for k in range(n)]
-
     me_1 = me.reshape(1).astype(jnp.int32)
     order = permutation.reshape(n, rows)
     params = pltpu.CompilerParams(vmem_limit_bytes=vmem_bytes)
+    qkv_weight = pl.pallas_call(
+        functools.partial(own_heads_kernel, width, n, n_w),
+        out_shape=jax.ShapeDtypeStruct((model, 3 * width), bf16),
+        in_specs=[pl.BlockSpec(memory_space=pltpu.SMEM)]
+        + [pl.BlockSpec(memory_space=pltpu.VMEM)] * 6,
+        out_specs=pl.BlockSpec(memory_space=pltpu.VMEM),
+        compiler_params=params,
+        name="own_heads",
+    )(me_1, *heads_mine, *heads_given)
     bias = pl.pallas_call(
         functools.partial(bias_kernel, rows, heads_here, heads, buckets),
         out_shape=jax.ShapeDtypeStruct((heads_here, 5, rows, rows), f32),
@@ -365,6 +459,16 @@
         compiler_params=params,
         name="bias_strips",
     )(me_1, bucket_bias)
+    if fast:
+        row_far, out_grad, qkv_weight, bias, gate_up_mine, gate_up_sent = hold(
+            (row_far, out_grad, qkv_weight, bias, gate_up_mine, gate_up_sent)
+        )
+        row_blocks = [inputs, row_mate, row_far, mate(row_far)]
+    else:
+        row_blocks = gather_blocks(inputs)
+    gate_up_given = mate(gate_up_sent)
+    dy = jnp.concatenate(gather_blocks(out_grad))
+
     x_all, normed, qkv = pl.pallas_call(
         functools.partial(arrange_kernel, rows, n),
         out_shape=(
@@ -442,26 +546,26 @@
         peer = me ^ k
         return (peer % n_w) * n_ctx + peer // n_w
 
-    def ring(take, swap, write):
+    def ring(take, swap, pieces):
         both_ways = (forward, backward)
         one, two = take(0, lax.rem(spot + 7, n_group)), take(1, lax.rem(spot + 1, n_group))
         for s in range(n_group - 1):
             came = yield (one, two), both_ways
             one = came[0] + take(0, lax.rem(spot + 14 - s, n_group))
             two = came[1] + take(1, lax.rem(spot + 2 + s, n_group))
-        blocks, join = swap(jnp.stack([one, two], axis=1))
+        blocks, join = swap(one, two)
         came = yield tuple(blocks[1:]), (mate, across, diagonal)
-        one, two = join([blocks[0], *came])
-        out = write(write(None, one, spot, 0), two, spot, 1)
+        pairs = join([blocks[0], *came])
+        for pair in pairs:
+            pieces.extend(pair)
         for s in range(n_group - 1):
-            one, two = yield (one, two), both_ways
-            out = write(out, one, lax.rem(spot + 15 - s, n_group), 0)
-            out = write(out, two, lax.rem(spot + 1 + s, n_group), 1)
-        return out
+            for c, pair in enumerate(pairs):
+                pairs[c] = yield pair, both_ways
+                pieces.extend(pairs[c])
 
     class Stream:
         def __init__(self, steps):
-            self.steps, self.result = steps, None
+            self.steps, self.result, self.came = steps, None, None
             self.pending = next(steps)
 
         def advance(self, came):
@@ -470,64 +574,68 @@
             except StopIteration as stop:
                 self.pending, self.result = None, stop.value
 
+    order_token = [me]
+
     def tick(values, *streams):
         live = [stream for stream in streams if stream is not None and stream.pending is not None]
         if not live:
             return values
-        operands, values = lax.optimization_barrier(
-            ([stream.pending[0] for stream in live], values)
+        arrived, values = hold(([stream.came for stream in live if stream.came], values))
+        for stream in live:
+            if stream.came:
+                stream.advance(arrived.pop(0))
+        live = [stream for stream in live if stream.pending is not None]
+        operands, values, order_token[0] = hold(
+            ([stream.pending[0] for stream in live], values, order_token[0])
         )
         for stream, sent in zip(live, operands):
-            stream.advance([send(x) for send, x in zip(stream.pending[1], sent)])
+            stream.came = [send(x) for send, x in zip(stream.pending[1], sent)]
         return values
 
     def rows_cut(grad):
         return grad.reshape(n, n_group, 2, part, grad.shape[1])
 
-    def put(out, block, at, h):
-        if out is None:
-            out = jnp.zeros((n_group, 2) + block.shape, block.dtype)
-        return lax.dynamic_update_slice(out, block[None, None], (at, h) + (0,) * block.ndim)
+    wide_pieces, narrow_pieces = [], []
 
     def wide_ring(grad_gate_up, grad_down):
         one, two = rows_cut(grad_gate_up), rows_cut(grad_down)
-        kinds = 3
+        columns = 3 * n * units
 
         def take(h, index):
-            return jnp.concatenate(
-                [pick(one[:, :, h], index, 1), pick(two[:, :, h], index, 1)], axis=-1
-            )
-
-        def swap(both):
+            return jnp.concatenate([pick(x[:, :, h], index, 1) for x in (one, two)], axis=-1)
+
+        def swap(one, two):
+            both = jnp.stack([one, two], axis=1)
+
             def join(came):
-                full = jnp.zeros((2, part, kinds * n * units), bf16)
+                full = jnp.zeros((2, part, columns), bf16)
                 for k in range(n):
-                    for t in range(kinds):
+                    for t in range(3):
                         full = lax.dynamic_update_slice_in_dim(
                             full,
                             came[k][:, :, t * units : (t + 1) * units],
                             t * n * units + rank_of(k) * units,
                             2,
                         )
-                return full[0], full[1]
+                middle = columns // 2
+                return [(full[0, :, :middle], full[1, :, :middle])] + [
+                    (full[0, :, middle:], full[1, :, middle:])
+                ]
 
             return [pick(both, me ^ k, 0) for k in range(n)], join
 
-        def write(outs, block, at, h):
-            outs = outs or [None] * kinds
-            cuts = [block[:, t * n * units :][:, :hidden_units] for t in range(kinds)]
-            cuts = [cuts[0].astype(f32), cuts[1].astype(f32), cuts[2]]
-            return [put(out, cut, at, h) for out, cut in zip(outs, cuts)]
-
-        return ring(take, swap, write)
+        return ring(take, swap, wide_pieces)
 
     def small_ring(grad_qkv, grad_out):
-        grad = rows_cut(jnp.concatenate([grad_qkv, grad_out], axis=1))
+        one, two = rows_cut(grad_qkv), rows_cut(grad_out)
 
         def take(h, index):
-            return pick(grad[:, :, h], index, 1)
-
-        def swap(both):
+            return jnp.concatenate(
+                [pick(one[:, :, h], index, 1), pick(two[:, :, h], index, 1)], axis=-1
+            )
+
+        def swap(one, two):
+            both = jnp.stack([one, two], axis=1)
             own = jnp.concatenate([both[k, :, :, 3 * width :] for k in range(n)], axis=2)
 
             def join(came):
@@ -538,19 +646,11 @@
                     + [own],
                     axis=2,
                 )
-                return full[0], full[1]
+                return [(full[0], full[1])]
 
             return [pick(both, me ^ k, 0)[:, :, : 3 * width] for k in range(n)], join
 
-        def write(outs, block, at, h):
-            outs = outs or [None] * 4
-            across_heads = n * width
-            cuts = [
-                block[:, k * across_heads : (k + 1) * across_heads].astype(f32) for k in range(4)
-            ]
-            return [put(out, cut, at, h) for out, cut in zip(outs, cuts)]
-
-        return ring(take, swap, write)
+        return ring(take, swap, narrow_pieces)
 
     def sum_ring(small):
         for axis, bit, count in (
@@ -577,7 +677,20 @@
     def scatter_far(near, away):
         return near + across(away).astype(f32) if fast else near
 
-    attended_blocks = gather_blocks(attended)
+    attended, out_mine, out_other, gate_up_mine = hold(
+        (attended, out_weight, out_other, gate_up_mine)
+    )
+    gate_up = in_order(gate_up_mine, gate_up_given)
+    if fast:
+        attended_far, attended_mate = across(attended), mate(attended)
+        attended_far, gate_up = hold((attended_far, gate_up))
+        attended_blocks = [attended, attended_mate, attended_far, mate(attended_far)]
+    else:
+        attended_blocks = gather_blocks(attended)
+    out_full = in_order(out_mine, out_other)
+    out_full = jnp.pad(out_full, ((0, n * width - out_full.shape[0]), (0, 0)))
+    out_blocks = [lax.dynamic_slice_in_dim(out_full, (me ^ k) * width, width, 0) for k in range(n)]
+    out_relative = jnp.concatenate(out_blocks, axis=0)
     by_rows = [
         jnp.concatenate(
             [attended_blocks[k][(m ^ k) * rows : ((m ^ k) + 1) * rows] for m in range(n)]
@@ -586,7 +699,7 @@
     ]
     attended_all = jnp.concatenate(by_rows, axis=1)
     residual_all = x_all.astype(f32) + forward_product(
-        attended_all, jnp.concatenate(out_blocks, axis=0)
+        attended_all, out_relative
     )
     residual = residual_all[:rows]
     normed_ff = rms_norm(residual_all, gain_feedforward).astype(bf16)
@@ -601,6 +714,7 @@
     d_hidden = backward_product(dy, down_own)
     d_gate_wide, d_up_wide = activate_back(d_hidden)
     d_gate_up = jnp.concatenate([d_gate_wide.astype(bf16), d_up_wide.astype(bf16)], axis=1)
+
     grad_gate_up = weight_product(normed_ff, d_gate_up).astype(bf16)
     grad_down = weight_product(dy, hidden).astype(bf16)
     wide = Stream(wide_ring(grad_gate_up, grad_down)) if fast else None
@@ -612,28 +726,23 @@
     out_partial = forward_product(hidden, down_own).astype(bf16)
     near, away, out_partial = tick((near, away, out_partial), wide)
     d_normed_ff = scatter_far(near, away)
-    out_near, out_away = scatter_near(out_partial)
-    out_near, out_away = tick((out_near, out_away), wide)
+    d_normed_ff, residual = tick((d_normed_ff, residual), wide)
     norm_ff_back = jax.vjp(rms_norm, residual, gain_feedforward)[1]
     d_residual_norm, grad_gain_ff = norm_ff_back(d_normed_ff)
     d_residual = dy[:rows].astype(f32) + d_residual_norm
     branch = d_residual.astype(bf16)
-    branch, out_away = tick((branch, out_away), wide)
+
     if fast:
-        branch_far, branch_mate = across(branch), mate(branch)
-        (branch_mate,) = tick((branch_mate,), wide)
-        branch_far, out_away = tick((branch_far, out_away), wide)
-        branch_blocks = [branch, branch_mate, branch_far, mate(branch_far)]
+        d_rows = backward_product(branch, out_relative).astype(bf16)
+        d_rows = [d_rows[:, k * width : (k + 1) * width] for k in range(n)]
+        d_rows = [d_rows[0], mate(d_rows[1]), across(d_rows[2]), diagonal(d_rows[3])]
+        d_attended, branch = hold((jnp.concatenate(d_rows), branch))
     else:
         branch_blocks = gather_blocks(branch)
-    outputs = (residual + scatter_far(out_near, out_away)).astype(bf16)
-
-    d_branch = jnp.concatenate(branch_blocks)
-    d_attended = backward_product(d_branch, out_blocks[0]).astype(bf16)
-    delta = jnp.sum(
-        (d_attended.astype(f32) * attended_wide).reshape(tokens, heads_here, size), axis=2
-    ).T
-    d_attended, delta = tick((d_attended, delta), wide)
+        d_attended = backward_product(jnp.concatenate(branch_blocks), out_blocks[0]).astype(bf16)
+    d_attended, branch = tick((d_attended, branch), wide)
+    if fast:
+        branch_blocks = gather_blocks(branch)
     d_qkv, d_table = pl.pallas_call(
         functools.partial(attend_back_kernel, rows, n, heads_here, size, seqs, buckets),
         out_shape=(
@@ -647,13 +756,14 @@
                 whole((tokens, 3 * width)),
                 whole((heads_here, 5, rows, rows)),
                 whole((heads_here, tokens)),
-                whole((heads_here, tokens)),
+                whole((tokens, width)),
                 whole((tokens, width)),
             ],
             out_specs=[whole((tokens, 3 * width)), whole((buckets, 128))],
             scratch_shapes=[
                 pltpu.VMEM((heads_here, n, size, rows), f32),
                 pltpu.VMEM((heads_here, 5, rows, rows), f32),
+                pltpu.VMEM((heads_here, tokens), f32),
             ],
         ),
         compiler_params=params,
@@ -663,22 +773,31 @@
             transcendentals=tokens * tokens * heads_here,
         ),
         name="attend_back",
-    )(me_1, lengths_row, qkv, bias, lse, delta, d_attended)
-    d_qkv, d_branch = tick((d_qkv, d_branch), wide)
+    )(me_1, lengths_row, qkv, bias, lse, attended_wide, d_attended)
+    d_qkv, branch_far, out_partial = tick((d_qkv, branch_blocks[2], out_partial), wide)
+    branch_blocks[2] = branch_far
     grad_qkv = weight_product(normed, d_qkv).astype(bf16)
-    grad_out = weight_product(d_branch, attended).astype(bf16)
+    grad_out = sum(
+        weight_product(branch_blocks[k], attended[k * rows : (k + 1) * rows]) for k in range(n)
+    ).astype(bf16)
+    grad_qkv, grad_out, d_qkv = tick((grad_qkv, grad_out, d_qkv), wide)
+    back = backward_product(d_qkv, qkv_weight).astype(bf16)
     narrow = Stream(small_ring(grad_qkv, grad_out)) if fast else None
-    (d_qkv,) = tick((d_qkv,), wide, narrow)
-
-    back = backward_product(d_qkv, qkv_weight).astype(bf16)
-    (back,) = tick((back,), narrow)
+    (back,) = tick((back,), wide, narrow)
+
     near, away = scatter_near(back)
-    near, away = tick((near, away), wide, narrow)
+    near, away = tick((near, away), narrow)
+    (away,) = tick((away,), wide)
     d_normed = scatter_far(near, away)
-    (d_normed,) = tick((d_normed,), narrow)
-    norm_attn_back = jax.vjp(rms_norm, x_all[:rows].astype(f32), gain_attention)[1]
+    tick((), narrow)
+    tick((), wide)
+    d_normed, x_own = tick((d_normed, x_all[:rows]), narrow)
+    norm_attn_back = jax.vjp(rms_norm, x_own.astype(f32), gain_attention)[1]
     d_input_norm, grad_gain_attn = norm_attn_back(d_normed)
     input_grad = (d_residual + d_input_norm).astype(bf16)
+    out_near, out_away = scatter_near(out_partial)
+    out_away, grad_gain_attn = tick((out_away, grad_gain_attn), wide)
+    outputs = (residual + scatter_far(out_near, out_away)).astype(bf16)
 
     table_here = jnp.pad(d_table[:, :heads_here], ((0, 0), (0, n * heads_here)))
     table_here = jnp.roll(table_here, me * heads_here, axis=1)[:, :heads]
@@ -686,20 +805,35 @@
     if fast:
         sums = Stream(sum_ring(small))
         while wide.pending or narrow.pending or sums.pending:
-            tick((), wide, narrow, sums)
-            tick((), narrow)
+            tick((), narrow, sums)
+            tick((), wide)
         small = sums.result
     else:
         small = lax.psum(small, ("group",) + peer_axes)
     share = model // n
-    gains = [lax.dynamic_slice_in_dim(small, k * model + me * share, share) for k in range(2)]
+    gains = [lax.dynamic_slice_in_dim(small, k * model + order_token[0] * share, share) for k in range(2)]
     grad_table = small[2 * model :].reshape(buckets, heads)
 
     if fast:
-        total_gate, total_up = [x.reshape(model // n, hidden_units) for x in wide.result[:2]]
-        total_down = wide.result[2].reshape(model // n, hidden_units).T.astype(f32)
-        total_qkv = [x.reshape(model // n, n * width) for x in narrow.result[:3]]
-        total_out = narrow.result[3].reshape(-1, n, width).transpose(2, 1, 0).reshape(width, model)
+        own_rows, all_heads = model // n, n * width
+        wide_shape, down_shape = (own_rows, hidden_units), (hidden_units, own_rows)
+        out_shapes = [wide_shape, wide_shape, down_shape]
+        out_shapes += [(own_rows, all_heads)] * 3 + [(width, model)]
+        scratch = [wide_shape, wide_shape, wide_shape, down_shape]
+        scratch += [(own_rows, all_heads)] * 3 + [(n, own_rows, width), (width, model)]
+        total_gate, total_up, total_down, *total_qkv, total_out = pl.pallas_call(
+            functools.partial(
+                place_kernel, n_group, part, n * units, hidden_units, all_heads, width
+            ),
+            out_shape=[jax.ShapeDtypeStruct(shape, f32) for shape in out_shapes],
+            in_specs=[pl.BlockSpec(memory_space=pltpu.SMEM)]
+            + [pl.BlockSpec(memory_space=pltpu.VMEM)] * (6 * n_group),
+            out_specs=[pl.BlockSpec(memory_space=pl.ANY)] * 7,
+            scratch_shapes=[pltpu.VMEM(shape, f32) for shape in scratch]
+            + [pltpu.SemaphoreType.DMA((7,))],
+            compiler_params=params,
+            name="place",
+        )(spot.reshape(1).astype(jnp.int32), *wide_pieces, *narrow_pieces)
     else:
 
         def place_columns(grad, which, wide, total):

time: 542 us -> 477 us (0.88)
  waiting for transfers between devices: 170 us -> 130 us
  local copies, waits for them, and re-layouts: 82 us -> 47.1 us
  other arithmetic: 83.3 us -> 54.8 us
  starting transfers between devices: 78.9 us -> 94.4 us
  Pallas kernels: 61.5 us -> 72.9 us
  matrix products: 59.3 us -> 66.4 us
    ppermute x28 -> x35, waiting for transfers between devices: 104 us -> 65.9 us  [forward(): return lax.ppermute(block, 'group', ahead)]
    dynamic_update_slice x36 -> x0, other arithmetic: 34 us -> none  [put(): lax.dynamic_update_slice(out, block[None, None], (at, h) + (0,) * block.n...]
    ppermute x28 -> x35, waiting for transfers between devices: 39.7 us -> 19.4 us  [backward(): return lax.ppermute(block, 'group', behind)]
    pallas_call x0 -> x2, Pallas kernels: none -> 20 us  [the longest x1 15.1 us: per_device(): pl.pallas_call(functools.partial(place_kernel, n_group, part, n * units,...]
    unnamed x148 -> x266, local copies, waits for them, and re-layouts: 27.5 us -> 9.26 us
    dynamic_update_slice x16 -> x0, local copies, waits for them, and re-layouts: 11.8 us -> none  [put(): lax.dynamic_update_slice(out, block[None, None], (at, h) + (0,) * block.n...]
    ppermute x5, waiting for transfers between devices: 0.01 us -> 9.41 us  [sum_ring(): came = (yield ((small,), (lambda x: lax.ppermute(x, axis, pairs),)))]
    dot_general x11 -> x14, matrix products: 59.3 us -> 66.4 us  [dot(): lax.dot_general(left_side, right_side, (dims, ((), ())), precision=precis...]
  transfers between devices with their start and end apart: 89 -> 108, of which waited for: 46 -> 36; matrix products, arithmetic and copies ran while one was open for 29% -> 21% of each run, Pallas kernels for 11% -> 12%
where the time goes in v3:
time: 477 us; the launch traced here: 468 us
  waiting for transfers between devices  130 us (27%)
  starting transfers between devices  94.4 us (20%)
  Pallas kernels  72.9 us (15%)
  matrix products  66.4 us (14%)
  other arithmetic  54.8 us (11%)
  local copies, waits for them, and re-layouts  47.1 us (10%)
    dot_general x14, matrix products, dot(): lax.dot_general(left_side, right_side, (dims, ((), ())), precision=precis...  66.4 us
    ppermute x35, waiting for transfers between devices, forward(): return lax.ppermute(block, 'group', ahead)  65.9 us
    ppermute x35, starting transfers between devices, forward(): return lax.ppermute(block, 'group', ahead)  35.4 us
    ppermute x35, starting transfers between devices, backward(): return lax.ppermute(block, 'group', behind)  35.2 us
    ppermute x10, waiting for transfers between devices, across(): return lax.ppermute(block, 'ctx', flip_w)  27.3 us
    pallas_call x1, Pallas kernels, per_device(): pl.pallas_call(functools.partial(attend_back_kernel, rows, n, heads_here,...  21.7 us
    ppermute x35, waiting for transfers between devices, backward(): return lax.ppermute(block, 'group', behind)  19.4 us
    pallas_call x1, Pallas kernels, per_device(): pl.pallas_call(functools.partial(attend_kernel, rows, n, heads_here, size...  17.4 us
  transfers between devices with their start and end apart: 108, of which 36 were waited for; matrix products, arithmetic and copies ran while one was open for 21% of the time, Pallas kernels for 12%

profile of v3, /device:TPU:0, one launch (start us, length us, event | category | flops | bytes accessed | tf_op | source)
XLA Modules:
  0.0 468.2 jit_solution(16248652095668547326)
XLA Ops:
  5.4 3.9 pad_dynamic-slice_fusion.3
  16.4 4.8 %own_heads.1.weight_ref = bf16[1536,576]{1,0:T(8,128)(2,1)} custom-call(s32[1]{0:T(128)} %bitcast.me_ref, bf16[768,768]{1,0:T(8,128)(2,1)} %refs_0_.2, bf16[768,768]{1,0:T(8,128)(2,1)} %refs_1_.1, bf16[768,768]{1,0:T(8,128)(2,1)} %refs_2_.1, bf16[768,768]{1,0:T(8,128)(2,1)} %collective-permute-done.1.refs_3_, ...), custom_call_target="tpu_custom_call" | custom-call | tf_op jit(solution)/shard_map/own_heads/pallas_call | solution.py:442
  30.4 10.5 %arrange_project.1 = (bf16[1024,1536]{1,0:T(8,128)(2,1)}, bf16[1024,1536]{1,0:T(8,128)(2,1)}, bf16[1024,576]{1,0:T(8,128)(2,1)}) custom-call(s32[1]{0:T(128)} %bitcast.me_ref, s32[4,256]{1,0:T(4,128)} %reshape.273.order_ref, f32[1,1536]{1,0:T(1,128)} %reshape.274.gain_ref, bf16[1536,576]{1,0:T(8,128)(2,1)} %own_heads.1.weight_ref, ...), custom_call_target="tpu_custom_call" | custom-call | flops 5033164800 | bytes 12582912 | tf_op jit(solution)/shard_map/arrange_project/pallas_call | solution.py:472
  40.9 17.4 %attend.1 = (bf16[1024,192]{1,0:T(8,128)(2,1)}, f32[1024,192]{1,0:T(8,128)}, f32[3,1024]{1,0:T(4,128)}) custom-call(s32[1]{0:T(128)} %bitcast.me_ref, s32[4]{0:T(128)} %bitcast.261, bf16[1024,576]{1,0:T(8,128)(2,1)} %get-tuple-element.292.qkv_ref, f32[3,5,256,256]{3,2,1,0:T(8,128)} %bias_strips.1.bias_ref), custom_call_target="tpu_custom_call" | custom-call | flops 3221225472 | bytes 3145728 | tf_op jit(solution)/shard_map/attend/pallas_call | solution.py:499
  63.6 3.6 fusion.48
  70.3 3.8 pad_maximum_fusion
  76.5 4.9 %multiply_reduce_fusion = (f32[1024]{0:T(1024)S(1)}, f32[1024,1536]{1,0:T(8,128)S(1)}) fusion(bf16[192,1536]{1,0:T(8,128)(2,1)S(1)} %copy-done.34, bf16[192,1536]{1,0:T(8,128)(2,1)S(1)} %get-tuple-element.623, bf16[192,1536]{1,0:T(8,128)(2,1)S(1)} %get-tuple-element.622, bf16[192,1536]{1,0:T(8,128)(2,1)S(1)} %get-tuple-element.621, ...), kind=kOutput, calls=%fused_computation.6 | convolution fusion | flops 2448948224 | bytes 13373440 | tf_op jit(solution)/shard_map/dot_general | solution.py:38
  81.5 9.9 %fusion.88 = f32[1024,2048]{0,1:T(8,128)} fusion(bf16[1536,2048]{1,0:T(8,128)(2,1)S(1)} %bitcast.252, f32[1024,1536]{1,0:T(8,128)S(1)} %get-tuple-element.733, f32[1536]{0:T(1024)S(1)} %copy-done.106, f32[1024]{0:T(1024)S(1)} %add_rsqrt_fusion), kind=kOutput, calls=%fused_computation.318 | convolution fusion | flops 6447169536 | bytes 20981760 | tf_op jit(solution)/shard_map/dot_general | solution.py:38
  91.4 11.4 %fusion.6 = (bf16[1024,1024]{0,1:T(8,128)(2,1)S(1)}, bf16[1024,1024]{0,1:T(8,128)(2,1)S(1)}, bf16[1024,1024]{0,1:T(8,128)(2,1)}) fusion(f32[1024,2048]{0,1:T(8,128)} %fusion.88, bf16[1024,1536]{1,0:T(8,128)(2,1)S(1)} %copy-done.84, s32[]{:T(128)S(6)} %select_n.302, bf16[1984,1536]{1,0:T(8,128)(2,1)} %param.27, bf16[64,1536]{1,0:T(8,128)(2,1)S(1)} %copy-done.85, ...), kind=kOutput, calls=%fused_computation.20 | convolution fusion | flops 3257925632 | bytes 24313860 | tf_op jit(solution)/shard_map/dot_general | solution.py:38
  102.8 11.1 %convolution_convert_fusion = bf16[1536,2048]{1,0:T(8,128)(2,1)S(1)} fusion(f32[1024,1536]{1,0:T(8,128)} %copy-done.54, f32[1536]{0:T(1024)S(1)} %copy-done.106, f32[1024]{0:T(1024)S(1)} %add_rsqrt_fusion, bf16[1024,1024]{0,1:T(8,128)(2,1)S(1)} %get-tuple-element.583, bf16[1024,1024]{0,1:T(8,128)(2,1)S(1)} %get-tuple-element.582), kind=kOutput, calls=%fused_computation | convolution fusion | flops 6458703872 | bytes 16787456 | tf_op jit(solution)/shard_map/dot_general | solution.py:38
  116.4 4.1 convolution_convert_fusion.4
  128.0 7.1 %convolution_convert_fusion.1 = bf16[1024,1536]{1,0:T(8,128)(2,1)S(1)} fusion(bf16[1024,2048]{0,1:T(8,128)(2,1)S(1)} %copy-done.3, bf16[1536,2048]{1,0:T(8,128)(2,1)S(1)} %bitcast.252), kind=kOutput, calls=%fused_computation.25 | convolution fusion | flops 6444023808 | bytes 13631488 | tf_op jit(solution)/shard_map/dot_general | solution.py:38
  135.1 6.6 %collective-permute-done.15 = bf16[4,24,3072]{2,1,0:T(8,128)(2,1)S(1)} collective-permute-done((bf16[4,24,3072]{2,1,0:T(8,128)(2,1)S(1)}, bf16[4,24,3072]{2,1,0:T(8,128)(2,1)S(1)}, u32[]{:S(2)}, u32[]{:S(2)}) %collective-permute-start.15) | collective-permute-done | bytes 589856 | tf_op jit(solution)/shard_map/ppermute | solution.py:534
  145.9 6.4 %convolution_convert_fusion.3 = bf16[1024,1536]{1,0:T(8,128)(2,1)} fusion(bf16[1024,1024]{0,1:T(8,128)(2,1)S(1)} %copy-done.125, s32[]{:T(128)S(6)} %select_n.302, bf16[1984,1536]{1,0:T(8,128)(2,1)S(1)} %bitcast.260, bf16[64,1536]{1,0:T(8,128)(2,1)S(1)} %copy-done.86, bf16[64,1536]{1,0:T(8,128)(2,1)S(1)} %copy-done.88), kind=kOutput, calls=%fused_computation.27 | convolution fusion | flops 3232235520 | bytes 11730948 | tf_op jit(solution)/shard_map/dot_general | solution.py:38
  152.7 6.9 %collective-permute-done.17 = bf16[4,24,3072]{2,1,0:T(8,128)(2,1)S(1)} collective-permute-done((bf16[4,24,3072]{2,1,0:T(8,128)(2,1)S(1)}, bf16[4,24,3072]{2,1,0:T(8,128)(2,1)S(1)}, u32[]{:S(2)}, u32[]{:S(2)}) %collective-permute-start.17) | collective-permute-done | bytes 589856 | tf_op jit(solution)/shard_map/ppermute | solution.py:534
  166.3 13.5 %collective-permute-done.22 = bf16[256,1536]{1,0:T(8,128)(2,1)S(1)} collective-permute-done((bf16[256,1536]{1,0:T(8,128)(2,1)S(1)}, bf16[256,1536]{1,0:T(8,128)(2,1)S(1)}, u32[]{:S(2)}, u32[]{:S(2)}) %collective-permute-start.22) | collective-permute-done | bytes 786464 | tf_op jit(solution)/shard_map/ppermute | solution.py:394
  206.6 21.7 %attend_back.1 = (bf16[1024,576]{1,0:T(8,128)(2,1)}, f32[32,128]{1,0:T(8,128)}) custom-call(s32[1]{0:T(128)} %bitcast.me_ref, s32[4]{0:T(128)} %bitcast.262, bf16[1024,576]{1,0:T(8,128)(2,1)} %get-tuple-element.292.qkv_ref, f32[3,5,256,256]{3,2,1,0:T(8,128)} %bias_strips.1.bias_ref, f32[3,1024]{1,0:T(4,128)} %get-tuple-element.347.lse_ref, ...), custom_call_target="tpu_custom_call" | custom-call | flops 8053063680 | bytes 3145728 | tf_op jit(solution)/shard_map/attend_back/pallas_call | solution.py:746
  243.4 6.6 %collective-permute-done.32 = bf16[4,24,3072]{2,1,0:T(8,128)(2,1)S(1)} collective-permute-done((bf16[4,24,3072]{2,1,0:T(8,128)(2,1)S(1)}, bf16[4,24,3072]{2,1,0:T(8,128)(2,1)S(1)}, u32[]{:S(2)}, u32[]{:S(2)}) %collective-permute-start.32) | collective-permute-done | bytes 589856 | tf_op jit(solution)/shard_map/ppermute | solution.py:534
  259.6 3.9 copy.36
  285.8 6.0 %collective-permute-done.39 = bf16[2,24,3072]{2,1,0:T(8,128)(2,1)S(1)} collective-permute-done((bf16[2,24,3072]{2,1,0:T(8,128)(2,1)S(1)}, bf16[2,24,3072]{2,1,0:T(8,128)(2,1)S(1)}, u32[]{:S(2)}, u32[]{:S(2)}) %collective-permute-start.39) | collective-permute-done | bytes 294944 | tf_op jit(solution)/shard_map/ppermute | solution.py:394
  291.7 5.4 %collective-permute-done.40 = bf16[2,24,3072]{2,1,0:T(8,128)(2,1)S(1)} collective-permute-done((bf16[2,24,3072]{2,1,0:T(8,128)(2,1)S(1)}, bf16[2,24,3072]{2,1,0:T(8,128)(2,1)S(1)}, u32[]{:S(2)}, u32[]{:S(2)}) %collective-permute-start.40) | collective-permute-done | bytes 294944 | tf_op jit(solution)/shard_map/ppermute | solution.py:540
  307.9 5.5 %collective-permute-done.44.refs_4_ = bf16[24,6144]{1,0:T(8,128)(2,1)S(1)} collective-permute-done((bf16[24,6144]{1,0:T(8,128)(2,1)S(1)}, bf16[24,6144]{1,0:T(8,128)(2,1)S(1)}, u32[]{:S(2)}, u32[]{:S(2)}) %collective-permute-start.44) | collective-permute-done | bytes 294944 | tf_op jit(solution)/shard_map/ppermute | solution.py:534
  343.4 4.2 collective-permute-done.67.refs_10_
  350.5 3.4 collective-permute-done.73.refs_12_
  374.4 6.8 %collective-permute-done.77 = f32[3456]{0:T(1024)S(1)} collective-permute-done((f32[3456]{0:T(1024)S(1)}, f32[3456]{0:T(1024)S(1)}, u32[]{:S(2)}, u32[]{:S(2)}) %collective-permute-start.77) | collective-permute-done | bytes 13856 | tf_op jit(solution)/shard_map/ppermute | solution.py:664
  385.4 9.0 %collective-permute-done.82.refs_36_ = bf16[24,3072]{1,0:T(8,128)(2,1)S(1)} collective-permute-done((bf16[24,3072]{1,0:T(8,128)(2,1)S(1)}, bf16[24,3072]{1,0:T(8,128)(2,1)S(1)}, u32[]{:S(2)}, u32[]{:S(2)}) %collective-permute-start.82) | collective-permute-done | bytes 147488 | tf_op jit(solution)/shard_map/ppermute | solution.py:534
  406.4 4.5 collective-permute-done.90.refs_40_
  417.0 5.1 %collective-permute-done.96.refs_42_ = bf16[24,3072]{1,0:T(8,128)(2,1)S(1)} collective-permute-done((bf16[24,3072]{1,0:T(8,128)(2,1)S(1)}, bf16[24,3072]{1,0:T(8,128)(2,1)S(1)}, u32[]{:S(2)}, u32[]{:S(2)}) %collective-permute-start.96) | collective-permute-done | bytes 147488 | tf_op jit(solution)/shard_map/ppermute | solution.py:534
  429.0 6.1 %collective-permute-done.98.refs_44_ = bf16[24,3072]{1,0:T(8,128)(2,1)} collective-permute-done((bf16[24,3072]{1,0:T(8,128)(2,1)S(1)}, bf16[24,3072]{1,0:T(8,128)(2,1)}, u32[]{:S(2)}, u32[]{:S(2)}) %collective-permute-start.98) | collective-permute-done | bytes 147488 | tf_op jit(solution)/shard_map/ppermute | solution.py:534
  442.2 4.5 fusion.12
  448.7 3.4 collective-permute-done.107.refs_47_
  452.7 15.1 %place.1 = (f32[384,3968]{1,0:T(8,128)}, f32[384,3968]{1,0:T(8,128)}, f32[3968,384]{1,0:T(8,128)}, f32[384,768]{1,0:T(8,128)}, f32[384,768]{1,0:T(8,128)}, /*index=5*/f32[384,768]{1,0:T(8,128)}, f32[192,1536]{1,0:T(8,128)}) custom-call(s32[1]{0:T(128)} %bitcast.112.spot_ref, bf16[24,6144]{1,0:T(8,128)(2,1)} %copy-done.20, bf16[24,6144]{1,0:T(8,128)(2,1)} %copy-done.19, ...), custom_call_target="tpu_custom_call" | custom-call | tf_op jit(solution)/shard_map/place/pallas_call | solution.py:824
  (602 shorter events, 228.1 us)
Async XLA Ops:
  1.7 21.0 %collective-permute-start = (bf16[256,1536]{1,0:T(8,128)(2,1)}, bf16[256,1536]{1,0:T(8,128)(2,1)}, u32[]{:S(2)}, u32[]{:S(2)}) collective-permute-start(bf16[256,1536]{1,0:T(8,128)(2,1)} %refs_0_.3), channel_id=1, source_target_pairs={{0,2},{2,0},{1,3},{3,1},{4,6},{6,4},{5,7},{7,5},{8,10},{10,8},{9,1... | collective-permute-start | bytes 2359304 | tf_op jit(solution)/shard_map/ppermute | solution.py:394
  4.3 23.8 %collective-permute-start.4 = (bf16[256,1536]{1,0:T(8,128)(2,1)}, bf16[256,1536]{1,0:T(8,128)(2,1)}, u32[]{:S(2)}, u32[]{:S(2)}) collective-permute-start(bf16[256,1536]{1,0:T(8,128)(2,1)} %refs_0_.3), channel_id=1, source_target_pairs={{0,1},{1,0},{2,3},{3,2},{4,5},{5,4},{6,7},{7,6},{8,9},{9,8},{10,11... | collective-permute-start | bytes 2359304 | tf_op jit(solution)/shard_map/ppermute | solution.py:391
  22.7 35.5 %collective-permute-start.6 = (bf16[384,1536]{1,0:T(8,128)(2,1)}, bf16[384,1536]{1,0:T(8,128)(2,1)}, u32[]{:S(2)}, u32[]{:S(2)}) collective-permute-start(bf16[384,1536]{1,0:T(8,128)(2,1)} %param.22), channel_id=1, source_target_pairs={{0,1},{1,0},{2,3},{3,2},{4,5},{5,4},{6,7},{7,6},{8,9},{9,8},{10,11... | collective-permute-start | bytes 3538952 | tf_op jit(solution)/shard_map/ppermute | solution.py:391
  23.3 44.8 %collective-permute-start.9 = (bf16[768,2048]{1,0:T(8,128)(2,1)}, bf16[768,2048]{1,0:T(8,128)(2,1)}, u32[]{:S(2)}, u32[]{:S(2)}) collective-permute-start(bf16[768,2048]{1,0:T(8,128)(2,1)} %pad_maximum_fusion.3), channel_id=1, source_target_pairs={{0,1},{1,0},{2,3},{3,2},{4,5},{5,4},{6,7},{7,6},{8,9},{9,8},{10,11... | collective-permute-start | bytes 9437192 | tf_op jit(solution)/shard_map/ppermute | solution.py:391
  26.3 32.4 %collective-permute-start.12 = (bf16[256,1536]{1,0:T(8,128)(2,1)}, bf16[256,1536]{1,0:T(8,128)(2,1)S(1)}, u32[]{:S(2)}, u32[]{:S(2)}) collective-permute-start(bf16[256,1536]{1,0:T(8,128)(2,1)} %param.15), channel_id=1, source_target_pairs={{0,2},{2,0},{1,3},{3,1},{4,6},{6,4},{5,7},{7,5},{8,10},{10,8},{9,1... | collective-permute-start | bytes 2359304 | tf_op jit(solution)/shard_map/ppermute | solution.py:394
  28.1 31.1 %collective-permute-start.11 = (bf16[256,1536]{1,0:T(8,128)(2,1)}, bf16[256,1536]{1,0:T(8,128)(2,1)}, u32[]{:S(2)}, u32[]{:S(2)}) collective-permute-start(bf16[256,1536]{1,0:T(8,128)(2,1)} %param.15), channel_id=1, source_target_pairs={{0,1},{1,0},{2,3},{3,2},{4,5},{5,4},{6,7},{7,6},{8,9},{9,8},{10,11... | collective-permute-start | bytes 2359304 | tf_op jit(solution)/shard_map/ppermute | solution.py:391
  58.3 15.9 %collective-permute-start.8 = (bf16[1024,192]{1,0:T(8,128)(2,1)}, bf16[1024,192]{1,0:T(8,128)(2,1)}, u32[]{:S(2)}, u32[]{:S(2)}) collective-permute-start(bf16[1024,192]{1,0:T(8,128)(2,1)} %get-tuple-element.296), channel_id=1, source_target_pairs={{0,2},{2,0},{1,3},{3,1},{4,6},{6,4},{5,7},{7,5},{8,10},{10,8},{9,1... | collective-permute-start | bytes 1179656 | tf_op jit(solution)/shard_map/ppermute | solution.py:394
  58.7 15.6 %collective-permute-start.13 = (bf16[256,1536]{1,0:T(8,128)(2,1)S(1)}, bf16[256,1536]{1,0:T(8,128)(2,1)S(1)}, u32[]{:S(2)}, u32[]{:S(2)}) collective-permute-start(bf16[256,1536]{1,0:T(8,128)(2,1)S(1)} %collective-permute-done.12), channel_id=1, source_target_pairs={{0,1},{1,0},{2,3},{3,2},{4,5},{5,4},{6,7},{7,6},{8,9},{9,8},{10,11... | collective-permute-start | bytes 2359304 | tf_op jit(solution)/shard_map/ppermute | solution.py:391
  125.9 15.7 %collective-permute-start.15 = (bf16[4,24,3072]{2,1,0:T(8,128)(2,1)S(1)}, bf16[4,24,3072]{2,1,0:T(8,128)(2,1)S(1)}, u32[]{:S(2)}, u32[]{:S(2)}) collective-permute-start(bf16[4,24,3072]{2,1,0:T(8,128)(2,1)S(1)} %pad_maximum_fusion.8), channel_id=1, source_target_pairs={{0,8},{8,16},{16,24},{24,28},{28,20},{20,12},{12,4},{4,0},{1,9},{9... | collective-permute-start | bytes 1769480 | tf_op jit(solution)/shard_map/ppermute | solution.py:534
  127.7 15.4 %collective-permute-start.16 = (bf16[4,24,3072]{2,1,0:T(8,128)(2,1)S(1)}, bf16[4,24,3072]{2,1,0:T(8,128)(2,1)S(1)}, u32[]{:S(2)}, u32[]{:S(2)}) collective-permute-start(bf16[4,24,3072]{2,1,0:T(8,128)(2,1)S(1)} %pad_maximum_fusion.9), channel_id=1, source_target_pairs={{8,0},{16,8},{24,16},{28,24},{20,28},{12,20},{4,12},{0,4},{9,1},{1... | collective-permute-start | bytes 1769480 | tf_op jit(solution)/shard_map/ppermute | solution.py:537
  143.8 15.7 %collective-permute-start.17 = (bf16[4,24,3072]{2,1,0:T(8,128)(2,1)S(1)}, bf16[4,24,3072]{2,1,0:T(8,128)(2,1)S(1)}, u32[]{:S(2)}, u32[]{:S(2)}) collective-permute-start(bf16[4,24,3072]{2,1,0:T(8,128)(2,1)S(1)} %maximum_add_fusion), channel_id=1, source_target_pairs={{0,8},{8,16},{16,24},{24,28},{28,20},{20,12},{12,4},{4,0},{1,9},{9... | collective-permute-start | bytes 1769480 | tf_op jit(solution)/shard_map/ppermute | solution.py:534
  145.3 15.4 %collective-permute-start.18 = (bf16[4,24,3072]{2,1,0:T(8,128)(2,1)S(1)}, bf16[4,24,3072]{2,1,0:T(8,128)(2,1)S(1)}, u32[]{:S(2)}, u32[]{:S(2)}) collective-permute-start(bf16[4,24,3072]{2,1,0:T(8,128)(2,1)S(1)} %maximum_add_fusion.1), channel_id=1, source_target_pairs={{8,0},{16,8},{24,16},{28,24},{20,28},{12,20},{4,12},{0,4},{9,1},{1... | collective-permute-start | bytes 1769480 | tf_op jit(solution)/shard_map/ppermute | solution.py:537
  161.0 18.8 %collective-permute-start.22 = (bf16[256,1536]{1,0:T(8,128)(2,1)S(1)}, bf16[256,1536]{1,0:T(8,128)(2,1)S(1)}, u32[]{:S(2)}, u32[]{:S(2)}) collective-permute-start(bf16[256,1536]{1,0:T(8,128)(2,1)S(1)} %get-tuple-element.328), channel_id=1, source_target_pairs={{0,2},{2,0},{1,3},{3,1},{4,6},{6,4},{5,7},{7,5},{8,10},{10,8},{9,1... | collective-permute-start | bytes 2359304 | tf_op jit(solution)/shard_map/ppermute | solution.py:394
  162.6 17.4 %collective-permute-start.20 = (bf16[4,24,3072]{2,1,0:T(8,128)(2,1)S(1)}, bf16[4,24,3072]{2,1,0:T(8,128)(2,1)S(1)}, u32[]{:S(2)}, u32[]{:S(2)}) collective-permute-start(bf16[4,24,3072]{2,1,0:T(8,128)(2,1)S(1)} %maximum_add_fusion.2), channel_id=1, source_target_pairs={{0,8},{8,16},{16,24},{24,28},{28,20},{20,12},{12,4},{4,0},{1,9},{9... | collective-permute-start | bytes 1769480 | tf_op jit(solution)/shard_map/ppermute | solution.py:534
  164.3 15.7 %collective-permute-start.21 = (bf16[4,24,3072]{2,1,0:T(8,128)(2,1)S(1)}, bf16[4,24,3072]{2,1,0:T(8,128)(2,1)S(1)}, u32[]{:S(2)}, u32[]{:S(2)}) collective-permute-start(bf16[4,24,3072]{2,1,0:T(8,128)(2,1)S(1)} %maximum_add_fusion.3), channel_id=1, source_target_pairs={{8,0},{16,8},{24,16},{28,24},{20,28},{12,20},{4,12},{0,4},{9,1},{1... | collective-permute-start | bytes 1769480 | tf_op jit(solution)/shard_map/ppermute | solution.py:537
  203.1 26.7 %collective-permute-start.34 = (bf16[256,1536]{1,0:T(8,128)(2,1)S(1)}, bf16[256,1536]{1,0:T(8,128)(2,1)}, u32[]{:S(2)}, u32[]{:S(2)}) collective-permute-start(bf16[256,1536]{1,0:T(8,128)(2,1)S(1)} %copy-done.7), channel_id=1, source_target_pairs={{0,1},{1,0},{2,3},{3,2},{4,5},{5,4},{6,7},{7,6},{8,9},{9,8},{10,11... | collective-permute-start | bytes 2359304 | tf_op jit(solution)/shard_map/ppermute | solution.py:391
  203.1 28.6 %collective-permute-start.30 = (bf16[256,1536]{1,0:T(8,128)(2,1)S(1)}, bf16[256,1536]{1,0:T(8,128)(2,1)}, u32[]{:S(2)}, u32[]{:S(2)}) collective-permute-start(bf16[256,1536]{1,0:T(8,128)(2,1)S(1)} %copy-done.7), channel_id=1, source_target_pairs={{0,2},{2,0},{1,3},{3,1},{4,6},{6,4},{5,7},{7,5},{8,10},{10,8},{9,1... | collective-permute-start | bytes 2359304 | tf_op jit(solution)/shard_map/ppermute | solution.py:394
  204.6 27.1 %collective-permute-start.28 = (bf16[4,24,3072]{2,1,0:T(8,128)(2,1)}, bf16[4,24,3072]{2,1,0:T(8,128)(2,1)}, u32[]{:S(2)}, u32[]{:S(2)}) collective-permute-start(bf16[4,24,3072]{2,1,0:T(8,128)(2,1)} %maximum_add_fusion.6), channel_id=1, source_target_pairs={{0,8},{8,16},{16,24},{24,28},{28,20},{20,12},{12,4},{4,0},{1,9},{9... | collective-permute-start | bytes 1769480 | tf_op jit(solution)/shard_map/ppermute | solution.py:534
  205.4 26.3 %collective-permute-start.29 = (bf16[4,24,3072]{2,1,0:T(8,128)(2,1)}, bf16[4,24,3072]{2,1,0:T(8,128)(2,1)}, u32[]{:S(2)}, u32[]{:S(2)}) collective-permute-start(bf16[4,24,3072]{2,1,0:T(8,128)(2,1)} %maximum_add_fusion.7), channel_id=1, source_target_pairs={{8,0},{16,8},{24,16},{28,24},{20,28},{12,20},{4,12},{0,4},{9,1},{1... | collective-permute-start | bytes 1769480 | tf_op jit(solution)/shard_map/ppermute | solution.py:537
  252.7 18.9 %collective-permute-start.36 = (bf16[4,24,3072]{2,1,0:T(8,128)(2,1)}, bf16[4,24,3072]{2,1,0:T(8,128)(2,1)}, u32[]{:S(2)}, u32[]{:S(2)}) collective-permute-start(bf16[4,24,3072]{2,1,0:T(8,128)(2,1)} %maximum_add_fusion.10), channel_id=1, source_target_pairs={{0,8},{8,16},{16,24},{24,28},{28,20},{20,12},{12,4},{4,0},{1,9},{9... | collective-permute-start | bytes 1769480 | tf_op jit(solution)/shard_map/ppermute | solution.py:534
  253.0 18.5 %collective-permute-start.37 = (bf16[4,24,3072]{2,1,0:T(8,128)(2,1)}, bf16[4,24,3072]{2,1,0:T(8,128)(2,1)}, u32[]{:S(2)}, u32[]{:S(2)}) collective-permute-start(bf16[4,24,3072]{2,1,0:T(8,128)(2,1)} %maximum_add_fusion.11), channel_id=1, source_target_pairs={{8,0},{16,8},{24,16},{28,24},{20,28},{12,20},{4,12},{0,4},{9,1},{1... | collective-permute-start | bytes 1769480 | tf_op jit(solution)/shard_map/ppermute | solution.py:537
  279.0 21.7 %collective-permute-start.31 = (bf16[2,256,1536]{2,1,0:T(8,128)(2,1)S(1)}, bf16[2,256,1536]{2,1,0:T(8,128)(2,1)S(1)}, u32[]{:S(2)}, u32[]{:S(2)}) collective-permute-start(bf16[2,256,1536]{2,1,0:T(8,128)(2,1)S(1)} %pad_maximum_fusion.6), channel_id=1, source_target_pairs={{0,1},{1,0},{2,3},{3,2},{4,5},{5,4},{6,7},{7,6},{8,9},{9,8},{10,11... | collective-permute-start | bytes 4718600 | tf_op jit(solution)/shard_map/ppermute | solution.py:391
  299.6 19.2 %collective-permute-start.52 = (bf16[256,1536]{1,0:T(8,128)(2,1)S(1)}, bf16[256,1536]{1,0:T(8,128)(2,1)S(1)}, u32[]{:S(2)}, u32[]{:S(2)}) collective-permute-start(bf16[256,1536]{1,0:T(8,128)(2,1)S(1)} %get-tuple-element.412), channel_id=1, source_target_pairs={{0,2},{2,0},{1,3},{3,1},{4,6},{6,4},{5,7},{7,5},{8,10},{10,8},{9,1... | collective-permute-start | bytes 2359304 | tf_op jit(solution)/shard_map/ppermute | solution.py:394
  353.9 17.2 %collective-permute-start.78 = (bf16[24,6144]{1,0:T(8,128)(2,1)}, bf16[24,6144]{1,0:T(8,128)(2,1)}, u32[]{:S(2)}, u32[]{:S(2)}) collective-permute-start(bf16[24,6144]{1,0:T(8,128)(2,1)} %collective-permute-done.67.refs_10_), channel_id=1, source_target_pairs={{0,8},{8,16},{16,24},{24,28},{28,20},{20,12},{12,4},{4,0},{1,9},{9... | collective-permute-start | bytes 884744 | tf_op jit(solution)/shard_map/ppermute | solution.py:534
  364.2 19.2 %collective-permute-start.84 = (bf16[24,6144]{1,0:T(8,128)(2,1)}, bf16[24,6144]{1,0:T(8,128)(2,1)}, u32[]{:S(2)}, u32[]{:S(2)}) collective-permute-start(bf16[24,6144]{1,0:T(8,128)(2,1)} %collective-permute-done.73.refs_12_), channel_id=1, source_target_pairs={{0,8},{8,16},{16,24},{24,28},{28,20},{20,12},{12,4},{4,0},{1,9},{9... | collective-permute-start | bytes 884744 | tf_op jit(solution)/shard_map/ppermute | solution.py:534
  364.2 21.1 %collective-permute-start.85 = (bf16[24,6144]{1,0:T(8,128)(2,1)}, bf16[24,6144]{1,0:T(8,128)(2,1)}, u32[]{:S(2)}, u32[]{:S(2)}) collective-permute-start(bf16[24,6144]{1,0:T(8,128)(2,1)} %collective-permute-done.74.refs_13_), channel_id=1, source_target_pairs={{8,0},{16,8},{24,16},{28,24},{20,28},{12,20},{4,12},{0,4},{9,1},{1... | collective-permute-start | bytes 884744 | tf_op jit(solution)/shard_map/ppermute | solution.py:537
  381.2 15.3 %collective-permute-start.80 = (bf16[24,6144]{1,0:T(8,128)(2,1)}, bf16[24,6144]{1,0:T(8,128)(2,1)S(1)}, u32[]{:S(2)}, u32[]{:S(2)}) collective-permute-start(bf16[24,6144]{1,0:T(8,128)(2,1)} %collective-permute-done.78.refs_14_), channel_id=1, source_target_pairs={{0,8},{8,16},{16,24},{24,28},{28,20},{20,12},{12,4},{4,0},{1,9},{9... | collective-permute-start | bytes 884744 | tf_op jit(solution)/shard_map/ppermute | solution.py:534
  385.3 19.1 %collective-permute-start.92 = (bf16[24,6144]{1,0:T(8,128)(2,1)}, bf16[24,6144]{1,0:T(8,128)(2,1)S(1)}, u32[]{:S(2)}, u32[]{:S(2)}) collective-permute-start(bf16[24,6144]{1,0:T(8,128)(2,1)} %collective-permute-done.84.refs_16_), channel_id=1, source_target_pairs={{0,8},{8,16},{16,24},{24,28},{28,20},{20,12},{12,4},{4,0},{1,9},{9... | collective-permute-start | bytes 884744 | tf_op jit(solution)/shard_map/ppermute | solution.py:534
  396.5 43.6 %collective-permute-start.53 = (bf16[256,1536]{1,0:T(8,128)(2,1)}, bf16[256,1536]{1,0:T(8,128)(2,1)S(1)}, u32[]{:S(2)}, u32[]{:S(2)}) collective-permute-start(bf16[256,1536]{1,0:T(8,128)(2,1)} %fusion.41), channel_id=1, source_target_pairs={{0,2},{2,0},{1,3},{3,1},{4,6},{6,4},{5,7},{7,5},{8,10},{10,8},{9,1... | collective-permute-start | bytes 2359304 | tf_op jit(solution)/shard_map/ppermute | solution.py:394
  410.9 15.2 %collective-permute-start.100 = (bf16[24,6144]{1,0:T(8,128)(2,1)S(1)}, bf16[24,6144]{1,0:T(8,128)(2,1)}, u32[]{:S(2)}, u32[]{:S(2)}) collective-permute-start(bf16[24,6144]{1,0:T(8,128)(2,1)S(1)} %collective-permute-done.92.refs_20_), channel_id=1, source_target_pairs={{0,8},{8,16},{16,24},{24,28},{28,20},{20,12},{12,4},{4,0},{1,9},{9... | collective-permute-start | bytes 884744 | tf_op jit(solution)/shard_map/ppermute | solution.py:534
  422.2 15.8 %collective-permute-start.94 = (bf16[24,6144]{1,0:T(8,128)(2,1)S(1)}, bf16[24,6144]{1,0:T(8,128)(2,1)}, u32[]{:S(2)}, u32[]{:S(2)}) collective-permute-start(bf16[24,6144]{1,0:T(8,128)(2,1)S(1)} %collective-permute-done.86.refs_22_), channel_id=1, source_target_pairs={{0,8},{8,16},{16,24},{24,28},{28,20},{20,12},{12,4},{4,0},{1,9},{9... | collective-permute-start | bytes 884744 | tf_op jit(solution)/shard_map/ppermute | solution.py:534
  435.1 17.0 %collective-permute-start.102 = (bf16[24,6144]{1,0:T(8,128)(2,1)}, bf16[24,6144]{1,0:T(8,128)(2,1)}, u32[]{:S(2)}, u32[]{:S(2)}) collective-permute-start(bf16[24,6144]{1,0:T(8,128)(2,1)} %collective-permute-done.100.refs_24_), channel_id=1, source_target_pairs={{0,8},{8,16},{16,24},{24,28},{28,20},{20,12},{12,4},{4,0},{1,9},{9... | collective-permute-start | bytes 884744 | tf_op jit(solution)/shard_map/ppermute | solution.py:534
  (206 other events, 2268.2 us)

commit v4 on v3

--- a/solution.py
+++ b/solution.py
@@ -4,6 +4,7 @@
 import jax.numpy as jnp
 from jax import lax
 from jax.experimental import pallas as pl
+from jax.experimental.layout import Layout, with_layout_constraint
 from jax.experimental.pallas import tpu as pltpu
 from jax.sharding import PartitionSpec as P
 
@@ -287,13 +288,46 @@
         table_ref[...] = table
 
 
+def collect_kernel(n, n_w, me_ref, *refs):
+    blocks, (gate_up, out), results, sems = refs[:n], (refs[n : n + 2], refs[n + 2 : n + 4]), refs[-4:-1], refs[-1]
+    me = me_ref[0]
+    mine = lax.rem(me, n_w)
+    rows, half, own = blocks[0].shape[0], gate_up[0].shape[0], out[0].shape[0]
+    width = own * n_w // n
+    copies = [
+        pltpu.make_async_copy(block, results[0].at[k * rows : (k + 1) * rows], sems.at[k])
+        for k, block in enumerate(blocks)
+    ]
+    for k, place in enumerate((mine, n_w - 1 - mine)):
+        at = pl.ds(pl.multiple_of(place * half, half), half)
+        copies.append(pltpu.make_async_copy(gate_up[k], results[1].at[at], sems.at[n + k]))
+    for copy in copies:
+        copy.start()
+    for k in range(n):
+        head = me ^ k
+        source = pl.ds(pl.multiple_of(lax.rem(head, n // n_w) * width, width), width)
+        target = results[2].at[k * width : (k + 1) * width]
+        for which in range(2):
+            copy = pltpu.make_async_copy(out[which].at[source], target, sems.at[n + 2 + k])
+
+            @pl.when((head // (n // n_w) == mine) == (which == 0))
+            def _():
+                copy.start()
+
+        copies.append(copy)
+    for copy in copies:
+        copy.wait()
+
+
 def place_kernel(groups, part, units_all, hidden_units, heads_all, width, spot_ref, *refs):
     spot = spot_ref[0]
     wide, refs = refs[: 4 * groups], refs[4 * groups :]
     narrow, refs = refs[: 2 * groups], refs[2 * groups :]
     outs, scratch, sems = refs[:7], refs[7:-1], refs[-1]
     gate, up, down, turned, query, key, value, out_rows, out_turned = scratch
-    middle = 3 * units_all // 2
+    count = heads_all // width
+    units = units_all // count
+    middle = 3 * units // 2
 
     def row_of(j, h):
         index = lax.rem(spot + groups - j, groups) if h == 0 else lax.rem(spot + j, groups)
@@ -304,14 +338,18 @@
 
     def gather(target, t):
         for c in range(2):
-            low = max(c * middle, t * units_all)
-            high = min((c + 1) * middle, t * units_all + hidden_units)
-            if low < high:
+            low, high = max(c * middle, t * units), min((c + 1) * middle, (t + 1) * units)
+            for r in range(count):
+                first = r * units + low - t * units
+                size = min(high - low, hidden_units - first)
+                if low >= high or size <= 0:
+                    continue
+                start = r * middle + low - c * middle
                 for j in range(groups):
                     for h in range(2):
                         block = wide[(j * 2 + c) * 2 + h]
-                        target[pl.ds(row_of(j, h), part), low - t * units_all : high - t * units_all] = (
-                            block[:, low - c * middle : high - c * middle].astype(f32)
+                        target[pl.ds(row_of(j, h), part), first : first + size] = (
+                            block[:, start : start + size].astype(f32)
                         )
 
     gather(gate, 0)
@@ -329,7 +367,6 @@
                     narrow[j * 2 + h][:, k * heads_all : (k + 1) * heads_all].astype(f32)
                 )
         copy(3 + k, target).start()
-    count = heads_all // width
     for q in range(count):
         for j in range(groups):
             for h in range(2):
@@ -467,7 +504,7 @@
     else:
         row_blocks = gather_blocks(inputs)
     gate_up_given = mate(gate_up_sent)
-    dy = jnp.concatenate(gather_blocks(out_grad))
+    dy_blocks = gather_blocks(out_grad)
 
     x_all, normed, qkv = pl.pallas_call(
         functools.partial(arrange_kernel, rows, n),
@@ -553,9 +590,10 @@
             came = yield (one, two), both_ways
             one = came[0] + take(0, lax.rem(spot + 14 - s, n_group))
             two = came[1] + take(1, lax.rem(spot + 2 + s, n_group))
-        blocks, join = swap(one, two)
-        came = yield tuple(blocks[1:]), (mate, across, diagonal)
-        pairs = join([blocks[0], *came])
+        pairs, (blocks, join) = [], swap(one, two)
+        for block in blocks:
+            came = yield tuple(block[1:]), (mate, across, diagonal)
+            pairs.append(join([block[0], *came]))
         for pair in pairs:
             pieces.extend(pair)
         for s in range(n_group - 1):
@@ -592,6 +630,13 @@
             stream.came = [send(x) for send, x in zip(stream.pending[1], sent)]
         return values
 
+    def piece_of(cut, index, h):
+        zero = jnp.zeros((), index.dtype)
+        starts = (zero, index, zero + h, zero, zero)
+        return lax.squeeze(
+            lax.dynamic_slice(cut, starts, (n, 1, 1, part, cut.shape[4])), (1, 2)
+        )
+
     def rows_cut(grad):
         return grad.reshape(n, n_group, 2, part, grad.shape[1])
 
@@ -599,30 +644,22 @@
 
     def wide_ring(grad_gate_up, grad_down):
         one, two = rows_cut(grad_gate_up), rows_cut(grad_down)
-        columns = 3 * n * units
 
         def take(h, index):
-            return jnp.concatenate([pick(x[:, :, h], index, 1) for x in (one, two)], axis=-1)
+            return jnp.concatenate([piece_of(x, index, h) for x in (one, two)], axis=-1)
 
         def swap(one, two):
             both = jnp.stack([one, two], axis=1)
+            middle = 3 * units // 2
 
             def join(came):
-                full = jnp.zeros((2, part, columns), bf16)
+                full = jnp.zeros((2, part, n * middle), bf16)
                 for k in range(n):
-                    for t in range(3):
-                        full = lax.dynamic_update_slice_in_dim(
-                            full,
-                            came[k][:, :, t * units : (t + 1) * units],
-                            t * n * units + rank_of(k) * units,
-                            2,
-                        )
-                middle = columns // 2
-                return [(full[0, :, :middle], full[1, :, :middle])] + [
-                    (full[0, :, middle:], full[1, :, middle:])
-                ]
-
-            return [pick(both, me ^ k, 0) for k in range(n)], join
+                    full = lax.dynamic_update_slice_in_dim(full, came[k], rank_of(k) * middle, 2)
+                return full[0], full[1]
+
+            halves = [both[..., :middle], both[..., middle:]]
+            return [[pick(half, me ^ k, 0) for k in range(n)] for half in halves], join
 
         return ring(take, swap, wide_pieces)
 
@@ -630,9 +667,7 @@
         one, two = rows_cut(grad_qkv), rows_cut(grad_out)
 
         def take(h, index):
-            return jnp.concatenate(
-                [pick(one[:, :, h], index, 1), pick(two[:, :, h], index, 1)], axis=-1
-            )
+            return jnp.concatenate([piece_of(x, index, h) for x in (one, two)], axis=-1)
 
         def swap(one, two):
             both = jnp.stack([one, two], axis=1)
@@ -646,9 +681,9 @@
                     + [own],
                     axis=2,
                 )
-                return [(full[0], full[1])]
-
-            return [pick(both, me ^ k, 0)[:, :, : 3 * width] for k in range(n)], join
+                return full[0], full[1]
+
+            return [[pick(both, me ^ k, 0)[:, :, : 3 * width] for k in range(n)]], join
 
         return ring(take, swap, narrow_pieces)
 
@@ -680,17 +715,35 @@
     attended, out_mine, out_other, gate_up_mine = hold(
         (attended, out_weight, out_other, gate_up_mine)
     )
-    gate_up = in_order(gate_up_mine, gate_up_given)
     if fast:
         attended_far, attended_mate = across(attended), mate(attended)
-        attended_far, gate_up = hold((attended_far, gate_up))
+        anywhere = pl.BlockSpec(memory_space=pl.ANY)
+        shapes = [(tokens, model), (model, 2 * units), (n * width, model)]
+        dy, gate_up, out_relative = pl.pallas_call(
+            functools.partial(collect_kernel, n, n_w),
+            out_shape=[jax.ShapeDtypeStruct(shape, bf16) for shape in shapes],
+            in_specs=[pl.BlockSpec(memory_space=pltpu.SMEM)] + [anywhere] * (n + 4),
+            out_specs=[anywhere] * 3,
+            scratch_shapes=[pltpu.SemaphoreType.DMA((2 * n + 2,))],
+            compiler_params=params,
+            cost_estimate=pl.CostEstimate(
+                flops=0,
+                bytes_accessed=4 * sum(a * b for a, b in shapes),
+                transcendentals=0,
+            ),
+            name="collect",
+        )(me_1, *dy_blocks, gate_up_mine, gate_up_given, out_mine, out_other)
+        attended_far, dy, gate_up, out_relative = hold((attended_far, dy, gate_up, out_relative))
         attended_blocks = [attended, attended_mate, attended_far, mate(attended_far)]
     else:
+        dy = jnp.concatenate(dy_blocks)
+        gate_up = in_order(gate_up_mine, gate_up_given)
         attended_blocks = gather_blocks(attended)
-    out_full = in_order(out_mine, out_other)
-    out_full = jnp.pad(out_full, ((0, n * width - out_full.shape[0]), (0, 0)))
-    out_blocks = [lax.dynamic_slice_in_dim(out_full, (me ^ k) * width, width, 0) for k in range(n)]
-    out_relative = jnp.concatenate(out_blocks, axis=0)
+        out_full = in_order(out_mine, out_other)
+        out_full = jnp.pad(out_full, ((0, n * width - out_full.shape[0]), (0, 0)))
+        out_relative = jnp.concatenate(
+            [lax.dynamic_slice_in_dim(out_full, (me ^ k) * width, width, 0) for k in range(n)]
+        )
     by_rows = [
         jnp.concatenate(
             [attended_blocks[k][(m ^ k) * rows : ((m ^ k) + 1) * rows] for m in range(n)]
@@ -729,7 +782,7 @@
     d_normed_ff, residual = tick((d_normed_ff, residual), wide)
     norm_ff_back = jax.vjp(rms_norm, residual, gain_feedforward)[1]
     d_residual_norm, grad_gain_ff = norm_ff_back(d_normed_ff)
-    d_residual = dy[:rows].astype(f32) + d_residual_norm
+    d_residual = out_grad.astype(f32) + d_residual_norm
     branch = d_residual.astype(bf16)
 
     if fast:
@@ -739,7 +792,7 @@
         d_attended, branch = hold((jnp.concatenate(d_rows), branch))
     else:
         branch_blocks = gather_blocks(branch)
-        d_attended = backward_product(jnp.concatenate(branch_blocks), out_blocks[0]).astype(bf16)
+        d_attended = backward_product(jnp.concatenate(branch_blocks), out_relative[:width]).astype(bf16)
     d_attended, branch = tick((d_attended, branch), wide)
     if fast:
         branch_blocks = gather_blocks(branch)
@@ -780,6 +833,9 @@
     grad_out = sum(
         weight_product(branch_blocks[k], attended[k * rows : (k + 1) * rows]) for k in range(n)
     ).astype(bf16)
+    grad_qkv, grad_out = [
+        with_layout_constraint(grad, Layout(major_to_minor=(0, 1))) for grad in (grad_qkv, grad_out)
+    ]
     grad_qkv, grad_out, d_qkv = tick((grad_qkv, grad_out, d_qkv), wide)
     back = backward_product(d_qkv, qkv_weight).astype(bf16)
     narrow = Stream(small_ring(grad_qkv, grad_out)) if fast else None

time: 477 us -> 835 us (1.75)
  Pallas kernels: 72.9 us -> 424 us
  waiting for transfers between devices: 130 us -> 158 us
  local copies, waits for them, and re-layouts: 47.1 us -> 27.9 us
  other arithmetic: 54.8 us -> 40.4 us
  matrix products: 66.4 us -> 80.1 us
    pallas_call x0 -> x1, Pallas kernels: none -> 359 us  [per_device(): pl.pallas_call(functools.partial(collect_kernel, n, n_w), out_shape=[jax....]
    ppermute x10 -> x11, waiting for transfers between devices: 27.3 us -> 44.6 us  [across(): return lax.ppermute(block, 'ctx', flip_w)]
    dot_general x14, matrix products: 66.4 us -> 80.1 us  [dot(): lax.dot_general(left_side, right_side, (dims, ((), ())), precision=precis...]
    ppermute x35, waiting for transfers between devices: 65.9 us -> 75.8 us  [forward(): return lax.ppermute(block, 'group', ahead)]
    ppermute x35, starting transfers between devices: 35.2 us -> 43.6 us  [backward(): return lax.ppermute(block, 'group', behind)]
  transfers between devices with their start and end apart: 108 -> 111, of which waited for: 36 -> 43; matrix products, arithmetic and copies ran while one was open for 21% -> 9% of each run, Pallas kernels for 12% -> 49%
where the time goes in v4:
time: 835 us; the launch traced here: 831 us
  Pallas kernels  424 us (51%)
  waiting for transfers between devices  158 us (19%)
  starting transfers between devices  98.5 us (12%)
  matrix products  80.1 us (10%)
  other arithmetic  40.4 us (5%)
  local copies, waits for them, and re-layouts  27.9 us (3%)
    pallas_call x1, Pallas kernels, per_device(): pl.pallas_call(functools.partial(collect_kernel, n, n_w), out_shape=[jax....  359 us
    dot_general x14, matrix products, dot(): lax.dot_general(left_side, right_side, (dims, ((), ())), precision=precis...  80.1 us
    ppermute x35, waiting for transfers between devices, forward(): return lax.ppermute(block, 'group', ahead)  75.8 us
    ppermute x11, waiting for transfers between devices, across(): return lax.ppermute(block, 'ctx', flip_w)  44.6 us
    ppermute x35, starting transfers between devices, backward(): return lax.ppermute(block, 'group', behind)  43.6 us
    ppermute x35, starting transfers between devices, forward(): return lax.ppermute(block, 'group', ahead)  32.9 us
    pallas_call x1, Pallas kernels, per_device(): pl.pallas_call(functools.partial(attend_back_kernel, rows, n, heads_here,...  17.7 us
    ppermute x35, waiting for transfers between devices, backward(): return lax.ppermute(block, 'group', behind)  17.5 us
  transfers between devices with their start and end apart: 111, of which 43 were waited for; matrix products, arithmetic and copies ran while one was open for 9% of the time, Pallas kernels for 49%

profile of v4, /device:TPU:0, one launch (start us, length us, event | category | flops | bytes accessed | tf_op | source)
XLA Modules:
  0.0 831.4 jit_solution(16787116675241149461)
XLA Ops:
  9.0 3.9 pad_dynamic-slice_fusion.3
  16.9 5.0 own_heads.1.weight_ref
  31.1 12.2 %collective-permute-done.10.refs_2_ = bf16[256,1536]{1,0:T(8,128)(2,1)} collective-permute-done((bf16[256,1536]{1,0:T(8,128)(2,1)S(1)}, bf16[256,1536]{1,0:T(8,128)(2,1)}, u32[]{:S(2)}, u32[]{:S(2)}) %collective-permute-start.10) | collective-permute-done | bytes 786464 | tf_op jit(solution)/shard_map/ppermute | solution.py:431
  43.3 10.5 %arrange_project.1 = (bf16[1024,1536]{1,0:T(8,128)(2,1)}, bf16[1024,1536]{1,0:T(8,128)(2,1)}, bf16[1024,576]{1,0:T(8,128)(2,1)}) custom-call(s32[1]{0:T(128)} %bitcast.me_ref, s32[4,256]{1,0:T(4,128)} %reshape.145.order_ref, f32[1,1536]{1,0:T(1,128)} %reshape.146.gain_ref, bf16[1536,576]{1,0:T(8,128)(2,1)} %own_heads.1.weight_ref, ...), custom_call_target="tpu_custom_call" | custom-call | flops 5033164800 | bytes 12582912 | tf_op jit(solution)/shard_map/arrange_project/pallas_call | solution.py:509
  53.8 13.3 %attend.1 = (bf16[1024,192]{1,0:T(8,128)(2,1)}, f32[1024,192]{1,0:T(8,128)}, f32[3,1024]{1,0:T(4,128)}) custom-call(s32[1]{0:T(128)} %bitcast.me_ref, s32[4]{0:T(128)} %bitcast.337, bf16[1024,576]{1,0:T(8,128)(2,1)} %get-tuple-element.304.qkv_ref, f32[3,5,256,256]{3,2,1,0:T(8,128)} %bias_strips.1.bias_ref), custom_call_target="tpu_custom_call" | custom-call | flops 3221225472 | bytes 3145728 | tf_op jit(solution)/shard_map/attend/pallas_call | solution.py:536
  71.0 358.5 %collect.1 = (bf16[1024,1536]{1,0:T(8,128)(2,1)}, bf16[1536,2048]{1,0:T(8,128)(2,1)}, bf16[768,1536]{1,0:T(8,128)(2,1)}) custom-call(s32[1]{0:T(128)} %bitcast.me_ref, bf16[256,1536]{1,0:T(8,128)(2,1)} %refs_0_.4, bf16[256,1536]{1,0:T(8,128)(2,1)} %copy-done.33, bf16[256,1536]{1,0:T(8,128)(2,1)} %collective-permute-done.10.refs_2_, ...), custom_call_target="tpu_custom_call" | custom-call | bytes 23592960 | tf_op jit(solution)/shard_map/collect/pallas_call | solution.py:722
  431.7 16.8 %multiply_reduce_fusion = (f32[1024]{0:T(1024)S(1)}, f32[1024,1536]{1,0:T(8,128)S(1)}) fusion(bf16[768,1536]{1,0:T(8,128)(2,1)S(1)} %copy-done.105, bf16[256,192]{1,0:T(8,128)(2,1)S(1)} %get-tuple-element.706, bf16[256,192]{1,0:T(8,128)(2,1)S(1)} %get-tuple-element.707, bf16[256,192]{1,0:T(8,128)(2,1)S(1)} %get-tuple-element.708, ...), kind=kOutput, calls=%fused_computation.5 | convolution fusion | flops 2439511040 | bytes 13373440 | tf_op jit(solution)/shard_map/dot_general | solution.py:39
  448.5 11.7 %fusion.85 = f32[1024,2048]{0,1:T(8,128)} fusion(bf16[1536,2048]{1,0:T(8,128)(2,1)} %get-tuple-element.320, f32[1024,1536]{1,0:T(8,128)S(1)} %get-tuple-element.743, f32[1536]{0:T(1024)S(1)} %copy-done.93, f32[1024]{0:T(1024)S(1)} %add_rsqrt_fusion), kind=kOutput, calls=%fused_computation.297 | convolution fusion | flops 6447169536 | bytes 20981760 | tf_op jit(solution)/shard_map/dot_general | solution.py:39
  460.2 11.6 %fusion.6 = (bf16[1024,1024]{0,1:T(8,128)(2,1)S(1)}, bf16[1024,1024]{0,1:T(8,128)(2,1)S(1)}, bf16[1024,1024]{0,1:T(8,128)(2,1)}) fusion(f32[1024,2048]{0,1:T(8,128)} %fusion.85, bf16[1024,1536]{1,0:T(8,128)(2,1)} %get-tuple-element.319, s32[]{:T(128)S(6)} %select_n.228, bf16[1984,1536]{1,0:T(8,128)(2,1)S(1)} %bitcast.334, ...), kind=kOutput, calls=%fused_computation.19 | convolution fusion | flops 3257925632 | bytes 24313860 | tf_op jit(solution)/shard_map/dot_general | solution.py:39
  471.8 8.5 %convolution_convert_fusion = bf16[1536,2048]{1,0:T(8,128)(2,1)S(1)} fusion(f32[1024,1536]{1,0:T(8,128)S(1)} %get-tuple-element.743, f32[1536]{0:T(1024)S(1)} %copy-done.93, f32[1024]{0:T(1024)S(1)} %add_rsqrt_fusion, bf16[1024,1024]{0,1:T(8,128)(2,1)S(1)} %get-tuple-element.607, bf16[1024,1024]{0,1:T(8,128)(2,1)S(1)} %get-tuple-element.606), kind=kOutput, calls=%fused_computation | convolution fusion | flops 6458703872 | bytes 16787456 | tf_op jit(solution)/shard_map/dot_general | solution.py:39
  481.9 6.0 convolution_convert_fusion.4
  493.3 8.9 %convolution_convert_fusion.1 = bf16[1024,1536]{1,0:T(8,128)(2,1)S(1)} fusion(bf16[1024,2048]{0,1:T(8,128)(2,1)S(1)} %pad_maximum_fusion, bf16[1536,2048]{1,0:T(8,128)(2,1)} %get-tuple-element.320), kind=kOutput, calls=%fused_computation.24 | convolution fusion | flops 6444023808 | bytes 13631488 | tf_op jit(solution)/shard_map/dot_general | solution.py:39
  502.2 4.4 collective-permute-done.15
  508.6 5.5 collective-permute-start.17
  514.2 6.3 convolution_convert_fusion.3
  520.8 6.5 collective-permute-done.17
  532.7 16.0 %collective-permute-done.22 = bf16[256,1536]{1,0:T(8,128)(2,1)S(1)} collective-permute-done((bf16[256,1536]{1,0:T(8,128)(2,1)S(1)}, bf16[256,1536]{1,0:T(8,128)(2,1)S(1)}, u32[]{:S(2)}, u32[]{:S(2)}) %collective-permute-start.22) | collective-permute-done | bytes 786464 | tf_op jit(solution)/shard_map/ppermute | solution.py:431
  574.4 17.7 %attend_back.1 = (bf16[1024,576]{1,0:T(8,128)(2,1)}, f32[32,128]{1,0:T(8,128)}) custom-call(s32[1]{0:T(128)} %bitcast.me_ref, s32[4]{0:T(128)} %bitcast.338, bf16[1024,576]{1,0:T(8,128)(2,1)} %get-tuple-element.304.qkv_ref, f32[3,5,256,256]{3,2,1,0:T(8,128)} %bias_strips.1.bias_ref, f32[3,1024]{1,0:T(4,128)} %get-tuple-element.364.lse_ref, ...), custom_call_target="tpu_custom_call" | custom-call | flops 8053063680 | bytes 3145728 | tf_op jit(solution)/shard_map/attend_back/pallas_call | solution.py:799
  608.0 5.1 collective-permute-done.32
  614.7 4.3 collective-permute-start.36
  625.6 5.0 collective-permute-done.36
  663.4 12.9 %collective-permute-done.53 = bf16[256,1536]{1,0:T(8,128)(2,1)S(1)} collective-permute-done((bf16[256,1536]{1,0:T(8,128)(2,1)S(1)}, bf16[256,1536]{1,0:T(8,128)(2,1)S(1)}, u32[]{:S(2)}, u32[]{:S(2)}) %collective-permute-start.53) | collective-permute-done | bytes 786464 | tf_op jit(solution)/shard_map/ppermute | solution.py:431
  700.7 4.5 collective-permute-done.68.refs_8_
  707.2 4.3 collective-permute-done.74.refs_10_
  731.4 7.1 collective-permute-done.78
  742.7 9.0 %collective-permute-done.85.refs_36_ = bf16[24,3072]{1,0:T(8,128)(2,1)S(1)} collective-permute-done((bf16[24,3072]{1,0:T(8,128)(2,1)S(1)}, bf16[24,3072]{1,0:T(8,128)(2,1)S(1)}, u32[]{:S(2)}, u32[]{:S(2)}) %collective-permute-start.85) | collective-permute-done | bytes 147488 | tf_op jit(solution)/shard_map/ppermute | solution.py:571
  755.9 5.4 collective-permute-done.87.refs_38_
  774.6 7.5 collective-permute-done.95.refs_42_
  786.9 8.0 collective-permute-done.103.refs_44_
  799.7 5.1 collective-permute-done.99.refs_26_
  809.5 4.5 fusion.12
  815.5 15.4 %place.1 = (f32[384,3968]{1,0:T(8,128)}, f32[384,3968]{1,0:T(8,128)}, f32[3968,384]{1,0:T(8,128)}, f32[384,768]{1,0:T(8,128)}, f32[384,768]{1,0:T(8,128)}, /*index=5*/f32[384,768]{1,0:T(8,128)}, f32[192,1536]{1,0:T(8,128)}) custom-call(s32[1]{0:T(128)} %bitcast.116.spot_ref, bf16[24,6144]{1,0:T(8,128)(2,1)} %copy-done.24, bf16[24,6144]{1,0:T(8,128)(2,1)} %copy-done.23, ...), custom_call_target="tpu_custom_call" | custom-call | tf_op jit(solution)/shard_map/place/pallas_call | solution.py:880
  (559 shorter events, 207.0 us)
Async XLA Ops:
  0.6 16.3 %collective-permute-start.1 = (bf16[768,768]{1,0:T(8,128)(2,1)}, bf16[768,768]{1,0:T(8,128)(2,1)}, u32[]{:S(2)}, u32[]{:S(2)}) collective-permute-start(bf16[768,768]{1,0:T(8,128)(2,1)} %refs_0_.2), channel_id=1, source_target_pairs={{0,1},{1,0},{2,3},{3,2},{4,5},{5,4},{6,7},{7,6},{8,9},{9,8},{10,11... | collective-permute-start | bytes 3538952 | tf_op jit(solution)/shard_map/ppermute | solution.py:428
  1.7 21.0 %collective-permute-start = (bf16[256,1536]{1,0:T(8,128)(2,1)}, bf16[256,1536]{1,0:T(8,128)(2,1)}, u32[]{:S(2)}, u32[]{:S(2)}) collective-permute-start(bf16[256,1536]{1,0:T(8,128)(2,1)} %refs_0_.3), channel_id=1, source_target_pairs={{0,2},{2,0},{1,3},{3,1},{4,6},{6,4},{5,7},{7,5},{8,10},{10,8},{9,1... | collective-permute-start | bytes 2359304 | tf_op jit(solution)/shard_map/ppermute | solution.py:431
  22.7 47.4 %collective-permute-start.12 = (bf16[768,2048]{1,0:T(8,128)(2,1)}, bf16[768,2048]{1,0:T(8,128)(2,1)}, u32[]{:S(2)}, u32[]{:S(2)}) collective-permute-start(bf16[768,2048]{1,0:T(8,128)(2,1)} %pad_maximum_fusion.2), channel_id=1, source_target_pairs={{0,1},{1,0},{2,3},{3,2},{4,5},{5,4},{6,7},{7,6},{8,9},{9,8},{10,11... | collective-permute-start | bytes 9437192 | tf_op jit(solution)/shard_map/ppermute | solution.py:428
  23.3 20.1 %collective-permute-start.10 = (bf16[256,1536]{1,0:T(8,128)(2,1)S(1)}, bf16[256,1536]{1,0:T(8,128)(2,1)}, u32[]{:S(2)}, u32[]{:S(2)}) collective-permute-start(bf16[256,1536]{1,0:T(8,128)(2,1)S(1)} %copy-done.6), channel_id=1, source_target_pairs={{0,2},{2,0},{1,3},{3,1},{4,6},{6,4},{5,7},{7,5},{8,10},{10,8},{9,1... | collective-permute-start | bytes 2359304 | tf_op jit(solution)/shard_map/ppermute | solution.py:431
  25.0 42.1 %collective-permute-start.6 = (bf16[384,1536]{1,0:T(8,128)(2,1)S(1)}, bf16[384,1536]{1,0:T(8,128)(2,1)S(1)}, u32[]{:S(2)}, u32[]{:S(2)}) collective-permute-start(bf16[384,1536]{1,0:T(8,128)(2,1)S(1)} %copy-done.21), channel_id=1, source_target_pairs={{0,1},{1,0},{2,3},{3,2},{4,5},{5,4},{6,7},{7,6},{8,9},{9,8},{10,11... | collective-permute-start | bytes 3538952 | tf_op jit(solution)/shard_map/ppermute | solution.py:428
  29.9 39.1 %collective-permute-start.14 = (bf16[64,1536]{1,0:T(8,128)(2,1)S(1)}, bf16[64,1536]{1,0:T(8,128)(2,1)}, u32[]{:S(2)}, u32[]{:S(2)}) collective-permute-start(bf16[64,1536]{1,0:T(8,128)(2,1)S(1)} %slice.270), channel_id=1, source_target_pairs={{0,1},{1,0},{2,3},{3,2},{4,5},{5,4},{6,7},{7,6},{8,9},{9,8},{10,11... | collective-permute-start | bytes 589832 | tf_op jit(solution)/shard_map/ppermute | solution.py:428
  31.0 39.1 %collective-permute-start.9 = (bf16[256,1536]{1,0:T(8,128)(2,1)S(1)}, bf16[256,1536]{1,0:T(8,128)(2,1)S(1)}, u32[]{:S(2)}, u32[]{:S(2)}) collective-permute-start(bf16[256,1536]{1,0:T(8,128)(2,1)S(1)} %copy-done.6), channel_id=1, source_target_pairs={{0,1},{1,0},{2,3},{3,2},{4,5},{5,4},{6,7},{7,6},{8,9},{9,8},{10,11... | collective-permute-start | bytes 2359304 | tf_op jit(solution)/shard_map/ppermute | solution.py:428
  43.3 26.8 %collective-permute-start.11 = (bf16[256,1536]{1,0:T(8,128)(2,1)}, bf16[256,1536]{1,0:T(8,128)(2,1)}, u32[]{:S(2)}, u32[]{:S(2)}) collective-permute-start(bf16[256,1536]{1,0:T(8,128)(2,1)} %collective-permute-done.10.refs_2_), channel_id=1, source_target_pairs={{0,1},{1,0},{2,3},{3,2},{4,5},{5,4},{6,7},{7,6},{8,9},{9,8},{10,11... | collective-permute-start | bytes 2359304 | tf_op jit(solution)/shard_map/ppermute | solution.py:428
  67.1 362.5 %collective-permute-start.8 = (bf16[1024,192]{1,0:T(8,128)(2,1)}, bf16[1024,192]{1,0:T(8,128)(2,1)S(1)}, u32[]{:S(2)}, u32[]{:S(2)}) collective-permute-start(bf16[1024,192]{1,0:T(8,128)(2,1)} %get-tuple-element.308), channel_id=1, source_target_pairs={{0,2},{2,0},{1,3},{3,1},{4,6},{6,4},{5,7},{7,5},{8,10},{10,8},{9,1... | collective-permute-start | bytes 1179656 | tf_op jit(solution)/shard_map/ppermute | solution.py:431
  68.9 360.7 %collective-permute-start.7 = (bf16[1024,192]{1,0:T(8,128)(2,1)}, bf16[1024,192]{1,0:T(8,128)(2,1)S(1)}, u32[]{:S(2)}, u32[]{:S(2)}) collective-permute-start(bf16[1024,192]{1,0:T(8,128)(2,1)} %get-tuple-element.308), channel_id=1, source_target_pairs={{0,1},{1,0},{2,3},{3,2},{4,5},{5,4},{6,7},{7,6},{8,9},{9,8},{10,11... | collective-permute-start | bytes 1179656 | tf_op jit(solution)/shard_map/ppermute | solution.py:428
  508.6 18.7 %collective-permute-start.17 = (bf16[4,24,3072]{2,1,0:T(8,128)(2,1)S(1)}, bf16[4,24,3072]{2,1,0:T(8,128)(2,1)S(1)}, u32[]{:S(2)}, u32[]{:S(2)}) collective-permute-start(bf16[4,24,3072]{2,1,0:T(8,128)(2,1)S(1)} %maximum_add_fusion), channel_id=1, source_target_pairs={{0,8},{8,16},{16,24},{24,28},{28,20},{20,12},{12,4},{4,0},{1,9},{9... | collective-permute-start | bytes 1769480 | tf_op jit(solution)/shard_map/ppermute | solution.py:571
  529.8 18.8 %collective-permute-start.22 = (bf16[256,1536]{1,0:T(8,128)(2,1)S(1)}, bf16[256,1536]{1,0:T(8,128)(2,1)S(1)}, u32[]{:S(2)}, u32[]{:S(2)}) collective-permute-start(bf16[256,1536]{1,0:T(8,128)(2,1)S(1)} %get-tuple-element.345), channel_id=1, source_target_pairs={{0,2},{2,0},{1,3},{3,1},{4,6},{6,4},{5,7},{7,5},{8,10},{10,8},{9,1... | collective-permute-start | bytes 2359304 | tf_op jit(solution)/shard_map/ppermute | solution.py:431
  530.4 18.5 %collective-permute-start.20 = (bf16[4,24,3072]{2,1,0:T(8,128)(2,1)S(1)}, bf16[4,24,3072]{2,1,0:T(8,128)(2,1)S(1)}, u32[]{:S(2)}, u32[]{:S(2)}) collective-permute-start(bf16[4,24,3072]{2,1,0:T(8,128)(2,1)S(1)} %maximum_add_fusion.2), channel_id=1, source_target_pairs={{0,8},{8,16},{16,24},{24,28},{28,20},{20,12},{12,4},{4,0},{1,9},{9... | collective-permute-start | bytes 1769480 | tf_op jit(solution)/shard_map/ppermute | solution.py:571
  532.1 16.8 %collective-permute-start.21 = (bf16[4,24,3072]{2,1,0:T(8,128)(2,1)S(1)}, bf16[4,24,3072]{2,1,0:T(8,128)(2,1)S(1)}, u32[]{:S(2)}, u32[]{:S(2)}) collective-permute-start(bf16[4,24,3072]{2,1,0:T(8,128)(2,1)S(1)} %maximum_add_fusion.3), channel_id=1, source_target_pairs={{8,0},{16,8},{24,16},{28,24},{20,28},{12,20},{4,12},{0,4},{9,1},{1... | collective-permute-start | bytes 1769480 | tf_op jit(solution)/shard_map/ppermute | solution.py:574
  571.9 21.0 %collective-permute-start.34 = (bf16[256,1536]{1,0:T(8,128)(2,1)S(1)}, bf16[256,1536]{1,0:T(8,128)(2,1)}, u32[]{:S(2)}, u32[]{:S(2)}) collective-permute-start(bf16[256,1536]{1,0:T(8,128)(2,1)S(1)} %copy-done.12), channel_id=1, source_target_pairs={{0,1},{1,0},{2,3},{3,2},{4,5},{5,4},{6,7},{7,6},{8,9},{9,8},{10,11... | collective-permute-start | bytes 2359304 | tf_op jit(solution)/shard_map/ppermute | solution.py:428
  571.9 23.0 %collective-permute-start.30 = (bf16[256,1536]{1,0:T(8,128)(2,1)S(1)}, bf16[256,1536]{1,0:T(8,128)(2,1)}, u32[]{:S(2)}, u32[]{:S(2)}) collective-permute-start(bf16[256,1536]{1,0:T(8,128)(2,1)S(1)} %copy-done.12), channel_id=1, source_target_pairs={{0,2},{2,0},{1,3},{3,1},{4,6},{6,4},{5,7},{7,5},{8,10},{10,8},{9,1... | collective-permute-start | bytes 2359304 | tf_op jit(solution)/shard_map/ppermute | solution.py:431
  572.4 22.5 %collective-permute-start.28 = (bf16[4,24,3072]{2,1,0:T(8,128)(2,1)}, bf16[4,24,3072]{2,1,0:T(8,128)(2,1)}, u32[]{:S(2)}, u32[]{:S(2)}) collective-permute-start(bf16[4,24,3072]{2,1,0:T(8,128)(2,1)} %maximum_add_fusion.6), channel_id=1, source_target_pairs={{0,8},{8,16},{16,24},{24,28},{28,20},{20,12},{12,4},{4,0},{1,9},{9... | collective-permute-start | bytes 1769480 | tf_op jit(solution)/shard_map/ppermute | solution.py:571
  573.9 21.1 %collective-permute-start.29 = (bf16[4,24,3072]{2,1,0:T(8,128)(2,1)}, bf16[4,24,3072]{2,1,0:T(8,128)(2,1)}, u32[]{:S(2)}, u32[]{:S(2)}) collective-permute-start(bf16[4,24,3072]{2,1,0:T(8,128)(2,1)} %maximum_add_fusion.7), channel_id=1, source_target_pairs={{8,0},{16,8},{24,16},{28,24},{20,28},{12,20},{4,12},{0,4},{9,1},{1... | collective-permute-start | bytes 1769480 | tf_op jit(solution)/shard_map/ppermute | solution.py:574
  601.8 37.0 %collective-permute-start.31 = (bf16[2,256,1536]{2,1,0:T(8,128)(2,1)}, bf16[2,256,1536]{2,1,0:T(8,128)(2,1)}, u32[]{:S(2)}, u32[]{:S(2)}) collective-permute-start(bf16[2,256,1536]{2,1,0:T(8,128)(2,1)} %pad_maximum_fusion.4), channel_id=1, source_target_pairs={{0,1},{1,0},{2,3},{3,2},{4,5},{5,4},{6,7},{7,6},{8,9},{9,8},{10,11... | collective-permute-start | bytes 4718600 | tf_op jit(solution)/shard_map/ppermute | solution.py:428
  614.7 15.8 %collective-permute-start.36 = (bf16[4,24,3072]{2,1,0:T(8,128)(2,1)S(1)}, bf16[4,24,3072]{2,1,0:T(8,128)(2,1)S(1)}, u32[]{:S(2)}, u32[]{:S(2)}) collective-permute-start(bf16[4,24,3072]{2,1,0:T(8,128)(2,1)S(1)} %maximum_add_fusion.10), channel_id=1, source_target_pairs={{0,8},{8,16},{16,24},{24,28},{28,20},{20,12},{12,4},{4,0},{1,9},{9... | collective-permute-start | bytes 1769480 | tf_op jit(solution)/shard_map/ppermute | solution.py:571
  654.1 22.2 %collective-permute-start.53 = (bf16[256,1536]{1,0:T(8,128)(2,1)S(1)}, bf16[256,1536]{1,0:T(8,128)(2,1)S(1)}, u32[]{:S(2)}, u32[]{:S(2)}) collective-permute-start(bf16[256,1536]{1,0:T(8,128)(2,1)S(1)} %get-tuple-element.431), channel_id=1, source_target_pairs={{0,2},{2,0},{1,3},{3,1},{4,6},{6,4},{5,7},{7,5},{8,10},{10,8},{9,1... | collective-permute-start | bytes 2359304 | tf_op jit(solution)/shard_map/ppermute | solution.py:431
  659.1 17.4 %collective-permute-start.51 = (bf16[4,24,768]{2,1,0:T(8,128)(2,1)S(1)}, bf16[4,24,768]{2,1,0:T(8,128)(2,1)S(1)}, u32[]{:S(2)}, u32[]{:S(2)}) collective-permute-start(bf16[4,24,768]{2,1,0:T(8,128)(2,1)S(1)} %maximum_add_fusion.16), channel_id=1, source_target_pairs={{0,8},{8,16},{16,24},{24,28},{28,20},{20,12},{12,4},{4,0},{1,9},{9... | collective-permute-start | bytes 442376 | tf_op jit(solution)/shard_map/ppermute | solution.py:571
  659.8 16.7 %collective-permute-start.52 = (bf16[4,24,768]{2,1,0:T(8,128)(2,1)S(1)}, bf16[4,24,768]{2,1,0:T(8,128)(2,1)S(1)}, u32[]{:S(2)}, u32[]{:S(2)}) collective-permute-start(bf16[4,24,768]{2,1,0:T(8,128)(2,1)S(1)} %maximum_add_fusion.17), channel_id=1, source_target_pairs={{8,0},{16,8},{24,16},{28,24},{20,28},{12,20},{4,12},{0,4},{9,1},{1... | collective-permute-start | bytes 442376 | tf_op jit(solution)/shard_map/ppermute | solution.py:574
  661.2 19.0 %collective-permute-start.49 = (bf16[24,6144]{1,0:T(8,128)(2,1)S(1)}, bf16[24,6144]{1,0:T(8,128)(2,1)S(1)}, u32[]{:S(2)}, u32[]{:S(2)}) collective-permute-start(bf16[24,6144]{1,0:T(8,128)(2,1)S(1)} %get-tuple-element.426.refs_0_), channel_id=1, source_target_pairs={{0,8},{8,16},{16,24},{24,28},{28,20},{20,12},{12,4},{4,0},{1,9},{9... | collective-permute-start | bytes 884744 | tf_op jit(solution)/shard_map/ppermute | solution.py:571
  661.9 18.4 %collective-permute-start.50 = (bf16[24,6144]{1,0:T(8,128)(2,1)S(1)}, bf16[24,6144]{1,0:T(8,128)(2,1)S(1)}, u32[]{:S(2)}, u32[]{:S(2)}) collective-permute-start(bf16[24,6144]{1,0:T(8,128)(2,1)S(1)} %get-tuple-element.427.refs_1_), channel_id=1, source_target_pairs={{8,0},{16,8},{24,16},{28,24},{20,28},{12,20},{4,12},{0,4},{9,1},{1... | collective-permute-start | bytes 884744 | tf_op jit(solution)/shard_map/ppermute | solution.py:574
  711.5 17.2 %collective-permute-start.81 = (bf16[24,6144]{1,0:T(8,128)(2,1)}, bf16[24,6144]{1,0:T(8,128)(2,1)}, u32[]{:S(2)}, u32[]{:S(2)}) collective-permute-start(bf16[24,6144]{1,0:T(8,128)(2,1)} %collective-permute-done.68.refs_8_), channel_id=1, source_target_pairs={{0,8},{8,16},{16,24},{24,28},{28,20},{20,12},{12,4},{4,0},{1,9},{9... | collective-permute-start | bytes 884744 | tf_op jit(solution)/shard_map/ppermute | solution.py:571
  721.8 18.9 %collective-permute-start.79 = (bf16[24,6144]{1,0:T(8,128)(2,1)}, bf16[24,6144]{1,0:T(8,128)(2,1)}, u32[]{:S(2)}, u32[]{:S(2)}) collective-permute-start(bf16[24,6144]{1,0:T(8,128)(2,1)} %collective-permute-done.74.refs_10_), channel_id=1, source_target_pairs={{0,8},{8,16},{16,24},{24,28},{28,20},{20,12},{12,4},{4,0},{1,9},{9... | collective-permute-start | bytes 884744 | tf_op jit(solution)/shard_map/ppermute | solution.py:571
  721.8 20.8 %collective-permute-start.80 = (bf16[24,6144]{1,0:T(8,128)(2,1)}, bf16[24,6144]{1,0:T(8,128)(2,1)}, u32[]{:S(2)}, u32[]{:S(2)}) collective-permute-start(bf16[24,6144]{1,0:T(8,128)(2,1)} %collective-permute-done.75.refs_11_), channel_id=1, source_target_pairs={{8,0},{16,8},{24,16},{28,24},{20,28},{12,20},{4,12},{0,4},{9,1},{1... | collective-permute-start | bytes 884744 | tf_op jit(solution)/shard_map/ppermute | solution.py:574
  742.6 21.1 %collective-permute-start.83 = (bf16[24,6144]{1,0:T(8,128)(2,1)}, bf16[24,6144]{1,0:T(8,128)(2,1)S(1)}, u32[]{:S(2)}, u32[]{:S(2)}) collective-permute-start(bf16[24,6144]{1,0:T(8,128)(2,1)} %collective-permute-done.79.refs_14_), channel_id=1, source_target_pairs={{0,8},{8,16},{16,24},{24,28},{28,20},{20,12},{12,4},{4,0},{1,9},{9... | collective-permute-start | bytes 884744 | tf_op jit(solution)/shard_map/ppermute | solution.py:571
  753.8 17.6 %collective-permute-start.97 = (bf16[24,6144]{1,0:T(8,128)(2,1)S(1)}, bf16[24,6144]{1,0:T(8,128)(2,1)S(1)}, u32[]{:S(2)}, u32[]{:S(2)}) collective-permute-start(bf16[24,6144]{1,0:T(8,128)(2,1)S(1)} %collective-permute-done.89.refs_16_), channel_id=1, source_target_pairs={{0,8},{8,16},{16,24},{24,28},{28,20},{20,12},{12,4},{4,0},{1,9},{9... | collective-permute-start | bytes 884744 | tf_op jit(solution)/shard_map/ppermute | solution.py:571
  765.7 41.1 %collective-permute-start.54 = (bf16[256,1536]{1,0:T(8,128)(2,1)}, bf16[256,1536]{1,0:T(8,128)(2,1)S(1)}, u32[]{:S(2)}, u32[]{:S(2)}) collective-permute-start(bf16[256,1536]{1,0:T(8,128)(2,1)} %fusion.41), channel_id=1, source_target_pairs={{0,2},{2,0},{1,3},{3,1},{4,6},{6,4},{5,7},{7,5},{8,10},{10,8},{9,1... | collective-permute-start | bytes 2359304 | tf_op jit(solution)/shard_map/ppermute | solution.py:431
  797.7 16.3 %collective-permute-start.110 = (bf16[24,3072]{1,0:T(8,128)(2,1)S(1)}, bf16[24,3072]{1,0:T(8,128)(2,1)}, u32[]{:S(2)}, u32[]{:S(2)}) collective-permute-start(bf16[24,3072]{1,0:T(8,128)(2,1)S(1)} %collective-permute-done.104.refs_45_), channel_id=1, source_target_pairs={{8,0},{16,8},{24,16},{28,24},{20,28},{12,20},{4,12},{0,4},{9,1},{1... | collective-permute-start | bytes 442376 | tf_op jit(solution)/shard_map/ppermute | solution.py:574
  (193 other events, 2877.9 us)

commit v5 on v4

--- a/solution.py
+++ b/solution.py
@@ -286,37 +286,6 @@
             column = column + jnp.where(bucket_rows == buckets - 1, jnp.sum(sums_ref[h, 4]), 0.0)
             table = jnp.where(lanes == h, column, table)
         table_ref[...] = table
-
-
-def collect_kernel(n, n_w, me_ref, *refs):
-    blocks, (gate_up, out), results, sems = refs[:n], (refs[n : n + 2], refs[n + 2 : n + 4]), refs[-4:-1], refs[-1]
-    me = me_ref[0]
-    mine = lax.rem(me, n_w)
-    rows, half, own = blocks[0].shape[0], gate_up[0].shape[0], out[0].shape[0]
-    width = own * n_w // n
-    copies = [
-        pltpu.make_async_copy(block, results[0].at[k * rows : (k + 1) * rows], sems.at[k])
-        for k, block in enumerate(blocks)
-    ]
-    for k, place in enumerate((mine, n_w - 1 - mine)):
-        at = pl.ds(pl.multiple_of(place * half, half), half)
-        copies.append(pltpu.make_async_copy(gate_up[k], results[1].at[at], sems.at[n + k]))
-    for copy in copies:
-        copy.start()
-    for k in range(n):
-        head = me ^ k
-        source = pl.ds(pl.multiple_of(lax.rem(head, n // n_w) * width, width), width)
-        target = results[2].at[k * width : (k + 1) * width]
-        for which in range(2):
-            copy = pltpu.make_async_copy(out[which].at[source], target, sems.at[n + 2 + k])
-
-            @pl.when((head // (n // n_w) == mine) == (which == 0))
-            def _():
-                copy.start()
-
-        copies.append(copy)
-    for copy in copies:
-        copy.wait()
 
 
 def place_kernel(groups, part, units_all, hidden_units, heads_all, width, spot_ref, *refs):
@@ -504,7 +473,7 @@
     else:
         row_blocks = gather_blocks(inputs)
     gate_up_given = mate(gate_up_sent)
-    dy_blocks = gather_blocks(out_grad)
+    dy = jnp.concatenate(gather_blocks(out_grad))
 
     x_all, normed, qkv = pl.pallas_call(
         functools.partial(arrange_kernel, rows, n),
@@ -715,35 +684,17 @@
     attended, out_mine, out_other, gate_up_mine = hold(
         (attended, out_weight, out_other, gate_up_mine)
     )
+    gate_up = in_order(gate_up_mine, gate_up_given)
     if fast:
         attended_far, attended_mate = across(attended), mate(attended)
-        anywhere = pl.BlockSpec(memory_space=pl.ANY)
-        shapes = [(tokens, model), (model, 2 * units), (n * width, model)]
-        dy, gate_up, out_relative = pl.pallas_call(
-            functools.partial(collect_kernel, n, n_w),
-            out_shape=[jax.ShapeDtypeStruct(shape, bf16) for shape in shapes],
-            in_specs=[pl.BlockSpec(memory_space=pltpu.SMEM)] + [anywhere] * (n + 4),
-            out_specs=[anywhere] * 3,
-            scratch_shapes=[pltpu.SemaphoreType.DMA((2 * n + 2,))],
-            compiler_params=params,
-            cost_estimate=pl.CostEstimate(
-                flops=0,
-                bytes_accessed=4 * sum(a * b for a, b in shapes),
-                transcendentals=0,
-            ),
-            name="collect",
-        )(me_1, *dy_blocks, gate_up_mine, gate_up_given, out_mine, out_other)
-        attended_far, dy, gate_up, out_relative = hold((attended_far, dy, gate_up, out_relative))
+        attended_far, gate_up = hold((attended_far, gate_up))
         attended_blocks = [attended, attended_mate, attended_far, mate(attended_far)]
     else:
-        dy = jnp.concatenate(dy_blocks)
-        gate_up = in_order(gate_up_mine, gate_up_given)
         attended_blocks = gather_blocks(attended)
-        out_full = in_order(out_mine, out_other)
-        out_full = jnp.pad(out_full, ((0, n * width - out_full.shape[0]), (0, 0)))
-        out_relative = jnp.concatenate(
-            [lax.dynamic_slice_in_dim(out_full, (me ^ k) * width, width, 0) for k in range(n)]
-        )
+    out_full = in_order(out_mine, out_other)
+    out_full = jnp.pad(out_full, ((0, n * width - out_full.shape[0]), (0, 0)))
+    out_blocks = [lax.dynamic_slice_in_dim(out_full, (me ^ k) * width, width, 0) for k in range(n)]
+    out_relative = jnp.concatenate(out_blocks, axis=0)
     by_rows = [
         jnp.concatenate(
             [attended_blocks[k][(m ^ k) * rows : ((m ^ k) + 1) * rows] for m in range(n)]
@@ -782,7 +733,7 @@
     d_normed_ff, residual = tick((d_normed_ff, residual), wide)
     norm_ff_back = jax.vjp(rms_norm, residual, gain_feedforward)[1]
     d_residual_norm, grad_gain_ff = norm_ff_back(d_normed_ff)
-    d_residual = out_grad.astype(f32) + d_residual_norm
+    d_residual = dy[:rows].astype(f32) + d_residual_norm
     branch = d_residual.astype(bf16)
 
     if fast:
@@ -792,7 +743,7 @@
         d_attended, branch = hold((jnp.concatenate(d_rows), branch))
     else:
         branch_blocks = gather_blocks(branch)
-        d_attended = backward_product(jnp.concatenate(branch_blocks), out_relative[:width]).astype(bf16)
+        d_attended = backward_product(jnp.concatenate(branch_blocks), out_blocks[0]).astype(bf16)
     d_attended, branch = tick((d_attended, branch), wide)
     if fast:
         branch_blocks = gather_blocks(branch)

time: 835 us -> 467 us (0.56)
  Pallas kernels: 424 us -> 65 us
  waiting for transfers between devices: 158 us -> 133 us
  matrix products: 80.1 us -> 68 us
  starting transfers between devices: 98.5 us -> 108 us
  other arithmetic: 40.4 us -> 49.6 us
  local copies, waits for them, and re-layouts: 27.9 us -> 36.5 us
    pallas_call x1 -> x0, Pallas kernels: 359 us -> none  [per_device(): pl.pallas_call(functools.partial(collect_kernel, n, n_w), out_shape=[jax....]
    ppermute x11, waiting for transfers between devices: 44.6 us -> 32.1 us  [across(): return lax.ppermute(block, 'ctx', flip_w)]
    dot_general x14, matrix products: 80.1 us -> 68 us  [dot(): lax.dot_general(left_side, right_side, (dims, ((), ())), precision=precis...]
    ppermute x35, starting transfers between devices: 32.9 us -> 41.6 us  [forward(): return lax.ppermute(block, 'group', ahead)]
    ppermute x35, waiting for transfers between devices: 75.8 us -> 67.2 us  [forward(): return lax.ppermute(block, 'group', ahead)]
  transfers between devices with their start and end apart: 111 -> 111, of which waited for: 43 -> 40; matrix products, arithmetic and copies ran while one was open for 9% -> 19% of each run, Pallas kernels for 49% -> 11%
where the time goes in v5:
time: 467 us; the launch traced here: 463 us
  waiting for transfers between devices  133 us (28%)
  starting transfers between devices  108 us (23%)
  matrix products  68 us (15%)
  Pallas kernels  65 us (14%)
  other arithmetic  49.6 us (11%)
  local copies, waits for them, and re-layouts  36.5 us (8%)
    dot_general x14, matrix products, dot(): lax.dot_general(left_side, right_side, (dims, ((), ())), precision=precis...  68 us
    ppermute x35, waiting for transfers between devices, forward(): return lax.ppermute(block, 'group', ahead)  67.2 us
    ppermute x35, starting transfers between devices, forward(): return lax.ppermute(block, 'group', ahead)  41.6 us
    ppermute x35, starting transfers between devices, backward(): return lax.ppermute(block, 'group', behind)  41.5 us
    ppermute x11, waiting for transfers between devices, across(): return lax.ppermute(block, 'ctx', flip_w)  32.1 us
    ppermute x35, waiting for transfers between devices, backward(): return lax.ppermute(block, 'group', behind)  17.9 us
    pallas_call x1, Pallas kernels, per_device(): pl.pallas_call(functools.partial(attend_back_kernel, rows, n, heads_here,...  17.7 us
    ppermute x11, starting transfers between devices, across(): return lax.ppermute(block, 'ctx', flip_w)  15.7 us
  transfers between devices with their start and end apart: 111, of which 40 were waited for; matrix products, arithmetic and copies ran while one was open for 19% of the time, Pallas kernels for 11%

profile of v5, /device:TPU:0, one launch (start us, length us, event | category | flops | bytes accessed | tf_op | source)
XLA Modules:
  0.0 463.1 jit_solution(6121661904850323024)
XLA Ops:
  5.4 3.9 pad_dynamic-slice_fusion.3
  16.4 4.9 %own_heads.1.weight_ref = bf16[1536,576]{1,0:T(8,128)(2,1)} custom-call(s32[1]{0:T(128)} %bitcast.me_ref, bf16[768,768]{1,0:T(8,128)(2,1)} %refs_0_.2, bf16[768,768]{1,0:T(8,128)(2,1)} %refs_1_.1, bf16[768,768]{1,0:T(8,128)(2,1)} %refs_2_.1, bf16[768,768]{1,0:T(8,128)(2,1)} %collective-permute-done.1.refs_3_, ...), custom_call_target="tpu_custom_call" | custom-call | tf_op jit(solution)/shard_map/own_heads/pallas_call | solution.py:448
  30.4 10.5 %arrange_project.1 = (bf16[1024,1536]{1,0:T(8,128)(2,1)}, bf16[1024,1536]{1,0:T(8,128)(2,1)}, bf16[1024,576]{1,0:T(8,128)(2,1)}) custom-call(s32[1]{0:T(128)} %bitcast.me_ref, s32[4,256]{1,0:T(4,128)} %reshape.145.order_ref, f32[1,1536]{1,0:T(1,128)} %reshape.146.gain_ref, bf16[1536,576]{1,0:T(8,128)(2,1)} %own_heads.1.weight_ref, ...), custom_call_target="tpu_custom_call" | custom-call | flops 5033164800 | bytes 12582912 | tf_op jit(solution)/shard_map/arrange_project/pallas_call | solution.py:478
  40.8 13.3 %attend.1 = (bf16[1024,192]{1,0:T(8,128)(2,1)}, f32[1024,192]{1,0:T(8,128)}, f32[3,1024]{1,0:T(4,128)}) custom-call(s32[1]{0:T(128)} %bitcast.me_ref, s32[4]{0:T(128)} %bitcast.335, bf16[1024,576]{1,0:T(8,128)(2,1)} %get-tuple-element.299.qkv_ref, f32[3,5,256,256]{3,2,1,0:T(8,128)} %bias_strips.1.bias_ref), custom_call_target="tpu_custom_call" | custom-call | flops 3221225472 | bytes 3145728 | tf_op jit(solution)/shard_map/attend/pallas_call | solution.py:505
  59.5 3.6 fusion.49
  66.2 3.8 pad_maximum_fusion
  72.3 4.9 %multiply_reduce_fusion = (f32[1024]{0:T(1024)S(1)}, f32[1024,1536]{1,0:T(8,128)S(1)}) fusion(bf16[192,1536]{1,0:T(8,128)(2,1)S(1)} %copy-done.31, bf16[192,1536]{1,0:T(8,128)(2,1)S(1)} %get-tuple-element.649, bf16[192,1536]{1,0:T(8,128)(2,1)S(1)} %get-tuple-element.648, bf16[192,1536]{1,0:T(8,128)(2,1)S(1)} %get-tuple-element.647, ...), kind=kOutput, calls=%fused_computation.6 | convolution fusion | flops 2448948224 | bytes 13373440 | tf_op jit(solution)/shard_map/dot_general | solution.py:39
  77.2 9.9 %fusion.90 = f32[1024,2048]{0,1:T(8,128)} fusion(bf16[1536,2048]{1,0:T(8,128)(2,1)S(1)} %bitcast.325, f32[1024,1536]{1,0:T(8,128)S(1)} %get-tuple-element.741, f32[1536]{0:T(1024)S(1)} %copy-done.95, f32[1024]{0:T(1024)S(1)} %add_rsqrt_fusion), kind=kOutput, calls=%fused_computation.320 | convolution fusion | flops 6447169536 | bytes 20981760 | tf_op jit(solution)/shard_map/dot_general | solution.py:39
  87.2 12.3 %fusion.6 = (bf16[1024,1024]{0,1:T(8,128)(2,1)S(1)}, bf16[1024,1024]{0,1:T(8,128)(2,1)S(1)}, bf16[1024,1024]{0,1:T(8,128)(2,1)}) fusion(f32[1024,2048]{0,1:T(8,128)} %fusion.90, bf16[1024,1536]{1,0:T(8,128)(2,1)} %constant_dynamic-update-slice_fusion.6, s32[]{:T(128)S(6)} %select_n.274, bf16[1984,1536]{1,0:T(8,128)(2,1)} %param.27, ...), kind=kOutput, calls=%fused_computation.20 | convolution fusion | flops 3257925632 | bytes 24313860 | tf_op jit(solution)/shard_map/dot_general | solution.py:39
  99.5 11.1 %convolution_convert_fusion = bf16[1536,2048]{1,0:T(8,128)(2,1)S(1)} fusion(f32[1024,1536]{1,0:T(8,128)} %copy-done.50, f32[1536]{0:T(1024)S(1)} %copy-done.95, f32[1024]{0:T(1024)S(1)} %add_rsqrt_fusion, bf16[1024,1024]{0,1:T(8,128)(2,1)S(1)} %get-tuple-element.597, bf16[1024,1024]{0,1:T(8,128)(2,1)S(1)} %get-tuple-element.596), kind=kOutput, calls=%fused_computation | convolution fusion | flops 6458703872 | bytes 16787456 | tf_op jit(solution)/shard_map/dot_general | solution.py:39
  112.2 6.0 %convolution_convert_fusion.4 = bf16[1536,1024]{1,0:T(8,128)(2,1)S(1)} fusion(bf16[1024,1536]{1,0:T(8,128)(2,1)} %constant_dynamic-update-slice_fusion.6, bf16[1024,1024]{0,1:T(8,128)(2,1)S(1)} %copy-done.110), kind=kOutput, calls=%fused_computation.28 | convolution fusion | flops 3222798336 | bytes 8388608 | tf_op jit(solution)/shard_map/dot_general | solution.py:39
  121.4 5.9 %collective-permute-start.15 = (bf16[4,24,3072]{2,1,0:T(8,128)(2,1)S(1)}, bf16[4,24,3072]{2,1,0:T(8,128)(2,1)S(1)}, u32[]{:S(2)}, u32[]{:S(2)}) collective-permute-start(bf16[4,24,3072]{2,1,0:T(8,128)(2,1)S(1)} %pad_maximum_fusion.8), channel_id=1, source_target_pairs={{0,8},{8,16},{16,24},{24,28},{28,20},{20,12},{12,4},{4,0},{1,9},{9... | collective-permute-start | bytes 1769480 | tf_op jit(solution)/shard_map/ppermute | solution.py:540
  127.4 7.1 %convolution_convert_fusion.1 = bf16[1024,1536]{1,0:T(8,128)(2,1)S(1)} fusion(bf16[1024,2048]{0,1:T(8,128)(2,1)S(1)} %pad_maximum_fusion.1, bf16[1536,2048]{1,0:T(8,128)(2,1)S(1)} %bitcast.325), kind=kOutput, calls=%fused_computation.25 | convolution fusion | flops 6444023808 | bytes 13631488 | tf_op jit(solution)/shard_map/dot_general | solution.py:39
  134.5 6.7 %collective-permute-done.15 = bf16[4,24,3072]{2,1,0:T(8,128)(2,1)S(1)} collective-permute-done((bf16[4,24,3072]{2,1,0:T(8,128)(2,1)S(1)}, bf16[4,24,3072]{2,1,0:T(8,128)(2,1)S(1)}, u32[]{:S(2)}, u32[]{:S(2)}) %collective-permute-start.15) | collective-permute-done | bytes 589856 | tf_op jit(solution)/shard_map/ppermute | solution.py:540
  145.5 6.3 %convolution_convert_fusion.3 = bf16[1024,1536]{1,0:T(8,128)(2,1)} fusion(bf16[1024,1024]{0,1:T(8,128)(2,1)S(1)} %copy-done.111, s32[]{:T(128)S(6)} %select_n.274, bf16[1984,1536]{1,0:T(8,128)(2,1)S(1)} %bitcast.334, bf16[64,1536]{1,0:T(8,128)(2,1)S(1)} %copy-done.76, bf16[64,1536]{1,0:T(8,128)(2,1)S(1)} %broadcast.121), kind=kOutput, calls=%fused_computation.27 | convolution fusion | flops 3232235520 | bytes 11730948 | tf_op jit(solution)/shard_map/dot_general | solution.py:39
  152.2 6.9 %collective-permute-done.17 = bf16[4,24,3072]{2,1,0:T(8,128)(2,1)S(1)} collective-permute-done((bf16[4,24,3072]{2,1,0:T(8,128)(2,1)S(1)}, bf16[4,24,3072]{2,1,0:T(8,128)(2,1)S(1)}, u32[]{:S(2)}, u32[]{:S(2)}) %collective-permute-start.17) | collective-permute-done | bytes 589856 | tf_op jit(solution)/shard_map/ppermute | solution.py:540
  165.9 13.7 %collective-permute-done.22 = bf16[256,1536]{1,0:T(8,128)(2,1)S(1)} collective-permute-done((bf16[256,1536]{1,0:T(8,128)(2,1)S(1)}, bf16[256,1536]{1,0:T(8,128)(2,1)S(1)}, u32[]{:S(2)}, u32[]{:S(2)}) %collective-permute-start.22) | collective-permute-done | bytes 786464 | tf_op jit(solution)/shard_map/ppermute | solution.py:400
  206.0 17.7 %attend_back.1 = (bf16[1024,576]{1,0:T(8,128)(2,1)}, f32[32,128]{1,0:T(8,128)}) custom-call(s32[1]{0:T(128)} %bitcast.me_ref, s32[4]{0:T(128)} %bitcast.336, bf16[1024,576]{1,0:T(8,128)(2,1)} %get-tuple-element.299.qkv_ref, f32[3,5,256,256]{3,2,1,0:T(8,128)} %bias_strips.1.bias_ref, f32[3,1024]{1,0:T(4,128)} %get-tuple-element.354.lse_ref, ...), custom_call_target="tpu_custom_call" | custom-call | flops 8053063680 | bytes 3145728 | tf_op jit(solution)/shard_map/attend_back/pallas_call | solution.py:750
  229.9 5.8 %collective-permute-start.32 = (bf16[4,24,3072]{2,1,0:T(8,128)(2,1)S(1)}, bf16[4,24,3072]{2,1,0:T(8,128)(2,1)S(1)}, u32[]{:S(2)}, u32[]{:S(2)}) collective-permute-start(bf16[4,24,3072]{2,1,0:T(8,128)(2,1)S(1)} %maximum_add_fusion.8), channel_id=1, source_target_pairs={{0,8},{8,16},{16,24},{24,28},{28,20},{20,12},{12,4},{4,0},{1,9},{9... | collective-permute-start | bytes 1769480 | tf_op jit(solution)/shard_map/ppermute | solution.py:540
  243.5 4.6 collective-permute-done.32
  259.4 5.2 %collective-permute-done.36 = bf16[4,24,3072]{2,1,0:T(8,128)(2,1)S(1)} collective-permute-done((bf16[4,24,3072]{2,1,0:T(8,128)(2,1)S(1)}, bf16[4,24,3072]{2,1,0:T(8,128)(2,1)S(1)}, u32[]{:S(2)}, u32[]{:S(2)}) %collective-permute-start.36) | collective-permute-done | bytes 589856 | tf_op jit(solution)/shard_map/ppermute | solution.py:540
  295.5 12.8 %collective-permute-done.53 = bf16[256,1536]{1,0:T(8,128)(2,1)S(1)} collective-permute-done((bf16[256,1536]{1,0:T(8,128)(2,1)S(1)}, bf16[256,1536]{1,0:T(8,128)(2,1)S(1)}, u32[]{:S(2)}, u32[]{:S(2)}) %collective-permute-start.53) | collective-permute-done | bytes 786464 | tf_op jit(solution)/shard_map/ppermute | solution.py:400
  332.6 4.5 collective-permute-done.68.refs_8_
  363.2 7.1 %collective-permute-done.78 = f32[3456]{0:T(1024)S(1)} collective-permute-done((f32[3456]{0:T(1024)S(1)}, f32[3456]{0:T(1024)S(1)}, u32[]{:S(2)}, u32[]{:S(2)}) %collective-permute-start.78) | collective-permute-done | bytes 13856 | tf_op jit(solution)/shard_map/ppermute | solution.py:668
  376.1 7.4 %collective-permute-done.85.refs_36_ = bf16[24,3072]{1,0:T(8,128)(2,1)S(1)} collective-permute-done((bf16[24,3072]{1,0:T(8,128)(2,1)S(1)}, bf16[24,3072]{1,0:T(8,128)(2,1)S(1)}, u32[]{:S(2)}, u32[]{:S(2)}) %collective-permute-start.85) | collective-permute-done | bytes 147488 | tf_op jit(solution)/shard_map/ppermute | solution.py:540
  387.7 5.4 %collective-permute-done.87.refs_38_ = bf16[24,3072]{1,0:T(8,128)(2,1)S(1)} collective-permute-done((bf16[24,3072]{1,0:T(8,128)(2,1)S(1)}, bf16[24,3072]{1,0:T(8,128)(2,1)S(1)}, u32[]{:S(2)}, u32[]{:S(2)}) %collective-permute-start.87) | collective-permute-done | bytes 147488 | tf_op jit(solution)/shard_map/ppermute | solution.py:540
  405.8 4.2 collective-permute-done.95.refs_42_
  412.5 3.6 collective-permute-start.103
  416.9 6.3 %collective-permute-done.103.refs_44_ = bf16[24,3072]{1,0:T(8,128)(2,1)S(1)} collective-permute-done((bf16[24,3072]{1,0:T(8,128)(2,1)S(1)}, bf16[24,3072]{1,0:T(8,128)(2,1)S(1)}, u32[]{:S(2)}, u32[]{:S(2)}) %collective-permute-start.103) | collective-permute-done | bytes 147488 | tf_op jit(solution)/shard_map/ppermute | solution.py:540
  430.7 4.3 collective-permute-done.99.refs_26_
  440.5 4.5 fusion.12
  447.5 15.3 %place.1 = (f32[384,3968]{1,0:T(8,128)}, f32[384,3968]{1,0:T(8,128)}, f32[3968,384]{1,0:T(8,128)}, f32[384,768]{1,0:T(8,128)}, f32[384,768]{1,0:T(8,128)}, /*index=5*/f32[384,768]{1,0:T(8,128)}, f32[192,1536]{1,0:T(8,128)}) custom-call(s32[1]{0:T(128)} %bitcast.116.spot_ref, bf16[24,6144]{1,0:T(8,128)(2,1)} %copy-done.22, bf16[24,6144]{1,0:T(8,128)(2,1)} %copy-done.21, ...), custom_call_target="tpu_custom_call" | custom-call | tf_op jit(solution)/shard_map/place/pallas_call | solution.py:831
  (570 shorter events, 220.8 us)
Async XLA Ops:
  1.7 21.0 %collective-permute-start = (bf16[256,1536]{1,0:T(8,128)(2,1)}, bf16[256,1536]{1,0:T(8,128)(2,1)}, u32[]{:S(2)}, u32[]{:S(2)}) collective-permute-start(bf16[256,1536]{1,0:T(8,128)(2,1)} %refs_0_.3), channel_id=1, source_target_pairs={{0,2},{2,0},{1,3},{3,1},{4,6},{6,4},{5,7},{7,5},{8,10},{10,8},{9,1... | collective-permute-start | bytes 2359304 | tf_op jit(solution)/shard_map/ppermute | solution.py:400
  4.3 23.8 %collective-permute-start.4 = (bf16[256,1536]{1,0:T(8,128)(2,1)}, bf16[256,1536]{1,0:T(8,128)(2,1)}, u32[]{:S(2)}, u32[]{:S(2)}) collective-permute-start(bf16[256,1536]{1,0:T(8,128)(2,1)} %refs_0_.3), channel_id=1, source_target_pairs={{0,1},{1,0},{2,3},{3,2},{4,5},{5,4},{6,7},{7,6},{8,9},{9,8},{10,11... | collective-permute-start | bytes 2359304 | tf_op jit(solution)/shard_map/ppermute | solution.py:397
  22.7 31.4 %collective-permute-start.6 = (bf16[384,1536]{1,0:T(8,128)(2,1)}, bf16[384,1536]{1,0:T(8,128)(2,1)}, u32[]{:S(2)}, u32[]{:S(2)}) collective-permute-start(bf16[384,1536]{1,0:T(8,128)(2,1)} %param.22), channel_id=1, source_target_pairs={{0,1},{1,0},{2,3},{3,2},{4,5},{5,4},{6,7},{7,6},{8,9},{9,8},{10,11... | collective-permute-start | bytes 3538952 | tf_op jit(solution)/shard_map/ppermute | solution.py:397
  23.3 40.6 %collective-permute-start.9 = (bf16[768,2048]{1,0:T(8,128)(2,1)}, bf16[768,2048]{1,0:T(8,128)(2,1)}, u32[]{:S(2)}, u32[]{:S(2)}) collective-permute-start(bf16[768,2048]{1,0:T(8,128)(2,1)} %pad_maximum_fusion.3), channel_id=1, source_target_pairs={{0,1},{1,0},{2,3},{3,2},{4,5},{5,4},{6,7},{7,6},{8,9},{9,8},{10,11... | collective-permute-start | bytes 9437192 | tf_op jit(solution)/shard_map/ppermute | solution.py:397
  26.3 28.3 %collective-permute-start.12 = (bf16[256,1536]{1,0:T(8,128)(2,1)}, bf16[256,1536]{1,0:T(8,128)(2,1)S(1)}, u32[]{:S(2)}, u32[]{:S(2)}) collective-permute-start(bf16[256,1536]{1,0:T(8,128)(2,1)} %param.15), channel_id=1, source_target_pairs={{0,2},{2,0},{1,3},{3,1},{4,6},{6,4},{5,7},{7,5},{8,10},{10,8},{9,1... | collective-permute-start | bytes 2359304 | tf_op jit(solution)/shard_map/ppermute | solution.py:400
  28.1 27.0 %collective-permute-start.11 = (bf16[256,1536]{1,0:T(8,128)(2,1)}, bf16[256,1536]{1,0:T(8,128)(2,1)}, u32[]{:S(2)}, u32[]{:S(2)}) collective-permute-start(bf16[256,1536]{1,0:T(8,128)(2,1)} %param.15), channel_id=1, source_target_pairs={{0,1},{1,0},{2,3},{3,2},{4,5},{5,4},{6,7},{7,6},{8,9},{9,8},{10,11... | collective-permute-start | bytes 2359304 | tf_op jit(solution)/shard_map/ppermute | solution.py:397
  54.2 15.8 %collective-permute-start.8 = (bf16[1024,192]{1,0:T(8,128)(2,1)}, bf16[1024,192]{1,0:T(8,128)(2,1)}, u32[]{:S(2)}, u32[]{:S(2)}) collective-permute-start(bf16[1024,192]{1,0:T(8,128)(2,1)} %get-tuple-element.303), channel_id=1, source_target_pairs={{0,2},{2,0},{1,3},{3,1},{4,6},{6,4},{5,7},{7,5},{8,10},{10,8},{9,1... | collective-permute-start | bytes 1179656 | tf_op jit(solution)/shard_map/ppermute | solution.py:400
  121.4 19.7 %collective-permute-start.15 = (bf16[4,24,3072]{2,1,0:T(8,128)(2,1)S(1)}, bf16[4,24,3072]{2,1,0:T(8,128)(2,1)S(1)}, u32[]{:S(2)}, u32[]{:S(2)}) collective-permute-start(bf16[4,24,3072]{2,1,0:T(8,128)(2,1)S(1)} %pad_maximum_fusion.8), channel_id=1, source_target_pairs={{0,8},{8,16},{16,24},{24,28},{28,20},{20,12},{12,4},{4,0},{1,9},{9... | collective-permute-start | bytes 1769480 | tf_op jit(solution)/shard_map/ppermute | solution.py:540
  143.4 15.7 %collective-permute-start.17 = (bf16[4,24,3072]{2,1,0:T(8,128)(2,1)S(1)}, bf16[4,24,3072]{2,1,0:T(8,128)(2,1)S(1)}, u32[]{:S(2)}, u32[]{:S(2)}) collective-permute-start(bf16[4,24,3072]{2,1,0:T(8,128)(2,1)S(1)} %maximum_add_fusion), channel_id=1, source_target_pairs={{0,8},{8,16},{16,24},{24,28},{28,20},{20,12},{12,4},{4,0},{1,9},{9... | collective-permute-start | bytes 1769480 | tf_op jit(solution)/shard_map/ppermute | solution.py:540
  160.7 18.8 %collective-permute-start.22 = (bf16[256,1536]{1,0:T(8,128)(2,1)S(1)}, bf16[256,1536]{1,0:T(8,128)(2,1)S(1)}, u32[]{:S(2)}, u32[]{:S(2)}) collective-permute-start(bf16[256,1536]{1,0:T(8,128)(2,1)S(1)} %get-tuple-element.335), channel_id=1, source_target_pairs={{0,2},{2,0},{1,3},{3,1},{4,6},{6,4},{5,7},{7,5},{8,10},{10,8},{9,1... | collective-permute-start | bytes 2359304 | tf_op jit(solution)/shard_map/ppermute | solution.py:400
  162.3 17.5 %collective-permute-start.20 = (bf16[4,24,3072]{2,1,0:T(8,128)(2,1)S(1)}, bf16[4,24,3072]{2,1,0:T(8,128)(2,1)S(1)}, u32[]{:S(2)}, u32[]{:S(2)}) collective-permute-start(bf16[4,24,3072]{2,1,0:T(8,128)(2,1)S(1)} %maximum_add_fusion.2), channel_id=1, source_target_pairs={{0,8},{8,16},{16,24},{24,28},{28,20},{20,12},{12,4},{4,0},{1,9},{9... | collective-permute-start | bytes 1769480 | tf_op jit(solution)/shard_map/ppermute | solution.py:540
  163.7 16.1 %collective-permute-start.21 = (bf16[4,24,3072]{2,1,0:T(8,128)(2,1)S(1)}, bf16[4,24,3072]{2,1,0:T(8,128)(2,1)S(1)}, u32[]{:S(2)}, u32[]{:S(2)}) collective-permute-start(bf16[4,24,3072]{2,1,0:T(8,128)(2,1)S(1)} %maximum_add_fusion.3), channel_id=1, source_target_pairs={{8,0},{16,8},{24,16},{28,24},{20,28},{12,20},{4,12},{0,4},{9,1},{1... | collective-permute-start | bytes 1769480 | tf_op jit(solution)/shard_map/ppermute | solution.py:543
  183.0 15.5 %collective-permute-start.23 = (bf16[4,24,3072]{2,1,0:T(8,128)(2,1)}, bf16[4,24,3072]{2,1,0:T(8,128)(2,1)}, u32[]{:S(2)}, u32[]{:S(2)}) collective-permute-start(bf16[4,24,3072]{2,1,0:T(8,128)(2,1)} %maximum_add_fusion.4), channel_id=1, source_target_pairs={{0,8},{8,16},{16,24},{24,28},{28,20},{20,12},{12,4},{4,0},{1,9},{9... | collective-permute-start | bytes 1769480 | tf_op jit(solution)/shard_map/ppermute | solution.py:540
  202.8 21.7 %collective-permute-start.34 = (bf16[256,1536]{1,0:T(8,128)(2,1)S(1)}, bf16[256,1536]{1,0:T(8,128)(2,1)}, u32[]{:S(2)}, u32[]{:S(2)}) collective-permute-start(bf16[256,1536]{1,0:T(8,128)(2,1)S(1)} %copy-done.11), channel_id=1, source_target_pairs={{0,1},{1,0},{2,3},{3,2},{4,5},{5,4},{6,7},{7,6},{8,9},{9,8},{10,11... | collective-permute-start | bytes 2359304 | tf_op jit(solution)/shard_map/ppermute | solution.py:397
  202.8 23.8 %collective-permute-start.30 = (bf16[256,1536]{1,0:T(8,128)(2,1)S(1)}, bf16[256,1536]{1,0:T(8,128)(2,1)}, u32[]{:S(2)}, u32[]{:S(2)}) collective-permute-start(bf16[256,1536]{1,0:T(8,128)(2,1)S(1)} %copy-done.11), channel_id=1, source_target_pairs={{0,2},{2,0},{1,3},{3,1},{4,6},{6,4},{5,7},{7,5},{8,10},{10,8},{9,1... | collective-permute-start | bytes 2359304 | tf_op jit(solution)/shard_map/ppermute | solution.py:400
  204.0 22.5 %collective-permute-start.28 = (bf16[4,24,3072]{2,1,0:T(8,128)(2,1)}, bf16[4,24,3072]{2,1,0:T(8,128)(2,1)}, u32[]{:S(2)}, u32[]{:S(2)}) collective-permute-start(bf16[4,24,3072]{2,1,0:T(8,128)(2,1)} %maximum_add_fusion.6), channel_id=1, source_target_pairs={{0,8},{8,16},{16,24},{24,28},{28,20},{20,12},{12,4},{4,0},{1,9},{9... | collective-permute-start | bytes 1769480 | tf_op jit(solution)/shard_map/ppermute | solution.py:540
  205.8 20.8 %collective-permute-start.29 = (bf16[4,24,3072]{2,1,0:T(8,128)(2,1)}, bf16[4,24,3072]{2,1,0:T(8,128)(2,1)}, u32[]{:S(2)}, u32[]{:S(2)}) collective-permute-start(bf16[4,24,3072]{2,1,0:T(8,128)(2,1)} %maximum_add_fusion.7), channel_id=1, source_target_pairs={{8,0},{16,8},{24,16},{28,24},{20,28},{12,20},{4,12},{0,4},{9,1},{1... | collective-permute-start | bytes 1769480 | tf_op jit(solution)/shard_map/ppermute | solution.py:543
  229.9 18.2 %collective-permute-start.32 = (bf16[4,24,3072]{2,1,0:T(8,128)(2,1)S(1)}, bf16[4,24,3072]{2,1,0:T(8,128)(2,1)S(1)}, u32[]{:S(2)}, u32[]{:S(2)}) collective-permute-start(bf16[4,24,3072]{2,1,0:T(8,128)(2,1)S(1)} %maximum_add_fusion.8), channel_id=1, source_target_pairs={{0,8},{8,16},{16,24},{24,28},{28,20},{20,12},{12,4},{4,0},{1,9},{9... | collective-permute-start | bytes 1769480 | tf_op jit(solution)/shard_map/ppermute | solution.py:540
  237.4 34.4 %collective-permute-start.31 = (bf16[2,256,1536]{2,1,0:T(8,128)(2,1)}, bf16[2,256,1536]{2,1,0:T(8,128)(2,1)}, u32[]{:S(2)}, u32[]{:S(2)}) collective-permute-start(bf16[2,256,1536]{2,1,0:T(8,128)(2,1)} %pad_maximum_fusion.6), channel_id=1, source_target_pairs={{0,1},{1,0},{2,3},{3,2},{4,5},{5,4},{6,7},{7,6},{8,9},{9,8},{10,11... | collective-permute-start | bytes 4718600 | tf_op jit(solution)/shard_map/ppermute | solution.py:397
  286.0 22.2 %collective-permute-start.53 = (bf16[256,1536]{1,0:T(8,128)(2,1)S(1)}, bf16[256,1536]{1,0:T(8,128)(2,1)S(1)}, u32[]{:S(2)}, u32[]{:S(2)}) collective-permute-start(bf16[256,1536]{1,0:T(8,128)(2,1)S(1)} %get-tuple-element.421), channel_id=1, source_target_pairs={{0,2},{2,0},{1,3},{3,1},{4,6},{6,4},{5,7},{7,5},{8,10},{10,8},{9,1... | collective-permute-start | bytes 2359304 | tf_op jit(solution)/shard_map/ppermute | solution.py:400
  291.2 17.3 %collective-permute-start.51 = (bf16[4,24,768]{2,1,0:T(8,128)(2,1)S(1)}, bf16[4,24,768]{2,1,0:T(8,128)(2,1)S(1)}, u32[]{:S(2)}, u32[]{:S(2)}) collective-permute-start(bf16[4,24,768]{2,1,0:T(8,128)(2,1)S(1)} %maximum_add_fusion.16), channel_id=1, source_target_pairs={{0,8},{8,16},{16,24},{24,28},{28,20},{20,12},{12,4},{4,0},{1,9},{9... | collective-permute-start | bytes 442376 | tf_op jit(solution)/shard_map/ppermute | solution.py:540
  291.7 16.8 %collective-permute-start.52 = (bf16[4,24,768]{2,1,0:T(8,128)(2,1)S(1)}, bf16[4,24,768]{2,1,0:T(8,128)(2,1)S(1)}, u32[]{:S(2)}, u32[]{:S(2)}) collective-permute-start(bf16[4,24,768]{2,1,0:T(8,128)(2,1)S(1)} %maximum_add_fusion.17), channel_id=1, source_target_pairs={{8,0},{16,8},{24,16},{28,24},{20,28},{12,20},{4,12},{0,4},{9,1},{1... | collective-permute-start | bytes 442376 | tf_op jit(solution)/shard_map/ppermute | solution.py:543
  293.3 18.9 %collective-permute-start.49 = (bf16[24,6144]{1,0:T(8,128)(2,1)S(1)}, bf16[24,6144]{1,0:T(8,128)(2,1)S(1)}, u32[]{:S(2)}, u32[]{:S(2)}) collective-permute-start(bf16[24,6144]{1,0:T(8,128)(2,1)S(1)} %get-tuple-element.416.refs_0_), channel_id=1, source_target_pairs={{0,8},{8,16},{16,24},{24,28},{28,20},{20,12},{12,4},{4,0},{1,9},{9... | collective-permute-start | bytes 884744 | tf_op jit(solution)/shard_map/ppermute | solution.py:540
  293.7 18.5 %collective-permute-start.50 = (bf16[24,6144]{1,0:T(8,128)(2,1)S(1)}, bf16[24,6144]{1,0:T(8,128)(2,1)S(1)}, u32[]{:S(2)}, u32[]{:S(2)}) collective-permute-start(bf16[24,6144]{1,0:T(8,128)(2,1)S(1)} %get-tuple-element.417.refs_1_), channel_id=1, source_target_pairs={{8,0},{16,8},{24,16},{28,24},{20,28},{12,20},{4,12},{0,4},{9,1},{1... | collective-permute-start | bytes 884744 | tf_op jit(solution)/shard_map/ppermute | solution.py:543
  343.4 17.3 %collective-permute-start.81 = (bf16[24,6144]{1,0:T(8,128)(2,1)}, bf16[24,6144]{1,0:T(8,128)(2,1)}, u32[]{:S(2)}, u32[]{:S(2)}) collective-permute-start(bf16[24,6144]{1,0:T(8,128)(2,1)} %collective-permute-done.68.refs_8_), channel_id=1, source_target_pairs={{0,8},{8,16},{16,24},{24,28},{28,20},{20,12},{12,4},{4,0},{1,9},{9... | collective-permute-start | bytes 884744 | tf_op jit(solution)/shard_map/ppermute | solution.py:540
  353.7 20.3 %collective-permute-start.79 = (bf16[24,6144]{1,0:T(8,128)(2,1)}, bf16[24,6144]{1,0:T(8,128)(2,1)}, u32[]{:S(2)}, u32[]{:S(2)}) collective-permute-start(bf16[24,6144]{1,0:T(8,128)(2,1)} %collective-permute-done.74.refs_10_), channel_id=1, source_target_pairs={{0,8},{8,16},{16,24},{24,28},{28,20},{20,12},{12,4},{4,0},{1,9},{9... | collective-permute-start | bytes 884744 | tf_op jit(solution)/shard_map/ppermute | solution.py:540
  353.8 20.7 %collective-permute-start.80 = (bf16[24,6144]{1,0:T(8,128)(2,1)}, bf16[24,6144]{1,0:T(8,128)(2,1)}, u32[]{:S(2)}, u32[]{:S(2)}) collective-permute-start(bf16[24,6144]{1,0:T(8,128)(2,1)} %collective-permute-done.75.refs_11_), channel_id=1, source_target_pairs={{8,0},{16,8},{24,16},{28,24},{20,28},{12,20},{4,12},{0,4},{9,1},{1... | collective-permute-start | bytes 884744 | tf_op jit(solution)/shard_map/ppermute | solution.py:543
  374.4 20.6 %collective-permute-start.83 = (bf16[24,6144]{1,0:T(8,128)(2,1)}, bf16[24,6144]{1,0:T(8,128)(2,1)S(1)}, u32[]{:S(2)}, u32[]{:S(2)}) collective-permute-start(bf16[24,6144]{1,0:T(8,128)(2,1)} %collective-permute-done.79.refs_14_), channel_id=1, source_target_pairs={{0,8},{8,16},{16,24},{24,28},{28,20},{20,12},{12,4},{4,0},{1,9},{9... | collective-permute-start | bytes 884744 | tf_op jit(solution)/shard_map/ppermute | solution.py:540
  387.4 15.8 %collective-permute-start.97 = (bf16[24,6144]{1,0:T(8,128)(2,1)S(1)}, bf16[24,6144]{1,0:T(8,128)(2,1)S(1)}, u32[]{:S(2)}, u32[]{:S(2)}) collective-permute-start(bf16[24,6144]{1,0:T(8,128)(2,1)S(1)} %collective-permute-done.89.refs_16_), channel_id=1, source_target_pairs={{0,8},{8,16},{16,24},{24,28},{28,20},{20,12},{12,4},{4,0},{1,9},{9... | collective-permute-start | bytes 884744 | tf_op jit(solution)/shard_map/ppermute | solution.py:540
  396.9 40.8 %collective-permute-start.54 = (bf16[256,1536]{1,0:T(8,128)(2,1)}, bf16[256,1536]{1,0:T(8,128)(2,1)S(1)}, u32[]{:S(2)}, u32[]{:S(2)}) collective-permute-start(bf16[256,1536]{1,0:T(8,128)(2,1)} %fusion.41), channel_id=1, source_target_pairs={{0,2},{2,0},{1,3},{3,1},{4,6},{6,4},{5,7},{7,5},{8,10},{10,8},{9,1... | collective-permute-start | bytes 2359304 | tf_op jit(solution)/shard_map/ppermute | solution.py:400
  399.9 16.2 %collective-permute-start.91 = (bf16[24,6144]{1,0:T(8,128)(2,1)S(1)}, bf16[24,6144]{1,0:T(8,128)(2,1)S(1)}, u32[]{:S(2)}, u32[]{:S(2)}) collective-permute-start(bf16[24,6144]{1,0:T(8,128)(2,1)S(1)} %collective-permute-done.83.refs_18_), channel_id=1, source_target_pairs={{0,8},{8,16},{16,24},{24,28},{28,20},{20,12},{12,4},{4,0},{1,9},{9... | collective-permute-start | bytes 884744 | tf_op jit(solution)/shard_map/ppermute | solution.py:540
  410.0 17.1 %collective-permute-start.101 = (bf16[24,6144]{1,0:T(8,128)(2,1)S(1)}, bf16[24,6144]{1,0:T(8,128)(2,1)}, u32[]{:S(2)}, u32[]{:S(2)}) collective-permute-start(bf16[24,6144]{1,0:T(8,128)(2,1)S(1)} %collective-permute-done.97.refs_20_), channel_id=1, source_target_pairs={{0,8},{8,16},{16,24},{24,28},{28,20},{20,12},{12,4},{4,0},{1,9},{9... | collective-permute-start | bytes 884744 | tf_op jit(solution)/shard_map/ppermute | solution.py:540
  (195 other events, 2484.4 us)

commit v6 on v5

--- a/solution.py
+++ b/solution.py
@@ -288,19 +288,15 @@
         table_ref[...] = table
 
 
-def place_kernel(groups, part, units_all, hidden_units, heads_all, width, spot_ref, *refs):
+def place_kernel(groups, part, count, units_all, hidden_units, spot_ref, *refs):
     spot = spot_ref[0]
     wide, refs = refs[: 4 * groups], refs[4 * groups :]
-    narrow, refs = refs[: 2 * groups], refs[2 * groups :]
-    outs, scratch, sems = refs[:7], refs[7:-1], refs[-1]
-    gate, up, down, turned, query, key, value, out_rows, out_turned = scratch
-    count = heads_all // width
+    outs, (gate, up, down, turned), sems = refs[:3], refs[3:-1], refs[-1]
     units = units_all // count
     middle = 3 * units // 2
 
     def row_of(j, h):
-        index = lax.rem(spot + groups - j, groups) if h == 0 else lax.rem(spot + j, groups)
-        return pl.multiple_of((2 * index + h) * part, 8)
+        return piece_row(spot, groups, part, j, h)
 
     def copy(k, source):
         return pltpu.make_async_copy(source, outs[k], sems.at[k])
@@ -329,25 +325,32 @@
     for first in range(0, hidden_units, 128):
         turned[first : first + 128, :] = down[:, first : first + 128].T
     copy(2, turned).start()
-    for k, target in enumerate((query, key, value)):
-        for j in range(groups):
-            for h in range(2):
-                target[pl.ds(row_of(j, h), part), :] = (
+    for k, source in enumerate((gate, up, turned)):
+        copy(k, source).wait()
+
+
+def piece_row(spot, groups, part, j, h):
+    index = lax.rem(spot + groups - j, groups) if h == 0 else lax.rem(spot + j, groups)
+    return pl.multiple_of((2 * index + h) * part, 8)
+
+
+def place_heads_kernel(groups, part, count, width, spot_ref, *refs):
+    spot = spot_ref[0]
+    narrow, outs, out_rows = refs[: 2 * groups], refs[2 * groups : -1], refs[-1]
+    heads_all = count * width
+    for j in range(groups):
+        for h in range(2):
+            rows = pl.ds(piece_row(spot, groups, part, j, h), part)
+            for k in range(3):
+                outs[k][rows, :] = (
                     narrow[j * 2 + h][:, k * heads_all : (k + 1) * heads_all].astype(f32)
                 )
-        copy(3 + k, target).start()
+            for q in range(count):
+                first = 3 * heads_all + q * width
+                out_rows[q, rows, :] = narrow[j * 2 + h][:, first : first + width].astype(f32)
+    size = out_rows.shape[1]
     for q in range(count):
-        for j in range(groups):
-            for h in range(2):
-                first = 3 * heads_all + q * width
-                out_rows[q, pl.ds(row_of(j, h), part), :] = (
-                    narrow[j * 2 + h][:, first : first + width].astype(f32)
-                )
-        rows = out_rows.shape[1]
-        out_turned[:, q * rows : (q + 1) * rows] = out_rows[q].T
-    copy(6, out_turned).start()
-    for k, source in enumerate((gate, up, turned, query, key, value, out_turned)):
-        copy(k, source).wait()
+        outs[3][:, q * size : (q + 1) * size] = out_rows[q].T
 
 
 def forward_product_exact(left_side, right_side):
@@ -796,8 +799,8 @@
     near, away = tick((near, away), narrow)
     (away,) = tick((away,), wide)
     d_normed = scatter_far(near, away)
-    tick((), narrow)
-    tick((), wide)
+    for stream in (narrow, wide, narrow, wide, narrow, wide):
+        tick((), stream)
     d_normed, x_own = tick((d_normed, x_all[:rows]), narrow)
     norm_attn_back = jax.vjp(rms_norm, x_own.astype(f32), gain_attention)[1]
     d_input_norm, grad_gain_attn = norm_attn_back(d_normed)
@@ -811,9 +814,24 @@
     small = jnp.concatenate([grad_gain_attn, grad_gain_ff, table_here.reshape(-1)])
     if fast:
         sums = Stream(sum_ring(small))
-        while wide.pending or narrow.pending or sums.pending:
+        own_rows, all_heads = model // n, n * width
+        spot_1 = spot.reshape(1).astype(jnp.int32)
+        in_vmem = pl.BlockSpec(memory_space=pltpu.VMEM)
+        while narrow.pending or sums.pending or len(wide_pieces) < 4 * n_group - 2:
             tick((), narrow, sums)
-            tick((), wide)
+            if len(wide_pieces) < 4 * n_group - 2:
+                tick((), wide)
+        heads_grads = pl.pallas_call(
+            functools.partial(place_heads_kernel, n_group, part, n, width),
+            out_shape=[jax.ShapeDtypeStruct((own_rows, all_heads), f32)] * 3
+            + [jax.ShapeDtypeStruct((width, model), f32)],
+            in_specs=[pl.BlockSpec(memory_space=pltpu.SMEM)] + [in_vmem] * (2 * n_group),
+            out_specs=[in_vmem] * 4,
+            scratch_shapes=[pltpu.VMEM((n, own_rows, width), f32)],
+            compiler_params=params,
+            name="place_heads",
+        )(spot_1, *narrow_pieces)
+        heads_grads = tick(heads_grads, wide)
         small = sums.result
     else:
         small = lax.psum(small, ("group",) + peer_axes)
@@ -822,25 +840,20 @@
     grad_table = small[2 * model :].reshape(buckets, heads)
 
     if fast:
-        own_rows, all_heads = model // n, n * width
+        *total_qkv, total_out = heads_grads
         wide_shape, down_shape = (own_rows, hidden_units), (hidden_units, own_rows)
-        out_shapes = [wide_shape, wide_shape, down_shape]
-        out_shapes += [(own_rows, all_heads)] * 3 + [(width, model)]
-        scratch = [wide_shape, wide_shape, wide_shape, down_shape]
-        scratch += [(own_rows, all_heads)] * 3 + [(n, own_rows, width), (width, model)]
-        total_gate, total_up, total_down, *total_qkv, total_out = pl.pallas_call(
-            functools.partial(
-                place_kernel, n_group, part, n * units, hidden_units, all_heads, width
-            ),
-            out_shape=[jax.ShapeDtypeStruct(shape, f32) for shape in out_shapes],
-            in_specs=[pl.BlockSpec(memory_space=pltpu.SMEM)]
-            + [pl.BlockSpec(memory_space=pltpu.VMEM)] * (6 * n_group),
-            out_specs=[pl.BlockSpec(memory_space=pl.ANY)] * 7,
-            scratch_shapes=[pltpu.VMEM(shape, f32) for shape in scratch]
-            + [pltpu.SemaphoreType.DMA((7,))],
+        total_gate, total_up, total_down = pl.pallas_call(
+            functools.partial(place_kernel, n_group, part, n, n * units, hidden_units),
+            out_shape=[
+                jax.ShapeDtypeStruct(shape, f32) for shape in (wide_shape, wide_shape, down_shape)
+            ],
+            in_specs=[pl.BlockSpec(memory_space=pltpu.SMEM)] + [in_vmem] * (4 * n_group),
+            out_specs=[pl.BlockSpec(memory_space=pl.ANY)] * 3,
+            scratch_shapes=[pltpu.VMEM(wide_shape, f32)] * 3
+            + [pltpu.VMEM(down_shape, f32), pltpu.SemaphoreType.DMA((3,))],
             compiler_params=params,
             name="place",
-        )(spot.reshape(1).astype(jnp.int32), *wide_pieces, *narrow_pieces)
+        )(spot_1, *wide_pieces)
     else:
 
         def place_columns(grad, which, wide, total):

time: 467 us -> 464 us (level)
  Pallas kernels: 65 us -> 74.7 us
  starting transfers between devices: 108 us -> 100 us
  waiting for transfers between devices: 133 us -> 127 us
    ppermute x11, waiting for transfers between devices: 32.1 us -> 19.5 us  [across(): return lax.ppermute(block, 'ctx', flip_w)]
    ppermute x5, waiting for transfers between devices: 11.3 us -> 19.9 us  [sum_ring(): came = (yield ((small,), (lambda x: lax.ppermute(x, axis, pairs),)))]
    ppermute x35, waiting for transfers between devices: 17.9 us -> 10.3 us  [backward(): return lax.ppermute(block, 'group', behind)]
    ppermute x35, starting transfers between devices: 41.6 us -> 35.6 us  [forward(): return lax.ppermute(block, 'group', ahead)]
    ppermute x35, waiting for transfers between devices: 67.2 us -> 72.8 us  [forward(): return lax.ppermute(block, 'group', ahead)]
    pallas_call x1 -> x2, Pallas kernels: 15.3 us -> 16.9 us  [the longest x1 12.6 us: per_device(): pl.pallas_call(functools.partial(place_kernel, n_group, part, n, n * unit...]
    unnamed x238 -> x240, local copies, waits for them, and re-layouts: 12.5 us -> 13.2 us
  transfers between devices with their start and end apart: 111 -> 111, of which waited for: 40 -> 41; matrix products, arithmetic and copies ran while one was open for 19% -> 19% of each run, Pallas kernels for 11% -> 14%
where the time goes in v6:
time: 464 us; the launch traced here: 459 us
  waiting for transfers between devices  127 us (27%)
  starting transfers between devices  100 us (22%)
  Pallas kernels  74.7 us (16%)
  matrix products  68 us (15%)
  other arithmetic  49.6 us (11%)
  local copies, waits for them, and re-layouts  37.2 us (8%)
    ppermute x35, waiting for transfers between devices, forward(): return lax.ppermute(block, 'group', ahead)  72.8 us
    dot_general x14, matrix products, dot(): lax.dot_general(left_side, right_side, (dims, ((), ())), precision=precis...  68 us
    ppermute x35, starting transfers between devices, backward(): return lax.ppermute(block, 'group', behind)  37.6 us
    ppermute x35, starting transfers between devices, forward(): return lax.ppermute(block, 'group', ahead)  35.6 us
    pallas_call x1, Pallas kernels, per_device(): pl.pallas_call(functools.partial(attend_back_kernel, rows, n, heads_here,...  21.7 us
    ppermute x5, waiting for transfers between devices, sum_ring(): came = (yield ((small,), (lambda x: lax.ppermute(x, axis, pairs),)))  19.9 us
    ppermute x11, waiting for transfers between devices, across(): return lax.ppermute(block, 'ctx', flip_w)  19.5 us
    ppermute x11, starting transfers between devices, across(): return lax.ppermute(block, 'ctx', flip_w)  17.6 us
  transfers between devices with their start and end apart: 111, of which 41 were waited for; matrix products, arithmetic and copies ran while one was open for 19% of the time, Pallas kernels for 14%

profile of v6, /device:TPU:0, one launch (start us, length us, event | category | flops | bytes accessed | tf_op | source)
XLA Modules:
  0.0 459.0 jit_solution(3084203945662387982)
XLA Ops:
  5.4 3.9 pad_dynamic-slice_fusion.3
  16.4 4.9 %own_heads.1.weight_ref = bf16[1536,576]{1,0:T(8,128)(2,1)} custom-call(s32[1]{0:T(128)} %bitcast.me_ref, bf16[768,768]{1,0:T(8,128)(2,1)} %refs_0_.2, bf16[768,768]{1,0:T(8,128)(2,1)} %refs_1_.1, bf16[768,768]{1,0:T(8,128)(2,1)} %refs_2_.1, bf16[768,768]{1,0:T(8,128)(2,1)} %collective-permute-done.1.refs_3_, ...), custom_call_target="tpu_custom_call" | custom-call | tf_op jit(solution)/shard_map/own_heads/pallas_call | solution.py:451
  30.4 10.4 %arrange_project.1 = (bf16[1024,1536]{1,0:T(8,128)(2,1)}, bf16[1024,1536]{1,0:T(8,128)(2,1)}, bf16[1024,576]{1,0:T(8,128)(2,1)}) custom-call(s32[1]{0:T(128)} %bitcast.me_ref, s32[4,256]{1,0:T(4,128)} %reshape.145.order_ref, f32[1,1536]{1,0:T(1,128)} %reshape.146.gain_ref, bf16[1536,576]{1,0:T(8,128)(2,1)} %own_heads.1.weight_ref, ...), custom_call_target="tpu_custom_call" | custom-call | flops 5033164800 | bytes 12582912 | tf_op jit(solution)/shard_map/arrange_project/pallas_call | solution.py:481
  40.8 17.4 %attend.1 = (bf16[1024,192]{1,0:T(8,128)(2,1)}, f32[1024,192]{1,0:T(8,128)}, f32[3,1024]{1,0:T(4,128)}) custom-call(s32[1]{0:T(128)} %bitcast.me_ref, s32[4]{0:T(128)} %bitcast.335, bf16[1024,576]{1,0:T(8,128)(2,1)} %get-tuple-element.308.qkv_ref, f32[3,5,256,256]{3,2,1,0:T(8,128)} %bias_strips.1.bias_ref), custom_call_target="tpu_custom_call" | custom-call | flops 3221225472 | bytes 3145728 | tf_op jit(solution)/shard_map/attend/pallas_call | solution.py:508
  63.6 3.6 fusion.49
  70.2 3.8 pad_maximum_fusion
  76.3 4.9 %multiply_reduce_fusion = (f32[1024]{0:T(1024)S(1)}, f32[1024,1536]{1,0:T(8,128)S(1)}) fusion(bf16[192,1536]{1,0:T(8,128)(2,1)S(1)} %copy-done.33, bf16[192,1536]{1,0:T(8,128)(2,1)S(1)} %get-tuple-element.667, bf16[192,1536]{1,0:T(8,128)(2,1)S(1)} %get-tuple-element.666, bf16[192,1536]{1,0:T(8,128)(2,1)S(1)} %get-tuple-element.665, ...), kind=kOutput, calls=%fused_computation.6 | convolution fusion | flops 2448948224 | bytes 13373440 | tf_op jit(solution)/shard_map/dot_general | solution.py:39
  81.3 9.9 %fusion.90 = f32[1024,2048]{0,1:T(8,128)} fusion(bf16[1536,2048]{1,0:T(8,128)(2,1)S(1)} %bitcast.325, f32[1024,1536]{1,0:T(8,128)S(1)} %get-tuple-element.759, f32[1536]{0:T(1024)S(1)} %copy-done.96, f32[1024]{0:T(1024)S(1)} %add_rsqrt_fusion), kind=kOutput, calls=%fused_computation.320 | convolution fusion | flops 6447169536 | bytes 20981760 | tf_op jit(solution)/shard_map/dot_general | solution.py:39
  91.2 12.3 %fusion.6 = (bf16[1024,1024]{0,1:T(8,128)(2,1)S(1)}, bf16[1024,1024]{0,1:T(8,128)(2,1)S(1)}, bf16[1024,1024]{0,1:T(8,128)(2,1)}) fusion(f32[1024,2048]{0,1:T(8,128)} %fusion.90, bf16[1024,1536]{1,0:T(8,128)(2,1)} %constant_dynamic-update-slice_fusion.6, s32[]{:T(128)S(6)} %select_n.274, bf16[1984,1536]{1,0:T(8,128)(2,1)} %param.27, ...), kind=kOutput, calls=%fused_computation.20 | convolution fusion | flops 3257925632 | bytes 24313860 | tf_op jit(solution)/shard_map/dot_general | solution.py:39
  103.5 11.1 %convolution_convert_fusion = bf16[1536,2048]{1,0:T(8,128)(2,1)S(1)} fusion(f32[1024,1536]{1,0:T(8,128)} %copy-done.50, f32[1536]{0:T(1024)S(1)} %copy-done.96, f32[1024]{0:T(1024)S(1)} %add_rsqrt_fusion, bf16[1024,1024]{0,1:T(8,128)(2,1)S(1)} %get-tuple-element.615, bf16[1024,1024]{0,1:T(8,128)(2,1)S(1)} %get-tuple-element.614), kind=kOutput, calls=%fused_computation | convolution fusion | flops 6458703872 | bytes 16787456 | tf_op jit(solution)/shard_map/dot_general | solution.py:39
  116.2 6.0 %convolution_convert_fusion.4 = bf16[1536,1024]{1,0:T(8,128)(2,1)S(1)} fusion(bf16[1024,1536]{1,0:T(8,128)(2,1)} %constant_dynamic-update-slice_fusion.6, bf16[1024,1024]{0,1:T(8,128)(2,1)S(1)} %copy-done.111), kind=kOutput, calls=%fused_computation.28 | convolution fusion | flops 3222798336 | bytes 8388608 | tf_op jit(solution)/shard_map/dot_general | solution.py:39
  127.5 7.1 %convolution_convert_fusion.1 = bf16[1024,1536]{1,0:T(8,128)(2,1)S(1)} fusion(bf16[1024,2048]{0,1:T(8,128)(2,1)S(1)} %pad_maximum_fusion.1, bf16[1536,2048]{1,0:T(8,128)(2,1)S(1)} %bitcast.325), kind=kOutput, calls=%fused_computation.25 | convolution fusion | flops 6444023808 | bytes 13631488 | tf_op jit(solution)/shard_map/dot_general | solution.py:39
  134.7 6.5 %collective-permute-done.15 = bf16[4,24,3072]{2,1,0:T(8,128)(2,1)S(1)} collective-permute-done((bf16[4,24,3072]{2,1,0:T(8,128)(2,1)S(1)}, bf16[4,24,3072]{2,1,0:T(8,128)(2,1)S(1)}, u32[]{:S(2)}, u32[]{:S(2)}) %collective-permute-start.15) | collective-permute-done | bytes 589856 | tf_op jit(solution)/shard_map/ppermute | solution.py:543
  145.4 6.4 %convolution_convert_fusion.3 = bf16[1024,1536]{1,0:T(8,128)(2,1)} fusion(bf16[1024,1024]{0,1:T(8,128)(2,1)S(1)} %copy-done.112, s32[]{:T(128)S(6)} %select_n.274, bf16[1984,1536]{1,0:T(8,128)(2,1)S(1)} %bitcast.334, bf16[64,1536]{1,0:T(8,128)(2,1)S(1)} %copy-done.76, bf16[64,1536]{1,0:T(8,128)(2,1)S(1)} %broadcast.121), kind=kOutput, calls=%fused_computation.27 | convolution fusion | flops 3232235520 | bytes 11730948 | tf_op jit(solution)/shard_map/dot_general | solution.py:39
  152.2 6.9 %collective-permute-done.17 = bf16[4,24,3072]{2,1,0:T(8,128)(2,1)S(1)} collective-permute-done((bf16[4,24,3072]{2,1,0:T(8,128)(2,1)S(1)}, bf16[4,24,3072]{2,1,0:T(8,128)(2,1)S(1)}, u32[]{:S(2)}, u32[]{:S(2)}) %collective-permute-start.17) | collective-permute-done | bytes 589856 | tf_op jit(solution)/shard_map/ppermute | solution.py:543
  165.7 13.7 %collective-permute-done.22 = bf16[256,1536]{1,0:T(8,128)(2,1)S(1)} collective-permute-done((bf16[256,1536]{1,0:T(8,128)(2,1)S(1)}, bf16[256,1536]{1,0:T(8,128)(2,1)S(1)}, u32[]{:S(2)}, u32[]{:S(2)}) %collective-permute-start.22) | collective-permute-done | bytes 786464 | tf_op jit(solution)/shard_map/ppermute | solution.py:403
  206.3 21.7 %attend_back.1 = (bf16[1024,576]{1,0:T(8,128)(2,1)}, f32[32,128]{1,0:T(8,128)}) custom-call(s32[1]{0:T(128)} %bitcast.me_ref, s32[4]{0:T(128)} %bitcast.336, bf16[1024,576]{1,0:T(8,128)(2,1)} %get-tuple-element.308.qkv_ref, f32[3,5,256,256]{3,2,1,0:T(8,128)} %bias_strips.1.bias_ref, f32[3,1024]{1,0:T(4,128)} %get-tuple-element.363.lse_ref, ...), custom_call_target="tpu_custom_call" | custom-call | flops 8053063680 | bytes 3145728 | tf_op jit(solution)/shard_map/attend_back/pallas_call | solution.py:753
  244.0 5.1 %collective-permute-done.32 = bf16[4,24,3072]{2,1,0:T(8,128)(2,1)S(1)} collective-permute-done((bf16[4,24,3072]{2,1,0:T(8,128)(2,1)S(1)}, bf16[4,24,3072]{2,1,0:T(8,128)(2,1)S(1)}, u32[]{:S(2)}, u32[]{:S(2)}) %collective-permute-start.32) | collective-permute-done | bytes 589856 | tf_op jit(solution)/shard_map/ppermute | solution.py:543
  258.7 5.2 %collective-permute-done.36 = bf16[4,24,3072]{2,1,0:T(8,128)(2,1)S(1)} collective-permute-done((bf16[4,24,3072]{2,1,0:T(8,128)(2,1)S(1)}, bf16[4,24,3072]{2,1,0:T(8,128)(2,1)S(1)}, u32[]{:S(2)}, u32[]{:S(2)}) %collective-permute-start.36) | collective-permute-done | bytes 589856 | tf_op jit(solution)/shard_map/ppermute | solution.py:543
  292.4 4.6 collective-permute-done.49
  306.3 4.0 collective-permute-done.53.refs_4_
  312.3 4.3 collective-permute-done.51.refs_6_
  332.1 4.8 %collective-permute-done.72.refs_10_ = bf16[24,6144]{1,0:T(8,128)(2,1)} collective-permute-done((bf16[24,6144]{1,0:T(8,128)(2,1)S(1)}, bf16[24,6144]{1,0:T(8,128)(2,1)}, u32[]{:S(2)}, u32[]{:S(2)}) %collective-permute-start.72) | collective-permute-done | bytes 294944 | tf_op jit(solution)/shard_map/ppermute | solution.py:543
  356.1 5.7 %collective-permute-done.76 = f32[3456]{0:T(1024)S(1)} collective-permute-done((f32[3456]{0:T(1024)S(1)}, f32[3456]{0:T(1024)S(1)}, u32[]{:S(2)}, u32[]{:S(2)}) %collective-permute-start.76) | collective-permute-done | bytes 13856 | tf_op jit(solution)/shard_map/ppermute | solution.py:671
  366.4 8.3 %collective-permute-done.81 = f32[3456]{0:T(1024)S(1)} collective-permute-done((f32[3456]{0:T(1024)S(1)}, f32[3456]{0:T(1024)S(1)}, u32[]{:S(2)}, u32[]{:S(2)}) %collective-permute-start.81) | collective-permute-done | bytes 13856 | tf_op jit(solution)/shard_map/ppermute | solution.py:671
  379.5 5.2 %collective-permute-done.86 = f32[3456]{0:T(1024)S(1)} collective-permute-done((f32[3456]{0:T(1024)S(1)}, f32[3456]{0:T(1024)S(1)}, u32[]{:S(2)}, u32[]{:S(2)}) %collective-permute-start.86) | collective-permute-done | bytes 13856 | tf_op jit(solution)/shard_map/ppermute | solution.py:671
  401.1 7.1 %collective-permute-done.95.refs_10_ = bf16[24,3072]{1,0:T(8,128)(2,1)S(1)} collective-permute-done((bf16[24,3072]{1,0:T(8,128)(2,1)S(1)}, bf16[24,3072]{1,0:T(8,128)(2,1)S(1)}, u32[]{:S(2)}, u32[]{:S(2)}) %collective-permute-start.95) | collective-permute-done | bytes 147488 | tf_op jit(solution)/shard_map/ppermute | solution.py:543
  413.6 6.6 %collective-permute-done.103.refs_12_ = bf16[24,3072]{1,0:T(8,128)(2,1)S(1)} collective-permute-done((bf16[24,3072]{1,0:T(8,128)(2,1)S(1)}, bf16[24,3072]{1,0:T(8,128)(2,1)S(1)}, u32[]{:S(2)}, u32[]{:S(2)}) %collective-permute-start.103) | collective-permute-done | bytes 147488 | tf_op jit(solution)/shard_map/ppermute | solution.py:543
  425.1 5.1 %collective-permute-done.99.refs_26_ = bf16[24,6144]{1,0:T(8,128)(2,1)} collective-permute-done((bf16[24,6144]{1,0:T(8,128)(2,1)S(1)}, bf16[24,6144]{1,0:T(8,128)(2,1)}, u32[]{:S(2)}, u32[]{:S(2)}) %collective-permute-start.99) | collective-permute-done | bytes 294944 | tf_op jit(solution)/shard_map/ppermute | solution.py:543
  435.1 4.5 fusion.12
  440.3 4.4 place_heads.1
  446.1 12.6 %place.1 = (f32[384,3968]{1,0:T(8,128)}, f32[384,3968]{1,0:T(8,128)}, f32[3968,384]{1,0:T(8,128)}) custom-call(s32[1]{0:T(128)} %bitcast.116.spot_ref, bf16[24,6144]{1,0:T(8,128)(2,1)} %copy-done.22, bf16[24,6144]{1,0:T(8,128)(2,1)} %copy-done.21, bf16[24,6144]{1,0:T(8,128)(2,1)} %copy-done.24, bf16[24,6144]{1,0:T(8,128)(2,1)} %copy-done.23, ...), custom_call_target="tpu_custom_call" | custom-call | tf_op jit(solution)/shard_map/place/pallas_call | solution.py:845
  (573 shorter events, 218.5 us)
Async XLA Ops:
  1.2 15.2 %collective-permute-start.2 = (bf16[768,768]{1,0:T(8,128)(2,1)}, bf16[768,768]{1,0:T(8,128)(2,1)}, u32[]{:S(2)}, u32[]{:S(2)}) collective-permute-start(bf16[768,768]{1,0:T(8,128)(2,1)} %refs_1_.1), channel_id=1, source_target_pairs={{0,1},{1,0},{2,3},{3,2},{4,5},{5,4},{6,7},{7,6},{8,9},{9,8},{10,11... | collective-permute-start | bytes 3538952 | tf_op jit(solution)/shard_map/ppermute | solution.py:400
  1.7 21.0 %collective-permute-start = (bf16[256,1536]{1,0:T(8,128)(2,1)}, bf16[256,1536]{1,0:T(8,128)(2,1)}, u32[]{:S(2)}, u32[]{:S(2)}) collective-permute-start(bf16[256,1536]{1,0:T(8,128)(2,1)} %refs_0_.3), channel_id=1, source_target_pairs={{0,2},{2,0},{1,3},{3,1},{4,6},{6,4},{5,7},{7,5},{8,10},{10,8},{9,1... | collective-permute-start | bytes 2359304 | tf_op jit(solution)/shard_map/ppermute | solution.py:403
  4.3 23.8 %collective-permute-start.4 = (bf16[256,1536]{1,0:T(8,128)(2,1)}, bf16[256,1536]{1,0:T(8,128)(2,1)}, u32[]{:S(2)}, u32[]{:S(2)}) collective-permute-start(bf16[256,1536]{1,0:T(8,128)(2,1)} %refs_0_.3), channel_id=1, source_target_pairs={{0,1},{1,0},{2,3},{3,2},{4,5},{5,4},{6,7},{7,6},{8,9},{9,8},{10,11... | collective-permute-start | bytes 2359304 | tf_op jit(solution)/shard_map/ppermute | solution.py:400
  22.7 35.5 %collective-permute-start.6 = (bf16[384,1536]{1,0:T(8,128)(2,1)}, bf16[384,1536]{1,0:T(8,128)(2,1)}, u32[]{:S(2)}, u32[]{:S(2)}) collective-permute-start(bf16[384,1536]{1,0:T(8,128)(2,1)} %param.22), channel_id=1, source_target_pairs={{0,1},{1,0},{2,3},{3,2},{4,5},{5,4},{6,7},{7,6},{8,9},{9,8},{10,11... | collective-permute-start | bytes 3538952 | tf_op jit(solution)/shard_map/ppermute | solution.py:400
  23.3 44.7 %collective-permute-start.9 = (bf16[768,2048]{1,0:T(8,128)(2,1)}, bf16[768,2048]{1,0:T(8,128)(2,1)}, u32[]{:S(2)}, u32[]{:S(2)}) collective-permute-start(bf16[768,2048]{1,0:T(8,128)(2,1)} %pad_maximum_fusion.3), channel_id=1, source_target_pairs={{0,1},{1,0},{2,3},{3,2},{4,5},{5,4},{6,7},{7,6},{8,9},{9,8},{10,11... | collective-permute-start | bytes 9437192 | tf_op jit(solution)/shard_map/ppermute | solution.py:400
  26.3 32.3 %collective-permute-start.12 = (bf16[256,1536]{1,0:T(8,128)(2,1)}, bf16[256,1536]{1,0:T(8,128)(2,1)S(1)}, u32[]{:S(2)}, u32[]{:S(2)}) collective-permute-start(bf16[256,1536]{1,0:T(8,128)(2,1)} %param.15), channel_id=1, source_target_pairs={{0,2},{2,0},{1,3},{3,1},{4,6},{6,4},{5,7},{7,5},{8,10},{10,8},{9,1... | collective-permute-start | bytes 2359304 | tf_op jit(solution)/shard_map/ppermute | solution.py:403
  28.1 31.0 %collective-permute-start.11 = (bf16[256,1536]{1,0:T(8,128)(2,1)}, bf16[256,1536]{1,0:T(8,128)(2,1)}, u32[]{:S(2)}, u32[]{:S(2)}) collective-permute-start(bf16[256,1536]{1,0:T(8,128)(2,1)} %param.15), channel_id=1, source_target_pairs={{0,1},{1,0},{2,3},{3,2},{4,5},{5,4},{6,7},{7,6},{8,9},{9,8},{10,11... | collective-permute-start | bytes 2359304 | tf_op jit(solution)/shard_map/ppermute | solution.py:400
  58.2 15.8 %collective-permute-start.8 = (bf16[1024,192]{1,0:T(8,128)(2,1)}, bf16[1024,192]{1,0:T(8,128)(2,1)}, u32[]{:S(2)}, u32[]{:S(2)}) collective-permute-start(bf16[1024,192]{1,0:T(8,128)(2,1)} %get-tuple-element.312), channel_id=1, source_target_pairs={{0,2},{2,0},{1,3},{3,1},{4,6},{6,4},{5,7},{7,5},{8,10},{10,8},{9,1... | collective-permute-start | bytes 1179656 | tf_op jit(solution)/shard_map/ppermute | solution.py:403
  58.7 15.5 %collective-permute-start.13 = (bf16[256,1536]{1,0:T(8,128)(2,1)S(1)}, bf16[256,1536]{1,0:T(8,128)(2,1)S(1)}, u32[]{:S(2)}, u32[]{:S(2)}) collective-permute-start(bf16[256,1536]{1,0:T(8,128)(2,1)S(1)} %collective-permute-done.12), channel_id=1, source_target_pairs={{0,1},{1,0},{2,3},{3,2},{4,5},{5,4},{6,7},{7,6},{8,9},{9,8},{10,11... | collective-permute-start | bytes 2359304 | tf_op jit(solution)/shard_map/ppermute | solution.py:400
  125.5 15.7 %collective-permute-start.15 = (bf16[4,24,3072]{2,1,0:T(8,128)(2,1)S(1)}, bf16[4,24,3072]{2,1,0:T(8,128)(2,1)S(1)}, u32[]{:S(2)}, u32[]{:S(2)}) collective-permute-start(bf16[4,24,3072]{2,1,0:T(8,128)(2,1)S(1)} %pad_maximum_fusion.8), channel_id=1, source_target_pairs={{0,8},{8,16},{16,24},{24,28},{28,20},{20,12},{12,4},{4,0},{1,9},{9... | collective-permute-start | bytes 1769480 | tf_op jit(solution)/shard_map/ppermute | solution.py:543
  127.3 15.4 %collective-permute-start.16 = (bf16[4,24,3072]{2,1,0:T(8,128)(2,1)S(1)}, bf16[4,24,3072]{2,1,0:T(8,128)(2,1)S(1)}, u32[]{:S(2)}, u32[]{:S(2)}) collective-permute-start(bf16[4,24,3072]{2,1,0:T(8,128)(2,1)S(1)} %pad_maximum_fusion.9), channel_id=1, source_target_pairs={{8,0},{16,8},{24,16},{28,24},{20,28},{12,20},{4,12},{0,4},{9,1},{1... | collective-permute-start | bytes 1769480 | tf_op jit(solution)/shard_map/ppermute | solution.py:546
  143.3 15.7 %collective-permute-start.17 = (bf16[4,24,3072]{2,1,0:T(8,128)(2,1)S(1)}, bf16[4,24,3072]{2,1,0:T(8,128)(2,1)S(1)}, u32[]{:S(2)}, u32[]{:S(2)}) collective-permute-start(bf16[4,24,3072]{2,1,0:T(8,128)(2,1)S(1)} %maximum_add_fusion), channel_id=1, source_target_pairs={{0,8},{8,16},{16,24},{24,28},{28,20},{20,12},{12,4},{4,0},{1,9},{9... | collective-permute-start | bytes 1769480 | tf_op jit(solution)/shard_map/ppermute | solution.py:543
  144.8 15.4 %collective-permute-start.18 = (bf16[4,24,3072]{2,1,0:T(8,128)(2,1)S(1)}, bf16[4,24,3072]{2,1,0:T(8,128)(2,1)S(1)}, u32[]{:S(2)}, u32[]{:S(2)}) collective-permute-start(bf16[4,24,3072]{2,1,0:T(8,128)(2,1)S(1)} %maximum_add_fusion.1), channel_id=1, source_target_pairs={{8,0},{16,8},{24,16},{28,24},{20,28},{12,20},{4,12},{0,4},{9,1},{1... | collective-permute-start | bytes 1769480 | tf_op jit(solution)/shard_map/ppermute | solution.py:546
  160.5 18.8 %collective-permute-start.22 = (bf16[256,1536]{1,0:T(8,128)(2,1)S(1)}, bf16[256,1536]{1,0:T(8,128)(2,1)S(1)}, u32[]{:S(2)}, u32[]{:S(2)}) collective-permute-start(bf16[256,1536]{1,0:T(8,128)(2,1)S(1)} %get-tuple-element.344), channel_id=1, source_target_pairs={{0,2},{2,0},{1,3},{3,1},{4,6},{6,4},{5,7},{7,5},{8,10},{10,8},{9,1... | collective-permute-start | bytes 2359304 | tf_op jit(solution)/shard_map/ppermute | solution.py:403
  162.1 17.4 %collective-permute-start.20 = (bf16[4,24,3072]{2,1,0:T(8,128)(2,1)S(1)}, bf16[4,24,3072]{2,1,0:T(8,128)(2,1)S(1)}, u32[]{:S(2)}, u32[]{:S(2)}) collective-permute-start(bf16[4,24,3072]{2,1,0:T(8,128)(2,1)S(1)} %maximum_add_fusion.2), channel_id=1, source_target_pairs={{0,8},{8,16},{16,24},{24,28},{28,20},{20,12},{12,4},{4,0},{1,9},{9... | collective-permute-start | bytes 1769480 | tf_op jit(solution)/shard_map/ppermute | solution.py:543
  163.9 15.7 %collective-permute-start.21 = (bf16[4,24,3072]{2,1,0:T(8,128)(2,1)S(1)}, bf16[4,24,3072]{2,1,0:T(8,128)(2,1)S(1)}, u32[]{:S(2)}, u32[]{:S(2)}) collective-permute-start(bf16[4,24,3072]{2,1,0:T(8,128)(2,1)S(1)} %maximum_add_fusion.3), channel_id=1, source_target_pairs={{8,0},{16,8},{24,16},{28,24},{20,28},{12,20},{4,12},{0,4},{9,1},{1... | collective-permute-start | bytes 1769480 | tf_op jit(solution)/shard_map/ppermute | solution.py:546
  182.8 15.5 %collective-permute-start.23 = (bf16[4,24,3072]{2,1,0:T(8,128)(2,1)}, bf16[4,24,3072]{2,1,0:T(8,128)(2,1)}, u32[]{:S(2)}, u32[]{:S(2)}) collective-permute-start(bf16[4,24,3072]{2,1,0:T(8,128)(2,1)} %maximum_add_fusion.4), channel_id=1, source_target_pairs={{0,8},{8,16},{16,24},{24,28},{28,20},{20,12},{12,4},{4,0},{1,9},{9... | collective-permute-start | bytes 1769480 | tf_op jit(solution)/shard_map/ppermute | solution.py:543
  202.7 26.1 %collective-permute-start.34 = (bf16[256,1536]{1,0:T(8,128)(2,1)S(1)}, bf16[256,1536]{1,0:T(8,128)(2,1)}, u32[]{:S(2)}, u32[]{:S(2)}) collective-permute-start(bf16[256,1536]{1,0:T(8,128)(2,1)S(1)} %copy-done.11), channel_id=1, source_target_pairs={{0,1},{1,0},{2,3},{3,2},{4,5},{5,4},{6,7},{7,6},{8,9},{9,8},{10,11... | collective-permute-start | bytes 2359304 | tf_op jit(solution)/shard_map/ppermute | solution.py:400
  202.7 28.2 %collective-permute-start.30 = (bf16[256,1536]{1,0:T(8,128)(2,1)S(1)}, bf16[256,1536]{1,0:T(8,128)(2,1)}, u32[]{:S(2)}, u32[]{:S(2)}) collective-permute-start(bf16[256,1536]{1,0:T(8,128)(2,1)S(1)} %copy-done.11), channel_id=1, source_target_pairs={{0,2},{2,0},{1,3},{3,1},{4,6},{6,4},{5,7},{7,5},{8,10},{10,8},{9,1... | collective-permute-start | bytes 2359304 | tf_op jit(solution)/shard_map/ppermute | solution.py:403
  204.2 26.6 %collective-permute-start.28 = (bf16[4,24,3072]{2,1,0:T(8,128)(2,1)}, bf16[4,24,3072]{2,1,0:T(8,128)(2,1)}, u32[]{:S(2)}, u32[]{:S(2)}) collective-permute-start(bf16[4,24,3072]{2,1,0:T(8,128)(2,1)} %maximum_add_fusion.6), channel_id=1, source_target_pairs={{0,8},{8,16},{16,24},{24,28},{28,20},{20,12},{12,4},{4,0},{1,9},{9... | collective-permute-start | bytes 1769480 | tf_op jit(solution)/shard_map/ppermute | solution.py:543
  205.0 25.8 %collective-permute-start.29 = (bf16[4,24,3072]{2,1,0:T(8,128)(2,1)}, bf16[4,24,3072]{2,1,0:T(8,128)(2,1)}, u32[]{:S(2)}, u32[]{:S(2)}) collective-permute-start(bf16[4,24,3072]{2,1,0:T(8,128)(2,1)} %maximum_add_fusion.7), channel_id=1, source_target_pairs={{8,0},{16,8},{24,16},{28,24},{20,28},{12,20},{4,12},{0,4},{9,1},{1... | collective-permute-start | bytes 1769480 | tf_op jit(solution)/shard_map/ppermute | solution.py:546
  237.8 33.1 %collective-permute-start.31 = (bf16[2,256,1536]{2,1,0:T(8,128)(2,1)}, bf16[2,256,1536]{2,1,0:T(8,128)(2,1)}, u32[]{:S(2)}, u32[]{:S(2)}) collective-permute-start(bf16[2,256,1536]{2,1,0:T(8,128)(2,1)} %pad_maximum_fusion.6), channel_id=1, source_target_pairs={{0,1},{1,0},{2,3},{3,2},{4,5},{5,4},{6,7},{7,6},{8,9},{9,8},{10,11... | collective-permute-start | bytes 4718600 | tf_op jit(solution)/shard_map/ppermute | solution.py:400
  285.2 33.5 %collective-permute-start.61 = (bf16[256,1536]{1,0:T(8,128)(2,1)S(1)}, bf16[256,1536]{1,0:T(8,128)(2,1)S(1)}, u32[]{:S(2)}, u32[]{:S(2)}) collective-permute-start(bf16[256,1536]{1,0:T(8,128)(2,1)S(1)} %get-tuple-element.450), channel_id=1, source_target_pairs={{0,2},{2,0},{1,3},{3,1},{4,6},{6,4},{5,7},{7,5},{8,10},{10,8},{9,1... | collective-permute-start | bytes 2359304 | tf_op jit(solution)/shard_map/ppermute | solution.py:403
  336.9 16.2 %collective-permute-start.77 = (bf16[24,6144]{1,0:T(8,128)(2,1)}, bf16[24,6144]{1,0:T(8,128)(2,1)}, u32[]{:S(2)}, u32[]{:S(2)}) collective-permute-start(bf16[24,6144]{1,0:T(8,128)(2,1)} %collective-permute-done.57.refs_8_), channel_id=1, source_target_pairs={{0,8},{8,16},{16,24},{24,28},{28,20},{20,12},{12,4},{4,0},{1,9},{9... | collective-permute-start | bytes 884744 | tf_op jit(solution)/shard_map/ppermute | solution.py:543
  345.5 18.9 %collective-permute-start.82 = (bf16[24,6144]{1,0:T(8,128)(2,1)}, bf16[24,6144]{1,0:T(8,128)(2,1)}, u32[]{:S(2)}, u32[]{:S(2)}) collective-permute-start(bf16[24,6144]{1,0:T(8,128)(2,1)} %collective-permute-done.72.refs_10_), channel_id=1, source_target_pairs={{0,8},{8,16},{16,24},{24,28},{28,20},{20,12},{12,4},{4,0},{1,9},{9... | collective-permute-start | bytes 884744 | tf_op jit(solution)/shard_map/ppermute | solution.py:543
  346.2 20.2 %collective-permute-start.83 = (bf16[24,6144]{1,0:T(8,128)(2,1)}, bf16[24,6144]{1,0:T(8,128)(2,1)}, u32[]{:S(2)}, u32[]{:S(2)}) collective-permute-start(bf16[24,6144]{1,0:T(8,128)(2,1)} %collective-permute-done.73.refs_11_), channel_id=1, source_target_pairs={{8,0},{16,8},{24,16},{28,24},{20,28},{12,20},{4,12},{0,4},{9,1},{1... | collective-permute-start | bytes 884744 | tf_op jit(solution)/shard_map/ppermute | solution.py:546
  362.9 15.9 %collective-permute-start.90 = (bf16[24,6144]{1,0:T(8,128)(2,1)}, bf16[24,6144]{1,0:T(8,128)(2,1)S(1)}, u32[]{:S(2)}, u32[]{:S(2)}) collective-permute-start(bf16[24,6144]{1,0:T(8,128)(2,1)} %collective-permute-done.78.refs_13_), channel_id=1, source_target_pairs={{8,0},{16,8},{24,16},{28,24},{20,28},{12,20},{4,12},{0,4},{9,1},{1... | collective-permute-start | bytes 884744 | tf_op jit(solution)/shard_map/ppermute | solution.py:546
  374.7 15.3 %collective-permute-start.87 = (bf16[24,6144]{1,0:T(8,128)(2,1)}, bf16[24,6144]{1,0:T(8,128)(2,1)S(1)}, u32[]{:S(2)}, u32[]{:S(2)}) collective-permute-start(bf16[24,6144]{1,0:T(8,128)(2,1)} %collective-permute-done.82.refs_14_), channel_id=1, source_target_pairs={{0,8},{8,16},{16,24},{24,28},{28,20},{20,12},{12,4},{4,0},{1,9},{9... | collective-permute-start | bytes 884744 | tf_op jit(solution)/shard_map/ppermute | solution.py:543
  374.7 16.0 %collective-permute-start.88 = (bf16[24,6144]{1,0:T(8,128)(2,1)}, bf16[24,6144]{1,0:T(8,128)(2,1)S(1)}, u32[]{:S(2)}, u32[]{:S(2)}) collective-permute-start(bf16[24,6144]{1,0:T(8,128)(2,1)} %collective-permute-done.83.refs_15_), channel_id=1, source_target_pairs={{8,0},{16,8},{24,16},{28,24},{20,28},{12,20},{4,12},{0,4},{9,1},{1... | collective-permute-start | bytes 884744 | tf_op jit(solution)/shard_map/ppermute | solution.py:546
  390.7 41.6 %collective-permute-start.62 = (bf16[256,1536]{1,0:T(8,128)(2,1)}, bf16[256,1536]{1,0:T(8,128)(2,1)S(1)}, u32[]{:S(2)}, u32[]{:S(2)}) collective-permute-start(bf16[256,1536]{1,0:T(8,128)(2,1)} %fusion.41), channel_id=1, source_target_pairs={{0,2},{2,0},{1,3},{3,1},{4,6},{6,4},{5,7},{7,5},{8,10},{10,8},{9,1... | collective-permute-start | bytes 2359304 | tf_op jit(solution)/shard_map/ppermute | solution.py:403
  397.0 16.4 %collective-permute-start.91 = (bf16[24,6144]{1,0:T(8,128)(2,1)S(1)}, bf16[24,6144]{1,0:T(8,128)(2,1)S(1)}, u32[]{:S(2)}, u32[]{:S(2)}) collective-permute-start(bf16[24,6144]{1,0:T(8,128)(2,1)S(1)} %collective-permute-done.87.refs_18_), channel_id=1, source_target_pairs={{0,8},{8,16},{16,24},{24,28},{28,20},{20,12},{12,4},{4,0},{1,9},{9... | collective-permute-start | bytes 884744 | tf_op jit(solution)/shard_map/ppermute | solution.py:543
  424.3 15.3 %collective-permute-start.108 = (bf16[24,3072]{1,0:T(8,128)(2,1)S(1)}, bf16[24,3072]{1,0:T(8,128)(2,1)S(1)}, u32[]{:S(2)}, u32[]{:S(2)}) collective-permute-start(bf16[24,3072]{1,0:T(8,128)(2,1)S(1)} %collective-permute-done.104.refs_13_), channel_id=1, source_target_pairs={{8,0},{16,8},{24,16},{28,24},{20,28},{12,20},{4,12},{0,4},{9,1},{1... | collective-permute-start | bytes 442376 | tf_op jit(solution)/shard_map/ppermute | solution.py:546
  (196 other events, 2469.4 us)

commit v7 on v6

--- a/solution.py
+++ b/solution.py
@@ -291,7 +291,7 @@
 def place_kernel(groups, part, count, units_all, hidden_units, spot_ref, *refs):
     spot = spot_ref[0]
     wide, refs = refs[: 4 * groups], refs[4 * groups :]
-    outs, (gate, up, down, turned), sems = refs[:3], refs[3:-1], refs[-1]
+    outs, (up, down, turned), sems = refs[:2], refs[2:-1], refs[-1]
     units = units_all // count
     middle = 3 * units // 2
 
@@ -317,21 +317,33 @@
                             block[:, start : start + size].astype(f32)
                         )
 
-    gather(gate, 0)
-    copy(0, gate).start()
     gather(up, 1)
-    copy(1, up).start()
+    copy(0, up).start()
     gather(down, 2)
     for first in range(0, hidden_units, 128):
         turned[first : first + 128, :] = down[:, first : first + 128].T
-    copy(2, turned).start()
-    for k, source in enumerate((gate, up, turned)):
+    copy(1, turned).start()
+    for k, source in enumerate((up, turned)):
         copy(k, source).wait()
 
 
 def piece_row(spot, groups, part, j, h):
     index = lax.rem(spot + groups - j, groups) if h == 0 else lax.rem(spot + j, groups)
     return pl.multiple_of((2 * index + h) * part, 8)
+
+
+def place_gate_kernel(groups, part, count, units, hidden_units, spot_ref, *refs):
+    spot, pieces, out_ref = spot_ref[0], refs[:-1], refs[-1]
+    middle = pieces[0].shape[1] // count
+    for j in range(groups):
+        for h in range(2):
+            rows = pl.ds(piece_row(spot, groups, part, j, h), part)
+            for r in range(count):
+                first = r * units
+                size = min(units, hidden_units - first)
+                out_ref[rows, first : first + size] = (
+                    pieces[j * 2 + h][:, r * middle : r * middle + size].astype(f32)
+                )
 
 
 def place_heads_kernel(groups, part, count, width, spot_ref, *refs):
@@ -817,9 +829,13 @@
         own_rows, all_heads = model // n, n * width
         spot_1 = spot.reshape(1).astype(jnp.int32)
         in_vmem = pl.BlockSpec(memory_space=pltpu.VMEM)
+        rounds = 0
         while narrow.pending or sums.pending or len(wide_pieces) < 4 * n_group - 2:
+            rounds += 1
             tick((), narrow, sums)
-            if len(wide_pieces) < 4 * n_group - 2:
+            if rounds == n_group:
+                outputs, input_grad = tick((outputs, input_grad), wide)
+            elif len(wide_pieces) < 4 * n_group - 2:
                 tick((), wide)
         heads_grads = pl.pallas_call(
             functools.partial(place_heads_kernel, n_group, part, n, width),
@@ -831,7 +847,15 @@
             compiler_params=params,
             name="place_heads",
         )(spot_1, *narrow_pieces)
-        heads_grads = tick(heads_grads, wide)
+        total_gate = pl.pallas_call(
+            functools.partial(place_gate_kernel, n_group, part, n, units, hidden_units),
+            out_shape=jax.ShapeDtypeStruct((own_rows, hidden_units), f32),
+            in_specs=[pl.BlockSpec(memory_space=pltpu.SMEM)] + [in_vmem] * (2 * n_group),
+            out_specs=in_vmem,
+            compiler_params=params,
+            name="place_gate",
+        )(spot_1, *[wide_pieces[4 * j + h] for j in range(n_group) for h in range(2)])
+        heads_grads, total_gate = tick((heads_grads, total_gate), wide)
         small = sums.result
     else:
         small = lax.psum(small, ("group",) + peer_axes)
@@ -842,15 +866,15 @@
     if fast:
         *total_qkv, total_out = heads_grads
         wide_shape, down_shape = (own_rows, hidden_units), (hidden_units, own_rows)
-        total_gate, total_up, total_down = pl.pallas_call(
+        total_up, total_down = pl.pallas_call(
             functools.partial(place_kernel, n_group, part, n, n * units, hidden_units),
             out_shape=[
-                jax.ShapeDtypeStruct(shape, f32) for shape in (wide_shape, wide_shape, down_shape)
+                jax.ShapeDtypeStruct(shape, f32) for shape in (wide_shape, down_shape)
             ],
             in_specs=[pl.BlockSpec(memory_space=pltpu.SMEM)] + [in_vmem] * (4 * n_group),
-            out_specs=[pl.BlockSpec(memory_space=pl.ANY)] * 3,
-            scratch_shapes=[pltpu.VMEM(wide_shape, f32)] * 3
-            + [pltpu.VMEM(down_shape, f32), pltpu.SemaphoreType.DMA((3,))],
+            out_specs=[pl.BlockSpec(memory_space=pl.ANY)] * 2,
+            scratch_shapes=[pltpu.VMEM(wide_shape, f32)] * 2
+            + [pltpu.VMEM(down_shape, f32), pltpu.SemaphoreType.DMA((2,))],
             compiler_params=params,
             name="place",
         )(spot_1, *wide_pieces)

time: 464 us -> 480 us (1.034)
  waiting for transfers between devices: 127 us -> 146 us
    ppermute x35, waiting for transfers between devices: 10.3 us -> 35 us  [backward(): return lax.ppermute(block, 'group', behind)]
    ppermute x5, waiting for transfers between devices: 19.9 us -> 13.8 us  [sum_ring(): came = (yield ((small,), (lambda x: lax.ppermute(x, axis, pairs),)))]
    pallas_call x0 -> x1, Pallas kernels: none -> 5.34 us  [per_device(): pl.pallas_call(functools.partial(place_gate_kernel, n_group, part, n, uni...]
    ppermute x35, starting transfers between devices: 35.6 us -> 40.7 us  [forward(): return lax.ppermute(block, 'group', ahead)]
    unnamed x240 -> x254, local copies, waits for them, and re-layouts: 13.2 us -> 14 us
  transfers between devices with their start and end apart: 111 -> 111, of which waited for: 41 -> 50; matrix products, arithmetic and copies ran while one was open for 19% -> 19% of each run, Pallas kernels for 14% -> 12%
where the time goes in v7:
time: 480 us; the launch traced here: 476 us
  waiting for transfers between devices  146 us (30%)
  starting transfers between devices  99.8 us (21%)
  Pallas kernels  70 us (15%)
  matrix products  68.1 us (14%)
  other arithmetic  49.6 us (10%)
  local copies, waits for them, and re-layouts  39.7 us (8%)
    ppermute x35, waiting for transfers between devices, forward(): return lax.ppermute(block, 'group', ahead)  72.8 us
    dot_general x14, matrix products, dot(): lax.dot_general(left_side, right_side, (dims, ((), ())), precision=precis...  68.1 us
    ppermute x35, starting transfers between devices, forward(): return lax.ppermute(block, 'group', ahead)  40.7 us
    ppermute x35, waiting for transfers between devices, backward(): return lax.ppermute(block, 'group', behind)  35 us
    ppermute x35, starting transfers between devices, backward(): return lax.ppermute(block, 'group', behind)  34.9 us
    ppermute x11, waiting for transfers between devices, across(): return lax.ppermute(block, 'ctx', flip_w)  19.9 us
    pallas_call x1, Pallas kernels, per_device(): pl.pallas_call(functools.partial(attend_back_kernel, rows, n, heads_here,...  17.7 us
    ppermute x11, starting transfers between devices, across(): return lax.ppermute(block, 'ctx', flip_w)  14.3 us
  transfers between devices with their start and end apart: 111, of which 50 were waited for; matrix products, arithmetic and copies ran while one was open for 19% of the time, Pallas kernels for 12%

profile of v7, /device:TPU:0, one launch (start us, length us, event | category | flops | bytes accessed | tf_op | source)
XLA Modules:
  0.0 475.8 jit_solution(5229922279779465477)
XLA Ops:
  5.4 3.9 pad_dynamic-slice_fusion.3
  16.4 4.9 %own_heads.1.weight_ref = bf16[1536,576]{1,0:T(8,128)(2,1)} custom-call(s32[1]{0:T(128)} %bitcast.me_ref, bf16[768,768]{1,0:T(8,128)(2,1)} %refs_0_.2, bf16[768,768]{1,0:T(8,128)(2,1)} %refs_1_.1, bf16[768,768]{1,0:T(8,128)(2,1)} %refs_2_.1, bf16[768,768]{1,0:T(8,128)(2,1)} %collective-permute-done.1.refs_3_, ...), custom_call_target="tpu_custom_call" | custom-call | tf_op jit(solution)/shard_map/own_heads/pallas_call | solution.py:463
  30.4 10.4 %arrange_project.1 = (bf16[1024,1536]{1,0:T(8,128)(2,1)}, bf16[1024,1536]{1,0:T(8,128)(2,1)}, bf16[1024,576]{1,0:T(8,128)(2,1)}) custom-call(s32[1]{0:T(128)} %bitcast.me_ref, s32[4,256]{1,0:T(4,128)} %reshape.145.order_ref, f32[1,1536]{1,0:T(1,128)} %reshape.146.gain_ref, bf16[1536,576]{1,0:T(8,128)(2,1)} %own_heads.1.weight_ref, ...), custom_call_target="tpu_custom_call" | custom-call | flops 5033164800 | bytes 12582912 | tf_op jit(solution)/shard_map/arrange_project/pallas_call | solution.py:493
  40.9 13.3 %attend.1 = (bf16[1024,192]{1,0:T(8,128)(2,1)}, f32[1024,192]{1,0:T(8,128)}, f32[3,1024]{1,0:T(4,128)}) custom-call(s32[1]{0:T(128)} %bitcast.me_ref, s32[4]{0:T(128)} %bitcast.335, bf16[1024,576]{1,0:T(8,128)(2,1)} %get-tuple-element.313.qkv_ref, f32[3,5,256,256]{3,2,1,0:T(8,128)} %bias_strips.1.bias_ref), custom_call_target="tpu_custom_call" | custom-call | flops 3221225472 | bytes 3145728 | tf_op jit(solution)/shard_map/attend/pallas_call | solution.py:520
  72.3 4.9 %multiply_reduce_fusion = (f32[1024]{0:T(1024)S(1)}, f32[1024,1536]{1,0:T(8,128)S(1)}) fusion(bf16[192,1536]{1,0:T(8,128)(2,1)S(1)} %copy-done.42, bf16[192,1536]{1,0:T(8,128)(2,1)S(1)} %get-tuple-element.677, bf16[192,1536]{1,0:T(8,128)(2,1)S(1)} %get-tuple-element.676, bf16[192,1536]{1,0:T(8,128)(2,1)S(1)} %get-tuple-element.675, ...), kind=kOutput, calls=%fused_computation.6 | convolution fusion | flops 2448948224 | bytes 13373440 | tf_op jit(solution)/shard_map/dot_general | solution.py:39
  77.2 9.9 %fusion.90 = f32[1024,2048]{0,1:T(8,128)} fusion(bf16[1536,2048]{1,0:T(8,128)(2,1)S(1)} %bitcast.325, f32[1024,1536]{1,0:T(8,128)S(1)} %get-tuple-element.769, f32[1536]{0:T(1024)S(1)} %copy-done.103, f32[1024]{0:T(1024)S(1)} %add_rsqrt_fusion), kind=kOutput, calls=%fused_computation.320 | convolution fusion | flops 6447169536 | bytes 20981760 | tf_op jit(solution)/shard_map/dot_general | solution.py:39
  87.1 12.4 %fusion.6 = (bf16[1024,1024]{0,1:T(8,128)(2,1)S(1)}, bf16[1024,1024]{0,1:T(8,128)(2,1)S(1)}, bf16[1024,1024]{0,1:T(8,128)(2,1)}) fusion(f32[1024,2048]{0,1:T(8,128)} %fusion.90, bf16[1024,1536]{1,0:T(8,128)(2,1)} %constant_dynamic-update-slice_fusion.6, s32[]{:T(128)S(6)} %select_n.274, bf16[1984,1536]{1,0:T(8,128)(2,1)} %param.27, ...), kind=kOutput, calls=%fused_computation.20 | convolution fusion | flops 3257925632 | bytes 24313860 | tf_op jit(solution)/shard_map/dot_general | solution.py:39
  99.5 11.1 %convolution_convert_fusion = bf16[1536,2048]{1,0:T(8,128)(2,1)S(1)} fusion(f32[1024,1536]{1,0:T(8,128)} %copy-done.59, f32[1536]{0:T(1024)S(1)} %copy-done.103, f32[1024]{0:T(1024)S(1)} %add_rsqrt_fusion, bf16[1024,1024]{0,1:T(8,128)(2,1)S(1)} %get-tuple-element.625, bf16[1024,1024]{0,1:T(8,128)(2,1)S(1)} %get-tuple-element.624), kind=kOutput, calls=%fused_computation | convolution fusion | flops 6458703872 | bytes 16787456 | tf_op jit(solution)/shard_map/dot_general | solution.py:39
  112.2 6.0 %convolution_convert_fusion.4 = bf16[1536,1024]{1,0:T(8,128)(2,1)S(1)} fusion(bf16[1024,1536]{1,0:T(8,128)(2,1)} %constant_dynamic-update-slice_fusion.6, bf16[1024,1024]{0,1:T(8,128)(2,1)S(1)} %copy-done.118), kind=kOutput, calls=%fused_computation.28 | convolution fusion | flops 3222798336 | bytes 8388608 | tf_op jit(solution)/shard_map/dot_general | solution.py:39
  121.5 5.9 %collective-permute-start.15 = (bf16[4,24,3072]{2,1,0:T(8,128)(2,1)S(1)}, bf16[4,24,3072]{2,1,0:T(8,128)(2,1)S(1)}, u32[]{:S(2)}, u32[]{:S(2)}) collective-permute-start(bf16[4,24,3072]{2,1,0:T(8,128)(2,1)S(1)} %pad_maximum_fusion.8), channel_id=1, source_target_pairs={{0,8},{8,16},{16,24},{24,28},{28,20},{20,12},{12,4},{4,0},{1,9},{9... | collective-permute-start | bytes 1769480 | tf_op jit(solution)/shard_map/ppermute | solution.py:555
  127.4 7.1 %convolution_convert_fusion.1 = bf16[1024,1536]{1,0:T(8,128)(2,1)S(1)} fusion(bf16[1024,2048]{0,1:T(8,128)(2,1)S(1)} %pad_maximum_fusion.1, bf16[1536,2048]{1,0:T(8,128)(2,1)S(1)} %bitcast.325), kind=kOutput, calls=%fused_computation.25 | convolution fusion | flops 6444023808 | bytes 13631488 | tf_op jit(solution)/shard_map/dot_general | solution.py:39
  134.5 6.7 %collective-permute-done.15 = bf16[4,24,3072]{2,1,0:T(8,128)(2,1)S(1)} collective-permute-done((bf16[4,24,3072]{2,1,0:T(8,128)(2,1)S(1)}, bf16[4,24,3072]{2,1,0:T(8,128)(2,1)S(1)}, u32[]{:S(2)}, u32[]{:S(2)}) %collective-permute-start.15) | collective-permute-done | bytes 589856 | tf_op jit(solution)/shard_map/ppermute | solution.py:555
  145.5 6.4 %convolution_convert_fusion.3 = bf16[1024,1536]{1,0:T(8,128)(2,1)} fusion(bf16[1024,1024]{0,1:T(8,128)(2,1)S(1)} %copy-done.119, s32[]{:T(128)S(6)} %select_n.274, bf16[1984,1536]{1,0:T(8,128)(2,1)S(1)} %bitcast.334, bf16[64,1536]{1,0:T(8,128)(2,1)S(1)} %copy-done.83, bf16[64,1536]{1,0:T(8,128)(2,1)S(1)} %broadcast.122), kind=kOutput, calls=%fused_computation.27 | convolution fusion | flops 3232235520 | bytes 11730948 | tf_op jit(solution)/shard_map/dot_general | solution.py:39
  152.2 6.9 %collective-permute-done.17 = bf16[4,24,3072]{2,1,0:T(8,128)(2,1)S(1)} collective-permute-done((bf16[4,24,3072]{2,1,0:T(8,128)(2,1)S(1)}, bf16[4,24,3072]{2,1,0:T(8,128)(2,1)S(1)}, u32[]{:S(2)}, u32[]{:S(2)}) %collective-permute-start.17) | collective-permute-done | bytes 589856 | tf_op jit(solution)/shard_map/ppermute | solution.py:555
  165.7 13.7 %collective-permute-done.22 = bf16[256,1536]{1,0:T(8,128)(2,1)S(1)} collective-permute-done((bf16[256,1536]{1,0:T(8,128)(2,1)S(1)}, bf16[256,1536]{1,0:T(8,128)(2,1)S(1)}, u32[]{:S(2)}, u32[]{:S(2)}) %collective-permute-start.22) | collective-permute-done | bytes 786464 | tf_op jit(solution)/shard_map/ppermute | solution.py:415
  206.3 17.7 %attend_back.1 = (bf16[1024,576]{1,0:T(8,128)(2,1)}, f32[32,128]{1,0:T(8,128)}) custom-call(s32[1]{0:T(128)} %bitcast.me_ref, s32[4]{0:T(128)} %bitcast.336, bf16[1024,576]{1,0:T(8,128)(2,1)} %get-tuple-element.313.qkv_ref, f32[3,5,256,256]{3,2,1,0:T(8,128)} %bias_strips.1.bias_ref, f32[3,1024]{1,0:T(4,128)} %get-tuple-element.368.lse_ref, ...), custom_call_target="tpu_custom_call" | custom-call | flops 8053063680 | bytes 3145728 | tf_op jit(solution)/shard_map/attend_back/pallas_call | solution.py:765
  230.1 4.9 %collective-permute-start.31 = (bf16[4,24,3072]{2,1,0:T(8,128)(2,1)S(1)}, bf16[4,24,3072]{2,1,0:T(8,128)(2,1)S(1)}, u32[]{:S(2)}, u32[]{:S(2)}) collective-permute-start(bf16[4,24,3072]{2,1,0:T(8,128)(2,1)S(1)} %maximum_add_fusion.8), channel_id=1, source_target_pairs={{0,8},{8,16},{16,24},{24,28},{28,20},{20,12},{12,4},{4,0},{1,9},{9... | collective-permute-start | bytes 1769480 | tf_op jit(solution)/shard_map/ppermute | solution.py:555
  242.8 4.8 %collective-permute-done.31 = bf16[4,24,3072]{2,1,0:T(8,128)(2,1)S(1)} collective-permute-done((bf16[4,24,3072]{2,1,0:T(8,128)(2,1)S(1)}, bf16[4,24,3072]{2,1,0:T(8,128)(2,1)S(1)}, u32[]{:S(2)}, u32[]{:S(2)}) %collective-permute-start.31) | collective-permute-done | bytes 589856 | tf_op jit(solution)/shard_map/ppermute | solution.py:555
  258.7 5.2 %collective-permute-done.35 = bf16[4,24,3072]{2,1,0:T(8,128)(2,1)S(1)} collective-permute-done((bf16[4,24,3072]{2,1,0:T(8,128)(2,1)S(1)}, bf16[4,24,3072]{2,1,0:T(8,128)(2,1)S(1)}, u32[]{:S(2)}, u32[]{:S(2)}) %collective-permute-start.35) | collective-permute-done | bytes 589856 | tf_op jit(solution)/shard_map/ppermute | solution.py:555
  293.3 4.6 collective-permute-done.48
  307.5 4.0 collective-permute-done.52.refs_2_.refs_4_
  313.6 4.3 collective-permute-done.50.refs_6_
  333.7 4.1 collective-permute-done.62.refs_10_
  357.6 4.9 %collective-permute-done.77 = f32[3456]{0:T(1024)S(1)} collective-permute-done((f32[3456]{0:T(1024)S(1)}, f32[3456]{0:T(1024)S(1)}, u32[]{:S(2)}, u32[]{:S(2)}) %collective-permute-start.77) | collective-permute-done | bytes 13856 | tf_op jit(solution)/shard_map/ppermute | solution.py:683
  365.1 5.9 %collective-permute-done.84 = f32[3456]{0:T(1024)S(1)} collective-permute-done((f32[3456]{0:T(1024)S(1)}, f32[3456]{0:T(1024)S(1)}, u32[]{:S(2)}, u32[]{:S(2)}) %collective-permute-start.84) | collective-permute-done | bytes 13856 | tf_op jit(solution)/shard_map/ppermute | solution.py:683
  412.6 4.5 fusion.12
  419.7 4.8 collective-permute-done.97.refs_13_.refs_25_
  428.5 9.0 %collective-permute-done.103.refs_12_ = bf16[24,3072]{1,0:T(8,128)(2,1)S(1)} collective-permute-done((bf16[24,3072]{1,0:T(8,128)(2,1)S(1)}, bf16[24,3072]{1,0:T(8,128)(2,1)S(1)}, u32[]{:S(2)}, u32[]{:S(2)}) %collective-permute-start.103) | collective-permute-done | bytes 147488 | tf_op jit(solution)/shard_map/ppermute | solution.py:555
  445.7 5.6 %collective-permute-done.108.refs_15_ = bf16[24,3072]{1,0:T(8,128)(2,1)S(1)} collective-permute-done((bf16[24,3072]{1,0:T(8,128)(2,1)S(1)}, bf16[24,3072]{1,0:T(8,128)(2,1)S(1)}, u32[]{:S(2)}, u32[]{:S(2)}) %collective-permute-start.108) | collective-permute-done | bytes 147488 | tf_op jit(solution)/shard_map/ppermute | solution.py:558
  452.0 4.4 place_heads.1
  457.9 5.3 %place_gate.1 = f32[384,3968]{1,0:T(8,128)} custom-call(s32[1]{0:T(128)} %bitcast.116.spot_ref, bf16[24,6144]{1,0:T(8,128)(2,1)} %copy-done.13, bf16[24,6144]{1,0:T(8,128)(2,1)} %copy-done.12, bf16[24,6144]{1,0:T(8,128)(2,1)} %copy-done.22, bf16[24,6144]{1,0:T(8,128)(2,1)} %copy-done.23, bf16[24,6144]{1,0:T(8,128)(2,1)} %copy-done.24, ...), custom_call_target="tpu_custom_call" | custom-call | tf_op jit(solution)/shard_map/place_gate/pallas_call | solution.py:850
  464.8 10.7 %place.1 = (f32[384,3968]{1,0:T(8,128)}, f32[3968,384]{1,0:T(8,128)}) custom-call(s32[1]{0:T(128)} %bitcast.116.spot_ref, bf16[24,6144]{1,0:T(8,128)(2,1)} %copy-done.13, bf16[24,6144]{1,0:T(8,128)(2,1)} %copy-done.12, bf16[24,6144]{1,0:T(8,128)(2,1)} %copy-done.33, bf16[24,6144]{1,0:T(8,128)(2,1)} %copy-done.32, bf16[24,6144]{1,0:T(8,128)(2,1)} %copy-done.22, ...), custom_call_target="tpu_custom_call" | custom-call | tf_op jit(solution)/shard_map/place/pallas_call | solution.py:869
  (588 shorter events, 245.0 us)
Async XLA Ops:
  1.7 21.0 %collective-permute-start = (bf16[256,1536]{1,0:T(8,128)(2,1)}, bf16[256,1536]{1,0:T(8,128)(2,1)}, u32[]{:S(2)}, u32[]{:S(2)}) collective-permute-start(bf16[256,1536]{1,0:T(8,128)(2,1)} %refs_0_.3), channel_id=1, source_target_pairs={{0,2},{2,0},{1,3},{3,1},{4,6},{6,4},{5,7},{7,5},{8,10},{10,8},{9,1... | collective-permute-start | bytes 2359304 | tf_op jit(solution)/shard_map/ppermute | solution.py:415
  4.3 23.8 %collective-permute-start.4 = (bf16[256,1536]{1,0:T(8,128)(2,1)}, bf16[256,1536]{1,0:T(8,128)(2,1)}, u32[]{:S(2)}, u32[]{:S(2)}) collective-permute-start(bf16[256,1536]{1,0:T(8,128)(2,1)} %refs_0_.3), channel_id=1, source_target_pairs={{0,1},{1,0},{2,3},{3,2},{4,5},{5,4},{6,7},{7,6},{8,9},{9,8},{10,11... | collective-permute-start | bytes 2359304 | tf_op jit(solution)/shard_map/ppermute | solution.py:412
  22.7 31.4 %collective-permute-start.6 = (bf16[384,1536]{1,0:T(8,128)(2,1)}, bf16[384,1536]{1,0:T(8,128)(2,1)}, u32[]{:S(2)}, u32[]{:S(2)}) collective-permute-start(bf16[384,1536]{1,0:T(8,128)(2,1)} %param.22), channel_id=1, source_target_pairs={{0,1},{1,0},{2,3},{3,2},{4,5},{5,4},{6,7},{7,6},{8,9},{9,8},{10,11... | collective-permute-start | bytes 3538952 | tf_op jit(solution)/shard_map/ppermute | solution.py:412
  23.3 40.6 %collective-permute-start.9 = (bf16[768,2048]{1,0:T(8,128)(2,1)}, bf16[768,2048]{1,0:T(8,128)(2,1)}, u32[]{:S(2)}, u32[]{:S(2)}) collective-permute-start(bf16[768,2048]{1,0:T(8,128)(2,1)} %pad_maximum_fusion.3), channel_id=1, source_target_pairs={{0,1},{1,0},{2,3},{3,2},{4,5},{5,4},{6,7},{7,6},{8,9},{9,8},{10,11... | collective-permute-start | bytes 9437192 | tf_op jit(solution)/shard_map/ppermute | solution.py:412
  26.3 28.3 %collective-permute-start.12 = (bf16[256,1536]{1,0:T(8,128)(2,1)}, bf16[256,1536]{1,0:T(8,128)(2,1)S(1)}, u32[]{:S(2)}, u32[]{:S(2)}) collective-permute-start(bf16[256,1536]{1,0:T(8,128)(2,1)} %param.15), channel_id=1, source_target_pairs={{0,2},{2,0},{1,3},{3,1},{4,6},{6,4},{5,7},{7,5},{8,10},{10,8},{9,1... | collective-permute-start | bytes 2359304 | tf_op jit(solution)/shard_map/ppermute | solution.py:415
  28.1 27.0 %collective-permute-start.11 = (bf16[256,1536]{1,0:T(8,128)(2,1)}, bf16[256,1536]{1,0:T(8,128)(2,1)}, u32[]{:S(2)}, u32[]{:S(2)}) collective-permute-start(bf16[256,1536]{1,0:T(8,128)(2,1)} %param.15), channel_id=1, source_target_pairs={{0,1},{1,0},{2,3},{3,2},{4,5},{5,4},{6,7},{7,6},{8,9},{9,8},{10,11... | collective-permute-start | bytes 2359304 | tf_op jit(solution)/shard_map/ppermute | solution.py:412
  54.2 15.8 %collective-permute-start.8 = (bf16[1024,192]{1,0:T(8,128)(2,1)}, bf16[1024,192]{1,0:T(8,128)(2,1)}, u32[]{:S(2)}, u32[]{:S(2)}) collective-permute-start(bf16[1024,192]{1,0:T(8,128)(2,1)} %get-tuple-element.317), channel_id=1, source_target_pairs={{0,2},{2,0},{1,3},{3,1},{4,6},{6,4},{5,7},{7,5},{8,10},{10,8},{9,1... | collective-permute-start | bytes 1179656 | tf_op jit(solution)/shard_map/ppermute | solution.py:415
  54.6 15.5 %collective-permute-start.13 = (bf16[256,1536]{1,0:T(8,128)(2,1)S(1)}, bf16[256,1536]{1,0:T(8,128)(2,1)S(1)}, u32[]{:S(2)}, u32[]{:S(2)}) collective-permute-start(bf16[256,1536]{1,0:T(8,128)(2,1)S(1)} %collective-permute-done.12), channel_id=1, source_target_pairs={{0,1},{1,0},{2,3},{3,2},{4,5},{5,4},{6,7},{7,6},{8,9},{9,8},{10,11... | collective-permute-start | bytes 2359304 | tf_op jit(solution)/shard_map/ppermute | solution.py:412
  121.5 19.7 %collective-permute-start.15 = (bf16[4,24,3072]{2,1,0:T(8,128)(2,1)S(1)}, bf16[4,24,3072]{2,1,0:T(8,128)(2,1)S(1)}, u32[]{:S(2)}, u32[]{:S(2)}) collective-permute-start(bf16[4,24,3072]{2,1,0:T(8,128)(2,1)S(1)} %pad_maximum_fusion.8), channel_id=1, source_target_pairs={{0,8},{8,16},{16,24},{24,28},{28,20},{20,12},{12,4},{4,0},{1,9},{9... | collective-permute-start | bytes 1769480 | tf_op jit(solution)/shard_map/ppermute | solution.py:555
  143.4 15.7 %collective-permute-start.17 = (bf16[4,24,3072]{2,1,0:T(8,128)(2,1)S(1)}, bf16[4,24,3072]{2,1,0:T(8,128)(2,1)S(1)}, u32[]{:S(2)}, u32[]{:S(2)}) collective-permute-start(bf16[4,24,3072]{2,1,0:T(8,128)(2,1)S(1)} %maximum_add_fusion), channel_id=1, source_target_pairs={{0,8},{8,16},{16,24},{24,28},{28,20},{20,12},{12,4},{4,0},{1,9},{9... | collective-permute-start | bytes 1769480 | tf_op jit(solution)/shard_map/ppermute | solution.py:555
  160.6 18.8 %collective-permute-start.22 = (bf16[256,1536]{1,0:T(8,128)(2,1)S(1)}, bf16[256,1536]{1,0:T(8,128)(2,1)S(1)}, u32[]{:S(2)}, u32[]{:S(2)}) collective-permute-start(bf16[256,1536]{1,0:T(8,128)(2,1)S(1)} %get-tuple-element.349), channel_id=1, source_target_pairs={{0,2},{2,0},{1,3},{3,1},{4,6},{6,4},{5,7},{7,5},{8,10},{10,8},{9,1... | collective-permute-start | bytes 2359304 | tf_op jit(solution)/shard_map/ppermute | solution.py:415
  162.2 17.4 %collective-permute-start.20 = (bf16[4,24,3072]{2,1,0:T(8,128)(2,1)S(1)}, bf16[4,24,3072]{2,1,0:T(8,128)(2,1)S(1)}, u32[]{:S(2)}, u32[]{:S(2)}) collective-permute-start(bf16[4,24,3072]{2,1,0:T(8,128)(2,1)S(1)} %maximum_add_fusion.2), channel_id=1, source_target_pairs={{0,8},{8,16},{16,24},{24,28},{28,20},{20,12},{12,4},{4,0},{1,9},{9... | collective-permute-start | bytes 1769480 | tf_op jit(solution)/shard_map/ppermute | solution.py:555
  163.9 15.7 %collective-permute-start.21 = (bf16[4,24,3072]{2,1,0:T(8,128)(2,1)S(1)}, bf16[4,24,3072]{2,1,0:T(8,128)(2,1)S(1)}, u32[]{:S(2)}, u32[]{:S(2)}) collective-permute-start(bf16[4,24,3072]{2,1,0:T(8,128)(2,1)S(1)} %maximum_add_fusion.3), channel_id=1, source_target_pairs={{8,0},{16,8},{24,16},{28,24},{20,28},{12,20},{4,12},{0,4},{9,1},{1... | collective-permute-start | bytes 1769480 | tf_op jit(solution)/shard_map/ppermute | solution.py:558
  202.8 22.0 %collective-permute-start.33 = (bf16[256,1536]{1,0:T(8,128)(2,1)S(1)}, bf16[256,1536]{1,0:T(8,128)(2,1)}, u32[]{:S(2)}, u32[]{:S(2)}) collective-permute-start(bf16[256,1536]{1,0:T(8,128)(2,1)S(1)} %copy-done.11), channel_id=1, source_target_pairs={{0,1},{1,0},{2,3},{3,2},{4,5},{5,4},{6,7},{7,6},{8,9},{9,8},{10,11... | collective-permute-start | bytes 2359304 | tf_op jit(solution)/shard_map/ppermute | solution.py:412
  202.8 24.1 %collective-permute-start.30 = (bf16[256,1536]{1,0:T(8,128)(2,1)S(1)}, bf16[256,1536]{1,0:T(8,128)(2,1)}, u32[]{:S(2)}, u32[]{:S(2)}) collective-permute-start(bf16[256,1536]{1,0:T(8,128)(2,1)S(1)} %copy-done.11), channel_id=1, source_target_pairs={{0,2},{2,0},{1,3},{3,1},{4,6},{6,4},{5,7},{7,5},{8,10},{10,8},{9,1... | collective-permute-start | bytes 2359304 | tf_op jit(solution)/shard_map/ppermute | solution.py:415
  204.3 22.5 %collective-permute-start.28 = (bf16[4,24,3072]{2,1,0:T(8,128)(2,1)}, bf16[4,24,3072]{2,1,0:T(8,128)(2,1)}, u32[]{:S(2)}, u32[]{:S(2)}) collective-permute-start(bf16[4,24,3072]{2,1,0:T(8,128)(2,1)} %maximum_add_fusion.6), channel_id=1, source_target_pairs={{0,8},{8,16},{16,24},{24,28},{28,20},{20,12},{12,4},{4,0},{1,9},{9... | collective-permute-start | bytes 1769480 | tf_op jit(solution)/shard_map/ppermute | solution.py:555
  205.1 21.8 %collective-permute-start.29 = (bf16[4,24,3072]{2,1,0:T(8,128)(2,1)}, bf16[4,24,3072]{2,1,0:T(8,128)(2,1)}, u32[]{:S(2)}, u32[]{:S(2)}) collective-permute-start(bf16[4,24,3072]{2,1,0:T(8,128)(2,1)} %maximum_add_fusion.7), channel_id=1, source_target_pairs={{8,0},{16,8},{24,16},{28,24},{20,28},{12,20},{4,12},{0,4},{9,1},{1... | collective-permute-start | bytes 1769480 | tf_op jit(solution)/shard_map/ppermute | solution.py:558
  230.1 17.5 %collective-permute-start.31 = (bf16[4,24,3072]{2,1,0:T(8,128)(2,1)S(1)}, bf16[4,24,3072]{2,1,0:T(8,128)(2,1)S(1)}, u32[]{:S(2)}, u32[]{:S(2)}) collective-permute-start(bf16[4,24,3072]{2,1,0:T(8,128)(2,1)S(1)} %maximum_add_fusion.8), channel_id=1, source_target_pairs={{0,8},{8,16},{16,24},{24,28},{28,20},{20,12},{12,4},{4,0},{1,9},{9... | collective-permute-start | bytes 1769480 | tf_op jit(solution)/shard_map/ppermute | solution.py:555
  236.7 34.4 %collective-permute-start.58 = (bf16[2,256,1536]{2,1,0:T(8,128)(2,1)}, bf16[2,256,1536]{2,1,0:T(8,128)(2,1)}, u32[]{:S(2)}, u32[]{:S(2)}) collective-permute-start(bf16[2,256,1536]{2,1,0:T(8,128)(2,1)} %pad_maximum_fusion.7), channel_id=1, source_target_pairs={{0,1},{1,0},{2,3},{3,2},{4,5},{5,4},{6,7},{7,6},{8,9},{9,8},{10,11... | collective-permute-start | bytes 4718600 | tf_op jit(solution)/shard_map/ppermute | solution.py:412
  286.1 33.8 %collective-permute-start.61 = (bf16[256,1536]{1,0:T(8,128)(2,1)S(1)}, bf16[256,1536]{1,0:T(8,128)(2,1)S(1)}, u32[]{:S(2)}, u32[]{:S(2)}) collective-permute-start(bf16[256,1536]{1,0:T(8,128)(2,1)S(1)} %get-tuple-element.455), channel_id=1, source_target_pairs={{0,2},{2,0},{1,3},{3,1},{4,6},{6,4},{5,7},{7,5},{8,10},{10,8},{9,1... | collective-permute-start | bytes 2359304 | tf_op jit(solution)/shard_map/ppermute | solution.py:415
  337.7 18.2 %collective-permute-start.78 = (bf16[24,6144]{1,0:T(8,128)(2,1)S(1)}, bf16[24,6144]{1,0:T(8,128)(2,1)}, u32[]{:S(2)}, u32[]{:S(2)}) collective-permute-start(bf16[24,6144]{1,0:T(8,128)(2,1)S(1)} %collective-permute-done.56.refs_4_.refs_8_), channel_id=1, source_target_pairs={{0,8},{8,16},{16,24},{24,28},{28,20},{20,12},{12,4},{4,0},{1,9},{9... | collective-permute-start | bytes 884744 | tf_op jit(solution)/shard_map/ppermute | solution.py:555
  346.2 25.1 %collective-permute-start.69 = (bf16[24,6144]{1,0:T(8,128)(2,1)}, bf16[24,6144]{1,0:T(8,128)(2,1)}, u32[]{:S(2)}, u32[]{:S(2)}) collective-permute-start(bf16[24,6144]{1,0:T(8,128)(2,1)} %collective-permute-done.62.refs_10_), channel_id=1, source_target_pairs={{0,8},{8,16},{16,24},{24,28},{28,20},{20,12},{12,4},{4,0},{1,9},{9... | collective-permute-start | bytes 884744 | tf_op jit(solution)/shard_map/ppermute | solution.py:555
  347.3 24.2 %collective-permute-start.70 = (bf16[24,6144]{1,0:T(8,128)(2,1)}, bf16[24,6144]{1,0:T(8,128)(2,1)}, u32[]{:S(2)}, u32[]{:S(2)}) collective-permute-start(bf16[24,6144]{1,0:T(8,128)(2,1)} %collective-permute-done.63.refs_11_), channel_id=1, source_target_pairs={{8,0},{16,8},{24,16},{28,24},{20,28},{12,20},{4,12},{0,4},{9,1},{1... | collective-permute-start | bytes 884744 | tf_op jit(solution)/shard_map/ppermute | solution.py:558
  362.5 21.8 %collective-permute-start.88 = (bf16[24,6144]{1,0:T(8,128)(2,1)}, bf16[24,6144]{1,0:T(8,128)(2,1)S(1)}, u32[]{:S(2)}, u32[]{:S(2)}) collective-permute-start(bf16[24,6144]{1,0:T(8,128)(2,1)} %collective-permute-done.78.refs_6_.refs_12_), channel_id=1, source_target_pairs={{0,8},{8,16},{16,24},{24,28},{28,20},{20,12},{12,4},{4,0},{1,9},{9... | collective-permute-start | bytes 884744 | tf_op jit(solution)/shard_map/ppermute | solution.py:555
  362.5 23.8 %collective-permute-start.89 = (bf16[24,6144]{1,0:T(8,128)(2,1)}, bf16[24,6144]{1,0:T(8,128)(2,1)S(1)}, u32[]{:S(2)}, u32[]{:S(2)}) collective-permute-start(bf16[24,6144]{1,0:T(8,128)(2,1)} %collective-permute-done.79.refs_7_.refs_13_), channel_id=1, source_target_pairs={{8,0},{16,8},{24,16},{28,24},{20,28},{12,20},{4,12},{0,4},{9,1},{1... | collective-permute-start | bytes 884744 | tf_op jit(solution)/shard_map/ppermute | solution.py:558
  371.0 39.5 %collective-permute-start.98 = (bf16[256,1536]{1,0:T(8,128)(2,1)}, bf16[256,1536]{1,0:T(8,128)(2,1)S(1)}, u32[]{:S(2)}, u32[]{:S(2)}) collective-permute-start(bf16[256,1536]{1,0:T(8,128)(2,1)} %fusion.44), channel_id=1, source_target_pairs={{0,2},{2,0},{1,3},{3,1},{4,6},{6,4},{5,7},{7,5},{8,10},{10,8},{9,1... | collective-permute-start | bytes 2359304 | tf_op jit(solution)/shard_map/ppermute | solution.py:415
  381.0 16.2 %collective-permute-start.80 = (bf16[24,6144]{1,0:T(8,128)(2,1)}, bf16[24,6144]{1,0:T(8,128)(2,1)S(1)}, u32[]{:S(2)}, u32[]{:S(2)}) collective-permute-start(bf16[24,6144]{1,0:T(8,128)(2,1)} %collective-permute-done.69.refs_14_), channel_id=1, source_target_pairs={{0,8},{8,16},{16,24},{24,28},{28,20},{20,12},{12,4},{4,0},{1,9},{9... | collective-permute-start | bytes 884744 | tf_op jit(solution)/shard_map/ppermute | solution.py:555
  424.5 17.2 %collective-permute-start.101 = (bf16[24,6144]{1,0:T(8,128)(2,1)S(1)}, bf16[24,6144]{1,0:T(8,128)(2,1)S(1)}, u32[]{:S(2)}, u32[]{:S(2)}) collective-permute-start(bf16[24,6144]{1,0:T(8,128)(2,1)S(1)} %collective-permute-done.90.refs_22_), channel_id=1, source_target_pairs={{0,8},{8,16},{16,24},{24,28},{28,20},{20,12},{12,4},{4,0},{1,9},{9... | collective-permute-start | bytes 884744 | tf_op jit(solution)/shard_map/ppermute | solution.py:555
  439.6 16.8 %collective-permute-start.109 = (bf16[24,6144]{1,0:T(8,128)(2,1)}, bf16[24,6144]{1,0:T(8,128)(2,1)S(1)}, u32[]{:S(2)}, u32[]{:S(2)}) collective-permute-start(bf16[24,6144]{1,0:T(8,128)(2,1)} %collective-permute-done.96.refs_12_.refs_24_), channel_id=1, source_target_pairs={{0,8},{8,16},{16,24},{24,28},{28,20},{20,12},{12,4},{4,0},{1,9},{9... | collective-permute-start | bytes 884744 | tf_op jit(solution)/shard_map/ppermute | solution.py:555
  439.7 16.7 %collective-permute-start.110 = (bf16[24,6144]{1,0:T(8,128)(2,1)}, bf16[24,6144]{1,0:T(8,128)(2,1)S(1)}, u32[]{:S(2)}, u32[]{:S(2)}) collective-permute-start(bf16[24,6144]{1,0:T(8,128)(2,1)} %collective-permute-done.97.refs_13_.refs_25_), channel_id=1, source_target_pairs={{8,0},{16,8},{24,16},{28,24},{20,28},{12,20},{4,12},{0,4},{9,1},{1... | collective-permute-start | bytes 884744 | tf_op jit(solution)/shard_map/ppermute | solution.py:558
  441.7 21.5 %collective-permute-start.105 = (bf16[24,6144]{1,0:T(8,128)(2,1)S(1)}, bf16[24,6144]{1,0:T(8,128)(2,1)S(1)}, u32[]{:S(2)}, u32[]{:S(2)}) collective-permute-start(bf16[24,6144]{1,0:T(8,128)(2,1)S(1)} %collective-permute-done.101.refs_26_), channel_id=1, source_target_pairs={{0,8},{8,16},{16,24},{24,28},{28,20},{20,12},{12,4},{4,0},{1,9},{9... | collective-permute-start | bytes 884744 | tf_op jit(solution)/shard_map/ppermute | solution.py:555
  441.8 21.4 %collective-permute-start.106 = (bf16[24,6144]{1,0:T(8,128)(2,1)S(1)}, bf16[24,6144]{1,0:T(8,128)(2,1)S(1)}, u32[]{:S(2)}, u32[]{:S(2)}) collective-permute-start(bf16[24,6144]{1,0:T(8,128)(2,1)S(1)} %collective-permute-done.102.refs_27_), channel_id=1, source_target_pairs={{8,0},{16,8},{24,16},{28,24},{20,28},{12,20},{4,12},{0,4},{9,1},{1... | collective-permute-start | bytes 884744 | tf_op jit(solution)/shard_map/ppermute | solution.py:558
  (203 other events, 2279.6 us)
